TPU v7x, 32 devices: a whole 2x2x4 slice. The times are simulated.
32 devices in a mesh: dp: 4 (over y, core), expert: 8 (over z, x).
Axes of the slice: x: 2, y: 2, z: 4, core: 2. Of those that a mesh axis runs over, the one named last changes fastest.
Arguments:
- tokens: bfloat16 [4096, 2048], P(('dp', 'expert')), may hold values from -6 to 6
- seq_lengths: int32 [4], replicated, may hold values from 256 to 1024, as said below
- routes: int32 [4096, 8], P(('dp', 'expert')), may hold values from 0 to 15, all different within a row; in each aligned block of 128 rows (0 to 127, 128 to 255, ...) at most 72 rows name the same one
- w_query: bfloat16 [2048, 2048], P(('dp', 'expert')), may hold values from -0.125 to 0.125
- w_key: bfloat16 [2048, 2048], P(('dp', 'expert')), may hold values from -0.125 to 0.125
- w_value: bfloat16 [2048, 2048], P(('dp', 'expert')), may hold values from -0.125 to 0.125
- w_out: bfloat16 [2048, 2048], P(('dp', 'expert')), may hold values from -2 to 2
- gain_attn: bfloat16 [2048], P(('dp', 'expert')), may hold values from 0.5 to 1.5
- gain_query: bfloat16 [2048], P(('dp', 'expert')), may hold values from 0.5 to 1.5
- gain_key: bfloat16 [2048], P(('dp', 'expert')), may hold values from 0.5 to 1.5
- gain_ffn: bfloat16 [2048], P(('dp', 'expert')), may hold values from 0.5 to 1.5
- w_router: bfloat16 [2048, 16], P(('dp', 'expert')), may hold values from -0.0625 to 0.0625
- w_gate: bfloat16 [16, 2048, 1024], P('expert'), may hold values from -0.125 to 0.125
- w_up: bfloat16 [16, 2048, 1024], P('expert'), may hold values from -0.125 to 0.125
- w_down_t: bfloat16 [16, 2048, 1024], P('expert'), may hold values from -3 to 3
- cotangent: bfloat16 [4096, 2048], P(('dp', 'expert')), may hold values from -6 to 6
Outputs:
- output: bfloat16 [4096, 2048], P(('dp', 'expert'))
- input_grad: bfloat16 [4096, 2048], P(('dp', 'expert'))
- grad_query: float32 [2048, 2048], P(('dp', 'expert'))
- grad_key: float32 [2048, 2048], P(('dp', 'expert'))
- grad_value: float32 [2048, 2048], P(('dp', 'expert'))
- grad_out: float32 [2048, 2048], P(('dp', 'expert'))
- grad_gain_attn: float32 [2048], P(('dp', 'expert'))
- grad_gain_query: float32 [2048], P(('dp', 'expert'))
- grad_gain_key: float32 [2048], P(('dp', 'expert'))
- grad_gain_ffn: float32 [2048], P(('dp', 'expert'))
- grad_router: float32 [2048, 16], P(('dp', 'expert'))
- grad_gate: float32 [16, 2048, 1024], P('expert', None, 'dp')
- grad_up: float32 [16, 2048, 1024], P('expert', None, 'dp')
- grad_down_t: float32 [16, 2048, 1024], P('expert', None, 'dp')
- rms_resid: float32 [], replicated
- rms_moe: float32 [], replicated
Inputs may be any that keep to these rules, and one draw needn't show every extreme that they name: `routes`: in the rows of one device no expert is named by more than 72 rows, a bound that some block reaches. `seq_lengths`: some sequence is full in every draw.
All inputs are finite; a program needn't handle non-finite values.
Results may differ from a plain program's by a relative error of at most 0.02.
Values may be sent and summed in bfloat16 or wider, within the bound.
No kernel may reach another device: no remote copies, remote signals or barrier semaphores. Data moves between devices by JAX's collectives and lax.ppermute only.
A program may use at most 320 MiB of HBM per device.

v0:
```python
import jax
import jax.numpy as jnp
from jax import lax
from jax.sharding import PartitionSpec as P

HEADS = 16
HEAD_DIM = 128
TOP = 8


EPSILON = 1e-05
ROPE_BASE = 10000.0


def norm_rows(values, gain):
    mean_square = jnp.mean(values * values, axis=-1, keepdims=True)
    return values * lax.rsqrt(mean_square + EPSILON) * gain


def rotary(values, positions):
    row_count = values.shape[0]
    half_dim = HEAD_DIM // 2
    frequency = ROPE_BASE ** (-(jnp.arange(half_dim, dtype=jnp.float32) * 2.0) / HEAD_DIM)
    angles = positions.astype(jnp.float32)[:, None] * frequency[None, :]
    cosine = jnp.cos(angles)[:, None, :]
    sine_part = jnp.sin(angles)[:, None, :]
    shaped = values.reshape(row_count, HEADS, HEAD_DIM)
    first_half = shaped[:, :, :half_dim]
    second_half = shaped[:, :, half_dim:]
    turned = jnp.concatenate(
        [
            first_half * cosine - second_half * sine_part,
            second_half * cosine + first_half * sine_part,
        ],
        axis=-1,
    )
    return turned.reshape(row_count, HEADS * HEAD_DIM)


def softmax_rows(scores):
    highest = jnp.max(scores, axis=-1, keepdims=True)
    expos = jnp.exp(scores - highest)
    return expos / jnp.sum(expos, axis=-1, keepdims=True)


def swiglu(gate_vals, up_vals):
    return jax.nn.silu(gate_vals) * up_vals


def matmul_low(left, right):
    return jnp.dot(left, right, preferred_element_type=jnp.float32)


def inner_rows(left, right):
    return lax.dot_general(
        left, right, (((0,), (0,)), ((), ())), preferred_element_type=jnp.float32
    )


def times_transposed(left, right):
    return lax.dot_general(
        left, right, (((1,), (1,)), ((), ())), preferred_element_type=jnp.float32
    )


def masked_scores(query_heads, key_heads, allowed):
    raw = jnp.einsum(
        "qhd,khd->hqk", query_heads, key_heads, preferred_element_type=jnp.float32
    ) * HEAD_DIM ** (-0.5)
    return jnp.where(allowed[None], raw, -1e30)


def body(
    tokens,
    seq_lengths,
    routes,
    w_query,
    w_key,
    w_value,
    w_out,
    gain_attn,
    gain_query,
    gain_key,
    gain_ffn,
    w_router,
    w_gate,
    w_up,
    w_down_t,
    cotangent,
):
    tok_rows, width = tokens.shape
    local_experts = w_gate.shape[0]
    groups = lax.axis_size("expert")
    experts_all = local_experts * groups
    capacity = tok_rows * TOP * 9 // (8 * experts_all)
    seq_rows = groups * tok_rows
    group_place = lax.axis_index("expert")
    seq_index = lax.axis_index("dp")
    positions = group_place * tok_rows + jnp.arange(tok_rows, dtype=jnp.int32)
    seq_length = lax.dynamic_index_in_dim(seq_lengths, seq_index, 0, keepdims=False)
    used = (positions < seq_length).astype(jnp.float32)[:, None]
    gathered = (
        lax.all_gather(w_query, ("dp", "expert"), axis=0, tiled=True),
        lax.all_gather(w_key, ("dp", "expert"), axis=0, tiled=True),
        lax.all_gather(w_value, ("dp", "expert"), axis=0, tiled=True),
        lax.all_gather(w_out, ("dp", "expert"), axis=0, tiled=True),
        lax.all_gather(w_router, ("dp", "expert"), axis=0, tiled=True),
        lax.all_gather(gain_attn, ("dp", "expert"), axis=0, tiled=True),
        lax.all_gather(gain_query, ("dp", "expert"), axis=0, tiled=True),
        lax.all_gather(gain_key, ("dp", "expert"), axis=0, tiled=True),
        lax.all_gather(gain_ffn, ("dp", "expert"), axis=0, tiled=True),
    )
    (
        full_query,
        full_key,
        full_value,
        full_out,
        full_router,
        attn_gain,
        query_gain,
        key_gain,
        ffn_gain,
    ) = gathered
    resid_in = tokens.astype(jnp.float32)
    normed_one, norm_one_back = jax.vjp(norm_rows, resid_in, attn_gain.astype(jnp.float32))
    attn_in = normed_one.astype(jnp.bfloat16)
    query_raw = matmul_low(attn_in, full_query)
    key_raw = matmul_low(attn_in, full_key)
    value_rows = matmul_low(attn_in, full_value).astype(jnp.bfloat16)
    query_rot, query_back = jax.vjp(
        lambda values, gain: rotary(norm_rows(values, gain), positions),
        query_raw,
        query_gain.astype(jnp.float32),
    )
    key_rot, key_back = jax.vjp(
        lambda values, gain: rotary(norm_rows(values, gain), positions),
        key_raw,
        key_gain.astype(jnp.float32),
    )
    query_rows = query_rot.astype(jnp.bfloat16)
    key_rows = key_rot.astype(jnp.bfloat16)
    key_window, value_window = (
        lax.all_gather(key_rows, "expert", axis=0, tiled=True),
        lax.all_gather(value_rows, "expert", axis=0, tiled=True),
    )
    key_positions = jnp.arange(seq_rows, dtype=jnp.int32)
    query_heads = query_rows.reshape(tok_rows, HEADS, HEAD_DIM)
    key_heads = key_window.reshape(-1, HEADS, HEAD_DIM)
    value_heads = value_window.reshape(-1, HEADS, HEAD_DIM)
    allowed = (key_positions[None, :] <= positions[:, None]) & (key_positions[None, :] < seq_length)
    scores = masked_scores(query_heads, key_heads, allowed)
    row_peak = jnp.max(scores, axis=-1, keepdims=True)
    log_total = row_peak + jnp.log(jnp.sum(jnp.exp(scores - row_peak), axis=-1, keepdims=True))
    attn_probs = jnp.exp(scores - log_total).astype(jnp.bfloat16)
    attn_heads = jnp.einsum(
        "hqk,khd->qhd", attn_probs, value_heads, preferred_element_type=jnp.float32
    )
    attn_rows = attn_heads.reshape(tok_rows, width).astype(jnp.bfloat16)
    resid_mid = resid_in + matmul_low(attn_rows, full_out)
    normed_two, norm_two_back = jax.vjp(norm_rows, resid_mid, ffn_gain.astype(jnp.float32))
    ffn_in = normed_two.astype(jnp.bfloat16)
    router_probs, router_back = jax.vjp(softmax_rows, matmul_low(ffn_in, full_router))
    expert_ids = jnp.arange(experts_all, dtype=jnp.int32)
    chosen = (routes[:, :, None] == expert_ids[None, None, :]).astype(jnp.float32)
    route_weights = jnp.sum(chosen * router_probs[:, None, :], axis=2)
    flat_routes = routes.reshape(-1)
    hits = (flat_routes[:, None] == expert_ids[None, :]).astype(jnp.int32)
    earlier = jnp.cumsum(hits, axis=0) - hits
    slot_of = jnp.sum(earlier * hits, axis=1)
    place = flat_routes * capacity + slot_of
    owners = jnp.arange(tok_rows * TOP, dtype=jnp.int32) // TOP
    slot_token = jnp.full((experts_all * capacity,), tok_rows, jnp.int32).at[place].set(owners)
    padded_in = jnp.concatenate([ffn_in, jnp.zeros((1, width), jnp.bfloat16)], axis=0)
    outgoing = padded_in[slot_token].reshape(groups, local_experts * capacity, width)
    arrived = lax.all_to_all(outgoing, "expert", split_axis=0, concat_axis=0, tiled=True)
    expert_in = arrived.reshape(groups, local_experts, capacity, width)
    gate_vals = jnp.einsum("secd,edf->secf", expert_in, w_gate, preferred_element_type=jnp.float32)
    up_vals = jnp.einsum("secd,edf->secf", expert_in, w_up, preferred_element_type=jnp.float32)
    hidden_vals, swiglu_back = jax.vjp(swiglu, gate_vals, up_vals)
    hidden_rows = hidden_vals.astype(jnp.bfloat16)
    expert_out = jnp.einsum(
        "secf,edf->secd", hidden_rows, w_down_t, preferred_element_type=jnp.float32
    ).astype(jnp.bfloat16)
    returned = lax.all_to_all(
        expert_out.reshape(groups, local_experts * capacity, width),
        "expert",
        split_axis=0,
        concat_axis=0,
        tiled=True,
    )
    picked = returned.reshape(experts_all * capacity, width)[place].reshape(tok_rows, TOP, width)
    moe_rows = jnp.sum(route_weights[:, :, None] * picked, axis=1)
    output = (resid_mid + moe_rows).astype(jnp.bfloat16)
    square_resid, square_moe = lax.psum(
        (jnp.sum(used * resid_mid * resid_mid), jnp.sum(used * moe_rows * moe_rows)),
        ("dp", "expert"),
    )
    counted = jnp.sum(seq_lengths).astype(jnp.float32) * width
    rms_resid = jnp.sqrt(square_resid / counted)
    rms_moe = jnp.sqrt(square_moe / counted)
    grad_rows = cotangent.astype(jnp.float32)
    weight_grads = jnp.sum(grad_rows[:, None, :] * picked, axis=2)
    out_grads = (
        (route_weights[:, :, None] * grad_rows[:, None, :])
        .astype(jnp.bfloat16)
        .reshape(tok_rows * TOP, width)
    )
    grad_send = jnp.zeros((experts_all * capacity, width), jnp.bfloat16).at[place].set(out_grads)
    grad_arrived = lax.all_to_all(
        grad_send.reshape(groups, local_experts * capacity, width),
        "expert",
        split_axis=0,
        concat_axis=0,
        tiled=True,
    )
    grad_expert = grad_arrived.reshape(groups, local_experts, capacity, width)
    grad_down = jnp.einsum(
        "secd,secf->edf", grad_expert, hidden_rows, preferred_element_type=jnp.float32
    )
    grad_hidden = jnp.einsum(
        "secd,edf->secf", grad_expert, w_down_t, preferred_element_type=jnp.float32
    )
    grad_gate_vals, grad_up_vals = swiglu_back(grad_hidden)
    gate_low = grad_gate_vals.astype(jnp.bfloat16)
    up_low = grad_up_vals.astype(jnp.bfloat16)
    grad_gate_w = jnp.einsum(
        "secd,secf->edf", expert_in, gate_low, preferred_element_type=jnp.float32
    )
    grad_up_w = jnp.einsum("secd,secf->edf", expert_in, up_low, preferred_element_type=jnp.float32)
    row_grads = jnp.einsum(
        "secf,edf->secd", gate_low, w_gate, preferred_element_type=jnp.float32
    ) + jnp.einsum("secf,edf->secd", up_low, w_up, preferred_element_type=jnp.float32)
    grad_back = lax.all_to_all(
        row_grads.astype(jnp.bfloat16).reshape(groups, local_experts * capacity, width),
        "expert",
        split_axis=0,
        concat_axis=0,
        tiled=True,
    )
    expert_part = jnp.sum(
        grad_back.reshape(experts_all * capacity, width)[place].reshape(tok_rows, TOP, width),
        axis=1,
        dtype=jnp.float32,
    )
    grad_gate_w, grad_up_w, grad_down = (
        lax.psum_scatter(
            grad_gate_w.astype(jnp.bfloat16), "dp", scatter_dimension=2, tiled=True
        ).astype(jnp.float32),
        lax.psum_scatter(
            grad_up_w.astype(jnp.bfloat16), "dp", scatter_dimension=2, tiled=True
        ).astype(jnp.float32),
        lax.psum_scatter(
            grad_down.astype(jnp.bfloat16), "dp", scatter_dimension=2, tiled=True
        ).astype(jnp.float32),
    )
    prob_grads = jnp.sum(chosen * weight_grads[:, :, None], axis=1)
    (logit_grads,) = router_back(prob_grads)
    logit_low = logit_grads.astype(jnp.bfloat16)
    grad_router = inner_rows(ffn_in, logit_low)
    ffn_grads = expert_part + times_transposed(logit_low, full_router)
    mid_from, grad_gain_ffn = norm_two_back(ffn_grads)
    mid_grads = grad_rows + mid_from
    mid_low = mid_grads.astype(jnp.bfloat16)
    grad_out = inner_rows(attn_rows, mid_low)
    attn_grads = times_transposed(mid_low, full_out).astype(jnp.bfloat16)
    attn_grad_heads = attn_grads.reshape(tok_rows, HEADS, HEAD_DIM)
    again_scores = masked_scores(query_heads, key_heads, allowed)
    again_probs = jnp.exp(again_scores - log_total)
    prob_terms = jnp.einsum(
        "qhd,khd->hqk", attn_grad_heads, value_heads, preferred_element_type=jnp.float32
    )
    value_grad_win = jnp.einsum(
        "hqk,qhd->khd",
        again_probs.astype(jnp.bfloat16),
        attn_grad_heads,
        preferred_element_type=jnp.float32,
    )
    score_grads = (
        again_probs * (prob_terms - jnp.sum(again_probs * prob_terms, axis=-1, keepdims=True))
    ).astype(jnp.bfloat16)
    query_grad_rot = jnp.einsum(
        "hqk,khd->qhd", score_grads, key_heads, preferred_element_type=jnp.float32
    ) * HEAD_DIM ** (-0.5)
    key_grad_win = jnp.einsum(
        "hqk,qhd->khd", score_grads, query_heads, preferred_element_type=jnp.float32
    ) * HEAD_DIM ** (-0.5)
    key_grad_own, value_grad_own = (
        lax.psum_scatter(
            key_grad_win.astype(jnp.bfloat16), "expert", scatter_dimension=0, tiled=True
        ).astype(jnp.float32),
        lax.psum_scatter(
            value_grad_win.astype(jnp.bfloat16), "expert", scatter_dimension=0, tiled=True
        ).astype(jnp.float32),
    )
    value_low = value_grad_own.reshape(tok_rows, width).astype(jnp.bfloat16)
    query_grad_raw, grad_gain_query = query_back(query_grad_rot.reshape(tok_rows, width))
    key_grad_raw, grad_gain_key = key_back(key_grad_own.reshape(tok_rows, width))
    query_low = query_grad_raw.astype(jnp.bfloat16)
    key_low = key_grad_raw.astype(jnp.bfloat16)
    grad_query = inner_rows(attn_in, query_low)
    grad_key = inner_rows(attn_in, key_low)
    grad_value = inner_rows(attn_in, value_low)
    attn_in_grads = (
        times_transposed(query_low, full_query)
        + times_transposed(key_low, full_key)
        + times_transposed(value_low, full_value)
    )
    input_from, grad_gain_attn = norm_one_back(attn_in_grads)
    input_grad = (mid_grads + input_from).astype(jnp.bfloat16)
    summed = (
        lax.psum_scatter(grad_query, ("dp", "expert"), scatter_dimension=0, tiled=True),
        lax.psum_scatter(grad_key, ("dp", "expert"), scatter_dimension=0, tiled=True),
        lax.psum_scatter(grad_value, ("dp", "expert"), scatter_dimension=0, tiled=True),
        lax.psum_scatter(grad_out, ("dp", "expert"), scatter_dimension=0, tiled=True),
        lax.psum_scatter(grad_router, ("dp", "expert"), scatter_dimension=0, tiled=True),
        lax.psum_scatter(grad_gain_attn, ("dp", "expert"), scatter_dimension=0, tiled=True),
        lax.psum_scatter(grad_gain_query, ("dp", "expert"), scatter_dimension=0, tiled=True),
        lax.psum_scatter(grad_gain_key, ("dp", "expert"), scatter_dimension=0, tiled=True),
        lax.psum_scatter(grad_gain_ffn, ("dp", "expert"), scatter_dimension=0, tiled=True),
    )
    return (
        output,
        input_grad,
        summed[0],
        summed[1],
        summed[2],
        summed[3],
        summed[5],
        summed[6],
        summed[7],
        summed[8],
        summed[4],
        grad_gate_w,
        grad_up_w,
        grad_down,
        rms_resid,
        rms_moe,
    )


def solution(mesh):
    placed = (
        P(("dp", "expert"), None),
        P(),
        P(("dp", "expert"), None),
        P(("dp", "expert"), None),
        P(("dp", "expert"), None),
        P(("dp", "expert"), None),
        P(("dp", "expert"), None),
        P(("dp", "expert")),
        P(("dp", "expert")),
        P(("dp", "expert")),
        P(("dp", "expert")),
        P(("dp", "expert"), None),
        P("expert", None, None),
        P("expert", None, None),
        P("expert", None, None),
        P(("dp", "expert"), None),
    )
    return jax.shard_map(
        body,
        mesh=mesh,
        in_specs=placed,
        out_specs=(
            P(("dp", "expert"), None),
            P(("dp", "expert"), None),
            P(("dp", "expert"), None),
            P(("dp", "expert"), None),
            P(("dp", "expert"), None),
            P(("dp", "expert"), None),
            P(("dp", "expert")),
            P(("dp", "expert")),
            P(("dp", "expert")),
            P(("dp", "expert")),
            P(("dp", "expert"), None),
            P("expert", None, "dp"),
            P("expert", None, "dp"),
            P("expert", None, "dp"),
            P(),
            P(),
        ),
        check_vma=False,
    )
```

profile of v0, /device:TPU:0, one launch (start us, length us, event | category | flops | bytes accessed | tf_op | source)
XLA Modules:
  0.0 2993.0 jit_solution(14875514304256216995)
XLA Ops:
  12.9 42.7 %all-reduce.14 = (bf16[2048]{0:T(1024)(128)(2,1)S(1)}, bf16[2048]{0:T(1024)(128)(2,1)S(1)}, bf16[2048]{0:T(1024)(128)(2,1)S(1)}, bf16[2048]{0:T(1024)(128)(2,1)S(1)}) all-reduce(bf16[2048]{0:T(1024)(128)(2,1)S(1)} %dynamic-update-slice, bf16[2048]{0:T(1024)(128)(2,1)S(1)} %dynamic-update-slice.2, ...), channel_id=1, replica_groups=mesh['dp'=4,'expert'=8] {'dp','expert'}, use_global_device_ids=true, to_apply=%add.5 | all-reduce | flops 8192 | bytes 32768
  57.7 34.0 %all-gather.12.cloned.1.call-done = bf16[2048,2048]{1,0:T(8,128)(2,1)} async-done(((bf16[64,2048]{1,0:T(8,128)(2,1)}), bf16[2048,2048]{1,0:T(8,128)(2,1)}) %all-gather.12.cloned.1.call-update) | async-done | bytes 8388624 | tf_op jit(solution)/shard_map/all_gather | solution.py:103
  91.6 5.0 multiply_reduce_fusion.7
  97.9 72.7 %all-gather.14.cloned.1.call-done = bf16[2048,2048]{1,0:T(8,128)(2,1)} async-done(((bf16[64,2048]{1,0:T(8,128)(2,1)}), bf16[2048,2048]{1,0:T(8,128)(2,1)}) %all-gather.14.cloned.1.call-update) | async-done | bytes 8388624 | tf_op jit(solution)/shard_map/all_gather | solution.py:104
  170.6 4.8 multiply_reduce_fusion.6
  180.3 69.2 %all-gather.8.cloned.1.call-done = bf16[2048,2048]{1,0:T(8,128)(2,1)} async-done(((bf16[64,2048]{1,0:T(8,128)(2,1)}), bf16[2048,2048]{1,0:T(8,128)(2,1)}) %all-gather.8.cloned.1.call-update) | async-done | bytes 8388624 | tf_op jit(solution)/shard_map/all_gather | solution.py:105
  249.5 5.5 convolution_convert_fusion.2
  256.2 4.5 reduce-window.6
  261.0 68.1 %all-gather = bf16[32,64,16]{1,2,0:T(8,128)(2,1)S(1)} all-gather(bf16[1,64,16]{1,2,0:T(8,128)(2,1)S(1)} %bitcast.237), channel_id=1, replica_groups=mesh['dp'=4,'expert'=8] {'dp','expert'}, dimensions={0}, use_global_device_ids=true | all-gather | bytes 67584 | tf_op jit(solution)/shard_map/all_gather | solution.py:107
  331.3 4.6 fusion.15
  340.9 60.6 %all-gather.10.cloned.1.call-done = bf16[1024,2048]{1,0:T(8,128)(2,1)} async-done(((bf16[128,2048]{1,0:T(8,128)(2,1)}), bf16[1024,2048]{1,0:T(8,128)(2,1)}) %all-gather.10.cloned.1.call-update) | async-done | bytes 4194320 | tf_op jit(solution)/shard_map/all_gather | solution.py:144
  401.5 7.6 fusion.49
  409.1 70.9 %all-gather.18.cloned.1.call-done = bf16[2048,2048]{1,0:T(8,128)(2,1)} async-done(((bf16[64,2048]{1,0:T(8,128)(2,1)}), bf16[2048,2048]{1,0:T(8,128)(2,1)}) %all-gather.18.cloned.1.call-update) | async-done | bytes 8388624 | tf_op jit(solution)/shard_map/all_gather | solution.py:106
  480.0 4.7 multiply_reduce_fusion.5
  485.5 10.1 scatter_custom_fusion.1
  495.7 4.6 all-to-all-start.2
  500.3 4.3 scatter_custom_fusion
  504.7 5.9 gather_fusion
  510.6 94.8 %all-to-all-done.2 = bf16[8,144,2048]{2,1,0:T(8,128)(2,1)} async-done(((bf16[8,144,2048]{2,1,0:T(8,128)(2,1)}), bf16[8,144,2048]{2,1,0:T(8,128)(2,1)}, u32[]{:S(2)}, u32[]{:S(2)}) %all-to-all-start.2) | async-done | bytes 4718624 | tf_op jit(solution)/shard_map/all_to_all | solution.py:209
  605.4 4.8 all-to-all-start
  610.2 10.8 fusion.10
  621.0 93.5 %all-to-all-done = bf16[8,144,2048]{2,1,0:T(8,128)(2,1)} async-done(((bf16[8,144,2048]{2,1,0:T(8,128)(2,1)}), bf16[8,144,2048]{2,1,0:T(8,128)(2,1)}, u32[]{:S(2)}, u32[]{:S(2)}) %all-to-all-start) | async-done | bytes 4718624 | tf_op jit(solution)/shard_map/all_to_all | solution.py:175
  714.5 10.9 fusion.4
  725.3 13.8 fusion.18
  739.2 5.4 convert_bitcast_fusion
  747.1 4.8 all-to-all-start.1
  751.9 8.2 fusion.2
  760.2 8.4 fusion.19
  771.3 84.4 %all-to-all-done.1 = bf16[8,144,2048]{2,1,0:T(8,128)(2,1)} async-done(((bf16[8,144,2048]{2,1,0:T(8,128)(2,1)}), bf16[8,144,2048]{2,1,0:T(8,128)(2,1)}, u32[]{:S(2)}, u32[]{:S(2)}) %all-to-all-start.1) | async-done | bytes 4718624 | tf_op jit(solution)/shard_map/all_to_all | solution.py:184
  855.6 4.6 all-to-all-start.3
  861.0 11.8 gather_fusion.1
  872.9 5.8 fusion.1
  878.8 85.1 %all-to-all-done.3 = bf16[8,144,2048]{2,1,0:T(8,128)(2,1)} async-done(((bf16[8,144,2048]{2,1,0:T(8,128)(2,1)}), bf16[8,144,2048]{2,1,0:T(8,128)(2,1)}, u32[]{:S(2)}, u32[]{:S(2)}) %all-to-all-start.3) | async-done | bytes 4718624 | tf_op jit(solution)/shard_map/all_to_all | solution.py:233
  964.0 12.1 gather_fusion.2
  976.1 5.2 convert_reduce_fusion
  983.8 6.3 convolution_convert_fusion.1
  990.4 8.1 convolution_convert_fusion
  998.5 6.4 copy.227
  1005.0 7.1 multiply_reduce_fusion
  1012.2 5.0 multiply_convert_fusion.1
  1024.0 11.3 bitcast_convert_fusion
  1035.4 11.4 bitcast_convert_fusion.2
  1046.9 11.6 bitcast_convert_fusion.1
  1059.5 8.1 fusion.68
  1067.6 24.5 reduce-scatter.31.cloned.1.call-done
  1092.1 9.2 fusion.97
  1101.4 6.3 fusion.48
  1107.7 77.3 %reduce-scatter.15.cloned.1.call-done = bf16[128,16,128]{2,0,1:T(8,128)(2,1)} async-done(((bf16[1024,16,128]{2,0,1:T(8,128)(2,1)}), bf16[128,16,128]{2,0,1:T(8,128)(2,1)}) %reduce-scatter.15.cloned.1.call-update) | async-done | bytes 524304 | tf_op jit(solution)/shard_map/reduce_scatter | solution.py:288
  1191.6 8.2 fusion.99
  1205.0 8.2 fusion.101
  1215.2 107.0 %reduce-scatter.33.cloned.1.call-done = f32[64,16]{1,0:T(8,128)} async-done(((f32[2048,16]{1,0:T(8,128)}), f32[64,16]{1,0:T(8,128)}) %reduce-scatter.33.cloned.1.call-update) | async-done | bytes 4112
  1323.6 7.1 fusion.112
  1330.7 8.3 convolution_add_fusion.2
  1342.1 38.1 %all-reduce.13 = (f32[2048]{0:T(1024)S(1)}, f32[2048]{0:T(1024)S(1)}, f32[2048]{0:T(1024)S(1)}, f32[2048]{0:T(1024)S(1)}, f32[]{:T(128)}, /*index=5*/f32[]{:T(128)}) all-reduce(f32[2048]{0:T(1024)S(1)} %get-tuple-element.24, f32[2048]{0:T(1024)S(1)} %get-tuple-element.22, ...), channel_id=8, replica_groups=mesh['dp'=4,'expert'=8] {'dp','expert'}, use_global_device_ids=true, to_apply=%region_33.34.clone | all-reduce | flops 8194 | bytes 65552
  1385.1 9.0 reduce-scatter.29.cloned.1.call-done
  1394.1 3.9 convert_element_type.228
  1398.0 70.2 %reduce-scatter.25.cloned.1.call-done = bf16[2,2048,256]{2,1,0:T(8,128)(2,1)} async-done(((bf16[2,2048,1024]{2,1,0:T(8,128)(2,1)}), bf16[2,2048,256]{2,1,0:T(8,128)(2,1)}) %reduce-scatter.25.cloned.1.call-update) | async-done | bytes 2097168 | tf_op jit(solution)/shard_map/reduce_scatter | solution.py:246
  1468.2 3.9 convert_element_type.224
  1472.1 70.4 %reduce-scatter.27.cloned.1.call-done = bf16[2,2048,256]{2,1,0:T(8,128)(2,1)} async-done(((bf16[2,2048,1024]{2,1,0:T(8,128)(2,1)}), bf16[2,2048,256]{2,1,0:T(8,128)(2,1)}) %reduce-scatter.27.cloned.1.call-update) | async-done | bytes 2097168 | tf_op jit(solution)/shard_map/reduce_scatter | solution.py:249
  1542.6 3.9 convert_element_type.226
  1546.5 357.0 %reduce-scatter.23.cloned.1.call-done = f32[64,2048]{1,0:T(8,128)} async-done(((f32[2048,2048]{1,0:T(8,128)}), f32[64,2048]{1,0:T(8,128)}) %reduce-scatter.23.cloned.1.call-update) | async-done | bytes 524304 | tf_op jit(solution)/shard_map/reduce_scatter | solution.py:314
  1903.5 360.1 %reduce-scatter.21.cloned.1.call-done = f32[64,2048]{1,0:T(8,128)} async-done(((f32[2048,2048]{1,0:T(8,128)}), f32[64,2048]{1,0:T(8,128)}) %reduce-scatter.21.cloned.1.call-update) | async-done | bytes 524304 | tf_op jit(solution)/shard_map/reduce_scatter | solution.py:313
  2263.6 360.1 %reduce-scatter.19.cloned.1.call-done = f32[64,2048]{1,0:T(8,128)} async-done(((f32[2048,2048]{1,0:T(8,128)}), f32[64,2048]{1,0:T(8,128)}) %reduce-scatter.19.cloned.1.call-update) | async-done | bytes 524304 | tf_op jit(solution)/shard_map/reduce_scatter | solution.py:312
  2623.7 360.1 %reduce-scatter.17.cloned.1.call-done = f32[64,2048]{1,0:T(8,128)} async-done(((f32[2048,2048]{1,0:T(8,128)}), f32[64,2048]{1,0:T(8,128)}) %reduce-scatter.17.cloned.1.call-update) | async-done | bytes 524304 | tf_op jit(solution)/shard_map/reduce_scatter | solution.py:311
  (252 shorter events, 60.8 us)
Async XLA Ops:
  7.2 84.4 %all-gather.12.cloned.1.call-start = ((), (), s32[]{:S(2)}) async-start(), calls=%async_computation.16 | async-start | bytes 8650752 | tf_op jit(solution)/shard_map/all_gather | solution.py:103
  7.9 162.7 %all-gather.14.cloned.1.call-start = ((), (), s32[]{:S(2)}) async-start(), calls=%async_computation.17 | async-start | bytes 8650752 | tf_op jit(solution)/shard_map/all_gather | solution.py:104
  8.7 240.9 %all-gather.8.cloned.1.call-start = ((), (), s32[]{:S(2)}) async-start(), calls=%async_computation.14 | async-start | bytes 8650752 | tf_op jit(solution)/shard_map/all_gather | solution.py:105
  9.4 321.8 %all-gather.16.cloned.1.call-start = ((), (), s32[]{:S(2)}) async-start(), calls=%async_computation.18 | async-start | bytes 4718592 | tf_op jit(solution)/shard_map/all_gather | solution.py:143
  55.6 194.0 %copy-start.23 = (f32[2048]{0:T(1024)}, f32[2048]{0:T(1024)S(1)}, u32[]{:S(2)}) copy-start(f32[2048]{0:T(1024)S(1)} %convert_element_type.180) | copy-start | bytes 24580
  55.6 119.9 %copy-start.34 = (f32[2048]{0:T(1024)}, f32[2048]{0:T(1024)S(1)}, u32[]{:S(2)}) copy-start(f32[2048]{0:T(1024)S(1)} %convert_element_type.185) | copy-start | bytes 24580
  55.6 41.1 %copy-start.32 = (f32[2048]{0:T(1024)}, f32[2048]{0:T(1024)S(1)}, u32[]{:S(2)}) copy-start(f32[2048]{0:T(1024)S(1)} %convert_element_type.183) | copy-start | bytes 24580
  57.3 192.2 %copy-start.38 = (f32[128]{0:T(128)}, f32[128]{0:T(128)S(1)}, u32[]{:S(2)}) copy-start(f32[128]{0:T(128)S(1)} %fusion.85) | copy-start | bytes 1540
  57.7 119.8 %copy-start.28 = (f32[128,64]{1,0:T(8,128)}, f32[128,64]{1,0:T(8,128)S(1)}, u32[]{:S(2)}) copy-start(f32[128,64]{1,0:T(8,128)S(1)} %get-tuple-element.66) | copy-start | bytes 98308
  57.7 119.8 %copy-start.30 = (f32[128,64]{1,0:T(8,128)}, f32[128,64]{1,0:T(8,128)S(1)}, u32[]{:S(2)}) copy-start(f32[128,64]{1,0:T(8,128)S(1)} %get-tuple-element.67) | copy-start | bytes 98308
  96.6 78.8 %copy-start.48 = (f32[128]{0:T(128)}, f32[128]{0:T(128)S(1)}, u32[]{:S(2)}) copy-start(f32[128]{0:T(128)S(1)} %get-tuple-element.68) | copy-start | bytes 1540
  96.6 74.0 %copy-start.1 = (bf16[128,2048]{1,0:T(8,128)(2,1)S(1)}, bf16[128,2048]{1,0:T(8,128)(2,1)}, u32[]{:S(2)}) copy-start(bf16[128,2048]{1,0:T(8,128)(2,1)} %param.16) | copy-start | bytes 1572868
  178.9 152.4 %copy-start.14 = (bf16[128,16,64]{2,0,1:T(8,128)(2,1)}, bf16[128,16,64]{2,0,1:T(8,128)(2,1)S(1)}, u32[]{:S(2)}) copy-start(bf16[128,16,64]{2,0,1:T(8,128)(2,1)S(1)} %get-tuple-element.44) | copy-start | bytes 786436
  178.9 152.4 %copy-start.16 = (bf16[128,16,64]{2,0,1:T(8,128)(2,1)}, bf16[128,16,64]{2,0,1:T(8,128)(2,1)S(1)}, u32[]{:S(2)}) copy-start(bf16[128,16,64]{2,0,1:T(8,128)(2,1)S(1)} %get-tuple-element.45) | copy-start | bytes 786436
  180.2 75.4 %copy-start.40 = (s32[128,8]{0,1:T(8,128)S(1)}, s32[128,8]{0,1:T(8,128)}, u32[]{:S(2)}) copy-start(s32[128,8]{0,1:T(8,128)} %param.18) | copy-start | bytes 12292
  180.2 80.8 %copy-start.45 = (bf16[64,16]{0,1:T(8,128)(2,1)S(1)}, bf16[64,16]{0,1:T(8,128)(2,1)}, u32[]{:S(2)}) copy-start(bf16[64,16]{0,1:T(8,128)(2,1)} %param.27) | copy-start | bytes 6148
  180.2 149.1 %copy-start.26 = (bf16[128,2048]{1,0:T(8,128)(2,1)S(1)}, bf16[128,2048]{1,0:T(8,128)(2,1)}, u32[]{:S(2)}) copy-start(bf16[128,2048]{1,0:T(8,128)(2,1)} %param.31) | copy-start | bytes 1572868
  180.3 149.3 %copy-start.52 = (s32[4]{0:T(128)S(1)}, s32[4]{0:T(128)}, u32[]{:S(2)}) copy-start(s32[4]{0:T(128)} %param.17) | copy-start | bytes 52
  180.3 221.2 %all-gather.10.cloned.1.call-start = ((), (), s32[]{:S(2)}) async-start(), calls=%async_computation.15 | async-start | bytes 4718592 | tf_op jit(solution)/shard_map/all_gather | solution.py:144
  255.1 225.0 %all-gather.18.cloned.1.call-start = ((), (), s32[]{:S(2)}) async-start(), calls=%async_computation.19 | async-start | bytes 8650752 | tf_op jit(solution)/shard_map/all_gather | solution.py:106
  329.5 156.0 %copy-start.8 = (f32[128,2048]{1,0:T(8,128)}, f32[128,2048]{1,0:T(8,128)S(1)}, u32[]{:S(2)}) copy-start(f32[128,2048]{1,0:T(8,128)S(1)} %convert_element_type.201) | copy-start | bytes 3145732
  331.2 70.3 %copy-start.12 = (pred[128,1024]{0,1:T(8,128)(4,1)}, pred[128,1024]{0,1:T(8,128)(4,1)S(1)}, u32[]{:S(2)}) copy-start(pred[128,1024]{0,1:T(8,128)(4,1)S(1)} %fusion.67) | copy-start | bytes 393220
  340.9 68.2 %copy-start.36 = (f32[16,128]{1,0:T(8,128)}, f32[16,128]{1,0:T(8,128)S(1)}, u32[]{:S(2)}) copy-start(f32[16,128]{1,0:T(8,128)S(1)} %log_add_fusion) | copy-start | bytes 24580
  409.1 75.7 %copy-start.20 = (bf16[16,128,128]{2,1,0:T(8,128)(2,1)}, bf16[16,128,128]{2,1,0:T(8,128)(2,1)S(1)}, u32[]{:S(2)}) copy-start(bf16[16,128,128]{2,1,0:T(8,128)(2,1)S(1)} %fusion.49) | copy-start | bytes 1572868
  485.0 19.7 copy-start.10
  495.7 109.7 %all-to-all-start.2 = ((bf16[8,144,2048]{2,1,0:T(8,128)(2,1)}), bf16[8,144,2048]{2,1,0:T(8,128)(2,1)}, u32[]{:S(2)}, u32[]{:S(2)}) async-start(bf16[8,144,2048]{2,1,0:T(8,128)(2,1)} %bitcast.218), calls=%async_computation.2 | async-start | bytes 9437184 | tf_op jit(solution)/shard_map/all_to_all | solution.py:209
  605.4 109.1 %all-to-all-start = ((bf16[8,144,2048]{2,1,0:T(8,128)(2,1)}), bf16[8,144,2048]{2,1,0:T(8,128)(2,1)}, u32[]{:S(2)}, u32[]{:S(2)}) async-start(bf16[8,144,2048]{2,1,0:T(8,128)(2,1)} %bitcast.220), calls=%async_computation | async-start | bytes 9437184 | tf_op jit(solution)/shard_map/all_to_all | solution.py:175
  714.5 10.9 copy-start.54
  714.5 24.7 slice-start.2
  725.3 13.8 slice-start.3
  739.2 5.4 copy-start.55
  747.1 108.5 %all-to-all-start.1 = ((bf16[8,144,2048]{2,1,0:T(8,128)(2,1)}), bf16[8,144,2048]{2,1,0:T(8,128)(2,1)}, u32[]{:S(2)}, u32[]{:S(2)}) async-start(bf16[8,144,2048]{2,1,0:T(8,128)(2,1)} %bitcast.219), calls=%async_computation.1 | async-start | bytes 9437184 | tf_op jit(solution)/shard_map/all_to_all | solution.py:184
  855.6 108.3 %all-to-all-start.3 = ((bf16[8,144,2048]{2,1,0:T(8,128)(2,1)}), bf16[8,144,2048]{2,1,0:T(8,128)(2,1)}, u32[]{:S(2)}, u32[]{:S(2)}) async-start(bf16[8,144,2048]{2,1,0:T(8,128)(2,1)} %bitcast.217), calls=%async_computation.3 | async-start | bytes 9437184 | tf_op jit(solution)/shard_map/all_to_all | solution.py:233
  860.3 231.8 %reduce-scatter.31.cloned.1.call-start = ((), (), s32[]{:S(2)}) async-start(), calls=%async_computation.28 | async-start | bytes 4718592 | tf_op jit(solution)/shard_map/convert_element_type | solution.py:295
  861.0 11.9 copy-start.9
  976.1 5.2 copy-start.22
  976.1 7.3 copy-start.27
  983.8 6.6 copy-start.13
  983.8 6.6 copy-start.37
  1005.0 180.1 %reduce-scatter.15.cloned.1.call-start = ((), (), s32[]{:S(2)}) async-start(), calls=%async_computation.20 | async-start | bytes 4718592 | tf_op jit(solution)/shard_map/reduce_scatter | solution.py:288
  1012.2 7.0 copy-start.15
  1012.2 7.0 copy-start.17
  1022.6 299.6 %reduce-scatter.33.cloned.1.call-start = ((), (), s32[]{:S(2)}) async-start(), calls=%async_computation.29 | async-start | bytes 1081344
  1024.0 370.1 %reduce-scatter.29.cloned.1.call-start = ((), (), s32[]{:S(2)}) async-start(), calls=%async_computation.27 | async-start | bytes 10485760 | tf_op jit(solution)/shard_map/reduce_scatter | solution.py:252
  1035.4 432.8 %reduce-scatter.25.cloned.1.call-start = ((), (), s32[]{:S(2)}) async-start(), calls=%async_computation.25 | async-start | bytes 10485760 | tf_op jit(solution)/shard_map/reduce_scatter | solution.py:246
  1046.8 495.8 %reduce-scatter.27.cloned.1.call-start = ((), (), s32[]{:S(2)}) async-start(), calls=%async_computation.26 | async-start | bytes 10485760 | tf_op jit(solution)/shard_map/reduce_scatter | solution.py:249
  1058.5 845.0 %reduce-scatter.23.cloned.1.call-start = ((), (), s32[]{:S(2)}) async-start(), calls=%async_computation.24 | async-start | bytes 17301504 | tf_op jit(solution)/shard_map/reduce_scatter | solution.py:314
  1067.6 24.5 copy-start.2
  1067.6 24.5 copy-start.24
  1067.6 24.5 copy-start.39
  1067.6 1196.0 %reduce-scatter.21.cloned.1.call-start = ((), (), s32[]{:S(2)}) async-start(), calls=%async_computation.23 | async-start | bytes 17301504 | tf_op jit(solution)/shard_map/reduce_scatter | solution.py:313
  1101.4 84.8 %copy-start.29 = (f32[128,64]{1,0:T(8,128)S(1)}, f32[128,64]{1,0:T(8,128)}, u32[]{:S(2)}) copy-start(f32[128,64]{1,0:T(8,128)} %copy-done.28) | copy-start | bytes 98308
  1101.4 84.8 %copy-start.31 = (f32[128,64]{1,0:T(8,128)S(1)}, f32[128,64]{1,0:T(8,128)}, u32[]{:S(2)}) copy-start(f32[128,64]{1,0:T(8,128)} %copy-done.30) | copy-start | bytes 98308
  1101.4 1522.3 %reduce-scatter.19.cloned.1.call-start = ((), (), s32[]{:S(2)}) async-start(), calls=%async_computation.22 | async-start | bytes 17301504 | tf_op jit(solution)/shard_map/reduce_scatter | solution.py:312
  1107.7 82.1 %copy-start.7 = (f32[128,2048]{1,0:T(8,128)S(1)}, f32[128,2048]{1,0:T(8,128)}, u32[]{:S(2)}) copy-start(f32[128,2048]{1,0:T(8,128)} %copy-done.6) | copy-start | bytes 3145732
  1107.7 82.1 %copy-start.35 = (f32[2048]{0:T(1024)S(1)}, f32[2048]{0:T(1024)}, u32[]{:S(2)}) copy-start(f32[2048]{0:T(1024)} %copy-done.34) | copy-start | bytes 24580
  1107.7 82.1 %copy-start.44 = (f32[128]{0:T(128)S(1)}, f32[128]{0:T(128)}, u32[]{:S(2)}) copy-start(f32[128]{0:T(128)} %copy-done.43) | copy-start | bytes 1540
  1186.2 4.1 copy-start.51
  1199.8 1784.0 %reduce-scatter.17.cloned.1.call-start = ((), (), s32[]{:S(2)}) async-start(), calls=%async_computation.21 | async-start | bytes 17301504 | tf_op jit(solution)/shard_map/reduce_scatter | solution.py:311
  1323.6 7.1 copy-start.19
  1323.6 15.4 slice-start
  1330.7 8.3 slice-start.1
  1330.7 8.3 copy-start.25
  1339.0 44.9 %copy-start.47 = (f32[128]{0:T(128)S(1)}, f32[128]{0:T(128)}, u32[]{:S(2)}) copy-start(f32[128]{0:T(128)} %copy-done.46) | copy-start | bytes 1540
  (16 other events, 25.6 us)
Sparse Core Ops, SparseCore 0:
  11.0 80.5 all-gather.11
  94.6 75.9 all-gather.13
  173.6 75.8 all-gather.7
  252.0 75.1 all-gather.15
  329.7 71.6 all-gather.9
  404.3 75.6 all-gather.17
  1005.1 86.9 reduce-scatter.30
  1096.7 88.2 reduce-scatter.14
  1187.3 134.8 reduce-scatter.32
  1324.8 69.2 reduce-scatter.28
  1396.7 71.4 reduce-scatter.24
  1470.8 71.7 reduce-scatter.26
  1545.4 358.0 reduce-scatter.22
  1906.2 357.3 reduce-scatter.20
  2266.3 357.3 reduce-scatter.18
  2626.4 357.3 reduce-scatter.16
where the time goes:
time: 3000 us; the launch traced here: 2990 us
  waiting for transfers between devices  2460 us (82%)
  matrix products  211 us (7%)
  blocking collectives  149 us (5%)
  local copies, waits for them, and re-layouts  68.4 us (2%)
  other arithmetic  61.7 us (2%)
    reduce_scatter x1, waiting for transfers between devices, body(): lax.psum_scatter(grad_query, ('dp', 'expert'), scatter_dimension=0, tiled...  360 us
    reduce_scatter x1, waiting for transfers between devices, body(): lax.psum_scatter(grad_value, ('dp', 'expert'), scatter_dimension=0, tiled...  360 us
    reduce_scatter x1, waiting for transfers between devices, body(): lax.psum_scatter(grad_key, ('dp', 'expert'), scatter_dimension=0, tiled=T...  360 us
    reduce_scatter x1, waiting for transfers between devices, body(): lax.psum_scatter(grad_out, ('dp', 'expert'), scatter_dimension=0, tiled=T...  357 us
    unnamed x17, waiting for transfers between devices  110 us
    all_to_all x1, waiting for transfers between devices, body(): lax.all_to_all(grad_send.reshape(groups, local_experts * capacity, width)...  94.8 us
    all_to_all x1, waiting for transfers between devices, body(): lax.all_to_all(outgoing, 'expert', split_axis=0, concat_axis=0, tiled=True)  93.5 us
    all_to_all x1, waiting for transfers between devices, body(): lax.all_to_all(row_grads.astype(jnp.bfloat16).reshape(groups, local_exper...  85.1 us
  transfers between devices with their start and end apart: 20, of which 19 were waited for; matrix products, arithmetic and copies ran while one was open for 8% of the time, Pallas kernels for 0%

commit v1 on v0

v1 whole, which is shorter than its diff:
```python
import jax
import jax.numpy as jnp
import numpy as np
from jax import lax
from jax.experimental import pallas as pl
from jax.experimental.pallas import tpu as pltpu
from jax.sharding import PartitionSpec as P

HEADS = 16
HEAD_DIM = 128
TOP = 8
EPSILON = 1e-05
ROPE_BASE = 10000.0
SCALE = HEAD_DIM ** (-0.5)
NEG = -1e30
Z_CHIPS = 4
CORES = 2
F32 = jnp.float32
BF16 = jnp.bfloat16


def ring_tables(groups):
    x_chips = groups // Z_CHIPS
    walk = []
    for x in range(x_chips):
        column = range(1, Z_CHIPS) if x % 2 == 0 else range(Z_CHIPS - 1, 0, -1)
        walk += [z * x_chips + x for z in column]
    walk += [x for x in range(x_chips - 1, -1, -1)]
    place = np.zeros((groups,), np.int32)
    for at, owner in enumerate(walk):
        place[owner] = at
    return np.array(walk, np.int32), place


class Ring:
    def __init__(self, groups):
        self.size = groups
        self.walk, self.place = ring_tables(groups)
        size = groups
        self.ahead = [(int(self.walk[i]), int(self.walk[(i + 1) % size])) for i in range(size)]
        self.back = [(b, a) for a, b in self.ahead]
        mine = jnp.asarray(self.place)[lax.axis_index("expert")]
        self.natural = jnp.asarray(self.walk)[(mine + jnp.arange(size, dtype=jnp.int32)) % size]

    def up(self, value):
        return lax.ppermute(value, "expert", self.ahead)

    def down(self, value):
        return lax.ppermute(value, "expert", self.back)

    def gather(self, block):
        half = self.size // 2
        rows = block.shape[0]
        pieces = [(0, 0, block)]
        up, down = block, block
        for step in range(1, half):
            up = self.up(up)
            down = self.down(down)
            pieces += [(self.size - step, 0, up), (step, 0, down)]
        pieces.append((half, 0, self.up(up[: rows // 2])))
        pieces.append((half, rows // 2, self.down(down[rows // 2 :])))
        return pieces

    def scatter(self, term):
        half = self.size // 2
        far = term(half)
        rows = far.shape[0]
        up = self.up(far[: rows // 2])
        down = self.down(far[rows // 2 :])

        def add(left, right):
            return (left.astype(F32) + right.astype(F32)).astype(BF16)

        for step in range(half - 1, 0, -1):
            ahead, behind = term(step), term(self.size - step)
            if step == half - 1:
                ahead = jnp.concatenate([add(up, ahead[: rows // 2]), ahead[rows // 2 :]], axis=0)
                behind = jnp.concatenate(
                    [behind[: rows // 2], add(down, behind[rows // 2 :])], axis=0
                )
            else:
                ahead, behind = add(up, ahead), add(down, behind)
            up, down = self.up(ahead), self.down(behind)
        return up.astype(F32) + down.astype(F32) + term(0).astype(F32)


def place_blocks(ring, pieces, rows, width, dtype=BF16):
    buffer = jnp.zeros((ring.size * rows, width), dtype)
    for o, start, piece in pieces:
        buffer = lax.dynamic_update_slice(
            buffer, piece.astype(dtype), (ring.natural[o] * rows + start, 0)
        )
    return buffer


def expert_sum(value, groups):
    step = 1
    while step < groups:
        value = value + lax.ppermute(value, "expert", [(i, i ^ step) for i in range(groups)])
        step *= 2
    return value


def dp_sum(value, n_dp):
    step = 1
    while step < n_dp:
        value = value + lax.ppermute(value, "dp", [(i, i ^ step) for i in range(n_dp)])
        step *= 2
    return value


def dp_gather(chunk, n_dp):
    rows, width = chunk.shape
    me = lax.axis_index("dp")
    held = [(0, chunk)]
    for y in range(1, n_dp // CORES):
        held.append((2 * y, lax.ppermute(chunk, "dp", [(i, i ^ (2 * y)) for i in range(n_dp)])))
    swap = [(i, i ^ 1) for i in range(n_dp)]
    held += [(rel ^ 1, lax.ppermute(part, "dp", swap)) for rel, part in held]
    buffer = jnp.zeros((n_dp * rows, width), chunk.dtype)
    for rel, part in held:
        buffer = lax.dynamic_update_slice(buffer, part, ((me ^ rel) * rows, 0))
    return buffer


def dp_reduce(term, n_dp):
    swap = [(i, i ^ 1) for i in range(n_dp)]
    chips = n_dp // CORES
    other = [lax.ppermute(term(2 * y + 1).astype(BF16), "dp", swap) for y in range(chips)]
    total = None
    for y in range(1, chips):
        part = (term(2 * y) + other[y].astype(F32)).astype(BF16)
        part = lax.ppermute(part, "dp", [(i, i ^ (2 * y)) for i in range(n_dp)]).astype(F32)
        total = part if total is None else total + part
    own = term(0) + other[0].astype(F32)
    return own if total is None else own + total


def norm_scale(values):
    return lax.rsqrt(jnp.mean(values * values, axis=-1, keepdims=True) + EPSILON)


def matmul(left, right):
    return jnp.dot(left, right, preferred_element_type=F32)


def matmul_nt(left, right):
    return lax.dot_general(left, right, (((1,), (1,)), ((), ())), preferred_element_type=F32)


def matmul_tn(left, right):
    return lax.dot_general(left, right, (((0,), (0,)), ((), ())), preferred_element_type=F32)


def masked(scores, first_row, length):
    rows, columns = scores.shape
    row = first_row + lax.broadcasted_iota(jnp.int32, (rows, columns), 0)
    column = lax.broadcasted_iota(jnp.int32, (rows, columns), 1)
    return jnp.where((column <= row) & (column < length), scores * SCALE, NEG)


def turn(values, cosine, sine):
    return values * cosine + pltpu.roll(values, HEAD_DIM // 2, 1) * sine


def turn_back(values, cosine, sine):
    return values * cosine - pltpu.roll(values, HEAD_DIM // 2, 1) * sine


def attend_kernel(
    length_ref, qkv_ref, squares_ref, gain_ref, cos_ref, sin_ref, q_ref, k_ref, v_ref, o_ref
):
    seq, own = q_ref.shape
    tile = min(256, seq)
    width = HEADS * HEAD_DIM
    length = length_ref[0]
    for start in range(0, seq, tile):
        rows = slice(start, start + tile)
        squares = squares_ref[rows, :]
        cosine, sine = cos_ref[rows, :], sin_ref[rows, :]
        for part, out_ref in ((0, q_ref), (1, k_ref)):
            scale = lax.rsqrt(squares[:, part : part + 1] / width + EPSILON)
            for first in range(0, own, HEAD_DIM):
                columns = slice(first, first + HEAD_DIM)
                raw = qkv_ref[rows, part * own + first : part * own + first + HEAD_DIM]
                normed = raw * scale * gain_ref[part : part + 1, columns]
                out_ref[rows, columns] = turn(normed, cosine, sine).astype(BF16)
        v_ref[rows, :] = qkv_ref[rows, 2 * own : 3 * own].astype(BF16)
    for first in range(0, own, HEAD_DIM):
        columns = slice(first, first + HEAD_DIM)
        for start in range(0, seq, tile):
            rows, keys = slice(start, start + tile), slice(0, start + tile)
            scores = masked(matmul_nt(q_ref[rows, columns], k_ref[keys, columns]), start, length)
            expo = jnp.exp(scores - jnp.max(scores, axis=-1, keepdims=True))
            total = jnp.sum(expo, axis=-1, keepdims=True)
            probs = (expo / total).astype(BF16)
            o_ref[rows, columns] = matmul(probs, v_ref[keys, columns]).astype(BF16)


def attend_back_kernel(
    length_ref,
    qkv_ref,
    squares_ref,
    gain_ref,
    cos_ref,
    sin_ref,
    q_ref,
    k_ref,
    v_ref,
    do_ref,
    dq_ref,
    dk_ref,
    dv_ref,
    dots_ref,
    dgain_ref,
    k_total,
    v_total,
):
    seq, own = q_ref.shape
    tile = min(256, seq)
    width = HEADS * HEAD_DIM
    length = length_ref[0]
    for first in range(0, own, HEAD_DIM):
        columns = slice(first, first + HEAD_DIM)
        k_total[...] = jnp.zeros_like(k_total)
        v_total[...] = jnp.zeros_like(v_total)
        for start in range(0, seq, tile):
            rows, keys = slice(start, start + tile), slice(0, start + tile)
            q, k, v = q_ref[rows, columns], k_ref[keys, columns], v_ref[keys, columns]
            do = do_ref[rows, columns]
            scores = masked(matmul_nt(q, k), start, length)
            expo = jnp.exp(scores - jnp.max(scores, axis=-1, keepdims=True))
            probs = expo / jnp.sum(expo, axis=-1, keepdims=True)
            dprobs = matmul_nt(do, v)
            mean = jnp.sum(probs * dprobs, axis=-1, keepdims=True)
            dscores = (probs * (dprobs - mean)).astype(BF16)
            dq_ref[rows, columns] = matmul(dscores, k) * SCALE
            k_total[keys, :] += matmul_tn(dscores, q)
            v_total[keys, :] += matmul_tn(probs.astype(BF16), do)
        dk_ref[:, columns] = k_total[...] * SCALE
        dv_ref[:, columns] = v_total[...].astype(BF16)
    dgain_ref[...] = jnp.zeros_like(dgain_ref)
    for start in range(0, seq, tile):
        rows = slice(start, start + tile)
        squares = squares_ref[rows, :]
        cosine, sine = cos_ref[rows, :], sin_ref[rows, :]
        for part, out_ref in ((0, dq_ref), (1, dk_ref)):
            scale = lax.rsqrt(squares[:, part : part + 1] / width + EPSILON)
            dot = jnp.zeros((tile, 1), F32)
            for first in range(0, own, HEAD_DIM):
                columns = slice(first, first + HEAD_DIM)
                raw = qkv_ref[rows, part * own + first : part * own + first + HEAD_DIM]
                grad = turn_back(out_ref[rows, columns], cosine, sine)
                dgain_ref[part : part + 1, columns] += jnp.sum(
                    grad * raw * scale, axis=0, keepdims=True
                )
                grad = grad * gain_ref[part : part + 1, columns]
                dot += jnp.sum(grad * raw, axis=-1, keepdims=True)
                out_ref[rows, columns] = grad * scale
            dots_ref[rows, part : part + 1] = dot


def attend(length, qkv, squares, gains, cosine, sine):
    seq, own = qkv.shape[0], qkv.shape[1] // 3
    shape = jax.ShapeDtypeStruct((seq, own), BF16)
    return pl.pallas_call(
        attend_kernel,
        out_shape=[shape] * 4,
        in_specs=[pl.BlockSpec(memory_space=pltpu.SMEM)]
        + [pl.BlockSpec(memory_space=pltpu.VMEM)] * 5,
        out_specs=[pl.BlockSpec(memory_space=pltpu.VMEM)] * 4,
        compiler_params=pltpu.CompilerParams(vmem_limit_bytes=56 << 20),
        cost_estimate=pl.CostEstimate(
            flops=4 * seq * seq * own, bytes_accessed=20 * seq * own, transcendentals=seq * seq
        ),
    )(length, qkv, squares, gains, cosine, sine)


def attend_back(length, qkv, squares, gains, cosine, sine, q, k, v, do):
    seq, own = q.shape
    wide = jax.ShapeDtypeStruct((seq, own), F32)
    return pl.pallas_call(
        attend_back_kernel,
        out_shape=[
            wide,
            wide,
            jax.ShapeDtypeStruct((seq, own), BF16),
            jax.ShapeDtypeStruct((seq, 2), F32),
            jax.ShapeDtypeStruct((2, own), F32),
        ],
        in_specs=[pl.BlockSpec(memory_space=pltpu.SMEM)]
        + [pl.BlockSpec(memory_space=pltpu.VMEM)] * 9,
        out_specs=[pl.BlockSpec(memory_space=pltpu.VMEM)] * 5,
        scratch_shapes=[pltpu.VMEM((seq, HEAD_DIM), F32)] * 2,
        compiler_params=pltpu.CompilerParams(vmem_limit_bytes=56 << 20),
        cost_estimate=pl.CostEstimate(
            flops=10 * seq * seq * own, bytes_accessed=40 * seq * own, transcendentals=seq * seq
        ),
    )(length, qkv, squares, gains, cosine, sine, q, k, v, do)


def body(
    tokens,
    seq_lengths,
    routes,
    w_query,
    w_key,
    w_value,
    w_out,
    gain_attn,
    gain_query,
    gain_key,
    gain_ffn,
    w_router,
    w_gate,
    w_up,
    w_down_t,
    cotangent,
):
    rows, width = tokens.shape
    local_experts, _, hidden_units = w_gate.shape
    groups, n_dp = lax.axis_size("expert"), lax.axis_size("dp")
    experts_all = local_experts * groups
    seq = groups * rows
    own = width // groups
    weight_rows = w_query.shape[0]
    me, dp = lax.axis_index("expert"), lax.axis_index("dp")
    ring = Ring(groups)
    positions = jnp.arange(seq, dtype=jnp.int32)
    my_rows = me * rows + jnp.arange(rows, dtype=jnp.int32)
    seq_length = lax.dynamic_index_in_dim(seq_lengths, dp, 0, keepdims=True)
    used = (my_rows < seq_length[0]).astype(F32)[:, None]

    expert_ids = jnp.arange(experts_all, dtype=jnp.int32)
    chosen = jnp.any(routes[:, :, None] == expert_ids[None, None, :], axis=1)
    chosen_low = chosen.astype(BF16)

    hit_columns = rows * local_experts // weight_rows
    hits_out = chosen_low.reshape(rows, groups, local_experts).transpose(1, 0, 2)
    extra = jnp.concatenate(
        [
            jnp.stack([gain_attn, gain_query, gain_key, gain_ffn], axis=1),
            w_router,
        ],
        axis=1,
    )
    extra_columns = extra.shape[1]
    pad = -(extra_columns + hit_columns) % 128
    send = jnp.concatenate(
        [w.reshape(weight_rows, groups, own).transpose(1, 0, 2) for w in (w_query, w_key, w_value)]
        + [
            jnp.broadcast_to(extra[None], (groups, weight_rows, extra_columns)),
            hits_out.reshape(groups, weight_rows, hit_columns),
            jnp.zeros((groups, weight_rows, pad), BF16),
        ],
        axis=2,
    )
    got = lax.all_to_all(send, "expert", split_axis=0, concat_axis=0, tiled=True)
    hits = got[:, :, 3 * own + extra_columns : 3 * own + extra_columns + hit_columns]
    hits = hits.reshape(seq, local_experts).astype(F32)
    projections = dp_gather(got.reshape(groups * weight_rows, -1), n_dp)
    w_qkv = projections[:, : 3 * own]
    small = projections[:, 3 * own : 3 * own + extra_columns]
    gains_full = small[:, :4].T.astype(F32)
    full_router = small[:, 4:]
    full_out = lax.all_gather(w_out, ("dp", "expert"), axis=0, tiled=True)
    cot_all = lax.all_gather(cotangent, "expert", axis=0, tiled=True)

    resid_in = tokens.astype(F32)
    attn_gain, ffn_gain = gains_full[0:1], gains_full[3:4]
    tokens_all = place_blocks(ring, ring.gather(tokens), rows, width)
    wide = tokens_all.astype(F32)
    attn_in = (wide * norm_scale(wide) * attn_gain).astype(BF16)
    qkv = matmul(attn_in, w_qkv)
    squares = jnp.stack(
        [
            jnp.sum(qkv[:, :own] ** 2, axis=1),
            jnp.sum(qkv[:, own : 2 * own] ** 2, axis=1),
        ]
    )
    squares = expert_sum(squares, groups).T
    gains_own = lax.dynamic_slice(gains_full, (1, me * own), (2, own))
    half = HEAD_DIM // 2
    frequency = ROPE_BASE ** (-(jnp.arange(half, dtype=F32) * 2.0) / HEAD_DIM)
    angles = positions.astype(F32)[:, None] * frequency[None, :]
    cosine, sine = jnp.cos(angles), jnp.sin(angles)
    cosine = jnp.concatenate([cosine, cosine], axis=1)
    sine = jnp.concatenate([-sine, sine], axis=1)
    q, k, v, attended = attend(seq_length, qkv, squares, gains_own, cosine, sine)
    attn_rows = lax.all_to_all(
        attended.reshape(groups, rows, own), "expert", split_axis=0, concat_axis=0, tiled=True
    )
    attn_rows = attn_rows.transpose(1, 0, 2).reshape(rows, width)
    attn_rows_all = lax.all_gather(attn_rows, "expert", axis=0, tiled=True)
    resid_mid = resid_in + matmul(attn_rows, full_out)
    mid_scale = norm_scale(resid_mid)
    ffn_in = (resid_mid * mid_scale * ffn_gain).astype(BF16)
    logits = matmul(ffn_in, full_router)
    probs = jax.nn.softmax(logits, axis=-1)

    ffn_all = place_blocks(ring, ring.gather(ffn_in), rows, width)
    logits_all = matmul(ffn_all, full_router)
    probs_all = jax.nn.softmax(logits_all, axis=-1)
    weights = lax.dynamic_slice(probs_all, (0, me * local_experts), (seq, local_experts)) * hits
    moe_part = 0.0
    pair_dots, scaled_hidden, dgates, dups = [], [], [], []
    for expert in range(local_experts):
        gate = matmul(ffn_all, w_gate[expert])
        up = matmul(ffn_all, w_up[expert])
        back = matmul(cot_all, w_down_t[expert])
        weight = weights[:, expert : expert + 1]
        sig = 1.0 / (1.0 + jnp.exp(-gate))
        silu = gate * sig
        hidden = silu * up
        pair_dots.append(jnp.sum(hidden * back, axis=1) * hits[:, expert])
        back = back * weight
        scaled_hidden.append((hidden * weight).astype(BF16))
        dgates.append((back * up * sig * (1.0 + gate * (1.0 - sig))).astype(BF16))
        dups.append((back * silu).astype(BF16))
        moe_part += matmul_nt(scaled_hidden[-1], w_down_t[expert])
    moe_rows = lax.psum_scatter(
        moe_part.astype(BF16), "expert", scatter_dimension=0, tiled=True
    ).astype(F32)
    output = (resid_mid + moe_rows).astype(BF16)
    drow_part = sum(
        matmul_nt(dgates[i], w_gate[i]) + matmul_nt(dups[i], w_up[i]) for i in range(local_experts)
    ).astype(BF16)
    pairs = jnp.stack(pair_dots, axis=1)
    spread = (
        (expert_ids[None, :] // local_experts == me) * jnp.tile(pairs, (1, groups))
    )
    high = spread.astype(BF16)
    low = (spread - high.astype(F32)).astype(BF16)
    drow_part = jnp.concatenate(
        [drow_part, high, low, jnp.zeros((seq, -2 * experts_all % 128), BF16)], axis=1
    )

    def drow_term(o):
        return lax.dynamic_slice(
            drow_part, (ring.natural[o] * rows, 0), (rows, drow_part.shape[1])
        )

    drow = ring.scatter(drow_term)

    slice_width = hidden_units // n_dp

    def expert_term(left, rights):
        def term(rel):
            first = (dp ^ rel) * slice_width
            return jnp.stack(
                [
                    matmul_tn(left, lax.dynamic_slice(right, (0, first), (seq, slice_width)))
                    for right in rights
                ]
            )

        return term

    expert_grads = [
        dp_reduce(expert_term(left, rights), n_dp)
        for left, rights in ((cot_all, scaled_hidden), (ffn_all, dgates), (ffn_all, dups))
    ]
    grad_down, grad_gate_w, grad_up_w = expert_grads

    grad_rows = cotangent.astype(F32)
    dprobs = drow[:, width : width + experts_all]
    dprobs = dprobs + drow[:, width + experts_all : width + 2 * experts_all]
    dlogits = probs * (dprobs - jnp.sum(probs * dprobs, axis=1, keepdims=True))
    dlogits = dlogits.astype(BF16)
    grad_router = matmul_tn(ffn_in, dlogits)
    dffn = drow[:, :width] + matmul_nt(dlogits, full_router)
    grad_gain_ffn = jnp.sum(dffn * resid_mid * mid_scale, axis=0, keepdims=True)
    scaled = dffn * ffn_gain
    mid_grads = (
        grad_rows
        + mid_scale * scaled
        - resid_mid * mid_scale**3 * jnp.mean(scaled * resid_mid, axis=1, keepdims=True)
    )
    mid_low = mid_grads.astype(BF16)
    attn_grads = matmul_nt(mid_low, full_out).astype(BF16)
    both = jnp.stack([attn_grads.reshape(rows, groups, own), mid_low.reshape(rows, groups, own)], 2)
    both = both.reshape(rows, groups, 2 * own).transpose(1, 0, 2)
    both = lax.all_to_all(both, "expert", split_axis=0, concat_axis=0, tiled=True)
    both = both.reshape(seq, 2 * own)
    grad_heads, mid_columns = both[:, :own], both[:, own:]

    dq, dk, dv, dots, dgains = attend_back(
        seq_length, qkv, squares, gains_own, cosine, sine, q, k, v, grad_heads
    )
    dots = expert_sum(dots.T, groups).T / width
    scales = lax.rsqrt(squares / width + EPSILON)
    factor = scales**3 * dots
    dq = (dq - qkv[:, :own] * factor[:, 0:1]).astype(BF16)
    dk = (dk - qkv[:, own : 2 * own] * factor[:, 1:2]).astype(BF16)
    dqkv = jnp.concatenate([dq, dk, dv], axis=1)
    dattn_part = matmul_nt(dqkv, w_qkv).astype(BF16)

    def dattn_term(o):
        return lax.dynamic_slice(dattn_part, (ring.natural[o] * rows, 0), (rows, width))

    dattn = ring.scatter(dattn_term)
    in_scale = norm_scale(resid_in)
    scaled = dattn * attn_gain
    input_grad = (
        mid_grads
        + in_scale * scaled
        - resid_in * in_scale**3 * jnp.mean(scaled * resid_in, axis=1, keepdims=True)
    ).astype(BF16)

    block = width // n_dp

    def projection_term(rel):
        first = (dp ^ rel) * block
        left = lax.dynamic_slice(attn_in, (0, first), (seq, block))
        left_out = lax.dynamic_slice(attn_rows_all, (0, first), (seq, block))
        return jnp.concatenate([matmul_tn(left, dqkv), matmul_tn(left_out, mid_columns)], axis=1)

    reduced = dp_reduce(projection_term, n_dp).astype(BF16)
    reduced = lax.all_to_all(
        reduced.reshape(groups, weight_rows, 4 * own),
        "expert",
        split_axis=0,
        concat_axis=0,
        tiled=True,
    ).astype(F32)
    grads = [
        reduced[:, :, i * own : (i + 1) * own].transpose(1, 0, 2).reshape(weight_rows, width)
        for i in range(4)
    ]
    grad_gain_attn = (
        sum(jnp.sum(g * w.astype(F32), axis=1) for g, w in zip(grads, (w_query, w_key, w_value)))
        / gain_attn.astype(F32)
    )

    spread_gains = lax.dynamic_update_slice(jnp.zeros((2, width), F32), dgains, (0, me * own))
    sums = jnp.zeros((1, width), F32)
    sums = sums.at[0, 0].set(jnp.sum(used * resid_mid * resid_mid))
    sums = sums.at[0, 1].set(jnp.sum(used * moe_rows * moe_rows))
    rest = jnp.concatenate([spread_gains, grad_gain_ffn, sums, grad_router.T], axis=0)
    rest = dp_sum(expert_sum(rest, groups), n_dp)
    mine = lax.dynamic_slice(
        rest, (0, (dp * groups + me) * weight_rows), (rest.shape[0], weight_rows)
    )
    counted = jnp.sum(seq_lengths).astype(F32) * width
    rms_resid = jnp.sqrt(rest[3, 0] / counted)
    rms_moe = jnp.sqrt(rest[3, 1] / counted)
    return (
        output,
        input_grad,
        grads[0],
        grads[1],
        grads[2],
        grads[3],
        grad_gain_attn,
        mine[0],
        mine[1],
        mine[2],
        mine[4:].T,
        grad_gate_w,
        grad_up_w,
        grad_down,
        rms_resid,
        rms_moe,
    )


def solution(mesh):
    both = ("dp", "expert")
    row, vector, expert = P(both, None), P(both), P("expert", None, None)
    placed = (
        row,
        P(),
        row,
        row,
        row,
        row,
        row,
        vector,
        vector,
        vector,
        vector,
        row,
        expert,
        expert,
        expert,
        row,
    )
    grads = P("expert", None, "dp")
    return jax.shard_map(
        body,
        mesh=mesh,
        in_specs=placed,
        out_specs=(row,) * 6 + (vector,) * 4 + (row, grads, grads, grads, P(), P()),
        check_vma=False,
    )
```

time: 3000 us -> 882 us (0.29)
  waiting for transfers between devices: 2460 us -> 340 us
  blocking collectives: 149 us -> 0 us
  starting transfers between devices: 19.7 us -> 102 us
  matrix products: 211 us -> 242 us
    reduce_scatter x8 -> x1, waiting for transfers between devices: 1660 us -> 0.01 us  [body(): lax.psum_scatter(moe_part.astype(BF16), 'expert', scatter_dimension=0, ti...]
    all_to_all x4, waiting for transfers between devices: 358 us -> 20.9 us  [the longest x1 13.3 us: body(): lax.all_to_all(attended.reshape(groups, rows, own), 'expert', split_axis=...]
    ppermute x0 -> x58, waiting for transfers between devices: none -> 319 us  [the longest x9 114 us: expert_sum(): lax.ppermute(value, 'expert', [(i, i ^ step) for i in range(groups)])]
    all_gather x6 -> x3, waiting for transfers between devices: 307 us -> 0.01 us  [the longest x1 0.01 us: body(): full_out = lax.all_gather(w_out, ('dp', 'expert'), axis=0, tiled=True)]
    unnamed x17 -> x4, waiting for transfers between devices: 110 us -> 0.73 us
    unnamed x2 -> x0, blocking collectives: 80.8 us -> none
    ppermute x0 -> x58, starting transfers between devices: none -> 80.5 us  [the longest x16 39.9 us: up(): return lax.ppermute(value, 'expert', self.ahead)]
    all_gather x1 -> x0, blocking collectives: 68.1 us -> none  [body(): lax.all_gather(w_router, ('dp', 'expert'), axis=0, tiled=True)]
  transfers between devices with their start and end apart: 20 -> 66, of which waited for: 19 -> 35; matrix products, arithmetic and copies ran while one was open for 8% -> 36% of each run, Pallas kernels for 0% -> 3%
where the time goes in v1:
time: 882 us; the launch traced here: 878 us
  waiting for transfers between devices  340 us (39%)
  matrix products  242 us (27%)
  starting transfers between devices  102 us (12%)
  other arithmetic  80.5 us (9%)
  local copies, waits for them, and re-layouts  61.6 us (7%)
  between operations  26.4 us (3%)
  Pallas kernels  24.8 us (3%)
    ppermute x9, waiting for transfers between devices, expert_sum(): lax.ppermute(value, 'expert', [(i, i ^ step) for i in range(groups)])  114 us
    dot_general x33, matrix products, matmul_tn(): lax.dot_general(left, right, (((0,), (0,)), ((), ())), preferred_element_...  99.9 us
    ppermute x16, waiting for transfers between devices, up(): return lax.ppermute(value, 'expert', self.ahead)  90.3 us
    dot_general x10, matrix products, matmul(): return jnp.dot(left, right, preferred_element_type=F32)  74 us
    ppermute x4, waiting for transfers between devices, dp_reduce(): lax.ppermute(part, 'dp', [(i, i ^ 2 * y) for i in range(n_dp)]).astype(F32)  69.3 us
    dot_general x9, matrix products, matmul_nt(): lax.dot_general(left, right, (((1,), (1,)), ((), ())), preferred_element_...  68.4 us
    ppermute x16, starting transfers between devices, up(): return lax.ppermute(value, 'expert', self.ahead)  39.9 us
    ppermute x16, waiting for transfers between devices, down(): return lax.ppermute(value, 'expert', self.back)  39.9 us
  transfers between devices with their start and end apart: 66, of which 35 were waited for; matrix products, arithmetic and copies ran while one was open for 36% of the time, Pallas kernels for 3%

profile of v1, /device:TPU:0, one launch (start us, length us, event | category | flops | bytes accessed | tf_op | source)
XLA Modules:
  0.0 877.8 jit_solution(3387824092683842054)
XLA Ops:
  15.4 7.3 all-to-all-start
  27.4 33.7 %collective-permute-done = bf16[128,2048]{1,0:T(8,128)(2,1)S(1)} collective-permute-done((bf16[128,2048]{1,0:T(8,128)(2,1)S(1)}, bf16[128,2048]{1,0:T(8,128)(2,1)S(1)}, u32[]{:S(2)}, u32[]{:S(2)}) %collective-permute-start) | collective-permute-done | bytes 524320 | tf_op jit(solution)/shard_map/ppermute | solution.py:46
  61.1 10.9 %collective-permute-start.2 = (bf16[128,2048]{1,0:T(8,128)(2,1)S(1)}, bf16[128,2048]{1,0:T(8,128)(2,1)}, u32[]{:S(2)}, u32[]{:S(2)}) collective-permute-start(bf16[128,2048]{1,0:T(8,128)(2,1)S(1)} %collective-permute-done), channel_id=1, source_target_pairs={{2,4},{4,6},{6,7},{7,5},{5,3},{3,1},{1,0},{0,2},{10,12},{12,14},{1... | collective-permute-start | bytes 1572872 | tf_op jit(solution)/shard_map/ppermute | solution.py:46
  81.5 11.4 %collective-permute-done.2 = bf16[128,2048]{1,0:T(8,128)(2,1)} collective-permute-done((bf16[128,2048]{1,0:T(8,128)(2,1)S(1)}, bf16[128,2048]{1,0:T(8,128)(2,1)}, u32[]{:S(2)}, u32[]{:S(2)}) %collective-permute-start.2) | collective-permute-done | bytes 524320 | tf_op jit(solution)/shard_map/ppermute | solution.py:46
  92.9 13.9 %collective-permute-start.4 = (bf16[128,2048]{1,0:T(8,128)(2,1)}, bf16[128,2048]{1,0:T(8,128)(2,1)S(1)}, u32[]{:S(2)}, u32[]{:S(2)}) collective-permute-start(bf16[128,2048]{1,0:T(8,128)(2,1)} %collective-permute-done.2), channel_id=1, source_target_pairs={{2,4},{4,6},{6,7},{7,5},{5,3},{3,1},{1,0},{0,2},{10,12},{12,14},{1... | collective-permute-start | bytes 1572872 | tf_op jit(solution)/shard_map/ppermute | solution.py:46
  113.3 4.2 collective-permute-done.4
  133.1 4.5 fusion.2
  148.4 18.2 %collective-permute-done.11 = f32[2,1024]{0,1:T(8,128)S(1)} collective-permute-done((f32[2,1024]{0,1:T(8,128)}, f32[2,1024]{0,1:T(8,128)S(1)}, u32[]{:S(2)}, u32[]{:S(2)}) %collective-permute-start.11) | collective-permute-done | bytes 8224 | tf_op jit(solution)/shard_map/ppermute | solution.py:99
  168.5 5.6 collective-permute-start.12
  175.9 26.2 %collective-permute-done.12 = f32[2,1024]{0,1:T(8,128)} collective-permute-done((f32[2,1024]{0,1:T(8,128)}, f32[2,1024]{0,1:T(8,128)}, u32[]{:S(2)}, u32[]{:S(2)}) %collective-permute-start.12) | collective-permute-done | bytes 8224 | tf_op jit(solution)/shard_map/ppermute | solution.py:99
  204.1 20.2 %collective-permute-done.13 = f32[2,1024]{0,1:T(8,128)S(1)} collective-permute-done((f32[2,1024]{0,1:T(8,128)S(1)}, f32[2,1024]{0,1:T(8,128)S(1)}, u32[]{:S(2)}, u32[]{:S(2)}) %collective-permute-start.13) | collective-permute-done | bytes 8224 | tf_op jit(solution)/shard_map/ppermute | solution.py:99
  225.1 9.1 %shard_map.297 = (bf16[1024,256]{1,0:T(8,128)(2,1)}, bf16[1024,256]{1,0:T(8,128)(2,1)}, bf16[1024,256]{1,0:T(8,128)(2,1)}, bf16[1024,256]{1,0:T(8,128)(2,1)}) custom-call(s32[1]{0:T(128)} %dynamic_slice.160.length_ref, f32[1024,768]{1,0:T(8,128)} %copy-done.2, f32[1024,2]{1,0:T(8,128)} %add_bitcast_fusion.squares_ref, ...), custom_call_target="tpu_custom_call" | custom-call | flops 1073741824 | bytes 5242880 | tf_op jit(solution)/shard_map/pallas_call | solution.py:266
  236.3 6.2 all-to-all-start.1
  243.9 13.3 %all-to-all-done.1 = bf16[8,128,256]{1,2,0:T(8,128)(2,1)S(1)} async-done(((bf16[8,128,256]{1,2,0:T(8,128)(2,1)}), bf16[8,128,256]{1,2,0:T(8,128)(2,1)S(1)}, u32[]{:S(2)}, u32[]{:S(2)}) %all-to-all-start.1) | async-done | bytes 524320 | tf_op jit(solution)/shard_map/all_to_all | solution.py:390
  257.2 4.9 multiply_reduce_fusion.4
  268.2 10.1 %fusion.21 = f32[1024,1024]{0,1:T(8,128)} fusion(bf16[1024,2048]{1,0:T(8,128)(2,1)} %all-gather.6.cloned.1.call-done, bf16[2,2048,1024]{2,1,0:T(8,128)(2,1)} %param.36), kind=kOutput, calls=%fused_computation.32 | convolution fusion | flops 4294967296 | bytes 12582912 | tf_op jit(solution)/shard_map/dot_general | solution.py:144
  280.9 8.3 fusion.9
  295.4 7.5 collective-permute-done.18
  314.3 8.5 fusion.31
  322.8 10.2 %fusion.19 = f32[1024,1024]{0,1:T(8,128)} fusion(bf16[1024,2048]{1,0:T(8,128)(2,1)} %constant_dynamic-update-slice_fusion.1, bf16[2,2048,1024]{2,1,0:T(8,128)(2,1)} %param.34), kind=kOutput, calls=%fused_computation.30 | convolution fusion | flops 4294967296 | bytes 12582912 | tf_op jit(solution)/shard_map/dot_general | solution.py:144
  333.1 12.1 %multiply_reduce_fusion = (f32[1024]{0:T(1024)S(1)}, bf16[1024,1024]{0,1:T(8,128)(2,1)}, bf16[1024,1024]{0,1:T(8,128)(2,1)}, bf16[1024,1024]{0,1:T(8,128)(2,1)}) fusion(f32[1024,1024]{0,1:T(8,128)} %fusion.9, f32[1024,1024]{0,1:T(8,128)} %fusion.19, f32[1024]{0:T(1024)S(1)} %bitcast.289, bf16[1024,2048]{1,0:T(8,128)(2,1)} %constant_dynamic-update-slice_fusion.1, ...), kind=kOutput, calls=%fused_computation.44 | convolution fusion | flops 4314889216 | bytes 23076864 | tf_op jit(solution)/shard_map/dot_general | solution.py:144
  345.2 8.6 fusion.11
  353.8 11.9 %multiply_reduce_fusion.1 = (f32[1024]{0:T(1024)S(1)}, bf16[1024,1024]{0,1:T(8,128)(2,1)}, bf16[1024,1024]{0,1:T(8,128)(2,1)}, bf16[1024,1024]{0,1:T(8,128)(2,1)}) fusion(f32[1024,1024]{0,1:T(8,128)} %fusion.21, f32[1024,1024]{0,1:T(8,128)} %fusion.31, f32[1024]{0:T(1024)S(1)} %bitcast.288, bf16[1024,2048]{1,0:T(8,128)(2,1)} %constant_dynamic-update-slice_fusion.1, ...), kind=kOutput, calls=%fused_computation.45 | convolution fusion | flops 4314889216 | bytes 23076864 | tf_op jit(solution)/shard_map/dot_general | solution.py:144
  365.7 9.1 %add_convert_fusion.1 = bf16[1024,2048]{1,0:T(8,128)(2,1)} fusion(f32[1024,2048]{1,0:T(8,128)} %fusion.11, bf16[1024,1024]{0,1:T(8,128)(2,1)} %get-tuple-element.176, bf16[2,2048,1024]{2,1,0:T(8,128)(2,1)S(1)} %bitcast.295), kind=kOutput, calls=%fused_computation.7 | convolution fusion | flops 4299161600 | bytes 18874368 | tf_op jit(solution)/shard_map/dot_general | solution.py:148
  388.1 4.7 fusion.58
  392.8 4.6 fusion.59
  397.4 4.9 convolution_bitcast_fusion.5
  402.3 5.0 convolution_bitcast_fusion.4
  407.3 4.9 convolution_bitcast_fusion.7
  412.3 5.0 convolution_bitcast_fusion.6
  417.3 4.8 fusion.52
  425.9 4.6 fusion.53
  430.5 4.5 fusion.55
  435.0 5.0 convolution_bitcast_fusion.9
  440.0 5.0 convolution_bitcast_fusion.8
  445.0 5.0 convolution_bitcast_fusion.11
  450.0 4.9 convolution_bitcast_fusion.10
  455.0 6.8 fusion.25
  461.7 6.8 fusion.13
  468.6 7.2 fusion.17
  486.8 16.9 %add_convert_fusion = bf16[1024,2048]{1,0:T(8,128)(2,1)} fusion(f32[1024,2048]{1,0:T(8,128)} %fusion.17, f32[1024,2048]{1,0:T(8,128)} %fusion.13, f32[1024,2048]{1,0:T(8,128)} %fusion.25, bf16[1024,1024]{0,1:T(8,128)(2,1)} %get-tuple-element.171, bf16[2,2048,1024]{2,1,0:T(8,128)(2,1)} %param.34), kind=kOutput, calls=%fused_computation.6 | convolution fusion | flops 4303355904 | bytes 35651584 | tf_op jit(solution)/shard_map/dot_general | solution.py:148
  503.7 7.8 concatenate.55
  518.7 9.6 %collective-permute-done.22 = bf16[64,2176]{1,0:T(8,128)(2,1)S(1)} collective-permute-done((bf16[64,2176]{1,0:T(8,128)(2,1)S(1)}, bf16[64,2176]{1,0:T(8,128)(2,1)S(1)}, u32[]{:S(2)}, u32[]{:S(2)}) %collective-permute-start.22) | collective-permute-done | bytes 278560 | tf_op jit(solution)/shard_map/ppermute | solution.py:46
  528.4 8.3 collective-permute-done.26
  542.1 13.7 %collective-permute-done.27 = bf16[128,2176]{1,0:T(8,128)(2,1)S(1)} collective-permute-done((bf16[128,2176]{1,0:T(8,128)(2,1)S(1)}, bf16[128,2176]{1,0:T(8,128)(2,1)S(1)}, u32[]{:S(2)}, u32[]{:S(2)}) %collective-permute-start.27) | collective-permute-done | bytes 557088 | tf_op jit(solution)/shard_map/ppermute | solution.py:49
  563.7 6.4 collective-permute-done.24
  579.2 7.2 collective-permute-done.25
  598.5 6.3 convolution_convert_fusion.13
  607.8 4.1 all-to-all-start.2
  612.2 4.8 fusion.6
  621.5 19.3 %collective-permute-done.57 = bf16[2,2048,256]{1,2,0:T(8,128)(2,1)} collective-permute-done((bf16[2,2048,256]{1,2,0:T(8,128)(2,1)}, bf16[2,2048,256]{1,2,0:T(8,128)(2,1)}, u32[]{:S(2)}, u32[]{:S(2)}) %collective-permute-start.57) | collective-permute-done | bytes 2097184 | tf_op jit(solution)/shard_map/ppermute | solution.py:133
  640.8 5.3 fusion.7
  652.5 15.7 %shard_map.298 = (f32[1024,256]{1,0:T(8,128)}, f32[1024,256]{1,0:T(8,128)}, bf16[1024,256]{1,0:T(8,128)(2,1)}, f32[1024,2]{1,0:T(8,128)}, f32[2,256]{1,0:T(2,128)}) custom-call(s32[1]{0:T(128)} %dynamic_slice.160.length_ref, f32[1024,768]{1,0:T(8,128)} %copy-done.2, f32[1024,2]{1,0:T(8,128)} %add_bitcast_fusion.squares_ref, ...), custom_call_target="tpu_custom_call" | custom-call | flops 2684354560 | bytes 10485760 | tf_op jit(solution)/shard_map/pallas_call | solution.py:282
  671.7 11.6 %collective-permute-done.30 = f32[2,1024]{0,1:T(8,128)S(1)} collective-permute-done((f32[2,1024]{0,1:T(8,128)}, f32[2,1024]{0,1:T(8,128)S(1)}, u32[]{:S(2)}, u32[]{:S(2)}) %collective-permute-start.30) | collective-permute-done | bytes 8224 | tf_op jit(solution)/shard_map/ppermute | solution.py:99
  688.0 9.1 %collective-permute-done.31 = f32[2,1024]{0,1:T(8,128)} collective-permute-done((f32[2,1024]{0,1:T(8,128)}, f32[2,1024]{0,1:T(8,128)}, u32[]{:S(2)}, u32[]{:S(2)}) %collective-permute-start.31) | collective-permute-done | bytes 8224 | tf_op jit(solution)/shard_map/ppermute | solution.py:99
  700.5 19.9 %collective-permute-done.32 = f32[2,1024]{0,1:T(8,128)S(1)} collective-permute-done((f32[2,1024]{0,1:T(8,128)S(1)}, f32[2,1024]{0,1:T(8,128)S(1)}, u32[]{:S(2)}, u32[]{:S(2)}) %collective-permute-start.32) | collective-permute-done | bytes 8224 | tf_op jit(solution)/shard_map/ppermute | solution.py:99
  728.7 4.9 collective-permute-done.33
  740.4 8.7 collective-permute-done.38
  752.1 7.1 collective-permute-done.46
  767.4 5.1 fusion.5
  780.4 50.0 %collective-permute-done.43 = bf16[512,1024]{1,0:T(8,128)(2,1)S(1)} collective-permute-done((bf16[512,1024]{1,0:T(8,128)(2,1)S(1)}, bf16[512,1024]{1,0:T(8,128)(2,1)S(1)}, u32[]{:S(2)}, u32[]{:S(2)}) %collective-permute-start.43) | collective-permute-done | bytes 1048608 | tf_op jit(solution)/shard_map/ppermute | solution.py:133
  838.3 6.0 fusion.3
  844.4 5.5 copy.207
  858.2 7.7 all-to-all-done.3
  (438 shorter events, 230.9 us)
Async XLA Ops:
  7.2 250.0 %all-gather.4.cloned.1.call-start = ((), (), s32[]{:S(2)}) async-start(), calls=%async_computation.5 | async-start | bytes 8650752 | tf_op jit(solution)/shard_map/all_gather | solution.py:366
  15.4 94.7 %all-to-all-start = ((bf16[8,64,896]{2,1,0:T(8,128)(2,1)}), bf16[8,64,896]{2,1,0:T(8,128)(2,1)S(1)}, u32[]{:S(2)}, u32[]{:S(2)}) async-start(bf16[8,64,896]{2,1,0:T(8,128)(2,1)} %copy.180), calls=%async_computation | async-start | bytes 1835008 | tf_op jit(solution)/shard_map/all_to_all | solution.py:358
  22.7 245.5 %all-gather.6.cloned.1.call-start = ((), (), s32[]{:S(2)}) async-start(), calls=%async_computation.7 | async-start | bytes 4718592 | tf_op jit(solution)/shard_map/all_gather | solution.py:367
  22.7 38.4 %collective-permute-start = (bf16[128,2048]{1,0:T(8,128)(2,1)S(1)}, bf16[128,2048]{1,0:T(8,128)(2,1)S(1)}, u32[]{:S(2)}, u32[]{:S(2)}) collective-permute-start(bf16[128,2048]{1,0:T(8,128)(2,1)S(1)} %copy-done.6), channel_id=1, source_target_pairs={{2,4},{4,6},{6,7},{7,5},{5,3},{3,1},{1,0},{0,2},{10,12},{12,14},{1... | collective-permute-start | bytes 1572872 | tf_op jit(solution)/shard_map/ppermute | solution.py:46
  24.8 47.3 %collective-permute-start.1 = (bf16[128,2048]{1,0:T(8,128)(2,1)S(1)}, bf16[128,2048]{1,0:T(8,128)(2,1)S(1)}, u32[]{:S(2)}, u32[]{:S(2)}) collective-permute-start(bf16[128,2048]{1,0:T(8,128)(2,1)S(1)} %copy-done.6), channel_id=1, source_target_pairs={{4,2},{6,4},{7,6},{5,7},{3,5},{1,3},{0,1},{2,0},{12,10},{14,12},{1... | collective-permute-start | bytes 1572872 | tf_op jit(solution)/shard_map/ppermute | solution.py:49
  61.1 31.8 %collective-permute-start.2 = (bf16[128,2048]{1,0:T(8,128)(2,1)S(1)}, bf16[128,2048]{1,0:T(8,128)(2,1)}, u32[]{:S(2)}, u32[]{:S(2)}) collective-permute-start(bf16[128,2048]{1,0:T(8,128)(2,1)S(1)} %collective-permute-done), channel_id=1, source_target_pairs={{2,4},{4,6},{6,7},{7,5},{5,3},{3,1},{1,0},{0,2},{10,12},{12,14},{1... | collective-permute-start | bytes 1572872 | tf_op jit(solution)/shard_map/ppermute | solution.py:46
  72.1 35.3 %collective-permute-start.3 = (bf16[128,2048]{1,0:T(8,128)(2,1)S(1)}, bf16[128,2048]{1,0:T(8,128)(2,1)S(1)}, u32[]{:S(2)}, u32[]{:S(2)}) collective-permute-start(bf16[128,2048]{1,0:T(8,128)(2,1)S(1)} %collective-permute-done.1), channel_id=1, source_target_pairs={{4,2},{6,4},{7,6},{5,7},{3,5},{1,3},{0,1},{2,0},{12,10},{14,12},{1... | collective-permute-start | bytes 1572872 | tf_op jit(solution)/shard_map/ppermute | solution.py:49
  92.9 24.6 %collective-permute-start.4 = (bf16[128,2048]{1,0:T(8,128)(2,1)}, bf16[128,2048]{1,0:T(8,128)(2,1)S(1)}, u32[]{:S(2)}, u32[]{:S(2)}) collective-permute-start(bf16[128,2048]{1,0:T(8,128)(2,1)} %collective-permute-done.2), channel_id=1, source_target_pairs={{2,4},{4,6},{6,7},{7,5},{5,3},{3,1},{1,0},{0,2},{10,12},{12,14},{1... | collective-permute-start | bytes 1572872 | tf_op jit(solution)/shard_map/ppermute | solution.py:46
  107.3 13.0 %collective-permute-start.5 = (bf16[128,2048]{1,0:T(8,128)(2,1)S(1)}, bf16[128,2048]{1,0:T(8,128)(2,1)S(1)}, u32[]{:S(2)}, u32[]{:S(2)}) collective-permute-start(bf16[128,2048]{1,0:T(8,128)(2,1)S(1)} %collective-permute-done.3), channel_id=1, source_target_pairs={{4,2},{6,4},{7,6},{5,7},{3,5},{1,3},{0,1},{2,0},{12,10},{14,12},{1... | collective-permute-start | bytes 1572872 | tf_op jit(solution)/shard_map/ppermute | solution.py:49
  110.7 18.2 %collective-permute-start.8 = (bf16[512,896]{0,1:T(8,128)(2,1)S(1)}, bf16[512,896]{0,1:T(8,128)(2,1)S(1)}, u32[]{:S(2)}, u32[]{:S(2)}) collective-permute-start(bf16[512,896]{0,1:T(8,128)(2,1)S(1)} %copy.181), channel_id=1, source_target_pairs={{0,16},{8,24},{16,0},{24,8},{1,17},{9,25},{17,1},{25,9},{2,18},{10... | collective-permute-start | bytes 2752520 | tf_op jit(solution)/shard_map/ppermute | solution.py:117
  117.5 8.3 collective-permute-start.6
  120.3 8.5 collective-permute-start.7
  123.4 9.4 %collective-permute-start.9 = (bf16[512,896]{0,1:T(8,128)(2,1)S(1)}, bf16[512,896]{0,1:T(8,128)(2,1)S(1)}, u32[]{:S(2)}, u32[]{:S(2)}) collective-permute-start(bf16[512,896]{0,1:T(8,128)(2,1)S(1)} %copy.181), channel_id=1, source_target_pairs={{0,8},{8,0},{16,24},{24,16},{1,9},{9,1},{17,25},{25,17},{2,10},{10... | collective-permute-start | bytes 2752520 | tf_op jit(solution)/shard_map/ppermute | solution.py:119
  143.0 23.6 %collective-permute-start.11 = (f32[2,1024]{0,1:T(8,128)}, f32[2,1024]{0,1:T(8,128)S(1)}, u32[]{:S(2)}, u32[]{:S(2)}) collective-permute-start(f32[2,1024]{0,1:T(8,128)} %copy.187), channel_id=1, source_target_pairs={{0,1},{1,0},{2,3},{3,2},{4,5},{5,4},{6,7},{7,6},{8,9},{9,8},{10,11... | collective-permute-start | bytes 24584 | tf_op jit(solution)/shard_map/ppermute | solution.py:99
  168.5 33.7 %collective-permute-start.12 = (f32[2,1024]{0,1:T(8,128)}, f32[2,1024]{0,1:T(8,128)}, u32[]{:S(2)}, u32[]{:S(2)}) collective-permute-start(f32[2,1024]{0,1:T(8,128)} %add.416), channel_id=1, source_target_pairs={{0,2},{1,3},{2,0},{3,1},{4,6},{5,7},{6,4},{7,5},{8,10},{9,11},{10,... | collective-permute-start | bytes 24584 | tf_op jit(solution)/shard_map/ppermute | solution.py:99
  203.4 20.9 %collective-permute-start.13 = (f32[2,1024]{0,1:T(8,128)S(1)}, f32[2,1024]{0,1:T(8,128)S(1)}, u32[]{:S(2)}, u32[]{:S(2)}) collective-permute-start(f32[2,1024]{0,1:T(8,128)S(1)} %add.417), channel_id=1, source_target_pairs={{0,4},{1,5},{2,6},{3,7},{4,0},{5,1},{6,2},{7,3},{8,12},{9,13},{10,... | collective-permute-start | bytes 24584 | tf_op jit(solution)/shard_map/ppermute | solution.py:99
  236.3 20.9 %all-to-all-start.1 = ((bf16[8,128,256]{1,2,0:T(8,128)(2,1)}), bf16[8,128,256]{1,2,0:T(8,128)(2,1)S(1)}, u32[]{:S(2)}, u32[]{:S(2)}) async-start(bf16[8,128,256]{1,2,0:T(8,128)(2,1)} %copy.189), calls=%async_computation.1 | async-start | bytes 1048576 | tf_op jit(solution)/shard_map/all_to_all | solution.py:390
  242.5 351.5 %reduce-scatter.2.cloned.1.call-start = ((), (), s32[]{:S(2)}) async-start(), calls=%async_computation.6 | async-start | bytes 4718592 | tf_op jit(solution)/shard_map/reduce_scatter | solution.py:421
  266.2 12.6 %collective-permute-start.14 = (bf16[128,2048]{1,0:T(8,128)(2,1)S(1)}, bf16[128,2048]{1,0:T(8,128)(2,1)S(1)}, u32[]{:S(2)}, u32[]{:S(2)}) collective-permute-start(bf16[128,2048]{1,0:T(8,128)(2,1)S(1)} %get-tuple-element.169), channel_id=1, source_target_pairs={{2,4},{4,6},{6,7},{7,5},{5,3},{3,1},{1,0},{0,2},{10,12},{12,14},{1... | collective-permute-start | bytes 1572872 | tf_op jit(solution)/shard_map/ppermute | solution.py:46
  266.9 12.2 %collective-permute-start.15 = (bf16[128,2048]{1,0:T(8,128)(2,1)S(1)}, bf16[128,2048]{1,0:T(8,128)(2,1)S(1)}, u32[]{:S(2)}, u32[]{:S(2)}) collective-permute-start(bf16[128,2048]{1,0:T(8,128)(2,1)S(1)} %get-tuple-element.169), channel_id=1, source_target_pairs={{4,2},{6,4},{7,6},{5,7},{3,5},{1,3},{0,1},{2,0},{12,10},{14,12},{1... | collective-permute-start | bytes 1572872 | tf_op jit(solution)/shard_map/ppermute | solution.py:49
  278.8 12.1 %collective-permute-start.16 = (bf16[128,2048]{1,0:T(8,128)(2,1)S(1)}, bf16[128,2048]{1,0:T(8,128)(2,1)S(1)}, u32[]{:S(2)}, u32[]{:S(2)}) collective-permute-start(bf16[128,2048]{1,0:T(8,128)(2,1)S(1)} %collective-permute-done.14), channel_id=1, source_target_pairs={{2,4},{4,6},{6,7},{7,5},{5,3},{3,1},{1,0},{0,2},{10,12},{12,14},{1... | collective-permute-start | bytes 1572872 | tf_op jit(solution)/shard_map/ppermute | solution.py:46
  279.1 11.8 %collective-permute-start.17 = (bf16[128,2048]{1,0:T(8,128)(2,1)S(1)}, bf16[128,2048]{1,0:T(8,128)(2,1)S(1)}, u32[]{:S(2)}, u32[]{:S(2)}) collective-permute-start(bf16[128,2048]{1,0:T(8,128)(2,1)S(1)} %collective-permute-done.15), channel_id=1, source_target_pairs={{4,2},{6,4},{7,6},{5,7},{3,5},{1,3},{0,1},{2,0},{12,10},{14,12},{1... | collective-permute-start | bytes 1572872 | tf_op jit(solution)/shard_map/ppermute | solution.py:49
  290.9 12.0 %collective-permute-start.18 = (bf16[128,2048]{1,0:T(8,128)(2,1)S(1)}, bf16[128,2048]{1,0:T(8,128)(2,1)S(1)}, u32[]{:S(2)}, u32[]{:S(2)}) collective-permute-start(bf16[128,2048]{1,0:T(8,128)(2,1)S(1)} %collective-permute-done.16), channel_id=1, source_target_pairs={{2,4},{4,6},{6,7},{7,5},{5,3},{3,1},{1,0},{0,2},{10,12},{12,14},{1... | collective-permute-start | bytes 1572872 | tf_op jit(solution)/shard_map/ppermute | solution.py:46
  290.9 12.1 %collective-permute-start.19 = (bf16[128,2048]{1,0:T(8,128)(2,1)S(1)}, bf16[128,2048]{1,0:T(8,128)(2,1)S(1)}, u32[]{:S(2)}, u32[]{:S(2)}) collective-permute-start(bf16[128,2048]{1,0:T(8,128)(2,1)S(1)} %collective-permute-done.17), channel_id=1, source_target_pairs={{4,2},{6,4},{7,6},{5,7},{3,5},{1,3},{0,1},{2,0},{12,10},{14,12},{1... | collective-permute-start | bytes 1572872 | tf_op jit(solution)/shard_map/ppermute | solution.py:49
  302.9 6.4 collective-permute-start.20
  303.0 7.0 collective-permute-start.21
  374.8 311.2 %all-gather.8.cloned.1.call-start = ((), (), s32[]{:S(2)}) async-start(), calls=%async_computation.8 | async-start | bytes 4718592 | tf_op jit(solution)/shard_map/all_gather | solution.py:394
  480.2 107.5 %collective-permute-start.56 = (bf16[2,2048,256]{1,2,0:T(8,128)(2,1)}, bf16[2,2048,256]{1,2,0:T(8,128)(2,1)}, u32[]{:S(2)}, u32[]{:S(2)}) collective-permute-start(bf16[2,2048,256]{1,2,0:T(8,128)(2,1)} %pad_maximum_fusion.5), channel_id=1, source_target_pairs={{0,8},{8,0},{16,24},{24,16},{1,9},{9,1},{17,25},{25,17},{2,10},{10... | collective-permute-start | bytes 6291464 | tf_op jit(solution)/shard_map/ppermute | solution.py:129
  484.2 137.2 %collective-permute-start.55 = (bf16[2,2048,256]{1,2,0:T(8,128)(2,1)}, bf16[2,2048,256]{1,2,0:T(8,128)(2,1)}, u32[]{:S(2)}, u32[]{:S(2)}) collective-permute-start(bf16[2,2048,256]{1,2,0:T(8,128)(2,1)} %pad_maximum_fusion.4), channel_id=1, source_target_pairs={{0,8},{8,0},{16,24},{24,16},{1,9},{9,1},{17,25},{25,17},{2,10},{10... | collective-permute-start | bytes 6291464 | tf_op jit(solution)/shard_map/ppermute | solution.py:129
  486.3 273.0 %collective-permute-start.52 = (bf16[2,2048,256]{2,1,0:T(8,128)(2,1)}, bf16[2,2048,256]{2,1,0:T(8,128)(2,1)}, u32[]{:S(2)}, u32[]{:S(2)}) collective-permute-start(bf16[2,2048,256]{2,1,0:T(8,128)(2,1)} %pad_maximum_fusion.2), channel_id=1, source_target_pairs={{0,8},{8,0},{16,24},{24,16},{1,9},{9,1},{17,25},{25,17},{2,10},{10... | collective-permute-start | bytes 6291464 | tf_op jit(solution)/shard_map/ppermute | solution.py:129
  513.0 15.4 %collective-permute-start.22 = (bf16[64,2176]{1,0:T(8,128)(2,1)S(1)}, bf16[64,2176]{1,0:T(8,128)(2,1)S(1)}, u32[]{:S(2)}, u32[]{:S(2)}) collective-permute-start(bf16[64,2176]{1,0:T(8,128)(2,1)S(1)} %get-tuple-element.184), channel_id=1, source_target_pairs={{2,4},{4,6},{6,7},{7,5},{5,3},{3,1},{1,0},{0,2},{10,12},{12,14},{1... | collective-permute-start | bytes 835592 | tf_op jit(solution)/shard_map/ppermute | solution.py:46
  514.3 22.4 %collective-permute-start.26 = (bf16[64,2176]{1,0:T(8,128)(2,1)S(1)}, bf16[64,2176]{1,0:T(8,128)(2,1)S(1)}, u32[]{:S(2)}, u32[]{:S(2)}) collective-permute-start(bf16[64,2176]{1,0:T(8,128)(2,1)S(1)} %get-tuple-element.187), channel_id=1, source_target_pairs={{4,2},{6,4},{7,6},{5,7},{3,5},{1,3},{0,1},{2,0},{12,10},{14,12},{1... | collective-permute-start | bytes 835592 | tf_op jit(solution)/shard_map/ppermute | solution.py:49
  536.9 18.9 %collective-permute-start.27 = (bf16[128,2176]{1,0:T(8,128)(2,1)S(1)}, bf16[128,2176]{1,0:T(8,128)(2,1)S(1)}, u32[]{:S(2)}, u32[]{:S(2)}) collective-permute-start(bf16[128,2176]{1,0:T(8,128)(2,1)S(1)} %pad_maximum_fusion.11), channel_id=1, source_target_pairs={{4,2},{6,4},{7,6},{5,7},{3,5},{1,3},{0,1},{2,0},{12,10},{14,12},{1... | collective-permute-start | bytes 1671176 | tf_op jit(solution)/shard_map/ppermute | solution.py:49
  537.0 18.8 %collective-permute-start.23 = (bf16[128,2176]{1,0:T(8,128)(2,1)S(1)}, bf16[128,2176]{1,0:T(8,128)(2,1)S(1)}, u32[]{:S(2)}, u32[]{:S(2)}) collective-permute-start(bf16[128,2176]{1,0:T(8,128)(2,1)S(1)} %pad_maximum_fusion.10), channel_id=1, source_target_pairs={{2,4},{4,6},{6,7},{7,5},{5,3},{3,1},{1,0},{0,2},{10,12},{12,14},{1... | collective-permute-start | bytes 1671176 | tf_op jit(solution)/shard_map/ppermute | solution.py:46
  556.1 14.0 %collective-permute-start.24 = (bf16[128,2176]{1,0:T(8,128)(2,1)S(1)}, bf16[128,2176]{1,0:T(8,128)(2,1)S(1)}, u32[]{:S(2)}, u32[]{:S(2)}) collective-permute-start(bf16[128,2176]{1,0:T(8,128)(2,1)S(1)} %get-tuple-element.180), channel_id=1, source_target_pairs={{2,4},{4,6},{6,7},{7,5},{5,3},{3,1},{1,0},{0,2},{10,12},{12,14},{1... | collective-permute-start | bytes 1671176 | tf_op jit(solution)/shard_map/ppermute | solution.py:46
  558.4 14.3 %collective-permute-start.28 = (bf16[128,2176]{1,0:T(8,128)(2,1)S(1)}, bf16[128,2176]{1,0:T(8,128)(2,1)S(1)}, u32[]{:S(2)}, u32[]{:S(2)}) collective-permute-start(bf16[128,2176]{1,0:T(8,128)(2,1)S(1)} %get-tuple-element.181), channel_id=1, source_target_pairs={{4,2},{6,4},{7,6},{5,7},{3,5},{1,3},{0,1},{2,0},{12,10},{14,12},{1... | collective-permute-start | bytes 1671176 | tf_op jit(solution)/shard_map/ppermute | solution.py:49
  573.0 13.4 %collective-permute-start.25 = (bf16[128,2176]{1,0:T(8,128)(2,1)S(1)}, bf16[128,2176]{1,0:T(8,128)(2,1)S(1)}, u32[]{:S(2)}, u32[]{:S(2)}) collective-permute-start(bf16[128,2176]{1,0:T(8,128)(2,1)S(1)} %get-tuple-element.178), channel_id=1, source_target_pairs={{2,4},{4,6},{6,7},{7,5},{5,3},{3,1},{1,0},{0,2},{10,12},{12,14},{1... | collective-permute-start | bytes 1671176 | tf_op jit(solution)/shard_map/ppermute | solution.py:46
  574.8 12.5 %collective-permute-start.29 = (bf16[128,2176]{1,0:T(8,128)(2,1)S(1)}, bf16[128,2176]{1,0:T(8,128)(2,1)S(1)}, u32[]{:S(2)}, u32[]{:S(2)}) collective-permute-start(bf16[128,2176]{1,0:T(8,128)(2,1)S(1)} %get-tuple-element.179), channel_id=1, source_target_pairs={{4,2},{6,4},{7,6},{5,7},{3,5},{1,3},{0,1},{2,0},{12,10},{14,12},{1... | collective-permute-start | bytes 1671176 | tf_op jit(solution)/shard_map/ppermute | solution.py:49
  586.4 25.8 %collective-permute-start.53 = (bf16[2,2048,256]{2,1,0:T(8,128)(2,1)}, bf16[2,2048,256]{2,1,0:T(8,128)(2,1)}, u32[]{:S(2)}, u32[]{:S(2)}) collective-permute-start(bf16[2,2048,256]{2,1,0:T(8,128)(2,1)} %pad_maximum_fusion.3), channel_id=1, source_target_pairs={{0,8},{8,0},{16,24},{24,16},{1,9},{9,1},{17,25},{25,17},{2,10},{10... | collective-permute-start | bytes 6291464 | tf_op jit(solution)/shard_map/ppermute | solution.py:129
  587.2 30.3 %collective-permute-start.50 = (bf16[2,2048,256]{2,1,0:T(8,128)(2,1)}, bf16[2,2048,256]{2,1,0:T(8,128)(2,1)}, u32[]{:S(2)}, u32[]{:S(2)}) collective-permute-start(bf16[2,2048,256]{2,1,0:T(8,128)(2,1)} %pad_maximum_fusion.1), channel_id=1, source_target_pairs={{0,8},{8,0},{16,24},{24,16},{1,9},{9,1},{17,25},{25,17},{2,10},{10... | collective-permute-start | bytes 6291464 | tf_op jit(solution)/shard_map/ppermute | solution.py:129
  591.5 49.3 %collective-permute-start.57 = (bf16[2,2048,256]{1,2,0:T(8,128)(2,1)}, bf16[2,2048,256]{1,2,0:T(8,128)(2,1)}, u32[]{:S(2)}, u32[]{:S(2)}) collective-permute-start(bf16[2,2048,256]{1,2,0:T(8,128)(2,1)} %fusion.8), channel_id=1, source_target_pairs={{0,16},{8,24},{16,0},{24,8},{1,17},{9,25},{17,1},{25,9},{2,18},{10... | collective-permute-start | bytes 6291464 | tf_op jit(solution)/shard_map/ppermute | solution.py:133
  607.8 43.9 %all-to-all-start.2 = ((bf16[8,128,512]{2,1,0:T(8,128)(2,1)}), bf16[8,128,512]{2,1,0:T(8,128)(2,1)S(1)}, u32[]{:S(2)}, u32[]{:S(2)}) async-start(bf16[8,128,512]{2,1,0:T(8,128)(2,1)} %bitcast.41), calls=%async_computation.3 | async-start | bytes 2097152 | tf_op jit(solution)/shard_map/all_to_all | solution.py:483
  617.0 143.2 %collective-permute-start.54 = (bf16[2,2048,256]{2,1,0:T(8,128)(2,1)}, bf16[2,2048,256]{2,1,0:T(8,128)(2,1)}, u32[]{:S(2)}, u32[]{:S(2)}) collective-permute-start(bf16[2,2048,256]{2,1,0:T(8,128)(2,1)} %fusion.6), channel_id=1, source_target_pairs={{0,16},{8,24},{16,0},{24,8},{1,17},{9,25},{17,1},{25,9},{2,18},{10... | collective-permute-start | bytes 6291464 | tf_op jit(solution)/shard_map/ppermute | solution.py:133
  668.3 15.0 %collective-permute-start.30 = (f32[2,1024]{0,1:T(8,128)}, f32[2,1024]{0,1:T(8,128)S(1)}, u32[]{:S(2)}, u32[]{:S(2)}) collective-permute-start(f32[2,1024]{0,1:T(8,128)} %bitcast.271), channel_id=1, source_target_pairs={{0,1},{1,0},{2,3},{3,2},{4,5},{5,4},{6,7},{7,6},{8,9},{9,8},{10,11... | collective-permute-start | bytes 24584 | tf_op jit(solution)/shard_map/ppermute | solution.py:99
  670.7 57.8 %collective-permute-start.44 = (f32[20,2048]{1,0:T(8,128)}, f32[20,2048]{1,0:T(8,128)S(1)}, u32[]{:S(2)}, u32[]{:S(2)}) collective-permute-start(f32[20,2048]{1,0:T(8,128)} %pad_maximum_fusion.16), channel_id=1, source_target_pairs={{0,1},{1,0},{2,3},{3,2},{4,5},{5,4},{6,7},{7,6},{8,9},{9,8},{10,11... | collective-permute-start | bytes 491528 | tf_op jit(solution)/shard_map/ppermute | solution.py:99
  685.2 11.9 %collective-permute-start.31 = (f32[2,1024]{0,1:T(8,128)}, f32[2,1024]{0,1:T(8,128)}, u32[]{:S(2)}, u32[]{:S(2)}) collective-permute-start(f32[2,1024]{0,1:T(8,128)} %bitcast_add_fusion), channel_id=1, source_target_pairs={{0,2},{1,3},{2,0},{3,1},{4,6},{5,7},{6,4},{7,5},{8,10},{9,11},{10,... | collective-permute-start | bytes 24584 | tf_op jit(solution)/shard_map/ppermute | solution.py:99
  698.3 22.0 %collective-permute-start.32 = (f32[2,1024]{0,1:T(8,128)S(1)}, f32[2,1024]{0,1:T(8,128)S(1)}, u32[]{:S(2)}, u32[]{:S(2)}) collective-permute-start(f32[2,1024]{0,1:T(8,128)S(1)} %add.447), channel_id=1, source_target_pairs={{0,4},{1,5},{2,6},{3,7},{4,0},{5,1},{6,2},{7,3},{8,12},{9,13},{10,... | collective-permute-start | bytes 24584 | tf_op jit(solution)/shard_map/ppermute | solution.py:99
  725.1 8.5 collective-permute-start.33
  725.4 9.2 %collective-permute-start.37 = (bf16[64,2048]{1,0:T(8,128)(2,1)S(1)}, bf16[64,2048]{1,0:T(8,128)(2,1)S(1)}, u32[]{:S(2)}, u32[]{:S(2)}) collective-permute-start(bf16[64,2048]{1,0:T(8,128)(2,1)S(1)} %get-tuple-element.197), channel_id=1, source_target_pairs={{4,2},{6,4},{7,6},{5,7},{3,5},{1,3},{0,1},{2,0},{12,10},{14,12},{1... | collective-permute-start | bytes 786440 | tf_op jit(solution)/shard_map/ppermute | solution.py:49
  728.6 10.2 %collective-permute-start.45 = (f32[20,2048]{1,0:T(8,128)S(1)}, f32[20,2048]{1,0:T(8,128)S(1)}, u32[]{:S(2)}, u32[]{:S(2)}) collective-permute-start(f32[20,2048]{1,0:T(8,128)S(1)} %fusion.163), channel_id=1, source_target_pairs={{0,2},{1,3},{2,0},{3,1},{4,6},{5,7},{6,4},{7,5},{8,10},{9,11},{10,... | collective-permute-start | bytes 491528 | tf_op jit(solution)/shard_map/ppermute | solution.py:99
  734.8 14.3 %collective-permute-start.38 = (bf16[128,2048]{1,0:T(8,128)(2,1)S(1)}, bf16[128,2048]{1,0:T(8,128)(2,1)S(1)}, u32[]{:S(2)}, u32[]{:S(2)}) collective-permute-start(bf16[128,2048]{1,0:T(8,128)(2,1)S(1)} %pad_maximum_fusion.15), channel_id=1, source_target_pairs={{4,2},{6,4},{7,6},{5,7},{3,5},{1,3},{0,1},{2,0},{12,10},{14,12},{1... | collective-permute-start | bytes 1572872 | tf_op jit(solution)/shard_map/ppermute | solution.py:49
  735.6 14.8 %collective-permute-start.34 = (bf16[128,2048]{1,0:T(8,128)(2,1)S(1)}, bf16[128,2048]{1,0:T(8,128)(2,1)S(1)}, u32[]{:S(2)}, u32[]{:S(2)}) collective-permute-start(bf16[128,2048]{1,0:T(8,128)(2,1)S(1)} %pad_maximum_fusion.14), channel_id=1, source_target_pairs={{2,4},{4,6},{6,7},{7,5},{5,3},{3,1},{1,0},{0,2},{10,12},{12,14},{1... | collective-permute-start | bytes 1572872 | tf_op jit(solution)/shard_map/ppermute | solution.py:46
  738.8 20.8 %collective-permute-start.42 = (bf16[512,1024]{1,0:T(8,128)(2,1)S(1)}, bf16[512,1024]{1,0:T(8,128)(2,1)S(1)}, u32[]{:S(2)}, u32[]{:S(2)}) collective-permute-start(bf16[512,1024]{1,0:T(8,128)(2,1)S(1)} %pad_maximum_fusion.9), channel_id=1, source_target_pairs={{0,8},{8,0},{16,24},{24,16},{1,9},{9,1},{17,25},{25,17},{2,10},{10... | collective-permute-start | bytes 3145736 | tf_op jit(solution)/shard_map/ppermute | solution.py:129
  749.1 10.1 %collective-permute-start.46 = (f32[20,2048]{1,0:T(8,128)S(1)}, f32[20,2048]{1,0:T(8,128)S(1)}, u32[]{:S(2)}, u32[]{:S(2)}) collective-permute-start(f32[20,2048]{1,0:T(8,128)S(1)} %add.466), channel_id=1, source_target_pairs={{0,4},{1,5},{2,6},{3,7},{4,0},{5,1},{6,2},{7,3},{8,12},{9,13},{10,... | collective-permute-start | bytes 491528 | tf_op jit(solution)/shard_map/ppermute | solution.py:99
  750.8 15.6 %collective-permute-start.35 = (bf16[128,2048]{1,0:T(8,128)(2,1)S(1)}, bf16[128,2048]{1,0:T(8,128)(2,1)S(1)}, u32[]{:S(2)}, u32[]{:S(2)}) collective-permute-start(bf16[128,2048]{1,0:T(8,128)(2,1)S(1)} %get-tuple-element.190), channel_id=1, source_target_pairs={{2,4},{4,6},{6,7},{7,5},{5,3},{3,1},{1,0},{0,2},{10,12},{12,14},{1... | collective-permute-start | bytes 1572872 | tf_op jit(solution)/shard_map/ppermute | solution.py:46
  759.2 79.1 %collective-permute-start.49 = (bf16[2,2048,256]{2,1,0:T(8,128)(2,1)}, bf16[2,2048,256]{2,1,0:T(8,128)(2,1)}, u32[]{:S(2)}, u32[]{:S(2)}) collective-permute-start(bf16[2,2048,256]{2,1,0:T(8,128)(2,1)} %pad_maximum_fusion), channel_id=1, source_target_pairs={{0,8},{8,0},{16,24},{24,16},{1,9},{9,1},{17,25},{25,17},{2,10},{10... | collective-permute-start | bytes 6291464 | tf_op jit(solution)/shard_map/ppermute | solution.py:129
  759.2 79.1 %collective-permute-start.51 = (bf16[2,2048,256]{2,1,0:T(8,128)(2,1)}, bf16[2,2048,256]{2,1,0:T(8,128)(2,1)}, u32[]{:S(2)}, u32[]{:S(2)}) collective-permute-start(bf16[2,2048,256]{2,1,0:T(8,128)(2,1)} %fusion.4), channel_id=1, source_target_pairs={{0,16},{8,24},{16,0},{24,8},{1,17},{9,25},{17,1},{25,9},{2,18},{10... | collective-permute-start | bytes 6291464 | tf_op jit(solution)/shard_map/ppermute | solution.py:133
  760.3 20.0 %collective-permute-start.41 = (bf16[512,1024]{1,0:T(8,128)(2,1)S(1)}, bf16[512,1024]{1,0:T(8,128)(2,1)S(1)}, u32[]{:S(2)}, u32[]{:S(2)}) collective-permute-start(bf16[512,1024]{1,0:T(8,128)(2,1)S(1)} %pad_maximum_fusion.8), channel_id=1, source_target_pairs={{0,8},{8,0},{16,24},{24,16},{1,9},{9,1},{17,25},{25,17},{2,10},{10... | collective-permute-start | bytes 3145736 | tf_op jit(solution)/shard_map/ppermute | solution.py:129
  763.6 14.3 %collective-permute-start.39 = (bf16[128,2048]{1,0:T(8,128)(2,1)S(1)}, bf16[128,2048]{1,0:T(8,128)(2,1)S(1)}, u32[]{:S(2)}, u32[]{:S(2)}) collective-permute-start(bf16[128,2048]{1,0:T(8,128)(2,1)S(1)} %get-tuple-element.191), channel_id=1, source_target_pairs={{4,2},{6,4},{7,6},{5,7},{3,5},{1,3},{0,1},{2,0},{12,10},{14,12},{1... | collective-permute-start | bytes 1572872 | tf_op jit(solution)/shard_map/ppermute | solution.py:49
  766.4 64.0 %collective-permute-start.43 = (bf16[512,1024]{1,0:T(8,128)(2,1)S(1)}, bf16[512,1024]{1,0:T(8,128)(2,1)S(1)}, u32[]{:S(2)}, u32[]{:S(2)}) collective-permute-start(bf16[512,1024]{1,0:T(8,128)(2,1)S(1)} %fusion.68), channel_id=1, source_target_pairs={{0,16},{8,24},{16,0},{24,8},{1,17},{9,25},{17,1},{25,9},{2,18},{10... | collective-permute-start | bytes 3145736 | tf_op jit(solution)/shard_map/ppermute | solution.py:133
  777.9 71.9 %collective-permute-start.48 = (f32[20,2048]{1,0:T(8,128)S(1)}, f32[20,2048]{1,0:T(8,128)}, u32[]{:S(2)}, u32[]{:S(2)}) collective-permute-start(f32[20,2048]{1,0:T(8,128)S(1)} %add.468), channel_id=1, source_target_pairs={{0,16},{8,24},{16,0},{24,8},{1,17},{9,25},{17,1},{25,9},{2,18},{10... | collective-permute-start | bytes 491528 | tf_op jit(solution)/shard_map/ppermute | solution.py:107
  780.3 73.8 %collective-permute-start.36 = (bf16[128,2048]{1,0:T(8,128)(2,1)}, bf16[128,2048]{1,0:T(8,128)(2,1)S(1)}, u32[]{:S(2)}, u32[]{:S(2)}) collective-permute-start(bf16[128,2048]{1,0:T(8,128)(2,1)} %get-tuple-element.188), channel_id=1, source_target_pairs={{2,4},{4,6},{6,7},{7,5},{5,3},{3,1},{1,0},{0,2},{10,12},{12,14},{1... | collective-permute-start | bytes 1572872 | tf_op jit(solution)/shard_map/ppermute | solution.py:46
  830.4 23.6 %collective-permute-start.40 = (bf16[128,2048]{1,0:T(8,128)(2,1)}, bf16[128,2048]{1,0:T(8,128)(2,1)}, u32[]{:S(2)}, u32[]{:S(2)}) collective-permute-start(bf16[128,2048]{1,0:T(8,128)(2,1)} %get-tuple-element.189), channel_id=1, source_target_pairs={{4,2},{6,4},{7,6},{5,7},{3,5},{1,3},{0,1},{2,0},{12,10},{14,12},{1... | collective-permute-start | bytes 1572872 | tf_op jit(solution)/shard_map/ppermute | solution.py:49
  834.7 31.1 %all-to-all-start.3 = ((bf16[8,64,1024]{2,1,0:T(8,128)(2,1)}), bf16[8,64,1024]{2,1,0:T(8,128)(2,1)S(1)}, u32[]{:S(2)}, u32[]{:S(2)}) async-start(bf16[8,64,1024]{2,1,0:T(8,128)(2,1)} %bitcast.46), calls=%async_computation.4 | async-start | bytes 2097152 | tf_op jit(solution)/shard_map/all_to_all | solution.py:519
  (74 other events, 1183.4 us)
Sparse Core Ops, SparseCore 0:
  11.0 100.7 all-gather.3
  114.0 88.6 all-gather.5
  374.9 88.9 reduce-scatter.1
  466.1 84.5 all-gather.7

commit v2 on v1

--- a/solution.py
+++ b/solution.py
@@ -48,20 +48,24 @@
     def down(self, value):
         return lax.ppermute(value, "expert", self.back)
 
-    def gather(self, block):
+    def gather(self, block, hooks=None):
+        hooks = hooks or {}
         half = self.size // 2
         rows = block.shape[0]
         pieces = [(0, 0, block)]
         up, down = block, block
         for step in range(1, half):
-            up = self.up(up)
-            down = self.down(down)
+            made = hooks[step](pieces) if step in hooks else ()
+            up, down = together((self.up(up), self.down(down)), made)
             pieces += [(self.size - step, 0, up), (step, 0, down)]
+        if half in hooks:
+            hooks[half](pieces)
         pieces.append((half, 0, self.up(up[: rows // 2])))
         pieces.append((half, rows // 2, self.down(down[rows // 2 :])))
         return pieces
 
-    def scatter(self, term):
+    def scatter(self, term, hooks=None):
+        hooks = hooks or {}
         half = self.size // 2
         far = term(half)
         rows = far.shape[0]
@@ -72,6 +76,8 @@
             return (left.astype(F32) + right.astype(F32)).astype(BF16)
 
         for step in range(half - 1, 0, -1):
+            made = hooks[half - step]() if half - step in hooks else ()
+            up, down = together((up, down), made)
             ahead, behind = term(step), term(self.size - step)
             if step == half - 1:
                 ahead = jnp.concatenate([add(up, ahead[: rows // 2]), ahead[rows // 2 :]], axis=0)
@@ -81,7 +87,15 @@
             else:
                 ahead, behind = add(up, ahead), add(down, behind)
             up, down = self.up(ahead), self.down(behind)
+        made = hooks[half]() if half in hooks else ()
+        up, down = together((up, down), made)
         return up.astype(F32) + down.astype(F32) + term(0).astype(F32)
+
+
+def together(values, made):
+    if not made:
+        return values
+    return lax.optimization_barrier((*values, *made))[: len(values)]
 
 
 def place_blocks(ring, pieces, rows, width, dtype=BF16):
@@ -167,6 +181,72 @@
     return values * cosine - pltpu.roll(values, HEAD_DIM // 2, 1) * sine
 
 
+VMEM_LIMIT = 56 << 20
+SMEM_SPEC = pl.BlockSpec(memory_space=pltpu.SMEM)
+VMEM_SPEC = pl.BlockSpec(memory_space=pltpu.VMEM)
+ANY_SPEC = pl.BlockSpec(memory_space=pl.ANY)
+
+
+def params():
+    return pltpu.CompilerParams(vmem_limit_bytes=VMEM_LIMIT)
+
+
+def cost(flops, bytes_accessed, transcendentals=0):
+    return pl.CostEstimate(
+        flops=flops, bytes_accessed=bytes_accessed, transcendentals=transcendentals
+    )
+
+
+def as_rows(first, second):
+    lane = lax.broadcasted_iota(jnp.int32, (first.shape[0], 128), 1)
+    both = jnp.where(lane == 0, first, jnp.where(lane == 1, second, 0.0))
+    return both.T[:8]
+
+
+def as_columns(rows):
+    return rows.T
+
+
+def project_kernel(tokens_ref, gain_ref, w_ref, in_ref, qkv_ref, squares_ref):
+    own = w_ref.shape[1] // 3
+    values = tokens_ref[...].astype(F32)
+    normed = (values * norm_scale(values) * gain_ref[...]).astype(BF16)
+    in_ref[...] = normed
+    qkv = matmul(normed, w_ref[...])
+    qkv_ref[...] = qkv
+    query, key = qkv[:, :own], qkv[:, own : 2 * own]
+    squares_ref[...] = as_rows(
+        jnp.sum(query * query, axis=1, keepdims=True), jnp.sum(key * key, axis=1, keepdims=True)
+    )
+
+
+def project(tokens, gain, w_qkv):
+    seq, width = tokens.shape
+    columns = w_qkv.shape[1]
+    tile = min(256, seq)
+    return pl.pallas_call(
+        project_kernel,
+        grid=(seq // tile,),
+        out_shape=[
+            jax.ShapeDtypeStruct((seq, width), BF16),
+            jax.ShapeDtypeStruct((seq, columns), F32),
+            jax.ShapeDtypeStruct((8, seq), F32),
+        ],
+        in_specs=[
+            pl.BlockSpec((tile, width), lambda i: (i, 0)),
+            pl.BlockSpec((1, width), lambda i: (0, 0)),
+            pl.BlockSpec((width, columns), lambda i: (0, 0)),
+        ],
+        out_specs=[
+            pl.BlockSpec((tile, width), lambda i: (i, 0)),
+            pl.BlockSpec((tile, columns), lambda i: (i, 0)),
+            pl.BlockSpec((8, tile), lambda i: (0, i)),
+        ],
+        compiler_params=params(),
+        cost_estimate=cost(2 * seq * width * columns, 8 * seq * width),
+    )(tokens, gain, w_qkv)
+
+
 def attend_kernel(
     length_ref, qkv_ref, squares_ref, gain_ref, cos_ref, sin_ref, q_ref, k_ref, v_ref, o_ref
 ):
@@ -176,7 +256,7 @@
     length = length_ref[0]
     for start in range(0, seq, tile):
         rows = slice(start, start + tile)
-        squares = squares_ref[rows, :]
+        squares = as_columns(squares_ref[:, rows])
         cosine, sine = cos_ref[rows, :], sin_ref[rows, :]
         for part, out_ref in ((0, q_ref), (1, k_ref)):
             scale = lax.rsqrt(squares[:, part : part + 1] / width + EPSILON)
@@ -242,8 +322,9 @@
     dgain_ref[...] = jnp.zeros_like(dgain_ref)
     for start in range(0, seq, tile):
         rows = slice(start, start + tile)
-        squares = squares_ref[rows, :]
+        squares = as_columns(squares_ref[:, rows])
         cosine, sine = cos_ref[rows, :], sin_ref[rows, :]
+        both = []
         for part, out_ref in ((0, dq_ref), (1, dk_ref)):
             scale = lax.rsqrt(squares[:, part : part + 1] / width + EPSILON)
             dot = jnp.zeros((tile, 1), F32)
@@ -257,7 +338,8 @@
                 grad = grad * gain_ref[part : part + 1, columns]
                 dot += jnp.sum(grad * raw, axis=-1, keepdims=True)
                 out_ref[rows, columns] = grad * scale
-            dots_ref[rows, part : part + 1] = dot
+            both.append(dot)
+        dots_ref[:, rows] = as_rows(*both)
 
 
 def attend(length, qkv, squares, gains, cosine, sine):
@@ -266,13 +348,10 @@
     return pl.pallas_call(
         attend_kernel,
         out_shape=[shape] * 4,
-        in_specs=[pl.BlockSpec(memory_space=pltpu.SMEM)]
-        + [pl.BlockSpec(memory_space=pltpu.VMEM)] * 5,
-        out_specs=[pl.BlockSpec(memory_space=pltpu.VMEM)] * 4,
-        compiler_params=pltpu.CompilerParams(vmem_limit_bytes=56 << 20),
-        cost_estimate=pl.CostEstimate(
-            flops=4 * seq * seq * own, bytes_accessed=20 * seq * own, transcendentals=seq * seq
-        ),
+        in_specs=[SMEM_SPEC] + [VMEM_SPEC] * 5,
+        out_specs=[VMEM_SPEC] * 4,
+        compiler_params=params(),
+        cost_estimate=cost(4 * seq * seq * own, 20 * seq * own, seq * seq),
     )(length, qkv, squares, gains, cosine, sine)
 
 
@@ -285,18 +364,354 @@
             wide,
             wide,
             jax.ShapeDtypeStruct((seq, own), BF16),
-            jax.ShapeDtypeStruct((seq, 2), F32),
+            jax.ShapeDtypeStruct((8, seq), F32),
             jax.ShapeDtypeStruct((2, own), F32),
         ],
-        in_specs=[pl.BlockSpec(memory_space=pltpu.SMEM)]
-        + [pl.BlockSpec(memory_space=pltpu.VMEM)] * 9,
-        out_specs=[pl.BlockSpec(memory_space=pltpu.VMEM)] * 5,
+        in_specs=[SMEM_SPEC] + [VMEM_SPEC] * 9,
+        out_specs=[VMEM_SPEC] * 5,
         scratch_shapes=[pltpu.VMEM((seq, HEAD_DIM), F32)] * 2,
-        compiler_params=pltpu.CompilerParams(vmem_limit_bytes=56 << 20),
-        cost_estimate=pl.CostEstimate(
-            flops=10 * seq * seq * own, bytes_accessed=40 * seq * own, transcendentals=seq * seq
+        compiler_params=params(),
+        cost_estimate=cost(10 * seq * seq * own, 40 * seq * own, seq * seq),
+    )(length, qkv, squares, gains, cosine, sine, q, k, v, do)
+
+
+def finish_kernel(
+    dq_ref, dk_ref, dv_ref, qkv_ref, squares_ref, dots_ref, w_ref, dqkv_ref, din_ref
+):
+    own = dq_ref.shape[1]
+    width = HEADS * HEAD_DIM
+    scale = lax.rsqrt(as_columns(squares_ref[...]) / width + EPSILON)
+    factor = scale * scale * scale * as_columns(dots_ref[...]) / width
+    for part, grad_ref in ((0, dq_ref), (1, dk_ref)):
+        columns = slice(part * own, (part + 1) * own)
+        grad = grad_ref[...] - qkv_ref[:, columns] * factor[:, part : part + 1]
+        dqkv_ref[:, columns] = grad.astype(BF16)
+    dqkv_ref[:, 2 * own :] = dv_ref[...]
+    din_ref[...] = matmul_nt(dqkv_ref[...], w_ref[...]).astype(BF16)
+
+
+def finish(dq, dk, dv, qkv, squares, dots, w_qkv):
+    seq, own = dq.shape
+    width = w_qkv.shape[0]
+    tile = min(256, seq)
+    narrow = pl.BlockSpec((tile, own), lambda i: (i, 0))
+    wide = pl.BlockSpec((tile, 3 * own), lambda i: (i, 0))
+    flat = pl.BlockSpec((8, tile), lambda i: (0, i))
+    return pl.pallas_call(
+        finish_kernel,
+        grid=(seq // tile,),
+        out_shape=[
+            jax.ShapeDtypeStruct((seq, 3 * own), BF16),
+            jax.ShapeDtypeStruct((seq, width), BF16),
+        ],
+        in_specs=[narrow, narrow, narrow, wide, flat, flat]
+        + [pl.BlockSpec((width, 3 * own), lambda i: (0, 0))],
+        out_specs=[wide, pl.BlockSpec((tile, width), lambda i: (i, 0))],
+        compiler_params=params(),
+        cost_estimate=cost(6 * seq * width * own, 4 * seq * width),
+    )(dq, dk, dv, qkv, squares, dots, w_qkv)
+
+
+def expert_kernel(n_pieces, piece_rows, n_blocks, n_slices, index_ref, column_ref, *refs):
+    pieces, refs = refs[:n_pieces], refs[n_pieces:]
+    hits_refs, router_ref, refs = refs[:n_blocks], refs[n_blocks], refs[n_blocks + 1 :]
+    local_experts, _, wide = refs[0].shape
+    gate_ref, up_ref, gate_rows_ref, up_rows_ref, refs = *refs[:4], refs[4:]
+    back_refs = refs[: n_blocks * local_experts]
+    x_ref, weight_ref, dots_ref, made_ref, grads_ref, sems, row_sems = refs[-7:]
+    rows_out, dots_out, *outs = refs[-7 - n_blocks - 5 : -7 - n_blocks]
+    grad_outs = refs[-7 - n_blocks : -7]
+    step = pl.program_id(0)
+    total, block = x_ref.shape[0], x_ref.shape[0] // n_blocks
+    hidden_units = wide * n_slices
+    slot = lax.rem(step, 2)
+    lane = lax.broadcasted_iota(jnp.int32, (total, 128), 1)
+
+    def row_copy(source, target, at, which):
+        return pltpu.make_async_copy(
+            source.at[pl.ds(at * block, block)],
+            target.at[pl.ds(index_ref[at] * block, block)],
+            row_sems.at[which, at],
+        )
+
+    def made_copy(which, at, of_step, from_slot):
+        span = local_experts * wide
+        return pltpu.make_async_copy(
+            made_ref.at[from_slot, which, pl.ds(at * block, block)],
+            outs[which].at[
+                pl.ds(index_ref[at] * block, block),
+                pl.ds(pl.multiple_of(column_ref[of_step] * span, span), span),
+            ],
+            sems.at[from_slot, which, at],
+        )
+
+    def all_made(of_step, from_slot):
+        return [made_copy(w, at, of_step, from_slot) for w in range(3) for at in range(n_blocks)]
+
+    def hit_of(expert):
+        return jnp.concatenate([ref[:, expert : expert + 1] for ref in hits_refs], axis=0)
+
+    @pl.when(step == 0)
+    def _():
+        start = 0
+        for piece, rows in zip(pieces, piece_rows):
+            x_ref[start : start + rows, :] = piece[...]
+            start += rows
+        for at in range(n_blocks):
+            row_copy(x_ref, rows_out, at, 0).start()
+        logits = matmul(x_ref[...], router_ref[...])
+        expo = jnp.exp(logits - jnp.max(logits, axis=-1, keepdims=True))
+        probs = expo / jnp.sum(expo, axis=-1, keepdims=True)
+        which = lax.broadcasted_iota(jnp.int32, probs.shape, 1)
+        weights = jnp.zeros((total, 128), F32)
+        for expert in range(local_experts):
+            mine = which == index_ref[n_blocks] * local_experts + expert
+            weight = jnp.sum(jnp.where(mine, probs, 0.0), axis=-1, keepdims=True)
+            weights = jnp.where(lane == expert, weight * hit_of(expert), weights)
+        weight_ref[...] = weights
+        dots_ref[...] = jnp.zeros_like(dots_ref)
+
+    @pl.when((step >= 2) & (step < n_slices))
+    def _():
+        for copy in all_made(step - 2, slot):
+            copy.wait()
+
+    @pl.when(step < n_slices)
+    def _():
+        for expert in range(local_experts):
+            gate = matmul(x_ref[...], gate_ref[expert])
+            up = matmul(x_ref[...], up_ref[expert])
+            back = jnp.concatenate(
+                [ref[...] for ref in back_refs[n_blocks * expert : n_blocks * (expert + 1)]], axis=0
+            ).astype(F32)
+            weight = weight_ref[:, expert : expert + 1]
+            sig = 0.5 + 0.5 * jnp.tanh(0.5 * gate)
+            silu = gate * sig
+            hidden = silu * up
+            dot = jnp.sum(hidden * back, axis=-1, keepdims=True)
+            dots_ref[...] += jnp.where(lane == expert, dot, 0.0)
+            back = back * weight
+            dgate = (back * up * (sig + silu * (1.0 - sig))).astype(BF16)
+            dup = (back * silu).astype(BF16)
+            columns = slice(expert * wide, (expert + 1) * wide)
+            made_ref[slot, 0, :, columns] = (hidden * weight).astype(BF16)
+            for which, value in ((0, dgate), (1, dup)):
+                made_ref[slot, 1 + which, :, columns] = value
+                first = (which * local_experts + expert) * hidden_units
+                grads_ref[:, pl.ds(pl.multiple_of(first + step * wide, wide), wide)] = value
+        for copy in all_made(step, slot):
+            copy.start()
+
+    @pl.when(step == n_slices - 1)
+    def _():
+        for expert in range(local_experts):
+            dots_ref[...] = jnp.where(lane == expert, dots_ref[...] * hit_of(expert), dots_ref[...])
+        for at in range(n_blocks):
+            row_copy(dots_ref, dots_out, at, 1).start()
+
+    @pl.when(step >= n_slices)
+    def _():
+        result = None
+        for which, weights in enumerate((gate_rows_ref, up_rows_ref)):
+            for expert in range(local_experts):
+                first = (which * local_experts + expert) * hidden_units
+                part = matmul_nt(grads_ref[:, first : first + hidden_units], weights[expert])
+                result = part if result is None else result + part
+        for at in range(n_blocks):
+            grad_outs[at][...] = result[at * block : (at + 1) * block].astype(BF16)
+
+    @pl.when(step == pl.num_programs(0) - 1)
+    def _():
+        for at in range(n_blocks):
+            row_copy(x_ref, rows_out, at, 0).wait()
+            row_copy(dots_ref, dots_out, at, 1).wait()
+        for copy in all_made(n_slices - 1, (n_slices - 1) % 2) + all_made(
+            n_slices - 2, n_slices % 2
+        ):
+            copy.wait()
+
+
+def expert_call(index, column_place, pieces, hits, router, w_gate, w_up, backs, held, seq):
+    local_experts, width, hidden_units = w_gate.shape
+    n_slices, n_blocks = column_place.shape[0], index.shape[0] - 1
+    wide = hidden_units // n_slices
+    total = sum(piece.shape[0] for piece in pieces)
+    block = total // n_blocks
+    span = local_experts * hidden_units
+    tile = 512
+    assert n_slices >= 2
+
+    def at_slice(step):
+        return jnp.minimum(step, n_slices - 1)
+
+    def at_tile(step):
+        return jnp.maximum(step - n_slices, 0)
+
+    weight_spec = pl.BlockSpec(
+        (local_experts, width, wide), lambda i, index, column: (0, 0, at_slice(i))
+    )
+    rows_spec = pl.BlockSpec(
+        (local_experts, tile, hidden_units), lambda i, index, column: (0, at_tile(i), 0)
+    )
+
+    def block_spec(at, columns, tiled):
+        if tiled:
+            return pl.BlockSpec(
+                (block, columns), lambda i, index, column: (index[at], at_slice(i))
+            )
+        return pl.BlockSpec((block, columns), lambda i, index, column: (index[at], 0))
+
+    in_specs = [pl.BlockSpec(piece.shape, lambda i, index, column: (0, 0)) for piece in pieces]
+    in_specs += [block_spec(at, local_experts, False) for at in range(n_blocks)]
+    in_specs += [pl.BlockSpec(router.shape, lambda i, index, column: (0, 0))]
+    in_specs += [weight_spec, weight_spec, rows_spec, rows_spec]
+    in_specs += [block_spec(at, wide, True) for _ in range(local_experts) for at in range(n_blocks)]
+    operands = [*pieces, *[hits] * n_blocks, router, w_gate, w_up, w_gate, w_up]
+    operands += [back for back in backs for _ in range(n_blocks)]
+    aliases = {}
+    if held is not None:
+        aliases = {2 + len(operands) + i: i for i in range(5)}
+        in_specs += [ANY_SPEC] * 5
+        operands += held
+    made = jax.ShapeDtypeStruct((seq, span), BF16)
+    rows = [piece.shape[0] for piece in pieces]
+    results = pl.pallas_call(
+        lambda *refs: expert_kernel(len(pieces), rows, n_blocks, n_slices, *refs),
+        out_shape=[
+            jax.ShapeDtypeStruct((seq, width), BF16),
+            jax.ShapeDtypeStruct((seq, 128), F32),
+            made,
+            made,
+            made,
+        ]
+        + [jax.ShapeDtypeStruct((block, width), BF16)] * n_blocks,
+        grid_spec=pltpu.PrefetchScalarGridSpec(
+            num_scalar_prefetch=2,
+            grid=(n_slices + width // tile,),
+            in_specs=in_specs,
+            out_specs=[ANY_SPEC] * 5
+            + [pl.BlockSpec((block, tile), lambda i, index, column: (0, at_tile(i)))] * n_blocks,
+            scratch_shapes=[
+                pltpu.VMEM((total, width), BF16),
+                pltpu.VMEM((total, 128), F32),
+                pltpu.VMEM((total, 128), F32),
+                pltpu.VMEM((2, 3, total, local_experts * wide), BF16),
+                pltpu.VMEM((total, 2 * span), BF16),
+                pltpu.SemaphoreType.DMA((2, 3, n_blocks)),
+                pltpu.SemaphoreType.DMA((2, n_blocks)),
+            ],
         ),
-    )(length, qkv, squares, gains, cosine, sine, q, k, v, do)
+        input_output_aliases=aliases,
+        compiler_params=params(),
+        cost_estimate=cost(
+            8 * total * width * span, 8 * width * span + 10 * total * span, total * span
+        ),
+    )(index, column_place, *operands)
+    return results[:5], results[5:]
+
+
+def back_rows_kernel(n_blocks, n_arrays, index_ref, column_ref, *refs):
+    rows_refs, refs = refs[: n_blocks * n_arrays], refs[n_blocks * n_arrays :]
+    weight_refs, outs, held = refs[:n_arrays], refs[n_arrays:-1], refs[-1]
+    local_experts, _, hidden_units = weight_refs[0].shape
+    n_slices = column_ref.shape[0]
+    wide = hidden_units // n_slices
+    block = rows_refs[0].shape[0]
+
+    @pl.when(pl.program_id(0) == 0)
+    def _():
+        for at in range(n_blocks):
+            for array in range(n_arrays):
+                for expert in range(local_experts):
+                    for part in range(n_slices):
+                        first = (array * local_experts + expert) * hidden_units + part * wide
+                        source = pl.multiple_of(
+                            (column_ref[part] * local_experts + expert) * wide, 128
+                        )
+                        held[at * block : (at + 1) * block, first : first + wide] = rows_refs[
+                            at * n_arrays + array
+                        ][:, pl.ds(source, wide)]
+
+    total = None
+    for array in range(n_arrays):
+        for expert in range(local_experts):
+            first = (array * local_experts + expert) * hidden_units
+            part = matmul_nt(held[:, first : first + hidden_units], weight_refs[array][expert])
+            total = part if total is None else total + part
+    for at in range(n_blocks):
+        outs[at][...] = total[at * block : (at + 1) * block].astype(BF16)
+
+
+def back_rows(index, column_place, arrays, weights, block, tile=256):
+    n_blocks, n_arrays = index.shape[0], len(arrays)
+    local_experts, width, hidden_units = weights[0].shape
+    span = local_experts * hidden_units
+
+    def row_spec(at):
+        return pl.BlockSpec((block, span), lambda i, index, column: (index[at], 0))
+
+    return pl.pallas_call(
+        lambda *refs: back_rows_kernel(n_blocks, n_arrays, *refs),
+        out_shape=[jax.ShapeDtypeStruct((block, width), BF16)] * n_blocks,
+        grid_spec=pltpu.PrefetchScalarGridSpec(
+            num_scalar_prefetch=2,
+            grid=(width // tile,),
+            in_specs=[row_spec(at) for at in range(n_blocks) for _ in range(n_arrays)]
+            + [
+                pl.BlockSpec(
+                    (local_experts, tile, hidden_units), lambda i, index, column: (0, i, 0)
+                )
+            ]
+            * n_arrays,
+            out_specs=[pl.BlockSpec((block, tile), lambda i, index, column: (0, i))] * n_blocks,
+            scratch_shapes=[pltpu.VMEM((n_blocks * block, n_arrays * span), BF16)],
+        ),
+        compiler_params=params(),
+        cost_estimate=cost(
+            2 * n_blocks * block * width * span * n_arrays, 2 * width * span * n_arrays
+        ),
+    )(index, column_place, *(list(arrays) * n_blocks), *weights)
+
+
+def weight_grad_kernel(n_adds, left_ref, right_ref, *refs):
+    total = matmul_tn(left_ref[...], right_ref[...])
+    for ref in refs[:n_adds]:
+        total += ref[...].astype(F32)
+    out_ref = refs[-1]
+    if len(out_ref.shape) == 2:
+        out_ref[...] = total.astype(out_ref.dtype)
+    else:
+        wide = out_ref.shape[2]
+        for expert in range(out_ref.shape[0]):
+            out_ref[expert] = total[:, expert * wide : (expert + 1) * wide]
+
+
+def weight_grad(left, right, first, columns, adds=(), experts=None, tile=512):
+    seq, width = left.shape
+    assert first % columns == 0
+    if experts is None:
+        out_shape = jax.ShapeDtypeStruct((width, columns), BF16)
+        out_spec = pl.BlockSpec((tile, columns), lambda i: (i, 0))
+    else:
+        out_shape = jax.ShapeDtypeStruct((experts, width, columns // experts), F32)
+        out_spec = pl.BlockSpec((experts, tile, columns // experts), lambda i: (0, i, 0))
+
+    def add_spec(at):
+        return pl.BlockSpec((tile, columns), lambda i: (i, at))
+
+    return pl.pallas_call(
+        lambda *refs: weight_grad_kernel(len(adds), *refs),
+        out_shape=out_shape,
+        grid=(width // tile,),
+        in_specs=[
+            pl.BlockSpec((seq, tile), lambda i: (0, i)),
+            pl.BlockSpec((seq, columns), lambda i: (0, first // columns)),
+        ]
+        + [add_spec(at) for _, at in adds],
+        out_specs=out_spec,
+        compiler_params=params(),
+        cost_estimate=cost(2 * seq * width * columns, 2 * width * (seq + columns)),
+    )(left, right, *(value for value, _ in adds))
 
 
 def body(
@@ -324,7 +739,9 @@
     seq = groups * rows
     own = width // groups
     weight_rows = w_query.shape[0]
+    chips = n_dp // CORES
     me, dp = lax.axis_index("expert"), lax.axis_index("dp")
+    both_axes = ("dp", "expert")
     ring = Ring(groups)
     positions = jnp.arange(seq, dtype=jnp.int32)
     my_rows = me * rows + jnp.arange(rows, dtype=jnp.int32)
@@ -338,11 +755,7 @@
     hit_columns = rows * local_experts // weight_rows
     hits_out = chosen_low.reshape(rows, groups, local_experts).transpose(1, 0, 2)
     extra = jnp.concatenate(
-        [
-            jnp.stack([gain_attn, gain_query, gain_key, gain_ffn], axis=1),
-            w_router,
-        ],
-        axis=1,
+        [jnp.stack([gain_attn, gain_query, gain_key, gain_ffn], axis=1), w_router], axis=1
     )
     extra_columns = extra.shape[1]
     pad = -(extra_columns + hit_columns) % 128
@@ -363,22 +776,17 @@
     small = projections[:, 3 * own : 3 * own + extra_columns]
     gains_full = small[:, :4].T.astype(F32)
     full_router = small[:, 4:]
-    full_out = lax.all_gather(w_out, ("dp", "expert"), axis=0, tiled=True)
-    cot_all = lax.all_gather(cotangent, "expert", axis=0, tiled=True)
+    moves = [(e * n_dp + i, i * groups + e) for e in range(groups) for i in range(n_dp)]
+    own_out = dp_gather(lax.ppermute(w_out, both_axes, moves), n_dp)
 
     resid_in = tokens.astype(F32)
     attn_gain, ffn_gain = gains_full[0:1], gains_full[3:4]
     tokens_all = place_blocks(ring, ring.gather(tokens), rows, width)
-    wide = tokens_all.astype(F32)
-    attn_in = (wide * norm_scale(wide) * attn_gain).astype(BF16)
-    qkv = matmul(attn_in, w_qkv)
-    squares = jnp.stack(
-        [
-            jnp.sum(qkv[:, :own] ** 2, axis=1),
-            jnp.sum(qkv[:, own : 2 * own] ** 2, axis=1),
-        ]
-    )
-    squares = expert_sum(squares, groups).T
+    [cot_own] = together((cotangent,), (tokens_all,))
+    cot_all = lax.all_gather(cot_own, "expert", axis=0, tiled=True)
+    attn_in, qkv, squares = project(tokens_all, attn_gain, w_qkv)
+    own_out, squares = lax.optimization_barrier((own_out, squares))
+    squares = expert_sum(squares, groups)
     gains_own = lax.dynamic_slice(gains_full, (1, me * own), (2, own))
     half = HEAD_DIM // 2
     frequency = ROPE_BASE ** (-(jnp.arange(half, dtype=F32) * 2.0) / HEAD_DIM)
@@ -387,88 +795,120 @@
     cosine = jnp.concatenate([cosine, cosine], axis=1)
     sine = jnp.concatenate([-sine, sine], axis=1)
     q, k, v, attended = attend(seq_length, qkv, squares, gains_own, cosine, sine)
-    attn_rows = lax.all_to_all(
-        attended.reshape(groups, rows, own), "expert", split_axis=0, concat_axis=0, tiled=True
-    )
-    attn_rows = attn_rows.transpose(1, 0, 2).reshape(rows, width)
-    attn_rows_all = lax.all_gather(attn_rows, "expert", axis=0, tiled=True)
-    resid_mid = resid_in + matmul(attn_rows, full_out)
+
+    def block_of(value, o):
+        return lax.dynamic_slice(value, (ring.natural[o] * rows, 0), (rows, value.shape[1]))
+
+    far = groups // 2
+    out_far = matmul(block_of(attended, far), own_out).astype(BF16)
+    out_part = matmul(attended, own_out).astype(BF16)
+    backs = []
+
+    def make_back(expert):
+        backs.append(matmul(cot_all, w_down_t[expert]).astype(BF16))
+        return (backs[-1],)
+
+    hooks = {
+        2: lambda: make_back(0),
+        3: lambda: [make_back(expert)[0] for expert in range(1, local_experts)],
+    }
+    resid_mid = resid_in + ring.scatter(
+        lambda o: out_far if o == far else block_of(out_part, o), hooks
+    )
     mid_scale = norm_scale(resid_mid)
     ffn_in = (resid_mid * mid_scale * ffn_gain).astype(BF16)
-    logits = matmul(ffn_in, full_router)
-    probs = jax.nn.softmax(logits, axis=-1)
-
-    ffn_all = place_blocks(ring, ring.gather(ffn_in), rows, width)
-    logits_all = matmul(ffn_all, full_router)
-    probs_all = jax.nn.softmax(logits_all, axis=-1)
-    weights = lax.dynamic_slice(probs_all, (0, me * local_experts), (seq, local_experts)) * hits
-    moe_part = 0.0
-    pair_dots, scaled_hidden, dgates, dups = [], [], [], []
-    for expert in range(local_experts):
-        gate = matmul(ffn_all, w_gate[expert])
-        up = matmul(ffn_all, w_up[expert])
-        back = matmul(cot_all, w_down_t[expert])
-        weight = weights[:, expert : expert + 1]
-        sig = 1.0 / (1.0 + jnp.exp(-gate))
-        silu = gate * sig
-        hidden = silu * up
-        pair_dots.append(jnp.sum(hidden * back, axis=1) * hits[:, expert])
-        back = back * weight
-        scaled_hidden.append((hidden * weight).astype(BF16))
-        dgates.append((back * up * sig * (1.0 + gate * (1.0 - sig))).astype(BF16))
-        dups.append((back * silu).astype(BF16))
-        moe_part += matmul_nt(scaled_hidden[-1], w_down_t[expert])
-    moe_rows = lax.psum_scatter(
-        moe_part.astype(BF16), "expert", scatter_dimension=0, tiled=True
-    ).astype(F32)
-    output = (resid_mid + moe_rows).astype(BF16)
-    drow_part = sum(
-        matmul_nt(dgates[i], w_gate[i]) + matmul_nt(dups[i], w_up[i]) for i in range(local_experts)
-    ).astype(BF16)
-    pairs = jnp.stack(pair_dots, axis=1)
-    spread = (
-        (expert_ids[None, :] // local_experts == me) * jnp.tile(pairs, (1, groups))
-    )
-    high = spread.astype(BF16)
-    low = (spread - high.astype(F32)).astype(BF16)
-    drow_part = jnp.concatenate(
-        [drow_part, high, low, jnp.zeros((seq, -2 * experts_all % 128), BF16)], axis=1
-    )
-
-    def drow_term(o):
-        return lax.dynamic_slice(
-            drow_part, (ring.natural[o] * rows, 0), (rows, drow_part.shape[1])
+
+    distances = (
+        [2 * y + 1 for y in range(chips)] + [2 * y for y in range(1, chips)] + [0]
+    )
+    place_of = np.zeros((n_dp,), np.int32)
+    place_of[np.array(distances)] = np.arange(n_dp)
+    column_place = jnp.asarray(place_of)[jnp.arange(n_dp, dtype=jnp.int32) ^ dp]
+    per_call = 4
+    calls = groups // per_call
+    held, drow_terms = [], {}
+
+    def expert_pieces(pieces, at):
+        given = pieces[at:] if at + per_call == groups else pieces[at : at + per_call]
+        order = [o for o, _, _ in given[:per_call]]
+        result, blocks = expert_call(
+            jnp.stack([ring.natural[o] for o in order] + [me]),
+            column_place,
+            [piece for _, _, piece in given],
+            hits,
+            full_router,
+            w_gate,
+            w_up,
+            backs,
+            held[-1] if held else None,
+            seq,
         )
-
-    drow = ring.scatter(drow_term)
-
-    slice_width = hidden_units // n_dp
-
-    def expert_term(left, rights):
-        def term(rel):
-            first = (dp ^ rel) * slice_width
-            return jnp.stack(
-                [
-                    matmul_tn(left, lax.dynamic_slice(right, (0, first), (seq, slice_width)))
-                    for right in rights
-                ]
+        held.append(result)
+        drow_terms.update(zip(order, blocks))
+        return result
+
+    hooks = {}
+    for call in range(calls - 1):
+        step = (call + 1) * per_call // 2 + 1
+        hooks[step] = lambda pieces, at=call * per_call: expert_pieces(pieces, at)
+    pieces = ring.gather(ffn_in, hooks)
+    expert_pieces(pieces, groups - per_call)
+    ffn_all, pair_dots, scaled_hidden, dgates, dups = held[-1]
+    pairs = []
+
+    def make_pairs():
+        out = pair_dots[:, :local_experts].reshape(groups, rows, local_experts).transpose(0, 2, 1)
+        pairs.append(lax.all_to_all(out, "expert", split_axis=0, concat_axis=0, tiled=True))
+        return tuple(pairs)
+
+    slice_columns = local_experts * hidden_units // n_dp
+    swap = [(i, i ^ 1) for i in range(n_dp)]
+    sides = [(cot_all, scaled_hidden), (ffn_all, dgates), (ffn_all, dups)]
+    other, adds = {}, {}
+
+    def make_sent(which):
+        sent = weight_grad(*sides[which], 0, chips * slice_columns)
+        other[which] = lax.ppermute(sent, "dp", swap)
+        adds[which] = [(other[which], 0)]
+        return (sent,)
+
+    parts = {}
+
+    def make_part(which):
+        parts[which] = [
+            weight_grad(
+                *sides[which],
+                (chips + y - 1) * slice_columns,
+                slice_columns,
+                [(other[which], y)],
             )
-
-        return term
-
-    expert_grads = [
-        dp_reduce(expert_term(left, rights), n_dp)
-        for left, rights in ((cot_all, scaled_hidden), (ffn_all, dgates), (ffn_all, dups))
-    ]
-    grad_down, grad_gate_w, grad_up_w = expert_grads
+            for y in range(1, chips)
+        ]
+        return tuple(parts[which])
+
+    def send_part(which, after):
+        sent = together(tuple(parts[which]), (after,))
+        got = [
+            lax.ppermute(part, "dp", [(i, i ^ (2 * y)) for i in range(n_dp)])
+            for y, part in zip(range(1, chips), sent)
+        ]
+        adds[which] += [(part, 0) for part in got]
+        return tuple(got)
+
+    hooks = {
+        far - 2: lambda: make_sent(0),
+        far - 1: lambda: (*make_sent(1), *make_part(0)),
+        far: lambda: (*make_pairs(), *make_sent(2), *make_part(1)),
+    }
+    drow = ring.scatter(lambda o: drow_terms[o], hooks)
 
     grad_rows = cotangent.astype(F32)
-    dprobs = drow[:, width : width + experts_all]
-    dprobs = dprobs + drow[:, width + experts_all : width + 2 * experts_all]
+    dprobs = pairs[0].reshape(experts_all, rows).T
+    probs = jax.nn.softmax(matmul(ffn_in, full_router), axis=-1)
     dlogits = probs * (dprobs - jnp.sum(probs * dprobs, axis=1, keepdims=True))
     dlogits = dlogits.astype(BF16)
     grad_router = matmul_tn(ffn_in, dlogits)
-    dffn = drow[:, :width] + matmul_nt(dlogits, full_router)
+    dffn = drow + matmul_nt(dlogits, full_router)
     grad_gain_ffn = jnp.sum(dffn * resid_mid * mid_scale, axis=0, keepdims=True)
     scaled = dffn * ffn_gain
     mid_grads = (
@@ -477,28 +917,57 @@
         - resid_mid * mid_scale**3 * jnp.mean(scaled * resid_mid, axis=1, keepdims=True)
     )
     mid_low = mid_grads.astype(BF16)
-    attn_grads = matmul_nt(mid_low, full_out).astype(BF16)
-    both = jnp.stack([attn_grads.reshape(rows, groups, own), mid_low.reshape(rows, groups, own)], 2)
-    both = both.reshape(rows, groups, 2 * own).transpose(1, 0, 2)
-    both = lax.all_to_all(both, "expert", split_axis=0, concat_axis=0, tiled=True)
-    both = both.reshape(seq, 2 * own)
-    grad_heads, mid_columns = both[:, :own], both[:, own:]
+
+    def make_moe(pieces):
+        return back_rows(
+            jnp.zeros((1,), jnp.int32), column_place, (scaled_hidden,), (w_down_t,), seq
+        )
+
+    moe_made = []
+    first = send_part(0, mid_low)
+    mid_pieces = ring.gather(
+        mid_low,
+        {
+            1: lambda pieces: make_part(2),
+            2: lambda pieces: moe_made.extend(make_moe(pieces)) or moe_made,
+        },
+    )
+    mid_all = place_blocks(ring, mid_pieces, rows, width)
+    [mid_all] = together((mid_all,), first)
+    second = send_part(1, mid_all)
+    grad_heads = matmul_nt(mid_all, own_out).astype(BF16)
+
+    moe_part, grad_heads = lax.optimization_barrier((moe_made[0], grad_heads))
+    moe_rows = lax.psum_scatter(moe_part, "expert", scatter_dimension=0, tiled=True).astype(F32)
+    output = (resid_mid + moe_rows).astype(BF16)
 
     dq, dk, dv, dots, dgains = attend_back(
         seq_length, qkv, squares, gains_own, cosine, sine, q, k, v, grad_heads
     )
-    dots = expert_sum(dots.T, groups).T / width
-    scales = lax.rsqrt(squares / width + EPSILON)
-    factor = scales**3 * dots
-    dq = (dq - qkv[:, :own] * factor[:, 0:1]).astype(BF16)
-    dk = (dk - qkv[:, own : 2 * own] * factor[:, 1:2]).astype(BF16)
-    dqkv = jnp.concatenate([dq, dk, dv], axis=1)
-    dattn_part = matmul_nt(dqkv, w_qkv).astype(BF16)
-
-    def dattn_term(o):
-        return lax.dynamic_slice(dattn_part, (ring.natural[o] * rows, 0), (rows, width))
-
-    dattn = ring.scatter(dattn_term)
+    dots = expert_sum(dots, groups)
+    dqkv, din_part = finish(dq, dk, dv, qkv, squares, dots, w_qkv)
+    third = []
+
+    def make_own(which, after):
+        left, right = sides[which]
+        [left] = together((left,), after)
+        return weight_grad(
+            left,
+            right,
+            (n_dp - 1) * slice_columns,
+            slice_columns,
+            adds[which],
+            local_experts,
+        )
+
+    def middle():
+        third.extend(send_part(2, second[0]))
+        return second
+
+    hooks = {far - 2: middle}
+    dattn = ring.scatter(lambda o: block_of(din_part, o), hooks)
+    grad_down, grad_gate_w = make_own(0, (dattn,)), make_own(1, (dattn,))
+    grad_up_w = make_own(2, (dattn,))
     in_scale = norm_scale(resid_in)
     scaled = dattn * attn_gain
     input_grad = (
@@ -510,14 +979,12 @@
     block = width // n_dp
 
     def projection_term(rel):
-        first = (dp ^ rel) * block
-        left = lax.dynamic_slice(attn_in, (0, first), (seq, block))
-        left_out = lax.dynamic_slice(attn_rows_all, (0, first), (seq, block))
-        return jnp.concatenate([matmul_tn(left, dqkv), matmul_tn(left_out, mid_columns)], axis=1)
+        left = lax.dynamic_slice(attn_in, (0, (dp ^ rel) * block), (seq, block))
+        return matmul_tn(left, dqkv)
 
     reduced = dp_reduce(projection_term, n_dp).astype(BF16)
     reduced = lax.all_to_all(
-        reduced.reshape(groups, weight_rows, 4 * own),
+        reduced.reshape(groups, weight_rows, 3 * own),
         "expert",
         split_axis=0,
         concat_axis=0,
@@ -525,18 +992,29 @@
     ).astype(F32)
     grads = [
         reduced[:, :, i * own : (i + 1) * own].transpose(1, 0, 2).reshape(weight_rows, width)
-        for i in range(4)
+        for i in range(3)
     ]
     grad_gain_attn = (
         sum(jnp.sum(g * w.astype(F32), axis=1) for g, w in zip(grads, (w_query, w_key, w_value)))
         / gain_attn.astype(F32)
     )
+    out_grads = matmul_tn(attended, mid_all)
+
+    def out_term(rel):
+        return lax.dynamic_slice(out_grads, ((dp ^ rel) * weight_rows, 0), (weight_rows, width))
+
+    grad_out = dp_reduce(out_term, n_dp).astype(BF16)
+    grad_out = lax.ppermute(grad_out, both_axes, [(b, a) for a, b in moves]).astype(F32)
 
     spread_gains = lax.dynamic_update_slice(jnp.zeros((2, width), F32), dgains, (0, me * own))
-    sums = jnp.zeros((1, width), F32)
-    sums = sums.at[0, 0].set(jnp.sum(used * resid_mid * resid_mid))
-    sums = sums.at[0, 1].set(jnp.sum(used * moe_rows * moe_rows))
+    lane = lax.broadcasted_iota(jnp.int32, (1, width), 1)
+    sums = jnp.where(
+        lane == 0,
+        jnp.sum(used * resid_mid * resid_mid),
+        jnp.where(lane == 1, jnp.sum(used * moe_rows * moe_rows), 0.0),
+    )
     rest = jnp.concatenate([spread_gains, grad_gain_ffn, sums, grad_router.T], axis=0)
+    [rest] = together((rest,), (dattn,))
     rest = dp_sum(expert_sum(rest, groups), n_dp)
     mine = lax.dynamic_slice(
         rest, (0, (dp * groups + me) * weight_rows), (rest.shape[0], weight_rows)
@@ -550,7 +1028,7 @@
         grads[0],
         grads[1],
         grads[2],
-        grads[3],
+        grad_out,
         grad_gain_attn,
         mine[0],
         mine[1],

time: 882 us -> 670 us (0.76)
  matrix products: 242 us -> 41 us
  waiting for transfers between devices: 340 us -> 143 us
  Pallas kernels: 24.8 us -> 191 us
  starting transfers between devices: 102 us -> 161 us
  other arithmetic: 80.5 us -> 49.6 us
    pallas_call x1 -> x15, Pallas kernels: 9.1 us -> 174 us  [the longest x9 67.7 us: weight_grad(): pl.pallas_call(lambda *refs: weight_grad_kernel(len(adds), *refs), out_sh...]
    ppermute x9, waiting for transfers between devices: 114 us -> 19.4 us  [expert_sum(): lax.ppermute(value, 'expert', [(i, i ^ step) for i in range(groups)])]
    dot_general x33 -> x6, matrix products: 99.9 us -> 11.5 us  [matmul_tn(): lax.dot_general(left, right, (((0,), (0,)), ((), ())), preferred_element_...]
    dot_general x9 -> x2, matrix products: 68.4 us -> 7.17 us  [matmul_nt(): lax.dot_general(left, right, (((1,), (1,)), ((), ())), preferred_element_...]
    ppermute x4 -> x2, waiting for transfers between devices: 69.3 us -> 13.6 us  [dp_reduce(): lax.ppermute(part, 'dp', [(i, i ^ 2 * y) for i in range(n_dp)]).astype(F32)]
    dot_general x10 -> x5, matrix products: 74 us -> 22.4 us  [matmul(): return jnp.dot(left, right, preferred_element_type=F32)]
    ppermute x0 -> x8, starting transfers between devices: none -> 41.7 us  [the longest x3 39.5 us: send_part(): lax.ppermute(part, 'dp', [(i, i ^ 2 * y) for i in range(n_dp)])]
    ppermute x16 -> x24, waiting for transfers between devices: 90.3 us -> 55.9 us  [up(): return lax.ppermute(value, 'expert', self.ahead)]
  transfers between devices with their start and end apart: 66 -> 84, of which waited for: 35 -> 43; matrix products, arithmetic and copies ran while one was open for 36% -> 20% of each run, Pallas kernels for 3% -> 23%
where the time goes in v2:
time: 670 us; the launch traced here: 665 us
  Pallas kernels  191 us (29%)
  starting transfers between devices  161 us (24%)
  waiting for transfers between devices  143 us (21%)
  local copies, waits for them, and re-layouts  54.3 us (8%)
  other arithmetic  49.6 us (7%)
  matrix products  41 us (6%)
  between operations  24.8 us (4%)
    pallas_call x9, Pallas kernels, weight_grad(): pl.pallas_call(lambda *refs: weight_grad_kernel(len(adds), *refs), out_sh...  67.7 us
    pallas_call x2, Pallas kernels, expert_call(): pl.pallas_call(lambda *refs: expert_kernel(len(pieces), rows, n_blocks, n...  63.4 us
    ppermute x24, waiting for transfers between devices, up(): return lax.ppermute(value, 'expert', self.ahead)  55.9 us
    ppermute x24, waiting for transfers between devices, down(): return lax.ppermute(value, 'expert', self.back)  43.3 us
    ppermute x3, starting transfers between devices, send_part(): lax.ppermute(part, 'dp', [(i, i ^ 2 * y) for i in range(n_dp)])  39.5 us
    ppermute x24, starting transfers between devices, up(): return lax.ppermute(value, 'expert', self.ahead)  36.8 us
    ppermute x9, starting transfers between devices, expert_sum(): lax.ppermute(value, 'expert', [(i, i ^ step) for i in range(groups)])  22.8 us
    dot_general x5, matrix products, matmul(): return jnp.dot(left, right, preferred_element_type=F32)  22.4 us
  transfers between devices with their start and end apart: 84, of which 43 were waited for; matrix products, arithmetic and copies ran while one was open for 20% of the time, Pallas kernels for 23%

profile of v2, /device:TPU:0, one launch (start us, length us, event | category | flops | bytes accessed | tf_op | source)
XLA Modules:
  0.0 664.5 jit_solution(3239709191685817231)
XLA Ops:
  7.2 3.1 collective-permute-start
  16.5 6.3 all-to-all-start
  32.7 2.5 broadcast.211.clone
  36.9 11.5 %collective-permute-done.2 = bf16[128,2048]{1,0:T(8,128)(2,1)} collective-permute-done((bf16[128,2048]{1,0:T(8,128)(2,1)S(1)}, bf16[128,2048]{1,0:T(8,128)(2,1)}, u32[]{:S(2)}, u32[]{:S(2)}) %collective-permute-start.2) | collective-permute-done | bytes 524320 | tf_op jit(solution)/shard_map/ppermute | solution.py:46
  48.4 6.4 collective-permute-start.4
  58.3 7.4 %collective-permute-done.4 = bf16[128,2048]{1,0:T(8,128)(2,1)S(1)} collective-permute-done((bf16[128,2048]{1,0:T(8,128)(2,1)}, bf16[128,2048]{1,0:T(8,128)(2,1)S(1)}, u32[]{:S(2)}, u32[]{:S(2)}) %collective-permute-start.4) | collective-permute-done | bytes 524320 | tf_op jit(solution)/shard_map/ppermute | solution.py:46
  65.7 2.6 collective-permute-start.6
  71.7 3.1 collective-permute-done.6
  79.4 12.4 %collective-permute-start.12 = (bf16[64,2048]{1,0:T(8,128)(2,1)}, bf16[64,2048]{1,0:T(8,128)(2,1)}, u32[]{:S(2)}, u32[]{:S(2)}) collective-permute-start(bf16[64,2048]{1,0:T(8,128)(2,1)} %collective-permute-done.11), channel_id=1, source_target_pairs={{0,16},{8,24},{16,0},{24,8},{1,17},{9,25},{17,1},{25,9},{2,18},{10... | collective-permute-start | bytes 786440 | tf_op jit(solution)/shard_map/ppermute | solution.py:131
  92.4 4.7 collective-permute-start.13
  98.2 8.5 %collective-permute-done.12 = bf16[64,2048]{1,0:T(8,128)(2,1)} collective-permute-done((bf16[64,2048]{1,0:T(8,128)(2,1)}, bf16[64,2048]{1,0:T(8,128)(2,1)}, u32[]{:S(2)}, u32[]{:S(2)}) %collective-permute-start.12) | collective-permute-done | bytes 262176 | tf_op jit(solution)/shard_map/ppermute | solution.py:131
  116.1 9.0 %shard_map.306 = (bf16[1024,2048]{1,0:T(8,128)(2,1)}, f32[1024,768]{1,0:T(8,128)}, f32[8,1024]{1,0:T(8,128)}) custom-call(bf16[1024,2048]{1,0:T(8,128)(2,1)} %constant_dynamic-update-slice_fusion.18.tokens_ref, f32[1,2048]{1,0:T(1,128)} %copy.86.gain_ref, bf16[2048,768]{1,0:T(8,128)(2,1)} %slice.249.w_ref), custom_call_target="tpu_custom_call" | custom-call | flops 3221225472 | bytes 16777216 | tf_op jit(solution)/shard_map/pallas_call | solution.py:227
  125.1 10.7 %collective-permute-start.15 = (f32[8,1024]{1,0:T(8,128)}, f32[8,1024]{1,0:T(8,128)S(1)}, u32[]{:S(2)}, u32[]{:S(2)}) collective-permute-start(f32[8,1024]{1,0:T(8,128)} %get-tuple-element.80), channel_id=1, source_target_pairs={{0,1},{1,0},{2,3},{3,2},{4,5},{5,4},{6,7},{7,6},{8,9},{9,8},{10,11... | collective-permute-start | bytes 98312 | tf_op jit(solution)/shard_map/ppermute | solution.py:113
  141.3 2.1 collective-permute-done.16
  145.5 4.5 collective-permute-done.17
  150.6 9.1 %shard_map.307 = (bf16[1024,256]{1,0:T(8,128)(2,1)}, bf16[1024,256]{1,0:T(8,128)(2,1)}, bf16[1024,256]{1,0:T(8,128)(2,1)}, bf16[1024,256]{1,0:T(8,128)(2,1)}) custom-call(s32[1]{0:T(128)} %dynamic_slice.85.length_ref, f32[1024,768]{1,0:T(8,128)} %get-tuple-element.78.qkv_ref, f32[8,1024]{1,0:T(8,128)} %add.357.squares_ref, f32[2,256]{1,0:T(2,128)} %copy.87.gain_ref, ...), custom_call_target="tpu_custom_call" | custom-call | flops 1073741824 | bytes 5242880 | tf_op jit(solution)/shard_map/pallas_call | solution.py:348
  163.3 2.3 convolution_convert_fusion
  165.7 3.4 collective-permute-done.20
  172.0 9.4 %fusion.6.refs_15_.refs_16_.refs_17_.refs_18_.refs_19_ = bf16[1024,1024]{1,0:T(8,128)(2,1)} fusion(bf16[1024,2048]{1,0:T(8,128)(2,1)} %all-gather.2.cloned.1.call-done.refs_0_, bf16[2,2048,1024]{2,1,0:T(8,128)(2,1)} %refs_3_.1), kind=kOutput, calls=%fused_computation.10 | convolution fusion | flops 4296015872 | bytes 10485760 | tf_op jit(solution)/shard_map/dot_general | solution.py:158
  187.6 7.9 %fusion.9.refs_19_.refs_20_.refs_21_.refs_22_.refs_23_ = bf16[1024,1024]{1,0:T(8,128)(2,1)} fusion(bf16[1024,2048]{1,0:T(8,128)(2,1)S(1)} %copy-done.5, bf16[2,2048,1024]{2,1,0:T(8,128)(2,1)} %refs_3_.1), kind=kOutput, calls=%fused_computation.11 | convolution fusion | flops 4296015872 | bytes 10485760 | tf_op jit(solution)/shard_map/dot_general | solution.py:158
  200.3 8.6 %collective-permute-done.25 = bf16[128,2048]{1,0:T(8,128)(2,1)S(1)} collective-permute-done((bf16[128,2048]{1,0:T(8,128)(2,1)S(1)}, bf16[128,2048]{1,0:T(8,128)(2,1)S(1)}, u32[]{:S(2)}, u32[]{:S(2)}) %collective-permute-start.25) | collective-permute-done | bytes 524320 | tf_op jit(solution)/shard_map/ppermute | solution.py:49
  213.0 9.9 %collective-permute-done.28.refs_3_ = bf16[128,2048]{1,0:T(8,128)(2,1)} collective-permute-done((bf16[128,2048]{1,0:T(8,128)(2,1)S(1)}, bf16[128,2048]{1,0:T(8,128)(2,1)}, u32[]{:S(2)}, u32[]{:S(2)}) %collective-permute-start.28) | collective-permute-done | bytes 524320 | tf_op jit(solution)/shard_map/ppermute | solution.py:46
  224.9 3.1 stack.28.refs_0_
  233.2 2.5 collective-permute-done.29.refs_5_
  237.8 31.7 %shard_map.308 = (bf16[1024,2048]{1,0:T(8,128)(2,1)}, f32[1024,128]{1,0:T(8,128)}, bf16[1024,2048]{1,0:T(8,128)(2,1)}, bf16[1024,2048]{1,0:T(8,128)(2,1)}, bf16[...) custom-call(s32[5]{0:T(128)} %stack.28.refs_0_, ...), custom_call_target="tpu_custom_call" | custom-call | flops 17179869184 | bytes 44040192 | tf_op jit(solution)/shard_map/pallas_call | solution.py:578
  273.8 2.1 collective-permute-done.32.refs_5_
  278.5 31.7 %shard_map.309 = (bf16[1024,2048]{1,0:T(8,128)(2,1)}, f32[1024,128]{1,0:T(8,128)}, bf16[1024,2048]{1,0:T(8,128)(2,1)}, bf16[1024,2048]{1,0:T(8,128)(2,1)}, bf16[...) custom-call(s32[5]{0:T(128)} %pad_add_fusion.refs_0_, ...), custom_call_target="tpu_custom_call", output_to_operand_aliasing={{0}: (24, {}), {1}: (25, {}), {2}: (26, {}), {3}: (27, {}),... | custom-call | flops 17179869184 | bytes 44040192 | tf_op jit(solution)/shard_map/pallas_call | solution.py:578
  310.2 8.6 %shard_map.311 = bf16[2048,1024]{1,0:T(8,128)(2,1)} custom-call(bf16[1024,2048]{1,0:T(8,128)(2,1)} %all-gather.2.cloned.1.call-done.refs_0_, bf16[1024,2048]{1,0:T(8,128)(2,1)} %get-tuple-element.95.refs_2_.refs_1_), custom_call_target="tpu_custom_call" | custom-call | flops 4294967296 | bytes 8388608 | tf_op jit(solution)/shard_map/pallas_call | solution.py:702
  321.0 8.5 %shard_map.312 = bf16[2048,1024]{1,0:T(8,128)(2,1)} custom-call(bf16[1024,2048]{1,0:T(8,128)(2,1)} %get-tuple-element.137.refs_0_, bf16[1024,2048]{1,0:T(8,128)(2,1)} %get-tuple-element.104.refs_1_), custom_call_target="tpu_custom_call" | custom-call | flops 4294967296 | bytes 8388608 | tf_op jit(solution)/shard_map/pallas_call | solution.py:702
  333.9 8.6 %shard_map.314 = bf16[2048,1024]{1,0:T(8,128)(2,1)} custom-call(bf16[1024,2048]{1,0:T(8,128)(2,1)} %get-tuple-element.137.refs_0_, bf16[1024,2048]{1,0:T(8,128)(2,1)} %get-tuple-element.110.refs_1_), custom_call_target="tpu_custom_call" | custom-call | flops 4294967296 | bytes 8388608 | tf_op jit(solution)/shard_map/pallas_call | solution.py:702
  342.5 2.5 collective-permute-done.35
  355.6 3.3 all-to-all-start.1
  359.0 6.6 shard_map.313
  372.0 6.5 shard_map.315
  380.6 3.7 collective-permute-done.42
  384.2 2.9 multiply_reduce_fusion
  387.1 2.5 broadcast.211
  393.1 6.4 shard_map.316
  405.6 15.3 %shard_map.310 = bf16[1024,2048]{1,0:T(8,128)(2,1)} custom-call(s32[1]{0:T(128)} %constant.95.clone.1.refs_0_, s32[4]{0:T(128)} %gather_fusion.1, bf16[1024,2048]{1,0:T(8,128)(2,1)} %get-tuple-element.95.refs_2_.refs_1_, bf16[2,2048,1024]{2,1,0:T(8,128)(2,1)} %refs_3_.1), custom_call_target="tpu_custom_call" | custom-call | flops 8589934592 | bytes 8388608 | tf_op jit(solution)/shard_map/pallas_call | solution.py:653
  430.6 4.4 collective-permute-done.49
  438.9 2.6 collective-permute-done.51
  444.2 4.3 convolution_convert_fusion.4.do_ref
  448.6 16.2 %shard_map.317 = (f32[1024,256]{1,0:T(8,128)}, f32[1024,256]{1,0:T(8,128)}, bf16[1024,256]{1,0:T(8,128)(2,1)}, f32[8,1024]{1,0:T(8,128)}, f32[2,256]{1,0:T(2,128)}) custom-call(s32[1]{0:T(128)} %dynamic_slice.85.length_ref, f32[1024,768]{1,0:T(8,128)} %get-tuple-element.78.qkv_ref, f32[8,1024]{1,0:T(8,128)} %add.357.squares_ref, f32[2,256]{1,0:T(2,128)} %copy.87.gain_ref, ...), custom_call_target="tpu_custom_call" | custom-call | flops 2684354560 | bytes 10485760 | tf_op jit(solution)/shard_map/pallas_call | solution.py:361
  466.8 2.1 collective-permute-done.54
  471.3 3.6 fusion.51
  478.7 4.3 collective-permute-done.56
  483.6 9.8 %shard_map.318 = (bf16[1024,768]{1,0:T(8,128)(2,1)}, bf16[1024,2048]{1,0:T(8,128)(2,1)}) custom-call(f32[1024,256]{1,0:T(8,128)} %get-tuple-element.125.dq_ref, f32[1024,256]{1,0:T(8,128)} %get-tuple-element.126.dk_ref, bf16[1024,256]{1,0:T(8,128)(2,1)} %get-tuple-element.127.dv_ref, f32[1024,768]{1,0:T(8,128)} %get-tuple-element.78.qkv_ref, ...), custom_call_target="tpu_custom_call" | custom-call | flops 3221225472 | bytes 8388608 | tf_op jit(solution)/shard_map/pallas_call | solution.py:400
  493.4 3.0 convolution_convert_fusion.2
  496.5 2.6 fusion.23
  503.5 8.1 %collective-permute-done.59 = bf16[64,2048]{1,0:T(8,128)(2,1)S(1)} collective-permute-done((bf16[64,2048]{1,0:T(8,128)(2,1)S(1)}, bf16[64,2048]{1,0:T(8,128)(2,1)S(1)}, u32[]{:S(2)}, u32[]{:S(2)}) %collective-permute-start.59) | collective-permute-done | bytes 262176 | tf_op jit(solution)/shard_map/ppermute | solution.py:49
  521.1 13.6 %collective-permute-done.68 = bf16[512,768]{1,0:T(8,128)(2,1)S(1)} collective-permute-done((bf16[512,768]{1,0:T(8,128)(2,1)S(1)}, bf16[512,768]{1,0:T(8,128)(2,1)S(1)}, u32[]{:S(2)}, u32[]{:S(2)}) %collective-permute-start.68) | collective-permute-done | bytes 786464 | tf_op jit(solution)/shard_map/ppermute | solution.py:147
  537.3 4.6 all-to-all-start.2
  541.8 7.0 %collective-permute-done.60 = bf16[128,2048]{1,0:T(8,128)(2,1)} collective-permute-done((bf16[128,2048]{1,0:T(8,128)(2,1)}, bf16[128,2048]{1,0:T(8,128)(2,1)}, u32[]{:S(2)}, u32[]{:S(2)}) %collective-permute-start.60) | collective-permute-done | bytes 524320 | tf_op jit(solution)/shard_map/ppermute | solution.py:49
  555.8 36.4 %collective-permute-start.78 = (bf16[2048,512]{1,0:T(8,128)(2,1)}, bf16[2048,512]{1,0:T(8,128)(2,1)}, u32[]{:S(2)}, u32[]{:S(2)}) collective-permute-start(bf16[2048,512]{1,0:T(8,128)(2,1)} %shard_map.316), channel_id=1, source_target_pairs={{0,16},{8,24},{16,0},{24,8},{1,17},{9,25},{17,1},{25,9},{2,18},{10... | collective-permute-start | bytes 6291464 | tf_op jit(solution)/shard_map/ppermute | solution.py:892
  592.2 2.6 add_convert_fusion.4
  599.5 4.8 collective-permute-done.65
  607.1 2.6 fusion.14
  613.6 3.9 collective-permute-done.73
  619.5 2.4 fusion.18
  623.3 3.6 collective-permute-start.75
  626.9 7.5 %shard_map.319 = f32[2,2048,256]{2,1,0:T(8,128)} custom-call(bf16[1024,2048]{1,0:T(8,128)(2,1)} %get-tuple-element.137.refs_0_, bf16[1024,2048]{1,0:T(8,128)(2,1)} %get-tuple-element.104.refs_1_, bf16[2048,1024]{1,0:T(8,128)(2,1)} %collective-permute-done.43.refs_2_, bf16[2048,512]{1,0:T(8,128)(2,1)} %collective-permute-done.61.refs_3_), custom_call_target="tpu_custom_call" | custom-call | flops 2147483648 | bytes 6291456 | tf_op jit(solution)/shard_map/pallas_call | solution.py:702
  634.5 7.6 %shard_map.321 = f32[2,2048,256]{2,1,0:T(8,128)} custom-call(bf16[1024,2048]{1,0:T(8,128)(2,1)} %all-gather.2.cloned.1.call-done.refs_0_, bf16[1024,2048]{1,0:T(8,128)(2,1)} %get-tuple-element.95.refs_2_.refs_1_, bf16[2048,1024]{1,0:T(8,128)(2,1)} %collective-permute-done.40.refs_2_, bf16[2048,512]{1,0:T(8,128)(2,1)} %collective-permute-done.53.refs_3_), custom_call_target="tpu_custom_call" | custom-call | flops 2147483648 | bytes 6291456 | tf_op jit(solution)/shard_map/pallas_call | solution.py:702
  642.1 2.3 collective-permute-start.77
  644.4 7.6 %shard_map.320 = f32[2,2048,256]{2,1,0:T(8,128)} custom-call(bf16[1024,2048]{1,0:T(8,128)(2,1)} %get-tuple-element.137.refs_0_, bf16[1024,2048]{1,0:T(8,128)(2,1)} %get-tuple-element.110.refs_1_, bf16[2048,1024]{1,0:T(8,128)(2,1)} %collective-permute-done.46.refs_2_, bf16[2048,512]{1,0:T(8,128)(2,1)} %collective-permute-done.78.refs_3_), custom_call_target="tpu_custom_call" | custom-call | flops 2147483648 | bytes 6291456 | tf_op jit(solution)/shard_map/pallas_call | solution.py:702
  (360 shorter events, 180.8 us)
Async XLA Ops:
  7.2 17.5 %collective-permute-start = (bf16[128,2048]{1,0:T(8,128)(2,1)}, bf16[128,2048]{1,0:T(8,128)(2,1)S(1)}, u32[]{:S(2)}, u32[]{:S(2)}) collective-permute-start(bf16[128,2048]{1,0:T(8,128)(2,1)} %param.19), channel_id=1, source_target_pairs={{2,4},{4,6},{6,7},{7,5},{5,3},{3,1},{1,0},{0,2},{10,12},{12,14},{1... | collective-permute-start | bytes 1572872 | tf_op jit(solution)/shard_map/ppermute | solution.py:46
  10.3 16.5 %collective-permute-start.1 = (bf16[128,2048]{1,0:T(8,128)(2,1)}, bf16[128,2048]{1,0:T(8,128)(2,1)S(1)}, u32[]{:S(2)}, u32[]{:S(2)}) collective-permute-start(bf16[128,2048]{1,0:T(8,128)(2,1)} %param.19), channel_id=1, source_target_pairs={{4,2},{6,4},{7,6},{5,7},{3,5},{1,3},{0,1},{2,0},{12,10},{14,12},{1... | collective-permute-start | bytes 1572872 | tf_op jit(solution)/shard_map/ppermute | solution.py:49
  16.5 59.7 %all-to-all-start = ((bf16[8,64,896]{2,1,0:T(8,128)(2,1)}), bf16[8,64,896]{2,1,0:T(8,128)(2,1)S(1)}, u32[]{:S(2)}, u32[]{:S(2)}) async-start(bf16[8,64,896]{2,1,0:T(8,128)(2,1)} %concatenate.34), calls=%async_computation | async-start | bytes 1835008 | tf_op jit(solution)/shard_map/all_to_all | solution.py:771
  22.8 149.2 %all-gather.2.cloned.1.call-start = ((), (), s32[]{:S(2)}) async-start(), calls=%async_computation.4 | async-start | bytes 4718592 | tf_op jit(solution)/shard_map/all_gather | solution.py:786
  24.7 23.6 %collective-permute-start.2 = (bf16[128,2048]{1,0:T(8,128)(2,1)S(1)}, bf16[128,2048]{1,0:T(8,128)(2,1)}, u32[]{:S(2)}, u32[]{:S(2)}) collective-permute-start(bf16[128,2048]{1,0:T(8,128)(2,1)S(1)} %collective-permute-done), channel_id=1, source_target_pairs={{2,4},{4,6},{6,7},{7,5},{5,3},{3,1},{1,0},{0,2},{10,12},{12,14},{1... | collective-permute-start | bytes 1572872 | tf_op jit(solution)/shard_map/ppermute | solution.py:46
  26.8 28.0 %collective-permute-start.3 = (bf16[128,2048]{1,0:T(8,128)(2,1)S(1)}, bf16[128,2048]{1,0:T(8,128)(2,1)S(1)}, u32[]{:S(2)}, u32[]{:S(2)}) collective-permute-start(bf16[128,2048]{1,0:T(8,128)(2,1)S(1)} %collective-permute-done.1), channel_id=1, source_target_pairs={{4,2},{6,4},{7,6},{5,7},{3,5},{1,3},{0,1},{2,0},{12,10},{14,12},{1... | collective-permute-start | bytes 1572872 | tf_op jit(solution)/shard_map/ppermute | solution.py:49
  48.4 17.3 %collective-permute-start.4 = (bf16[128,2048]{1,0:T(8,128)(2,1)}, bf16[128,2048]{1,0:T(8,128)(2,1)S(1)}, u32[]{:S(2)}, u32[]{:S(2)}) collective-permute-start(bf16[128,2048]{1,0:T(8,128)(2,1)} %collective-permute-done.2), channel_id=1, source_target_pairs={{2,4},{4,6},{6,7},{7,5},{5,3},{3,1},{1,0},{0,2},{10,12},{12,14},{1... | collective-permute-start | bytes 1572872 | tf_op jit(solution)/shard_map/ppermute | solution.py:46
  54.8 13.7 %collective-permute-start.5 = (bf16[128,2048]{1,0:T(8,128)(2,1)S(1)}, bf16[128,2048]{1,0:T(8,128)(2,1)S(1)}, u32[]{:S(2)}, u32[]{:S(2)}) collective-permute-start(bf16[128,2048]{1,0:T(8,128)(2,1)S(1)} %collective-permute-done.3), channel_id=1, source_target_pairs={{4,2},{6,4},{7,6},{5,7},{3,5},{1,3},{0,1},{2,0},{12,10},{14,12},{1... | collective-permute-start | bytes 1572872 | tf_op jit(solution)/shard_map/ppermute | solution.py:49
  65.7 9.1 %collective-permute-start.6 = (bf16[64,2048]{1,0:T(8,128)(2,1)S(1)}, bf16[64,2048]{1,0:T(8,128)(2,1)S(1)}, u32[]{:S(2)}, u32[]{:S(2)}) collective-permute-start(bf16[64,2048]{1,0:T(8,128)(2,1)S(1)} %slice.245), channel_id=1, source_target_pairs={{2,4},{4,6},{6,7},{7,5},{5,3},{3,1},{1,0},{0,2},{10,12},{12,14},{1... | collective-permute-start | bytes 786440 | tf_op jit(solution)/shard_map/ppermute | solution.py:46
  76.3 31.0 %collective-permute-start.8 = (bf16[512,896]{1,0:T(8,128)(2,1)S(1)}, bf16[512,896]{1,0:T(8,128)(2,1)S(1)}, u32[]{:S(2)}, u32[]{:S(2)}) collective-permute-start(bf16[512,896]{1,0:T(8,128)(2,1)S(1)} %bitcast.102), channel_id=1, source_target_pairs={{0,16},{8,24},{16,0},{24,8},{1,17},{9,25},{17,1},{25,9},{2,18},{10... | collective-permute-start | bytes 2752520 | tf_op jit(solution)/shard_map/ppermute | solution.py:131
  79.4 27.3 %collective-permute-start.12 = (bf16[64,2048]{1,0:T(8,128)(2,1)}, bf16[64,2048]{1,0:T(8,128)(2,1)}, u32[]{:S(2)}, u32[]{:S(2)}) collective-permute-start(bf16[64,2048]{1,0:T(8,128)(2,1)} %collective-permute-done.11), channel_id=1, source_target_pairs={{0,16},{8,24},{16,0},{24,8},{1,17},{9,25},{17,1},{25,9},{2,18},{10... | collective-permute-start | bytes 786440 | tf_op jit(solution)/shard_map/ppermute | solution.py:131
  92.4 15.9 %collective-permute-start.13 = (bf16[64,2048]{1,0:T(8,128)(2,1)}, bf16[64,2048]{1,0:T(8,128)(2,1)S(1)}, u32[]{:S(2)}, u32[]{:S(2)}) collective-permute-start(bf16[64,2048]{1,0:T(8,128)(2,1)} %collective-permute-done.11), channel_id=1, source_target_pairs={{0,8},{8,0},{16,24},{24,16},{1,9},{9,1},{17,25},{25,17},{2,10},{10... | collective-permute-start | bytes 786440 | tf_op jit(solution)/shard_map/ppermute | solution.py:133
  125.1 13.6 %collective-permute-start.15 = (f32[8,1024]{1,0:T(8,128)}, f32[8,1024]{1,0:T(8,128)S(1)}, u32[]{:S(2)}, u32[]{:S(2)}) collective-permute-start(f32[8,1024]{1,0:T(8,128)} %get-tuple-element.80), channel_id=1, source_target_pairs={{0,1},{1,0},{2,3},{3,2},{4,5},{5,4},{6,7},{7,6},{8,9},{9,8},{10,11... | collective-permute-start | bytes 98312 | tf_op jit(solution)/shard_map/ppermute | solution.py:113
  169.8 12.6 %collective-permute-start.19 = (bf16[128,2048]{1,0:T(8,128)(2,1)S(1)}, bf16[128,2048]{1,0:T(8,128)(2,1)S(1)}, u32[]{:S(2)}, u32[]{:S(2)}) collective-permute-start(bf16[128,2048]{1,0:T(8,128)(2,1)S(1)} %pad_maximum_fusion.2), channel_id=1, source_target_pairs={{2,4},{4,6},{6,7},{7,5},{5,3},{3,1},{1,0},{0,2},{10,12},{12,14},{1... | collective-permute-start | bytes 1572872 | tf_op jit(solution)/shard_map/ppermute | solution.py:46
  171.6 12.5 %collective-permute-start.21 = (bf16[128,2048]{1,0:T(8,128)(2,1)S(1)}, bf16[128,2048]{1,0:T(8,128)(2,1)}, u32[]{:S(2)}, u32[]{:S(2)}) collective-permute-start(bf16[128,2048]{1,0:T(8,128)(2,1)S(1)} %pad_maximum_fusion.3), channel_id=1, source_target_pairs={{4,2},{6,4},{7,6},{5,7},{3,5},{1,3},{0,1},{2,0},{12,10},{14,12},{1... | collective-permute-start | bytes 1572872 | tf_op jit(solution)/shard_map/ppermute | solution.py:49
  185.5 11.5 %collective-permute-start.22 = (bf16[128,2048]{1,0:T(8,128)(2,1)S(1)}, bf16[128,2048]{1,0:T(8,128)(2,1)S(1)}, u32[]{:S(2)}, u32[]{:S(2)}) collective-permute-start(bf16[128,2048]{1,0:T(8,128)(2,1)S(1)} %get-tuple-element.166), channel_id=1, source_target_pairs={{2,4},{4,6},{6,7},{7,5},{5,3},{3,1},{1,0},{0,2},{10,12},{12,14},{1... | collective-permute-start | bytes 1572872 | tf_op jit(solution)/shard_map/ppermute | solution.py:46
  186.2 11.6 %collective-permute-start.23 = (bf16[128,2048]{1,0:T(8,128)(2,1)S(1)}, bf16[128,2048]{1,0:T(8,128)(2,1)S(1)}, u32[]{:S(2)}, u32[]{:S(2)}) collective-permute-start(bf16[128,2048]{1,0:T(8,128)(2,1)S(1)} %get-tuple-element.165), channel_id=1, source_target_pairs={{4,2},{6,4},{7,6},{5,7},{3,5},{1,3},{0,1},{2,0},{12,10},{14,12},{1... | collective-permute-start | bytes 1572872 | tf_op jit(solution)/shard_map/ppermute | solution.py:49
  198.2 10.7 %collective-permute-start.25 = (bf16[128,2048]{1,0:T(8,128)(2,1)S(1)}, bf16[128,2048]{1,0:T(8,128)(2,1)S(1)}, u32[]{:S(2)}, u32[]{:S(2)}) collective-permute-start(bf16[128,2048]{1,0:T(8,128)(2,1)S(1)} %get-tuple-element.164), channel_id=1, source_target_pairs={{4,2},{6,4},{7,6},{5,7},{3,5},{1,3},{0,1},{2,0},{12,10},{14,12},{1... | collective-permute-start | bytes 1572872 | tf_op jit(solution)/shard_map/ppermute | solution.py:49
  199.7 10.6 %collective-permute-start.24 = (bf16[128,2048]{1,0:T(8,128)(2,1)S(1)}, bf16[128,2048]{1,0:T(8,128)(2,1)S(1)}, u32[]{:S(2)}, u32[]{:S(2)}) collective-permute-start(bf16[128,2048]{1,0:T(8,128)(2,1)S(1)} %get-tuple-element.163), channel_id=1, source_target_pairs={{2,4},{4,6},{6,7},{7,5},{5,3},{3,1},{1,0},{0,2},{10,12},{12,14},{1... | collective-permute-start | bytes 1572872 | tf_op jit(solution)/shard_map/ppermute | solution.py:46
  210.9 11.9 %collective-permute-start.28 = (bf16[128,2048]{1,0:T(8,128)(2,1)S(1)}, bf16[128,2048]{1,0:T(8,128)(2,1)}, u32[]{:S(2)}, u32[]{:S(2)}) collective-permute-start(bf16[128,2048]{1,0:T(8,128)(2,1)S(1)} %multiply_convert_fusion.refs_2_), channel_id=1, source_target_pairs={{2,4},{4,6},{6,7},{7,5},{5,3},{3,1},{1,0},{0,2},{10,12},{12,14},{1... | collective-permute-start | bytes 1572872 | tf_op jit(solution)/shard_map/ppermute | solution.py:46
  212.4 11.9 %collective-permute-start.26 = (bf16[128,2048]{1,0:T(8,128)(2,1)S(1)}, bf16[128,2048]{1,0:T(8,128)(2,1)}, u32[]{:S(2)}, u32[]{:S(2)}) collective-permute-start(bf16[128,2048]{1,0:T(8,128)(2,1)S(1)} %multiply_convert_fusion.refs_2_), channel_id=1, source_target_pairs={{4,2},{6,4},{7,6},{5,7},{3,5},{1,3},{0,1},{2,0},{12,10},{14,12},{1... | collective-permute-start | bytes 1572872 | tf_op jit(solution)/shard_map/ppermute | solution.py:49
  222.9 12.8 %collective-permute-start.29 = (bf16[128,2048]{1,0:T(8,128)(2,1)}, bf16[128,2048]{1,0:T(8,128)(2,1)}, u32[]{:S(2)}, u32[]{:S(2)}) collective-permute-start(bf16[128,2048]{1,0:T(8,128)(2,1)} %collective-permute-done.28.refs_3_), channel_id=1, source_target_pairs={{2,4},{4,6},{6,7},{7,5},{5,3},{3,1},{1,0},{0,2},{10,12},{12,14},{1... | collective-permute-start | bytes 1572872 | tf_op jit(solution)/shard_map/ppermute | solution.py:46
  224.3 13.0 %collective-permute-start.27 = (bf16[128,2048]{1,0:T(8,128)(2,1)}, bf16[128,2048]{1,0:T(8,128)(2,1)}, u32[]{:S(2)}, u32[]{:S(2)}) collective-permute-start(bf16[128,2048]{1,0:T(8,128)(2,1)} %collective-permute-done.26.refs_4_), channel_id=1, source_target_pairs={{4,2},{6,4},{7,6},{5,7},{3,5},{1,3},{0,1},{2,0},{12,10},{14,12},{1... | collective-permute-start | bytes 1572872 | tf_op jit(solution)/shard_map/ppermute | solution.py:49
  235.7 33.8 %collective-permute-start.30 = (bf16[128,2048]{1,0:T(8,128)(2,1)}, bf16[128,2048]{1,0:T(8,128)(2,1)S(1)}, u32[]{:S(2)}, u32[]{:S(2)}) collective-permute-start(bf16[128,2048]{1,0:T(8,128)(2,1)} %collective-permute-done.29.refs_5_), channel_id=1, source_target_pairs={{2,4},{4,6},{6,7},{7,5},{5,3},{3,1},{1,0},{0,2},{10,12},{12,14},{1... | collective-permute-start | bytes 1572872 | tf_op jit(solution)/shard_map/ppermute | solution.py:46
  237.3 32.2 %collective-permute-start.31 = (bf16[128,2048]{1,0:T(8,128)(2,1)}, bf16[128,2048]{1,0:T(8,128)(2,1)S(1)}, u32[]{:S(2)}, u32[]{:S(2)}) collective-permute-start(bf16[128,2048]{1,0:T(8,128)(2,1)} %collective-permute-done.27.refs_2_), channel_id=1, source_target_pairs={{4,2},{6,4},{7,6},{5,7},{3,5},{1,3},{0,1},{2,0},{12,10},{14,12},{1... | collective-permute-start | bytes 1572872 | tf_op jit(solution)/shard_map/ppermute | solution.py:49
  318.8 40.2 %collective-permute-start.40 = (bf16[2048,1024]{1,0:T(8,128)(2,1)}, bf16[2048,1024]{1,0:T(8,128)(2,1)}, u32[]{:S(2)}, u32[]{:S(2)}) collective-permute-start(bf16[2048,1024]{1,0:T(8,128)(2,1)} %shard_map.311), channel_id=1, source_target_pairs={{0,8},{8,0},{16,24},{24,16},{1,9},{9,1},{17,25},{25,17},{2,10},{10... | collective-permute-start | bytes 12582920 | tf_op jit(solution)/shard_map/ppermute | solution.py:871
  318.9 10.6 %collective-permute-start.34 = (bf16[64,2048]{1,0:T(8,128)(2,1)S(1)}, bf16[64,2048]{1,0:T(8,128)(2,1)S(1)}, u32[]{:S(2)}, u32[]{:S(2)}) collective-permute-start(bf16[64,2048]{1,0:T(8,128)(2,1)S(1)} %get-tuple-element.182), channel_id=1, source_target_pairs={{2,4},{4,6},{6,7},{7,5},{5,3},{3,1},{1,0},{0,2},{10,12},{12,14},{1... | collective-permute-start | bytes 786440 | tf_op jit(solution)/shard_map/ppermute | solution.py:46
  319.3 11.5 %collective-permute-start.36 = (bf16[64,2048]{1,0:T(8,128)(2,1)S(1)}, bf16[64,2048]{1,0:T(8,128)(2,1)S(1)}, u32[]{:S(2)}, u32[]{:S(2)}) collective-permute-start(bf16[64,2048]{1,0:T(8,128)(2,1)S(1)} %get-tuple-element.181), channel_id=1, source_target_pairs={{4,2},{6,4},{7,6},{5,7},{3,5},{1,3},{0,1},{2,0},{12,10},{14,12},{1... | collective-permute-start | bytes 786440 | tf_op jit(solution)/shard_map/ppermute | solution.py:49
  329.4 42.6 %collective-permute-start.43 = (bf16[2048,1024]{1,0:T(8,128)(2,1)}, bf16[2048,1024]{1,0:T(8,128)(2,1)}, u32[]{:S(2)}, u32[]{:S(2)}) collective-permute-start(bf16[2048,1024]{1,0:T(8,128)(2,1)} %shard_map.312), channel_id=1, source_target_pairs={{0,8},{8,0},{16,24},{24,16},{1,9},{9,1},{17,25},{25,17},{2,10},{10... | collective-permute-start | bytes 12582920 | tf_op jit(solution)/shard_map/ppermute | solution.py:871
  330.4 14.6 %collective-permute-start.35 = (bf16[128,2048]{1,0:T(8,128)(2,1)}, bf16[128,2048]{1,0:T(8,128)(2,1)}, u32[]{:S(2)}, u32[]{:S(2)}) collective-permute-start(bf16[128,2048]{1,0:T(8,128)(2,1)} %pad_maximum_fusion.4), channel_id=1, source_target_pairs={{2,4},{4,6},{6,7},{7,5},{5,3},{3,1},{1,0},{0,2},{10,12},{12,14},{1... | collective-permute-start | bytes 1572872 | tf_op jit(solution)/shard_map/ppermute | solution.py:46
  331.7 14.4 %collective-permute-start.37 = (bf16[128,2048]{1,0:T(8,128)(2,1)}, bf16[128,2048]{1,0:T(8,128)(2,1)}, u32[]{:S(2)}, u32[]{:S(2)}) collective-permute-start(bf16[128,2048]{1,0:T(8,128)(2,1)} %pad_maximum_fusion.5), channel_id=1, source_target_pairs={{4,2},{6,4},{7,6},{5,7},{3,5},{1,3},{0,1},{2,0},{12,10},{14,12},{1... | collective-permute-start | bytes 1572872 | tf_op jit(solution)/shard_map/ppermute | solution.py:49
  342.5 50.6 %collective-permute-start.46 = (bf16[2048,1024]{1,0:T(8,128)(2,1)}, bf16[2048,1024]{1,0:T(8,128)(2,1)}, u32[]{:S(2)}, u32[]{:S(2)}) collective-permute-start(bf16[2048,1024]{1,0:T(8,128)(2,1)} %shard_map.314), channel_id=1, source_target_pairs={{0,8},{8,0},{16,24},{24,16},{1,9},{9,1},{17,25},{25,17},{2,10},{10... | collective-permute-start | bytes 12582920 | tf_op jit(solution)/shard_map/ppermute | solution.py:871
  348.1 17.5 %collective-permute-start.38 = (bf16[128,2048]{1,0:T(8,128)(2,1)}, bf16[128,2048]{1,0:T(8,128)(2,1)}, u32[]{:S(2)}, u32[]{:S(2)}) collective-permute-start(bf16[128,2048]{1,0:T(8,128)(2,1)} %add_convert_fusion.9), channel_id=1, source_target_pairs={{2,4},{4,6},{6,7},{7,5},{5,3},{3,1},{1,0},{0,2},{10,12},{12,14},{1... | collective-permute-start | bytes 1572872 | tf_op jit(solution)/shard_map/ppermute | solution.py:46
  350.4 15.2 %collective-permute-start.39 = (bf16[128,2048]{1,0:T(8,128)(2,1)}, bf16[128,2048]{1,0:T(8,128)(2,1)}, u32[]{:S(2)}, u32[]{:S(2)}) collective-permute-start(bf16[128,2048]{1,0:T(8,128)(2,1)} %add_convert_fusion.8), channel_id=1, source_target_pairs={{4,2},{6,4},{7,6},{5,7},{3,5},{1,3},{0,1},{2,0},{12,10},{14,12},{1... | collective-permute-start | bytes 1572872 | tf_op jit(solution)/shard_map/ppermute | solution.py:49
  355.6 16.4 %all-to-all-start.1 = ((f32[8,2,128]{2,1,0:T(2,128)}), f32[8,2,128]{2,1,0:T(2,128)S(1)}, u32[]{:S(2)}, u32[]{:S(2)}) async-start(f32[8,2,128]{2,1,0:T(2,128)} %bitcast.28), calls=%async_computation.1 | async-start | bytes 16384 | tf_op jit(solution)/shard_map/all_to_all | solution.py:861
  358.9 248.2 %reduce-scatter.2.cloned.1.call-start = ((), (), s32[]{:S(2)}) async-start(), calls=%async_computation.5 | async-start | bytes 4718592 | tf_op jit(solution)/shard_map/reduce_scatter | solution.py:941
  367.6 13.0 %collective-permute-start.41 = (bf16[128,2048]{1,0:T(8,128)(2,1)}, bf16[128,2048]{1,0:T(8,128)(2,1)}, u32[]{:S(2)}, u32[]{:S(2)}) collective-permute-start(bf16[128,2048]{1,0:T(8,128)(2,1)} %add_convert_fusion.7), channel_id=1, source_target_pairs={{2,4},{4,6},{6,7},{7,5},{5,3},{3,1},{1,0},{0,2},{10,12},{12,14},{1... | collective-permute-start | bytes 1572872 | tf_op jit(solution)/shard_map/ppermute | solution.py:46
  371.4 12.8 %collective-permute-start.42 = (bf16[128,2048]{1,0:T(8,128)(2,1)}, bf16[128,2048]{1,0:T(8,128)(2,1)}, u32[]{:S(2)}, u32[]{:S(2)}) collective-permute-start(bf16[128,2048]{1,0:T(8,128)(2,1)} %add_convert_fusion.6), channel_id=1, source_target_pairs={{4,2},{6,4},{7,6},{5,7},{3,5},{1,3},{0,1},{2,0},{12,10},{14,12},{1... | collective-permute-start | bytes 1572872 | tf_op jit(solution)/shard_map/ppermute | solution.py:49
  391.1 11.3 %collective-permute-start.44 = (bf16[128,2048]{1,0:T(8,128)(2,1)S(1)}, bf16[128,2048]{1,0:T(8,128)(2,1)}, u32[]{:S(2)}, u32[]{:S(2)}) collective-permute-start(bf16[128,2048]{1,0:T(8,128)(2,1)S(1)} %get-tuple-element.149), channel_id=1, source_target_pairs={{2,4},{4,6},{6,7},{7,5},{5,3},{3,1},{1,0},{0,2},{10,12},{12,14},{1... | collective-permute-start | bytes 1572872 | tf_op jit(solution)/shard_map/ppermute | solution.py:46
  392.6 11.0 %collective-permute-start.45 = (bf16[128,2048]{1,0:T(8,128)(2,1)S(1)}, bf16[128,2048]{1,0:T(8,128)(2,1)}, u32[]{:S(2)}, u32[]{:S(2)}) collective-permute-start(bf16[128,2048]{1,0:T(8,128)(2,1)S(1)} %get-tuple-element.149), channel_id=1, source_target_pairs={{4,2},{6,4},{7,6},{5,7},{3,5},{1,3},{0,1},{2,0},{12,10},{14,12},{1... | collective-permute-start | bytes 1572872 | tf_op jit(solution)/shard_map/ppermute | solution.py:49
  399.6 44.6 %collective-permute-start.53 = (bf16[2048,512]{1,0:T(8,128)(2,1)}, bf16[2048,512]{1,0:T(8,128)(2,1)}, u32[]{:S(2)}, u32[]{:S(2)}) collective-permute-start(bf16[2048,512]{1,0:T(8,128)(2,1)} %shard_map.313), channel_id=1, source_target_pairs={{0,16},{8,24},{16,0},{24,8},{1,17},{9,25},{17,1},{25,9},{2,18},{10... | collective-permute-start | bytes 6291464 | tf_op jit(solution)/shard_map/ppermute | solution.py:892
  403.6 19.3 %collective-permute-start.47 = (bf16[128,2048]{1,0:T(8,128)(2,1)}, bf16[128,2048]{1,0:T(8,128)(2,1)}, u32[]{:S(2)}, u32[]{:S(2)}) collective-permute-start(bf16[128,2048]{1,0:T(8,128)(2,1)} %collective-permute-done.44), channel_id=1, source_target_pairs={{2,4},{4,6},{6,7},{7,5},{5,3},{3,1},{1,0},{0,2},{10,12},{12,14},{1... | collective-permute-start | bytes 1572872 | tf_op jit(solution)/shard_map/ppermute | solution.py:46
  405.1 17.8 %collective-permute-start.48 = (bf16[128,2048]{1,0:T(8,128)(2,1)}, bf16[128,2048]{1,0:T(8,128)(2,1)}, u32[]{:S(2)}, u32[]{:S(2)}) collective-permute-start(bf16[128,2048]{1,0:T(8,128)(2,1)} %collective-permute-done.45), channel_id=1, source_target_pairs={{4,2},{6,4},{7,6},{5,7},{3,5},{1,3},{0,1},{2,0},{12,10},{14,12},{1... | collective-permute-start | bytes 1572872 | tf_op jit(solution)/shard_map/ppermute | solution.py:49
  422.9 12.1 %collective-permute-start.49 = (bf16[128,2048]{1,0:T(8,128)(2,1)}, bf16[128,2048]{1,0:T(8,128)(2,1)S(1)}, u32[]{:S(2)}, u32[]{:S(2)}) collective-permute-start(bf16[128,2048]{1,0:T(8,128)(2,1)} %collective-permute-done.47), channel_id=1, source_target_pairs={{2,4},{4,6},{6,7},{7,5},{5,3},{3,1},{1,0},{0,2},{10,12},{12,14},{1... | collective-permute-start | bytes 1572872 | tf_op jit(solution)/shard_map/ppermute | solution.py:46
  424.4 12.2 %collective-permute-start.50 = (bf16[128,2048]{1,0:T(8,128)(2,1)}, bf16[128,2048]{1,0:T(8,128)(2,1)S(1)}, u32[]{:S(2)}, u32[]{:S(2)}) collective-permute-start(bf16[128,2048]{1,0:T(8,128)(2,1)} %collective-permute-done.48), channel_id=1, source_target_pairs={{4,2},{6,4},{7,6},{5,7},{3,5},{1,3},{0,1},{2,0},{12,10},{14,12},{1... | collective-permute-start | bytes 1572872 | tf_op jit(solution)/shard_map/ppermute | solution.py:49
  474.9 73.9 %collective-permute-start.61 = (bf16[2048,512]{1,0:T(8,128)(2,1)}, bf16[2048,512]{1,0:T(8,128)(2,1)}, u32[]{:S(2)}, u32[]{:S(2)}) collective-permute-start(bf16[2048,512]{1,0:T(8,128)(2,1)} %shard_map.315), channel_id=1, source_target_pairs={{0,16},{8,24},{16,0},{24,8},{1,17},{9,25},{17,1},{25,9},{2,18},{10... | collective-permute-start | bytes 6291464 | tf_op jit(solution)/shard_map/ppermute | solution.py:892
  478.6 39.7 %collective-permute-start.70 = (bf16[64,2048]{1,0:T(8,128)(2,1)S(1)}, bf16[64,2048]{1,0:T(8,128)(2,1)S(1)}, u32[]{:S(2)}, u32[]{:S(2)}) collective-permute-start(bf16[64,2048]{1,0:T(8,128)(2,1)S(1)} %get-tuple-element.174), channel_id=1, source_target_pairs={{0,8},{8,0},{16,24},{24,16},{1,9},{9,1},{17,25},{25,17},{2,10},{10... | collective-permute-start | bytes 786440 | tf_op jit(solution)/shard_map/ppermute | solution.py:143
  496.4 17.7 %collective-permute-start.67 = (bf16[512,768]{1,0:T(8,128)(2,1)S(1)}, bf16[512,768]{1,0:T(8,128)(2,1)S(1)}, u32[]{:S(2)}, u32[]{:S(2)}) collective-permute-start(bf16[512,768]{1,0:T(8,128)(2,1)S(1)} %convolution_convert_fusion.2), channel_id=1, source_target_pairs={{0,8},{8,0},{16,24},{24,16},{1,9},{9,1},{17,25},{25,17},{2,10},{10... | collective-permute-start | bytes 2359304 | tf_op jit(solution)/shard_map/ppermute | solution.py:143
  500.4 11.3 %collective-permute-start.59 = (bf16[64,2048]{1,0:T(8,128)(2,1)S(1)}, bf16[64,2048]{1,0:T(8,128)(2,1)S(1)}, u32[]{:S(2)}, u32[]{:S(2)}) collective-permute-start(bf16[64,2048]{1,0:T(8,128)(2,1)S(1)} %get-tuple-element.160), channel_id=1, source_target_pairs={{4,2},{6,4},{7,6},{5,7},{3,5},{1,3},{0,1},{2,0},{12,10},{14,12},{1... | collective-permute-start | bytes 786440 | tf_op jit(solution)/shard_map/ppermute | solution.py:49
  500.4 12.5 %collective-permute-start.57 = (bf16[64,2048]{1,0:T(8,128)(2,1)S(1)}, bf16[64,2048]{1,0:T(8,128)(2,1)S(1)}, u32[]{:S(2)}, u32[]{:S(2)}) collective-permute-start(bf16[64,2048]{1,0:T(8,128)(2,1)S(1)} %get-tuple-element.158), channel_id=1, source_target_pairs={{2,4},{4,6},{6,7},{7,5},{5,3},{3,1},{1,0},{0,2},{10,12},{12,14},{1... | collective-permute-start | bytes 786440 | tf_op jit(solution)/shard_map/ppermute | solution.py:46
  511.6 9.5 %collective-permute-start.66 = (bf16[512,768]{1,0:T(8,128)(2,1)S(1)}, bf16[512,768]{1,0:T(8,128)(2,1)S(1)}, u32[]{:S(2)}, u32[]{:S(2)}) collective-permute-start(bf16[512,768]{1,0:T(8,128)(2,1)S(1)} %convolution_convert_fusion.3), channel_id=1, source_target_pairs={{0,8},{8,0},{16,24},{24,16},{1,9},{9,1},{17,25},{25,17},{2,10},{10... | collective-permute-start | bytes 2359304 | tf_op jit(solution)/shard_map/ppermute | solution.py:143
  515.2 19.6 %collective-permute-start.68 = (bf16[512,768]{1,0:T(8,128)(2,1)S(1)}, bf16[512,768]{1,0:T(8,128)(2,1)S(1)}, u32[]{:S(2)}, u32[]{:S(2)}) collective-permute-start(bf16[512,768]{1,0:T(8,128)(2,1)S(1)} %add_convert_fusion.1), channel_id=1, source_target_pairs={{0,16},{8,24},{16,0},{24,8},{1,17},{9,25},{17,1},{25,9},{2,18},{10... | collective-permute-start | bytes 2359304 | tf_op jit(solution)/shard_map/ppermute | solution.py:147
  517.5 24.3 %collective-permute-start.58 = (bf16[128,2048]{1,0:T(8,128)(2,1)}, bf16[128,2048]{1,0:T(8,128)(2,1)}, u32[]{:S(2)}, u32[]{:S(2)}) collective-permute-start(bf16[128,2048]{1,0:T(8,128)(2,1)} %pad_maximum_fusion.6), channel_id=1, source_target_pairs={{2,4},{4,6},{6,7},{7,5},{5,3},{3,1},{1,0},{0,2},{10,12},{12,14},{1... | collective-permute-start | bytes 1572872 | tf_op jit(solution)/shard_map/ppermute | solution.py:46
  518.3 30.5 %collective-permute-start.60 = (bf16[128,2048]{1,0:T(8,128)(2,1)}, bf16[128,2048]{1,0:T(8,128)(2,1)}, u32[]{:S(2)}, u32[]{:S(2)}) collective-permute-start(bf16[128,2048]{1,0:T(8,128)(2,1)} %pad_maximum_fusion.7), channel_id=1, source_target_pairs={{4,2},{6,4},{7,6},{5,7},{3,5},{1,3},{0,1},{2,0},{12,10},{14,12},{1... | collective-permute-start | bytes 1572872 | tf_op jit(solution)/shard_map/ppermute | solution.py:49
  521.1 31.7 %collective-permute-start.69 = (bf16[64,2048]{1,0:T(8,128)(2,1)S(1)}, bf16[64,2048]{1,0:T(8,128)(2,1)S(1)}, u32[]{:S(2)}, u32[]{:S(2)}) collective-permute-start(bf16[64,2048]{1,0:T(8,128)(2,1)S(1)} %get-tuple-element.173), channel_id=1, source_target_pairs={{0,8},{8,0},{16,24},{24,16},{1,9},{9,1},{17,25},{25,17},{2,10},{10... | collective-permute-start | bytes 786440 | tf_op jit(solution)/shard_map/ppermute | solution.py:143
  534.8 18.1 %collective-permute-start.71 = (bf16[64,2048]{1,0:T(8,128)(2,1)}, bf16[64,2048]{1,0:T(8,128)(2,1)}, u32[]{:S(2)}, u32[]{:S(2)}) collective-permute-start(bf16[64,2048]{1,0:T(8,128)(2,1)} %add_convert_fusion.15), channel_id=1, source_target_pairs={{0,16},{8,24},{16,0},{24,8},{1,17},{9,25},{17,1},{25,9},{2,18},{10... | collective-permute-start | bytes 786440 | tf_op jit(solution)/shard_map/ppermute | solution.py:147
  537.3 59.5 %all-to-all-start.2 = ((bf16[8,64,768]{2,1,0:T(8,128)(2,1)}), bf16[8,64,768]{2,1,0:T(8,128)(2,1)S(1)}, u32[]{:S(2)}, u32[]{:S(2)}) async-start(bf16[8,64,768]{2,1,0:T(8,128)(2,1)} %bitcast.105), calls=%async_computation.3 | async-start | bytes 1572864 | tf_op jit(solution)/shard_map/all_to_all | solution.py:986
  550.8 41.4 %collective-permute-start.62 = (bf16[128,2048]{1,0:T(8,128)(2,1)S(1)}, bf16[128,2048]{1,0:T(8,128)(2,1)S(1)}, u32[]{:S(2)}, u32[]{:S(2)}) collective-permute-start(bf16[128,2048]{1,0:T(8,128)(2,1)S(1)} %get-tuple-element.155), channel_id=1, source_target_pairs={{2,4},{4,6},{6,7},{7,5},{5,3},{3,1},{1,0},{0,2},{10,12},{12,14},{1... | collective-permute-start | bytes 1572872 | tf_op jit(solution)/shard_map/ppermute | solution.py:46
  550.8 41.4 %collective-permute-start.64 = (bf16[128,2048]{1,0:T(8,128)(2,1)S(1)}, bf16[128,2048]{1,0:T(8,128)(2,1)S(1)}, u32[]{:S(2)}, u32[]{:S(2)}) collective-permute-start(bf16[128,2048]{1,0:T(8,128)(2,1)S(1)} %get-tuple-element.156), channel_id=1, source_target_pairs={{4,2},{6,4},{7,6},{5,7},{3,5},{1,3},{0,1},{2,0},{12,10},{14,12},{1... | collective-permute-start | bytes 1572872 | tf_op jit(solution)/shard_map/ppermute | solution.py:49
  555.8 88.6 %collective-permute-start.78 = (bf16[2048,512]{1,0:T(8,128)(2,1)}, bf16[2048,512]{1,0:T(8,128)(2,1)}, u32[]{:S(2)}, u32[]{:S(2)}) collective-permute-start(bf16[2048,512]{1,0:T(8,128)(2,1)} %shard_map.316), channel_id=1, source_target_pairs={{0,16},{8,24},{16,0},{24,8},{1,17},{9,25},{17,1},{25,9},{2,18},{10... | collective-permute-start | bytes 6291464 | tf_op jit(solution)/shard_map/ppermute | solution.py:892
  594.8 9.5 %collective-permute-start.65 = (bf16[128,2048]{1,0:T(8,128)(2,1)}, bf16[128,2048]{1,0:T(8,128)(2,1)}, u32[]{:S(2)}, u32[]{:S(2)}) collective-permute-start(bf16[128,2048]{1,0:T(8,128)(2,1)} %get-tuple-element.154), channel_id=1, source_target_pairs={{4,2},{6,4},{7,6},{5,7},{3,5},{1,3},{0,1},{2,0},{12,10},{14,12},{1... | collective-permute-start | bytes 1572872 | tf_op jit(solution)/shard_map/ppermute | solution.py:49
  595.7 9.6 %collective-permute-start.63 = (bf16[128,2048]{1,0:T(8,128)(2,1)}, bf16[128,2048]{1,0:T(8,128)(2,1)}, u32[]{:S(2)}, u32[]{:S(2)}) collective-permute-start(bf16[128,2048]{1,0:T(8,128)(2,1)} %get-tuple-element.153), channel_id=1, source_target_pairs={{2,4},{4,6},{6,7},{7,5},{5,3},{3,1},{1,0},{0,2},{10,12},{12,14},{1... | collective-permute-start | bytes 1572872 | tf_op jit(solution)/shard_map/ppermute | solution.py:46
  623.3 11.1 %collective-permute-start.75 = (f32[20,2048]{1,0:T(8,128)S(1)}, f32[20,2048]{1,0:T(8,128)S(1)}, u32[]{:S(2)}, u32[]{:S(2)}) collective-permute-start(f32[20,2048]{1,0:T(8,128)S(1)} %add.405), channel_id=1, source_target_pairs={{0,4},{1,5},{2,6},{3,7},{4,0},{5,1},{6,2},{7,3},{8,12},{9,13},{10,... | collective-permute-start | bytes 491528 | tf_op jit(solution)/shard_map/ppermute | solution.py:113
  642.1 9.8 %collective-permute-start.77 = (f32[20,2048]{1,0:T(8,128)S(1)}, f32[20,2048]{1,0:T(8,128)S(1)}, u32[]{:S(2)}, u32[]{:S(2)}) collective-permute-start(f32[20,2048]{1,0:T(8,128)S(1)} %add.407), channel_id=1, source_target_pairs={{0,16},{8,24},{16,0},{24,8},{1,17},{9,25},{17,1},{25,9},{2,18},{10... | collective-permute-start | bytes 491528 | tf_op jit(solution)/shard_map/ppermute | solution.py:121
  (61 other events, 710.7 us)
Sparse Core Ops, SparseCore 0:
  76.4 82.5 all-gather.1
  448.7 103.7 reduce-scatter.1

commit v3 on v2

--- a/solution.py
+++ b/solution.py
@@ -964,10 +964,25 @@
         third.extend(send_part(2, second[0]))
         return second
 
-    hooks = {far - 2: middle}
+    spread_gains = lax.dynamic_update_slice(jnp.zeros((2, width), F32), dgains, (0, me * own))
+    lane = lax.broadcasted_iota(jnp.int32, (1, width), 1)
+    sums = jnp.where(
+        lane == 0,
+        jnp.sum(used * resid_mid * resid_mid),
+        jnp.where(lane == 1, jnp.sum(used * moe_rows * moe_rows), 0.0),
+    )
+    rest = jnp.concatenate([spread_gains, grad_gain_ffn, sums, grad_router.T], axis=0)
+    hooks = {far - 2: middle, far: lambda: (rest,)}
     dattn = ring.scatter(lambda o: block_of(din_part, o), hooks)
-    grad_down, grad_gate_w = make_own(0, (dattn,)), make_own(1, (dattn,))
-    grad_up_w = make_own(2, (dattn,))
+    [rest] = together((rest,), (dattn,))
+    own_grads = []
+    for at in range(groups.bit_length() - 1):
+        rest = rest + lax.ppermute(rest, "expert", [(i, i ^ (1 << at)) for i in range(groups)])
+        if at < 3:
+            own_grads.append(make_own(at, (rest,)))
+            [rest] = together((rest,), ())
+    rest = dp_sum(rest, n_dp)
+    grad_down, grad_gate_w, grad_up_w = own_grads
     in_scale = norm_scale(resid_in)
     scaled = dattn * attn_gain
     input_grad = (
@@ -983,6 +998,7 @@
         return matmul_tn(left, dqkv)
 
     reduced = dp_reduce(projection_term, n_dp).astype(BF16)
+    [reduced] = together((reduced,), (dattn,))
     reduced = lax.all_to_all(
         reduced.reshape(groups, weight_rows, 3 * own),
         "expert",
@@ -1004,18 +1020,9 @@
         return lax.dynamic_slice(out_grads, ((dp ^ rel) * weight_rows, 0), (weight_rows, width))
 
     grad_out = dp_reduce(out_term, n_dp).astype(BF16)
+    [grad_out] = together((grad_out,), (dattn,))
     grad_out = lax.ppermute(grad_out, both_axes, [(b, a) for a, b in moves]).astype(F32)
 
-    spread_gains = lax.dynamic_update_slice(jnp.zeros((2, width), F32), dgains, (0, me * own))
-    lane = lax.broadcasted_iota(jnp.int32, (1, width), 1)
-    sums = jnp.where(
-        lane == 0,
-        jnp.sum(used * resid_mid * resid_mid),
-        jnp.where(lane == 1, jnp.sum(used * moe_rows * moe_rows), 0.0),
-    )
-    rest = jnp.concatenate([spread_gains, grad_gain_ffn, sums, grad_router.T], axis=0)
-    [rest] = together((rest,), (dattn,))
-    rest = dp_sum(expert_sum(rest, groups), n_dp)
     mine = lax.dynamic_slice(
         rest, (0, (dp * groups + me) * weight_rows), (rest.shape[0], weight_rows)
     )

time: 670 us -> 659 us (0.984)
  starting transfers between devices: 161 us -> 126 us
  waiting for transfers between devices: 143 us -> 175 us
  other arithmetic: 49.6 us -> 40.9 us
    ppermute x3, starting transfers between devices: 39.5 us -> 3.02 us  [send_part(): lax.ppermute(part, 'dp', [(i, i ^ 2 * y) for i in range(n_dp)])]
    ppermute x0 -> x3, waiting for transfers between devices: none -> 26.3 us  [body(): lax.ppermute(rest, 'expert', [(i, i ^ 1 << at) for i in range(groups)])]
    ppermute x24, waiting for transfers between devices: 55.9 us -> 76 us  [up(): return lax.ppermute(value, 'expert', self.ahead)]
    ppermute x24, starting transfers between devices: 21.2 us -> 31.1 us  [down(): return lax.ppermute(value, 'expert', self.back)]
    ppermute x24, waiting for transfers between devices: 43.3 us -> 34.1 us  [down(): return lax.ppermute(value, 'expert', self.back)]
    ppermute x9 -> x6, starting transfers between devices: 22.8 us -> 14.9 us  [expert_sum(): lax.ppermute(value, 'expert', [(i, i ^ step) for i in range(groups)])]
    ppermute x9 -> x6, waiting for transfers between devices: 19.4 us -> 15.7 us  [expert_sum(): lax.ppermute(value, 'expert', [(i, i ^ step) for i in range(groups)])]
  transfers between devices with their start and end apart: 84 -> 84, of which waited for: 43 -> 45; matrix products, arithmetic and copies ran while one was open for 20% -> 19% of each run, Pallas kernels for 23% -> 23%
where the time goes in v3:
time: 659 us; the launch traced here: 653 us
  Pallas kernels  191 us (29%)
  waiting for transfers between devices  175 us (27%)
  starting transfers between devices  126 us (19%)
  local copies, waits for them, and re-layouts  54.1 us (8%)
  matrix products  41.1 us (6%)
  other arithmetic  40.9 us (6%)
  between operations  24.8 us (4%)
    ppermute x24, waiting for transfers between devices, up(): return lax.ppermute(value, 'expert', self.ahead)  76 us
    pallas_call x9, Pallas kernels, weight_grad(): pl.pallas_call(lambda *refs: weight_grad_kernel(len(adds), *refs), out_sh...  67.9 us
    pallas_call x2, Pallas kernels, expert_call(): pl.pallas_call(lambda *refs: expert_kernel(len(pieces), rows, n_blocks, n...  63.3 us
    ppermute x24, starting transfers between devices, up(): return lax.ppermute(value, 'expert', self.ahead)  35.2 us
    ppermute x24, waiting for transfers between devices, down(): return lax.ppermute(value, 'expert', self.back)  34.1 us
    ppermute x24, starting transfers between devices, down(): return lax.ppermute(value, 'expert', self.back)  31.1 us
    ppermute x3, waiting for transfers between devices, body(): lax.ppermute(rest, 'expert', [(i, i ^ 1 << at) for i in range(groups)])  26.3 us
    dot_general x5, matrix products, matmul(): return jnp.dot(left, right, preferred_element_type=F32)  22.5 us
  transfers between devices with their start and end apart: 84, of which 45 were waited for; matrix products, arithmetic and copies ran while one was open for 19% of the time, Pallas kernels for 23%

profile of v3, /device:TPU:0, one launch (start us, length us, event | category | flops | bytes accessed | tf_op | source)
XLA Modules:
  0.0 653.1 jit_solution(5292572492536249551)
XLA Ops:
  7.2 3.1 collective-permute-start
  16.5 6.3 all-to-all-start
  32.6 2.5 broadcast.211.clone
  36.8 11.6 %collective-permute-done.2 = bf16[128,2048]{1,0:T(8,128)(2,1)} collective-permute-done((bf16[128,2048]{1,0:T(8,128)(2,1)S(1)}, bf16[128,2048]{1,0:T(8,128)(2,1)}, u32[]{:S(2)}, u32[]{:S(2)}) %collective-permute-start.2) | collective-permute-done | bytes 524320 | tf_op jit(solution)/shard_map/ppermute | solution.py:46
  48.4 6.4 collective-permute-start.4
  58.3 7.4 %collective-permute-done.4 = bf16[128,2048]{1,0:T(8,128)(2,1)S(1)} collective-permute-done((bf16[128,2048]{1,0:T(8,128)(2,1)}, bf16[128,2048]{1,0:T(8,128)(2,1)S(1)}, u32[]{:S(2)}, u32[]{:S(2)}) %collective-permute-start.4) | collective-permute-done | bytes 524320 | tf_op jit(solution)/shard_map/ppermute | solution.py:46
  65.7 2.6 collective-permute-start.6
  71.7 3.1 collective-permute-done.6
  79.4 12.5 %collective-permute-start.12 = (bf16[64,2048]{1,0:T(8,128)(2,1)}, bf16[64,2048]{1,0:T(8,128)(2,1)}, u32[]{:S(2)}, u32[]{:S(2)}) collective-permute-start(bf16[64,2048]{1,0:T(8,128)(2,1)} %collective-permute-done.11), channel_id=1, source_target_pairs={{0,16},{8,24},{16,0},{24,8},{1,17},{9,25},{17,1},{25,9},{2,18},{10... | collective-permute-start | bytes 786440 | tf_op jit(solution)/shard_map/ppermute | solution.py:131
  92.4 4.7 collective-permute-start.13
  98.2 8.5 %collective-permute-done.12 = bf16[64,2048]{1,0:T(8,128)(2,1)} collective-permute-done((bf16[64,2048]{1,0:T(8,128)(2,1)}, bf16[64,2048]{1,0:T(8,128)(2,1)}, u32[]{:S(2)}, u32[]{:S(2)}) %collective-permute-start.12) | collective-permute-done | bytes 262176 | tf_op jit(solution)/shard_map/ppermute | solution.py:131
  116.1 9.0 %shard_map.306 = (bf16[1024,2048]{1,0:T(8,128)(2,1)}, f32[1024,768]{1,0:T(8,128)}, f32[8,1024]{1,0:T(8,128)}) custom-call(bf16[1024,2048]{1,0:T(8,128)(2,1)} %constant_dynamic-update-slice_fusion.18.tokens_ref, f32[1,2048]{1,0:T(1,128)} %copy.86.gain_ref, bf16[2048,768]{1,0:T(8,128)(2,1)} %slice.249.w_ref), custom_call_target="tpu_custom_call" | custom-call | flops 3221225472 | bytes 16777216 | tf_op jit(solution)/shard_map/pallas_call | solution.py:227
  125.1 10.7 %collective-permute-start.15 = (f32[8,1024]{1,0:T(8,128)}, f32[8,1024]{1,0:T(8,128)S(1)}, u32[]{:S(2)}, u32[]{:S(2)}) collective-permute-start(f32[8,1024]{1,0:T(8,128)} %get-tuple-element.85), channel_id=1, source_target_pairs={{0,1},{1,0},{2,3},{3,2},{4,5},{5,4},{6,7},{7,6},{8,9},{9,8},{10,11... | collective-permute-start | bytes 98312 | tf_op jit(solution)/shard_map/ppermute | solution.py:113
  145.4 4.6 collective-permute-done.17
  150.6 9.2 %shard_map.307 = (bf16[1024,256]{1,0:T(8,128)(2,1)}, bf16[1024,256]{1,0:T(8,128)(2,1)}, bf16[1024,256]{1,0:T(8,128)(2,1)}, bf16[1024,256]{1,0:T(8,128)(2,1)}) custom-call(s32[1]{0:T(128)} %dynamic_slice.85.length_ref, f32[1024,768]{1,0:T(8,128)} %get-tuple-element.83.qkv_ref, f32[8,1024]{1,0:T(8,128)} %add.357.squares_ref, f32[2,256]{1,0:T(2,128)} %copy.87.gain_ref, ...), custom_call_target="tpu_custom_call" | custom-call | flops 1073741824 | bytes 5242880 | tf_op jit(solution)/shard_map/pallas_call | solution.py:348
  163.4 2.3 convolution_convert_fusion
  165.8 3.4 collective-permute-done.20
  172.1 9.5 %fusion.6.refs_15_.refs_16_.refs_17_.refs_18_.refs_19_ = bf16[1024,1024]{1,0:T(8,128)(2,1)} fusion(bf16[1024,2048]{1,0:T(8,128)(2,1)} %all-gather.2.cloned.1.call-done.refs_0_, bf16[2,2048,1024]{2,1,0:T(8,128)(2,1)} %refs_3_.1), kind=kOutput, calls=%fused_computation.10 | convolution fusion | flops 4296015872 | bytes 10485760 | tf_op jit(solution)/shard_map/dot_general | solution.py:158
  187.7 7.9 %fusion.9.refs_19_.refs_20_.refs_21_.refs_22_.refs_23_ = bf16[1024,1024]{1,0:T(8,128)(2,1)} fusion(bf16[1024,2048]{1,0:T(8,128)(2,1)S(1)} %copy-done.5, bf16[2,2048,1024]{2,1,0:T(8,128)(2,1)} %refs_3_.1), kind=kOutput, calls=%fused_computation.11 | convolution fusion | flops 4296015872 | bytes 10485760 | tf_op jit(solution)/shard_map/dot_general | solution.py:158
  200.4 8.6 %collective-permute-done.25 = bf16[128,2048]{1,0:T(8,128)(2,1)S(1)} collective-permute-done((bf16[128,2048]{1,0:T(8,128)(2,1)S(1)}, bf16[128,2048]{1,0:T(8,128)(2,1)S(1)}, u32[]{:S(2)}, u32[]{:S(2)}) %collective-permute-start.25) | collective-permute-done | bytes 524320 | tf_op jit(solution)/shard_map/ppermute | solution.py:49
  213.1 9.9 %collective-permute-done.28.refs_3_ = bf16[128,2048]{1,0:T(8,128)(2,1)} collective-permute-done((bf16[128,2048]{1,0:T(8,128)(2,1)S(1)}, bf16[128,2048]{1,0:T(8,128)(2,1)}, u32[]{:S(2)}, u32[]{:S(2)}) %collective-permute-start.28) | collective-permute-done | bytes 524320 | tf_op jit(solution)/shard_map/ppermute | solution.py:46
  225.0 3.1 stack.28.refs_0_
  233.2 2.5 collective-permute-done.29.refs_5_
  237.9 31.7 %shard_map.308 = (bf16[1024,2048]{1,0:T(8,128)(2,1)}, f32[1024,128]{1,0:T(8,128)}, bf16[1024,2048]{1,0:T(8,128)(2,1)}, bf16[1024,2048]{1,0:T(8,128)(2,1)}, bf16[...) custom-call(s32[5]{0:T(128)} %stack.28.refs_0_, ...), custom_call_target="tpu_custom_call" | custom-call | flops 17179869184 | bytes 44040192 | tf_op jit(solution)/shard_map/pallas_call | solution.py:578
  273.9 2.1 collective-permute-done.32.refs_5_
  278.6 31.7 %shard_map.309 = (bf16[1024,2048]{1,0:T(8,128)(2,1)}, f32[1024,128]{1,0:T(8,128)}, bf16[1024,2048]{1,0:T(8,128)(2,1)}, bf16[1024,2048]{1,0:T(8,128)(2,1)}, bf16[...) custom-call(s32[5]{0:T(128)} %pad_add_fusion.refs_0_, ...), custom_call_target="tpu_custom_call", output_to_operand_aliasing={{0}: (24, {}), {1}: (25, {}), {2}: (26, {}), {3}: (27, {}),... | custom-call | flops 17179869184 | bytes 44040192 | tf_op jit(solution)/shard_map/pallas_call | solution.py:578
  310.3 8.6 %shard_map.311 = bf16[2048,1024]{1,0:T(8,128)(2,1)} custom-call(bf16[1024,2048]{1,0:T(8,128)(2,1)} %all-gather.2.cloned.1.call-done.refs_0_, bf16[1024,2048]{1,0:T(8,128)(2,1)} %get-tuple-element.100.refs_2_.refs_1_), custom_call_target="tpu_custom_call" | custom-call | flops 4294967296 | bytes 8388608 | tf_op jit(solution)/shard_map/pallas_call | solution.py:702
  321.0 8.5 %shard_map.312 = bf16[2048,1024]{1,0:T(8,128)(2,1)} custom-call(bf16[1024,2048]{1,0:T(8,128)(2,1)} %get-tuple-element.147.refs_0_, bf16[1024,2048]{1,0:T(8,128)(2,1)} %get-tuple-element.109.refs_1_), custom_call_target="tpu_custom_call" | custom-call | flops 4294967296 | bytes 8388608 | tf_op jit(solution)/shard_map/pallas_call | solution.py:702
  334.0 8.6 %shard_map.314 = bf16[2048,1024]{1,0:T(8,128)(2,1)} custom-call(bf16[1024,2048]{1,0:T(8,128)(2,1)} %get-tuple-element.147.refs_0_, bf16[1024,2048]{1,0:T(8,128)(2,1)} %get-tuple-element.115.refs_1_), custom_call_target="tpu_custom_call" | custom-call | flops 4294967296 | bytes 8388608 | tf_op jit(solution)/shard_map/pallas_call | solution.py:702
  342.6 2.5 collective-permute-done.35
  355.7 3.3 all-to-all-start.1
  359.1 6.5 %shard_map.313 = bf16[2048,512]{1,0:T(8,128)(2,1)} custom-call(bf16[1024,2048]{1,0:T(8,128)(2,1)} %all-gather.2.cloned.1.call-done.refs_0_, bf16[1024,2048]{1,0:T(8,128)(2,1)} %get-tuple-element.100.refs_2_.refs_1_, bf16[2048,1024]{1,0:T(8,128)(2,1)} %collective-permute-done.40.refs_2_), custom_call_target="tpu_custom_call" | custom-call | flops 2147483648 | bytes 6291456 | tf_op jit(solution)/shard_map/pallas_call | solution.py:702
  372.1 6.5 shard_map.315
  380.6 3.7 collective-permute-done.42
  384.3 2.9 multiply_reduce_fusion
  387.2 2.5 broadcast.211
  393.2 6.4 shard_map.316
  405.7 15.3 %shard_map.310 = bf16[1024,2048]{1,0:T(8,128)(2,1)} custom-call(s32[1]{0:T(128)} %constant.95.clone.1.refs_0_, s32[4]{0:T(128)} %gather_fusion.1, bf16[1024,2048]{1,0:T(8,128)(2,1)} %get-tuple-element.100.refs_2_.refs_1_, bf16[2,2048,1024]{2,1,0:T(8,128)(2,1)} %refs_3_.1), custom_call_target="tpu_custom_call" | custom-call | flops 8589934592 | bytes 8388608 | tf_op jit(solution)/shard_map/pallas_call | solution.py:653
  430.7 4.4 collective-permute-done.49
  439.0 2.6 collective-permute-done.51
  444.3 4.3 convolution_convert_fusion.4.do_ref
  450.1 16.2 %shard_map.317 = (f32[1024,256]{1,0:T(8,128)}, f32[1024,256]{1,0:T(8,128)}, bf16[1024,256]{1,0:T(8,128)(2,1)}, f32[8,1024]{1,0:T(8,128)}, f32[2,256]{1,0:T(2,128)}) custom-call(s32[1]{0:T(128)} %dynamic_slice.85.length_ref, f32[1024,768]{1,0:T(8,128)} %get-tuple-element.83.qkv_ref, f32[8,1024]{1,0:T(8,128)} %add.357.squares_ref, f32[2,256]{1,0:T(2,128)} %copy.87.gain_ref, ...), custom_call_target="tpu_custom_call" | custom-call | flops 2684354560 | bytes 10485760 | tf_op jit(solution)/shard_map/pallas_call | solution.py:361
  467.2 3.5 fusion.52
  474.9 2.7 collective-permute-done.55
  479.1 5.4 collective-permute-done.56
  485.2 9.7 %shard_map.318 = (bf16[1024,768]{1,0:T(8,128)(2,1)}, bf16[1024,2048]{1,0:T(8,128)(2,1)}) custom-call(f32[1024,256]{1,0:T(8,128)} %get-tuple-element.130.dq_ref, f32[1024,256]{1,0:T(8,128)} %get-tuple-element.131.dk_ref, bf16[1024,256]{1,0:T(8,128)(2,1)} %get-tuple-element.132.dv_ref, f32[1024,768]{1,0:T(8,128)} %get-tuple-element.83.qkv_ref, ...), custom_call_target="tpu_custom_call" | custom-call | flops 3221225472 | bytes 8388608 | tf_op jit(solution)/shard_map/pallas_call | solution.py:400
  494.9 2.9 convolution_convert_fusion.2
  497.9 2.7 fusion.23
  503.9 6.6 %collective-permute-done.59 = bf16[64,2048]{1,0:T(8,128)(2,1)S(1)} collective-permute-done((bf16[64,2048]{1,0:T(8,128)(2,1)S(1)}, bf16[64,2048]{1,0:T(8,128)(2,1)S(1)}, u32[]{:S(2)}, u32[]{:S(2)}) %collective-permute-start.59) | collective-permute-done | bytes 262176 | tf_op jit(solution)/shard_map/ppermute | solution.py:49
  510.5 2.2 collective-permute-done.57
  516.2 15.1 %collective-permute-done.58 = bf16[128,2048]{1,0:T(8,128)(2,1)S(1)} collective-permute-done((bf16[128,2048]{1,0:T(8,128)(2,1)S(1)}, bf16[128,2048]{1,0:T(8,128)(2,1)S(1)}, u32[]{:S(2)}, u32[]{:S(2)}) %collective-permute-start.58) | collective-permute-done | bytes 524320 | tf_op jit(solution)/shard_map/ppermute | solution.py:46
  531.4 4.2 collective-permute-done.60
  536.0 4.2 collective-permute-start.64
  541.4 11.8 %collective-permute-done.68 = bf16[512,768]{1,0:T(8,128)(2,1)S(1)} collective-permute-done((bf16[512,768]{1,0:T(8,128)(2,1)S(1)}, bf16[512,768]{1,0:T(8,128)(2,1)S(1)}, u32[]{:S(2)}, u32[]{:S(2)}) %collective-permute-start.68) | collective-permute-done | bytes 786464 | tf_op jit(solution)/shard_map/ppermute | solution.py:147
  556.7 7.3 %collective-permute-start.65 = (bf16[128,2048]{1,0:T(8,128)(2,1)}, bf16[128,2048]{1,0:T(8,128)(2,1)}, u32[]{:S(2)}, u32[]{:S(2)}) collective-permute-start(bf16[128,2048]{1,0:T(8,128)(2,1)} %get-tuple-element.163), channel_id=1, source_target_pairs={{4,2},{6,4},{7,6},{5,7},{3,5},{1,3},{0,1},{2,0},{12,10},{14,12},{1... | collective-permute-start | bytes 1572872 | tf_op jit(solution)/shard_map/ppermute | solution.py:49
  563.9 2.6 fusion.14
  568.5 5.1 collective-permute-done.63
  575.3 4.3 all-to-all-start.2
  581.2 4.8 collective-permute-start.73
  586.0 10.5 %collective-permute-done.73 = f32[20,2048]{1,0:T(8,128)S(1)} collective-permute-done((f32[20,2048]{1,0:T(8,128)}, f32[20,2048]{1,0:T(8,128)S(1)}, u32[]{:S(2)}, u32[]{:S(2)}) %collective-permute-start.73) | collective-permute-done | bytes 163872 | tf_op jit(solution)/shard_map/ppermute | solution.py:980
  598.6 14.5 %collective-permute-done.74 = f32[20,2048]{1,0:T(8,128)S(1)} collective-permute-done((f32[20,2048]{1,0:T(8,128)S(1)}, f32[20,2048]{1,0:T(8,128)S(1)}, u32[]{:S(2)}, u32[]{:S(2)}) %collective-permute-start.74) | collective-permute-done | bytes 163872 | tf_op jit(solution)/shard_map/ppermute | solution.py:980
  613.3 7.8 %shard_map.321 = f32[2,2048,256]{2,1,0:T(8,128)} custom-call(bf16[1024,2048]{1,0:T(8,128)(2,1)} %all-gather.2.cloned.1.call-done.refs_0_, bf16[1024,2048]{1,0:T(8,128)(2,1)} %get-tuple-element.100.refs_2_.refs_1_, bf16[2048,1024]{1,0:T(8,128)(2,1)} %collective-permute-done.40.refs_2_, bf16[2048,512]{1,0:T(8,128)(2,1)} %collective-permute-done.53.refs_3_), custom_call_target="tpu_custom_call" | custom-call | flops 2147483648 | bytes 6291456 | tf_op jit(solution)/shard_map/pallas_call | solution.py:702
  623.3 7.6 %shard_map.319 = f32[2,2048,256]{2,1,0:T(8,128)} custom-call(bf16[1024,2048]{1,0:T(8,128)(2,1)} %get-tuple-element.147.refs_0_, bf16[1024,2048]{1,0:T(8,128)(2,1)} %get-tuple-element.109.refs_1_, bf16[2048,1024]{1,0:T(8,128)(2,1)} %collective-permute-done.43.refs_2_, bf16[2048,512]{1,0:T(8,128)(2,1)} %copy-done.13), custom_call_target="tpu_custom_call" | custom-call | flops 2147483648 | bytes 6291456 | tf_op jit(solution)/shard_map/pallas_call | solution.py:702
  631.0 7.6 %shard_map.320 = f32[2,2048,256]{2,1,0:T(8,128)} custom-call(bf16[1024,2048]{1,0:T(8,128)(2,1)} %get-tuple-element.147.refs_0_, bf16[1024,2048]{1,0:T(8,128)(2,1)} %get-tuple-element.115.refs_1_, bf16[2048,1024]{1,0:T(8,128)(2,1)} %collective-permute-done.46.refs_2_, bf16[2048,512]{1,0:T(8,128)(2,1)} %collective-permute-done.78.refs_3_), custom_call_target="tpu_custom_call" | custom-call | flops 2147483648 | bytes 6291456 | tf_op jit(solution)/shard_map/pallas_call | solution.py:702
  (374 shorter events, 167.9 us)
Async XLA Ops:
  7.2 17.5 %collective-permute-start = (bf16[128,2048]{1,0:T(8,128)(2,1)}, bf16[128,2048]{1,0:T(8,128)(2,1)S(1)}, u32[]{:S(2)}, u32[]{:S(2)}) collective-permute-start(bf16[128,2048]{1,0:T(8,128)(2,1)} %param.19), channel_id=1, source_target_pairs={{2,4},{4,6},{6,7},{7,5},{5,3},{3,1},{1,0},{0,2},{10,12},{12,14},{1... | collective-permute-start | bytes 1572872 | tf_op jit(solution)/shard_map/ppermute | solution.py:46
  10.3 16.5 %collective-permute-start.1 = (bf16[128,2048]{1,0:T(8,128)(2,1)}, bf16[128,2048]{1,0:T(8,128)(2,1)S(1)}, u32[]{:S(2)}, u32[]{:S(2)}) collective-permute-start(bf16[128,2048]{1,0:T(8,128)(2,1)} %param.19), channel_id=1, source_target_pairs={{4,2},{6,4},{7,6},{5,7},{3,5},{1,3},{0,1},{2,0},{12,10},{14,12},{1... | collective-permute-start | bytes 1572872 | tf_op jit(solution)/shard_map/ppermute | solution.py:49
  16.5 59.7 %all-to-all-start = ((bf16[8,64,896]{2,1,0:T(8,128)(2,1)}), bf16[8,64,896]{2,1,0:T(8,128)(2,1)S(1)}, u32[]{:S(2)}, u32[]{:S(2)}) async-start(bf16[8,64,896]{2,1,0:T(8,128)(2,1)} %concatenate.34), calls=%async_computation | async-start | bytes 1835008 | tf_op jit(solution)/shard_map/all_to_all | solution.py:771
  22.8 149.3 %all-gather.2.cloned.1.call-start = ((), (), s32[]{:S(2)}) async-start(), calls=%async_computation.4 | async-start | bytes 4718592 | tf_op jit(solution)/shard_map/all_gather | solution.py:786
  24.7 23.6 %collective-permute-start.2 = (bf16[128,2048]{1,0:T(8,128)(2,1)S(1)}, bf16[128,2048]{1,0:T(8,128)(2,1)}, u32[]{:S(2)}, u32[]{:S(2)}) collective-permute-start(bf16[128,2048]{1,0:T(8,128)(2,1)S(1)} %collective-permute-done), channel_id=1, source_target_pairs={{2,4},{4,6},{6,7},{7,5},{5,3},{3,1},{1,0},{0,2},{10,12},{12,14},{1... | collective-permute-start | bytes 1572872 | tf_op jit(solution)/shard_map/ppermute | solution.py:46
  26.8 28.0 %collective-permute-start.3 = (bf16[128,2048]{1,0:T(8,128)(2,1)S(1)}, bf16[128,2048]{1,0:T(8,128)(2,1)S(1)}, u32[]{:S(2)}, u32[]{:S(2)}) collective-permute-start(bf16[128,2048]{1,0:T(8,128)(2,1)S(1)} %collective-permute-done.1), channel_id=1, source_target_pairs={{4,2},{6,4},{7,6},{5,7},{3,5},{1,3},{0,1},{2,0},{12,10},{14,12},{1... | collective-permute-start | bytes 1572872 | tf_op jit(solution)/shard_map/ppermute | solution.py:49
  48.4 17.3 %collective-permute-start.4 = (bf16[128,2048]{1,0:T(8,128)(2,1)}, bf16[128,2048]{1,0:T(8,128)(2,1)S(1)}, u32[]{:S(2)}, u32[]{:S(2)}) collective-permute-start(bf16[128,2048]{1,0:T(8,128)(2,1)} %collective-permute-done.2), channel_id=1, source_target_pairs={{2,4},{4,6},{6,7},{7,5},{5,3},{3,1},{1,0},{0,2},{10,12},{12,14},{1... | collective-permute-start | bytes 1572872 | tf_op jit(solution)/shard_map/ppermute | solution.py:46
  54.8 13.7 %collective-permute-start.5 = (bf16[128,2048]{1,0:T(8,128)(2,1)S(1)}, bf16[128,2048]{1,0:T(8,128)(2,1)S(1)}, u32[]{:S(2)}, u32[]{:S(2)}) collective-permute-start(bf16[128,2048]{1,0:T(8,128)(2,1)S(1)} %collective-permute-done.3), channel_id=1, source_target_pairs={{4,2},{6,4},{7,6},{5,7},{3,5},{1,3},{0,1},{2,0},{12,10},{14,12},{1... | collective-permute-start | bytes 1572872 | tf_op jit(solution)/shard_map/ppermute | solution.py:49
  76.3 31.0 %collective-permute-start.8 = (bf16[512,896]{1,0:T(8,128)(2,1)S(1)}, bf16[512,896]{1,0:T(8,128)(2,1)S(1)}, u32[]{:S(2)}, u32[]{:S(2)}) collective-permute-start(bf16[512,896]{1,0:T(8,128)(2,1)S(1)} %bitcast.102), channel_id=1, source_target_pairs={{0,16},{8,24},{16,0},{24,8},{1,17},{9,25},{17,1},{25,9},{2,18},{10... | collective-permute-start | bytes 2752520 | tf_op jit(solution)/shard_map/ppermute | solution.py:131
  79.4 27.4 %collective-permute-start.12 = (bf16[64,2048]{1,0:T(8,128)(2,1)}, bf16[64,2048]{1,0:T(8,128)(2,1)}, u32[]{:S(2)}, u32[]{:S(2)}) collective-permute-start(bf16[64,2048]{1,0:T(8,128)(2,1)} %collective-permute-done.11), channel_id=1, source_target_pairs={{0,16},{8,24},{16,0},{24,8},{1,17},{9,25},{17,1},{25,9},{2,18},{10... | collective-permute-start | bytes 786440 | tf_op jit(solution)/shard_map/ppermute | solution.py:131
  92.4 15.9 %collective-permute-start.13 = (bf16[64,2048]{1,0:T(8,128)(2,1)}, bf16[64,2048]{1,0:T(8,128)(2,1)S(1)}, u32[]{:S(2)}, u32[]{:S(2)}) collective-permute-start(bf16[64,2048]{1,0:T(8,128)(2,1)} %collective-permute-done.11), channel_id=1, source_target_pairs={{0,8},{8,0},{16,24},{24,16},{1,9},{9,1},{17,25},{25,17},{2,10},{10... | collective-permute-start | bytes 786440 | tf_op jit(solution)/shard_map/ppermute | solution.py:133
  125.1 13.6 %collective-permute-start.15 = (f32[8,1024]{1,0:T(8,128)}, f32[8,1024]{1,0:T(8,128)S(1)}, u32[]{:S(2)}, u32[]{:S(2)}) collective-permute-start(f32[8,1024]{1,0:T(8,128)} %get-tuple-element.85), channel_id=1, source_target_pairs={{0,1},{1,0},{2,3},{3,2},{4,5},{5,4},{6,7},{7,6},{8,9},{9,8},{10,11... | collective-permute-start | bytes 98312 | tf_op jit(solution)/shard_map/ppermute | solution.py:113
  169.9 12.6 %collective-permute-start.19 = (bf16[128,2048]{1,0:T(8,128)(2,1)S(1)}, bf16[128,2048]{1,0:T(8,128)(2,1)S(1)}, u32[]{:S(2)}, u32[]{:S(2)}) collective-permute-start(bf16[128,2048]{1,0:T(8,128)(2,1)S(1)} %pad_maximum_fusion.2), channel_id=1, source_target_pairs={{2,4},{4,6},{6,7},{7,5},{5,3},{3,1},{1,0},{0,2},{10,12},{12,14},{1... | collective-permute-start | bytes 1572872 | tf_op jit(solution)/shard_map/ppermute | solution.py:46
  171.6 12.5 %collective-permute-start.21 = (bf16[128,2048]{1,0:T(8,128)(2,1)S(1)}, bf16[128,2048]{1,0:T(8,128)(2,1)}, u32[]{:S(2)}, u32[]{:S(2)}) collective-permute-start(bf16[128,2048]{1,0:T(8,128)(2,1)S(1)} %pad_maximum_fusion.3), channel_id=1, source_target_pairs={{4,2},{6,4},{7,6},{5,7},{3,5},{1,3},{0,1},{2,0},{12,10},{14,12},{1... | collective-permute-start | bytes 1572872 | tf_op jit(solution)/shard_map/ppermute | solution.py:49
  185.6 11.5 %collective-permute-start.22 = (bf16[128,2048]{1,0:T(8,128)(2,1)S(1)}, bf16[128,2048]{1,0:T(8,128)(2,1)S(1)}, u32[]{:S(2)}, u32[]{:S(2)}) collective-permute-start(bf16[128,2048]{1,0:T(8,128)(2,1)S(1)} %get-tuple-element.176), channel_id=1, source_target_pairs={{2,4},{4,6},{6,7},{7,5},{5,3},{3,1},{1,0},{0,2},{10,12},{12,14},{1... | collective-permute-start | bytes 1572872 | tf_op jit(solution)/shard_map/ppermute | solution.py:46
  186.3 11.6 %collective-permute-start.23 = (bf16[128,2048]{1,0:T(8,128)(2,1)S(1)}, bf16[128,2048]{1,0:T(8,128)(2,1)S(1)}, u32[]{:S(2)}, u32[]{:S(2)}) collective-permute-start(bf16[128,2048]{1,0:T(8,128)(2,1)S(1)} %get-tuple-element.175), channel_id=1, source_target_pairs={{4,2},{6,4},{7,6},{5,7},{3,5},{1,3},{0,1},{2,0},{12,10},{14,12},{1... | collective-permute-start | bytes 1572872 | tf_op jit(solution)/shard_map/ppermute | solution.py:49
  198.3 10.7 %collective-permute-start.25 = (bf16[128,2048]{1,0:T(8,128)(2,1)S(1)}, bf16[128,2048]{1,0:T(8,128)(2,1)S(1)}, u32[]{:S(2)}, u32[]{:S(2)}) collective-permute-start(bf16[128,2048]{1,0:T(8,128)(2,1)S(1)} %get-tuple-element.174), channel_id=1, source_target_pairs={{4,2},{6,4},{7,6},{5,7},{3,5},{1,3},{0,1},{2,0},{12,10},{14,12},{1... | collective-permute-start | bytes 1572872 | tf_op jit(solution)/shard_map/ppermute | solution.py:49
  199.8 10.6 %collective-permute-start.24 = (bf16[128,2048]{1,0:T(8,128)(2,1)S(1)}, bf16[128,2048]{1,0:T(8,128)(2,1)S(1)}, u32[]{:S(2)}, u32[]{:S(2)}) collective-permute-start(bf16[128,2048]{1,0:T(8,128)(2,1)S(1)} %get-tuple-element.173), channel_id=1, source_target_pairs={{2,4},{4,6},{6,7},{7,5},{5,3},{3,1},{1,0},{0,2},{10,12},{12,14},{1... | collective-permute-start | bytes 1572872 | tf_op jit(solution)/shard_map/ppermute | solution.py:46
  211.0 11.9 %collective-permute-start.28 = (bf16[128,2048]{1,0:T(8,128)(2,1)S(1)}, bf16[128,2048]{1,0:T(8,128)(2,1)}, u32[]{:S(2)}, u32[]{:S(2)}) collective-permute-start(bf16[128,2048]{1,0:T(8,128)(2,1)S(1)} %multiply_convert_fusion.refs_2_), channel_id=1, source_target_pairs={{2,4},{4,6},{6,7},{7,5},{5,3},{3,1},{1,0},{0,2},{10,12},{12,14},{1... | collective-permute-start | bytes 1572872 | tf_op jit(solution)/shard_map/ppermute | solution.py:46
  212.5 11.9 %collective-permute-start.26 = (bf16[128,2048]{1,0:T(8,128)(2,1)S(1)}, bf16[128,2048]{1,0:T(8,128)(2,1)}, u32[]{:S(2)}, u32[]{:S(2)}) collective-permute-start(bf16[128,2048]{1,0:T(8,128)(2,1)S(1)} %multiply_convert_fusion.refs_2_), channel_id=1, source_target_pairs={{4,2},{6,4},{7,6},{5,7},{3,5},{1,3},{0,1},{2,0},{12,10},{14,12},{1... | collective-permute-start | bytes 1572872 | tf_op jit(solution)/shard_map/ppermute | solution.py:49
  222.9 12.8 %collective-permute-start.29 = (bf16[128,2048]{1,0:T(8,128)(2,1)}, bf16[128,2048]{1,0:T(8,128)(2,1)}, u32[]{:S(2)}, u32[]{:S(2)}) collective-permute-start(bf16[128,2048]{1,0:T(8,128)(2,1)} %collective-permute-done.28.refs_3_), channel_id=1, source_target_pairs={{2,4},{4,6},{6,7},{7,5},{5,3},{3,1},{1,0},{0,2},{10,12},{12,14},{1... | collective-permute-start | bytes 1572872 | tf_op jit(solution)/shard_map/ppermute | solution.py:46
  224.4 13.0 %collective-permute-start.27 = (bf16[128,2048]{1,0:T(8,128)(2,1)}, bf16[128,2048]{1,0:T(8,128)(2,1)}, u32[]{:S(2)}, u32[]{:S(2)}) collective-permute-start(bf16[128,2048]{1,0:T(8,128)(2,1)} %collective-permute-done.26.refs_4_), channel_id=1, source_target_pairs={{4,2},{6,4},{7,6},{5,7},{3,5},{1,3},{0,1},{2,0},{12,10},{14,12},{1... | collective-permute-start | bytes 1572872 | tf_op jit(solution)/shard_map/ppermute | solution.py:49
  235.8 33.7 %collective-permute-start.30 = (bf16[128,2048]{1,0:T(8,128)(2,1)}, bf16[128,2048]{1,0:T(8,128)(2,1)S(1)}, u32[]{:S(2)}, u32[]{:S(2)}) collective-permute-start(bf16[128,2048]{1,0:T(8,128)(2,1)} %collective-permute-done.29.refs_5_), channel_id=1, source_target_pairs={{2,4},{4,6},{6,7},{7,5},{5,3},{3,1},{1,0},{0,2},{10,12},{12,14},{1... | collective-permute-start | bytes 1572872 | tf_op jit(solution)/shard_map/ppermute | solution.py:46
  237.4 32.2 %collective-permute-start.31 = (bf16[128,2048]{1,0:T(8,128)(2,1)}, bf16[128,2048]{1,0:T(8,128)(2,1)S(1)}, u32[]{:S(2)}, u32[]{:S(2)}) collective-permute-start(bf16[128,2048]{1,0:T(8,128)(2,1)} %collective-permute-done.27.refs_2_), channel_id=1, source_target_pairs={{4,2},{6,4},{7,6},{5,7},{3,5},{1,3},{0,1},{2,0},{12,10},{14,12},{1... | collective-permute-start | bytes 1572872 | tf_op jit(solution)/shard_map/ppermute | solution.py:49
  318.8 40.3 %collective-permute-start.40 = (bf16[2048,1024]{1,0:T(8,128)(2,1)}, bf16[2048,1024]{1,0:T(8,128)(2,1)}, u32[]{:S(2)}, u32[]{:S(2)}) collective-permute-start(bf16[2048,1024]{1,0:T(8,128)(2,1)} %shard_map.311), channel_id=1, source_target_pairs={{0,8},{8,0},{16,24},{24,16},{1,9},{9,1},{17,25},{25,17},{2,10},{10... | collective-permute-start | bytes 12582920 | tf_op jit(solution)/shard_map/ppermute | solution.py:871
  318.9 10.6 %collective-permute-start.34 = (bf16[64,2048]{1,0:T(8,128)(2,1)S(1)}, bf16[64,2048]{1,0:T(8,128)(2,1)S(1)}, u32[]{:S(2)}, u32[]{:S(2)}) collective-permute-start(bf16[64,2048]{1,0:T(8,128)(2,1)S(1)} %get-tuple-element.192), channel_id=1, source_target_pairs={{2,4},{4,6},{6,7},{7,5},{5,3},{3,1},{1,0},{0,2},{10,12},{12,14},{1... | collective-permute-start | bytes 786440 | tf_op jit(solution)/shard_map/ppermute | solution.py:46
  319.4 11.5 %collective-permute-start.36 = (bf16[64,2048]{1,0:T(8,128)(2,1)S(1)}, bf16[64,2048]{1,0:T(8,128)(2,1)S(1)}, u32[]{:S(2)}, u32[]{:S(2)}) collective-permute-start(bf16[64,2048]{1,0:T(8,128)(2,1)S(1)} %get-tuple-element.191), channel_id=1, source_target_pairs={{4,2},{6,4},{7,6},{5,7},{3,5},{1,3},{0,1},{2,0},{12,10},{14,12},{1... | collective-permute-start | bytes 786440 | tf_op jit(solution)/shard_map/ppermute | solution.py:49
  329.5 42.6 %collective-permute-start.43 = (bf16[2048,1024]{1,0:T(8,128)(2,1)}, bf16[2048,1024]{1,0:T(8,128)(2,1)}, u32[]{:S(2)}, u32[]{:S(2)}) collective-permute-start(bf16[2048,1024]{1,0:T(8,128)(2,1)} %shard_map.312), channel_id=1, source_target_pairs={{0,8},{8,0},{16,24},{24,16},{1,9},{9,1},{17,25},{25,17},{2,10},{10... | collective-permute-start | bytes 12582920 | tf_op jit(solution)/shard_map/ppermute | solution.py:871
  330.4 14.6 %collective-permute-start.35 = (bf16[128,2048]{1,0:T(8,128)(2,1)}, bf16[128,2048]{1,0:T(8,128)(2,1)}, u32[]{:S(2)}, u32[]{:S(2)}) collective-permute-start(bf16[128,2048]{1,0:T(8,128)(2,1)} %pad_maximum_fusion.4), channel_id=1, source_target_pairs={{2,4},{4,6},{6,7},{7,5},{5,3},{3,1},{1,0},{0,2},{10,12},{12,14},{1... | collective-permute-start | bytes 1572872 | tf_op jit(solution)/shard_map/ppermute | solution.py:46
  331.8 14.4 %collective-permute-start.37 = (bf16[128,2048]{1,0:T(8,128)(2,1)}, bf16[128,2048]{1,0:T(8,128)(2,1)}, u32[]{:S(2)}, u32[]{:S(2)}) collective-permute-start(bf16[128,2048]{1,0:T(8,128)(2,1)} %pad_maximum_fusion.5), channel_id=1, source_target_pairs={{4,2},{6,4},{7,6},{5,7},{3,5},{1,3},{0,1},{2,0},{12,10},{14,12},{1... | collective-permute-start | bytes 1572872 | tf_op jit(solution)/shard_map/ppermute | solution.py:49
  342.6 50.6 %collective-permute-start.46 = (bf16[2048,1024]{1,0:T(8,128)(2,1)}, bf16[2048,1024]{1,0:T(8,128)(2,1)}, u32[]{:S(2)}, u32[]{:S(2)}) collective-permute-start(bf16[2048,1024]{1,0:T(8,128)(2,1)} %shard_map.314), channel_id=1, source_target_pairs={{0,8},{8,0},{16,24},{24,16},{1,9},{9,1},{17,25},{25,17},{2,10},{10... | collective-permute-start | bytes 12582920 | tf_op jit(solution)/shard_map/ppermute | solution.py:871
  348.1 17.5 %collective-permute-start.38 = (bf16[128,2048]{1,0:T(8,128)(2,1)}, bf16[128,2048]{1,0:T(8,128)(2,1)}, u32[]{:S(2)}, u32[]{:S(2)}) collective-permute-start(bf16[128,2048]{1,0:T(8,128)(2,1)} %add_convert_fusion.9), channel_id=1, source_target_pairs={{2,4},{4,6},{6,7},{7,5},{5,3},{3,1},{1,0},{0,2},{10,12},{12,14},{1... | collective-permute-start | bytes 1572872 | tf_op jit(solution)/shard_map/ppermute | solution.py:46
  350.4 15.2 %collective-permute-start.39 = (bf16[128,2048]{1,0:T(8,128)(2,1)}, bf16[128,2048]{1,0:T(8,128)(2,1)}, u32[]{:S(2)}, u32[]{:S(2)}) collective-permute-start(bf16[128,2048]{1,0:T(8,128)(2,1)} %add_convert_fusion.8), channel_id=1, source_target_pairs={{4,2},{6,4},{7,6},{5,7},{3,5},{1,3},{0,1},{2,0},{12,10},{14,12},{1... | collective-permute-start | bytes 1572872 | tf_op jit(solution)/shard_map/ppermute | solution.py:49
  355.7 16.3 %all-to-all-start.1 = ((f32[8,2,128]{2,1,0:T(2,128)}), f32[8,2,128]{2,1,0:T(2,128)S(1)}, u32[]{:S(2)}, u32[]{:S(2)}) async-start(f32[8,2,128]{2,1,0:T(2,128)} %bitcast.28), calls=%async_computation.1 | async-start | bytes 16384 | tf_op jit(solution)/shard_map/all_to_all | solution.py:861
  359.0 204.9 %reduce-scatter.2.cloned.1.call-start = ((), (), s32[]{:S(2)}) async-start(), calls=%async_computation.5 | async-start | bytes 4718592 | tf_op jit(solution)/shard_map/reduce_scatter | solution.py:941
  367.6 13.0 %collective-permute-start.41 = (bf16[128,2048]{1,0:T(8,128)(2,1)}, bf16[128,2048]{1,0:T(8,128)(2,1)}, u32[]{:S(2)}, u32[]{:S(2)}) collective-permute-start(bf16[128,2048]{1,0:T(8,128)(2,1)} %add_convert_fusion.7), channel_id=1, source_target_pairs={{2,4},{4,6},{6,7},{7,5},{5,3},{3,1},{1,0},{0,2},{10,12},{12,14},{1... | collective-permute-start | bytes 1572872 | tf_op jit(solution)/shard_map/ppermute | solution.py:46
  371.5 12.8 %collective-permute-start.42 = (bf16[128,2048]{1,0:T(8,128)(2,1)}, bf16[128,2048]{1,0:T(8,128)(2,1)}, u32[]{:S(2)}, u32[]{:S(2)}) collective-permute-start(bf16[128,2048]{1,0:T(8,128)(2,1)} %add_convert_fusion.6), channel_id=1, source_target_pairs={{4,2},{6,4},{7,6},{5,7},{3,5},{1,3},{0,1},{2,0},{12,10},{14,12},{1... | collective-permute-start | bytes 1572872 | tf_op jit(solution)/shard_map/ppermute | solution.py:49
  391.2 11.3 %collective-permute-start.44 = (bf16[128,2048]{1,0:T(8,128)(2,1)S(1)}, bf16[128,2048]{1,0:T(8,128)(2,1)}, u32[]{:S(2)}, u32[]{:S(2)}) collective-permute-start(bf16[128,2048]{1,0:T(8,128)(2,1)S(1)} %get-tuple-element.159), channel_id=1, source_target_pairs={{2,4},{4,6},{6,7},{7,5},{5,3},{3,1},{1,0},{0,2},{10,12},{12,14},{1... | collective-permute-start | bytes 1572872 | tf_op jit(solution)/shard_map/ppermute | solution.py:46
  392.7 11.0 %collective-permute-start.45 = (bf16[128,2048]{1,0:T(8,128)(2,1)S(1)}, bf16[128,2048]{1,0:T(8,128)(2,1)}, u32[]{:S(2)}, u32[]{:S(2)}) collective-permute-start(bf16[128,2048]{1,0:T(8,128)(2,1)S(1)} %get-tuple-element.159), channel_id=1, source_target_pairs={{4,2},{6,4},{7,6},{5,7},{3,5},{1,3},{0,1},{2,0},{12,10},{14,12},{1... | collective-permute-start | bytes 1572872 | tf_op jit(solution)/shard_map/ppermute | solution.py:49
  399.6 44.7 %collective-permute-start.53 = (bf16[2048,512]{1,0:T(8,128)(2,1)}, bf16[2048,512]{1,0:T(8,128)(2,1)}, u32[]{:S(2)}, u32[]{:S(2)}) collective-permute-start(bf16[2048,512]{1,0:T(8,128)(2,1)} %shard_map.313), channel_id=1, source_target_pairs={{0,16},{8,24},{16,0},{24,8},{1,17},{9,25},{17,1},{25,9},{2,18},{10... | collective-permute-start | bytes 6291464 | tf_op jit(solution)/shard_map/ppermute | solution.py:892
  403.7 19.3 %collective-permute-start.47 = (bf16[128,2048]{1,0:T(8,128)(2,1)}, bf16[128,2048]{1,0:T(8,128)(2,1)}, u32[]{:S(2)}, u32[]{:S(2)}) collective-permute-start(bf16[128,2048]{1,0:T(8,128)(2,1)} %collective-permute-done.44), channel_id=1, source_target_pairs={{2,4},{4,6},{6,7},{7,5},{5,3},{3,1},{1,0},{0,2},{10,12},{12,14},{1... | collective-permute-start | bytes 1572872 | tf_op jit(solution)/shard_map/ppermute | solution.py:46
  405.2 17.8 %collective-permute-start.48 = (bf16[128,2048]{1,0:T(8,128)(2,1)}, bf16[128,2048]{1,0:T(8,128)(2,1)}, u32[]{:S(2)}, u32[]{:S(2)}) collective-permute-start(bf16[128,2048]{1,0:T(8,128)(2,1)} %collective-permute-done.45), channel_id=1, source_target_pairs={{4,2},{6,4},{7,6},{5,7},{3,5},{1,3},{0,1},{2,0},{12,10},{14,12},{1... | collective-permute-start | bytes 1572872 | tf_op jit(solution)/shard_map/ppermute | solution.py:49
  423.0 12.1 %collective-permute-start.49 = (bf16[128,2048]{1,0:T(8,128)(2,1)}, bf16[128,2048]{1,0:T(8,128)(2,1)S(1)}, u32[]{:S(2)}, u32[]{:S(2)}) collective-permute-start(bf16[128,2048]{1,0:T(8,128)(2,1)} %collective-permute-done.47), channel_id=1, source_target_pairs={{2,4},{4,6},{6,7},{7,5},{5,3},{3,1},{1,0},{0,2},{10,12},{12,14},{1... | collective-permute-start | bytes 1572872 | tf_op jit(solution)/shard_map/ppermute | solution.py:46
  424.5 12.2 %collective-permute-start.50 = (bf16[128,2048]{1,0:T(8,128)(2,1)}, bf16[128,2048]{1,0:T(8,128)(2,1)S(1)}, u32[]{:S(2)}, u32[]{:S(2)}) collective-permute-start(bf16[128,2048]{1,0:T(8,128)(2,1)} %collective-permute-done.48), channel_id=1, source_target_pairs={{4,2},{6,4},{7,6},{5,7},{3,5},{1,3},{0,1},{2,0},{12,10},{14,12},{1... | collective-permute-start | bytes 1572872 | tf_op jit(solution)/shard_map/ppermute | solution.py:49
  470.7 64.9 %collective-permute-start.61 = (bf16[2048,512]{1,0:T(8,128)(2,1)S(1)}, bf16[2048,512]{1,0:T(8,128)(2,1)S(1)}, u32[]{:S(2)}, u32[]{:S(2)}) collective-permute-start(bf16[2048,512]{1,0:T(8,128)(2,1)S(1)} %copy-done.12), channel_id=1, source_target_pairs={{0,16},{8,24},{16,0},{24,8},{1,17},{9,25},{17,1},{25,9},{2,18},{10... | collective-permute-start | bytes 6291464 | tf_op jit(solution)/shard_map/ppermute | solution.py:892
  474.4 38.6 %collective-permute-start.70 = (bf16[64,2048]{1,0:T(8,128)(2,1)S(1)}, bf16[64,2048]{1,0:T(8,128)(2,1)S(1)}, u32[]{:S(2)}, u32[]{:S(2)}) collective-permute-start(bf16[64,2048]{1,0:T(8,128)(2,1)S(1)} %get-tuple-element.184), channel_id=1, source_target_pairs={{0,8},{8,0},{16,24},{24,16},{1,9},{9,1},{17,25},{25,17},{2,10},{10... | collective-permute-start | bytes 786440 | tf_op jit(solution)/shard_map/ppermute | solution.py:143
  474.4 65.8 %collective-permute-start.69 = (bf16[64,2048]{1,0:T(8,128)(2,1)}, bf16[64,2048]{1,0:T(8,128)(2,1)S(1)}, u32[]{:S(2)}, u32[]{:S(2)}) collective-permute-start(bf16[64,2048]{1,0:T(8,128)(2,1)} %get-tuple-element.183), channel_id=1, source_target_pairs={{0,8},{8,0},{16,24},{24,16},{1,9},{9,1},{17,25},{25,17},{2,10},{10... | collective-permute-start | bytes 786440 | tf_op jit(solution)/shard_map/ppermute | solution.py:143
  500.7 9.7 %collective-permute-start.59 = (bf16[64,2048]{1,0:T(8,128)(2,1)S(1)}, bf16[64,2048]{1,0:T(8,128)(2,1)S(1)}, u32[]{:S(2)}, u32[]{:S(2)}) collective-permute-start(bf16[64,2048]{1,0:T(8,128)(2,1)S(1)} %get-tuple-element.170), channel_id=1, source_target_pairs={{4,2},{6,4},{7,6},{5,7},{3,5},{1,3},{0,1},{2,0},{12,10},{14,12},{1... | collective-permute-start | bytes 786440 | tf_op jit(solution)/shard_map/ppermute | solution.py:49
  502.2 10.4 %collective-permute-start.57 = (bf16[64,2048]{1,0:T(8,128)(2,1)S(1)}, bf16[64,2048]{1,0:T(8,128)(2,1)S(1)}, u32[]{:S(2)}, u32[]{:S(2)}) collective-permute-start(bf16[64,2048]{1,0:T(8,128)(2,1)S(1)} %get-tuple-element.168), channel_id=1, source_target_pairs={{2,4},{4,6},{6,7},{7,5},{5,3},{3,1},{1,0},{0,2},{10,12},{12,14},{1... | collective-permute-start | bytes 786440 | tf_op jit(solution)/shard_map/ppermute | solution.py:46
  512.8 18.6 %collective-permute-start.58 = (bf16[128,2048]{1,0:T(8,128)(2,1)S(1)}, bf16[128,2048]{1,0:T(8,128)(2,1)S(1)}, u32[]{:S(2)}, u32[]{:S(2)}) collective-permute-start(bf16[128,2048]{1,0:T(8,128)(2,1)S(1)} %pad_maximum_fusion.6), channel_id=1, source_target_pairs={{2,4},{4,6},{6,7},{7,5},{5,3},{3,1},{1,0},{0,2},{10,12},{12,14},{1... | collective-permute-start | bytes 1572872 | tf_op jit(solution)/shard_map/ppermute | solution.py:46
  513.0 22.6 %collective-permute-start.60 = (bf16[128,2048]{1,0:T(8,128)(2,1)S(1)}, bf16[128,2048]{1,0:T(8,128)(2,1)S(1)}, u32[]{:S(2)}, u32[]{:S(2)}) collective-permute-start(bf16[128,2048]{1,0:T(8,128)(2,1)S(1)} %pad_maximum_fusion.7), channel_id=1, source_target_pairs={{4,2},{6,4},{7,6},{5,7},{3,5},{1,3},{0,1},{2,0},{12,10},{14,12},{1... | collective-permute-start | bytes 1572872 | tf_op jit(solution)/shard_map/ppermute | solution.py:49
  515.1 26.3 %collective-permute-start.66 = (bf16[512,768]{1,0:T(8,128)(2,1)S(1)}, bf16[512,768]{1,0:T(8,128)(2,1)S(1)}, u32[]{:S(2)}, u32[]{:S(2)}) collective-permute-start(bf16[512,768]{1,0:T(8,128)(2,1)S(1)} %convolution_convert_fusion.3), channel_id=1, source_target_pairs={{0,8},{8,0},{16,24},{24,16},{1,9},{9,1},{17,25},{25,17},{2,10},{10... | collective-permute-start | bytes 2359304 | tf_op jit(solution)/shard_map/ppermute | solution.py:143
  531.4 9.2 %collective-permute-start.71 = (bf16[64,2048]{1,0:T(8,128)(2,1)S(1)}, bf16[64,2048]{1,0:T(8,128)(2,1)S(1)}, u32[]{:S(2)}, u32[]{:S(2)}) collective-permute-start(bf16[64,2048]{1,0:T(8,128)(2,1)S(1)} %add_convert_fusion.15), channel_id=1, source_target_pairs={{0,16},{8,24},{16,0},{24,8},{1,17},{9,25},{17,1},{25,9},{2,18},{10... | collective-permute-start | bytes 786440 | tf_op jit(solution)/shard_map/ppermute | solution.py:147
  535.6 17.7 %collective-permute-start.68 = (bf16[512,768]{1,0:T(8,128)(2,1)S(1)}, bf16[512,768]{1,0:T(8,128)(2,1)S(1)}, u32[]{:S(2)}, u32[]{:S(2)}) collective-permute-start(bf16[512,768]{1,0:T(8,128)(2,1)S(1)} %add_convert_fusion.1), channel_id=1, source_target_pairs={{0,16},{8,24},{16,0},{24,8},{1,17},{9,25},{17,1},{25,9},{2,18},{10... | collective-permute-start | bytes 2359304 | tf_op jit(solution)/shard_map/ppermute | solution.py:147
  536.0 18.4 %collective-permute-start.64 = (bf16[128,2048]{1,0:T(8,128)(2,1)S(1)}, bf16[128,2048]{1,0:T(8,128)(2,1)S(1)}, u32[]{:S(2)}, u32[]{:S(2)}) collective-permute-start(bf16[128,2048]{1,0:T(8,128)(2,1)S(1)} %get-tuple-element.165), channel_id=1, source_target_pairs={{4,2},{6,4},{7,6},{5,7},{3,5},{1,3},{0,1},{2,0},{12,10},{14,12},{1... | collective-permute-start | bytes 1572872 | tf_op jit(solution)/shard_map/ppermute | solution.py:49
  540.2 14.2 %collective-permute-start.62 = (bf16[128,2048]{1,0:T(8,128)(2,1)S(1)}, bf16[128,2048]{1,0:T(8,128)(2,1)S(1)}, u32[]{:S(2)}, u32[]{:S(2)}) collective-permute-start(bf16[128,2048]{1,0:T(8,128)(2,1)S(1)} %get-tuple-element.166), channel_id=1, source_target_pairs={{2,4},{4,6},{6,7},{7,5},{5,3},{3,1},{1,0},{0,2},{10,12},{12,14},{1... | collective-permute-start | bytes 1572872 | tf_op jit(solution)/shard_map/ppermute | solution.py:46
  554.4 76.6 %collective-permute-start.78 = (bf16[2048,512]{1,0:T(8,128)(2,1)}, bf16[2048,512]{1,0:T(8,128)(2,1)}, u32[]{:S(2)}, u32[]{:S(2)}) collective-permute-start(bf16[2048,512]{1,0:T(8,128)(2,1)} %shard_map.316), channel_id=1, source_target_pairs={{0,16},{8,24},{16,0},{24,8},{1,17},{9,25},{17,1},{25,9},{2,18},{10... | collective-permute-start | bytes 6291464 | tf_op jit(solution)/shard_map/ppermute | solution.py:892
  555.8 17.9 %collective-permute-start.63 = (bf16[128,2048]{1,0:T(8,128)(2,1)}, bf16[128,2048]{1,0:T(8,128)(2,1)S(1)}, u32[]{:S(2)}, u32[]{:S(2)}) collective-permute-start(bf16[128,2048]{1,0:T(8,128)(2,1)} %get-tuple-element.164), channel_id=1, source_target_pairs={{2,4},{4,6},{6,7},{7,5},{5,3},{3,1},{1,0},{0,2},{10,12},{12,14},{1... | collective-permute-start | bytes 1572872 | tf_op jit(solution)/shard_map/ppermute | solution.py:46
  556.7 17.0 %collective-permute-start.65 = (bf16[128,2048]{1,0:T(8,128)(2,1)}, bf16[128,2048]{1,0:T(8,128)(2,1)}, u32[]{:S(2)}, u32[]{:S(2)}) collective-permute-start(bf16[128,2048]{1,0:T(8,128)(2,1)} %get-tuple-element.163), channel_id=1, source_target_pairs={{4,2},{6,4},{7,6},{5,7},{3,5},{1,3},{0,1},{2,0},{12,10},{14,12},{1... | collective-permute-start | bytes 1572872 | tf_op jit(solution)/shard_map/ppermute | solution.py:49
  575.3 66.5 %all-to-all-start.2 = ((bf16[8,64,768]{2,1,0:T(8,128)(2,1)}), bf16[8,64,768]{2,1,0:T(8,128)(2,1)S(1)}, u32[]{:S(2)}, u32[]{:S(2)}) async-start(bf16[8,64,768]{2,1,0:T(8,128)(2,1)} %bitcast.105), calls=%async_computation.3 | async-start | bytes 1572864 | tf_op jit(solution)/shard_map/all_to_all | solution.py:1002
  579.6 41.4 %collective-permute-start.72 = (bf16[64,2048]{1,0:T(8,128)(2,1)}, bf16[64,2048]{1,0:T(8,128)(2,1)S(1)}, u32[]{:S(2)}, u32[]{:S(2)}) collective-permute-start(bf16[64,2048]{1,0:T(8,128)(2,1)} %add_convert_fusion.14), channel_id=1, source_target_pairs={{0,0},{8,1},{16,2},{24,3},{1,4},{9,5},{17,6},{25,7},{2,8},{10,9},{... | collective-permute-start | bytes 786440 | tf_op jit(solution)/shard_map/ppermute | solution.py:1024
  581.2 15.2 %collective-permute-start.73 = (f32[20,2048]{1,0:T(8,128)}, f32[20,2048]{1,0:T(8,128)S(1)}, u32[]{:S(2)}, u32[]{:S(2)}) collective-permute-start(f32[20,2048]{1,0:T(8,128)} %pad_maximum_fusion.8), channel_id=1, source_target_pairs={{0,1},{1,0},{2,3},{3,2},{4,5},{5,4},{6,7},{7,6},{8,9},{9,8},{10,11... | collective-permute-start | bytes 491528 | tf_op jit(solution)/shard_map/ppermute | solution.py:980
  597.4 15.7 %collective-permute-start.74 = (f32[20,2048]{1,0:T(8,128)S(1)}, f32[20,2048]{1,0:T(8,128)S(1)}, u32[]{:S(2)}, u32[]{:S(2)}) collective-permute-start(f32[20,2048]{1,0:T(8,128)S(1)} %add.404), channel_id=1, source_target_pairs={{0,2},{1,3},{2,0},{3,1},{4,6},{5,7},{6,4},{7,5},{8,10},{9,11},{10,... | collective-permute-start | bytes 491528 | tf_op jit(solution)/shard_map/ppermute | solution.py:980
  613.2 10.0 %collective-permute-start.75 = (f32[20,2048]{1,0:T(8,128)S(1)}, f32[20,2048]{1,0:T(8,128)S(1)}, u32[]{:S(2)}, u32[]{:S(2)}) collective-permute-start(f32[20,2048]{1,0:T(8,128)S(1)} %add.405), channel_id=1, source_target_pairs={{0,4},{1,5},{2,6},{3,7},{4,0},{5,1},{6,2},{7,3},{8,12},{9,13},{10,... | collective-permute-start | bytes 491528 | tf_op jit(solution)/shard_map/ppermute | solution.py:980
  (68 other events, 718.6 us)
Sparse Core Ops, SparseCore 0:
  76.4 82.5 all-gather.1
  448.7 97.3 reduce-scatter.1

commit v4 on v3

--- a/solution.py
+++ b/solution.py
@@ -58,10 +58,9 @@
             made = hooks[step](pieces) if step in hooks else ()
             up, down = together((self.up(up), self.down(down)), made)
             pieces += [(self.size - step, 0, up), (step, 0, down)]
-        if half in hooks:
-            hooks[half](pieces)
-        pieces.append((half, 0, self.up(up[: rows // 2])))
-        pieces.append((half, rows // 2, self.down(down[rows // 2 :])))
+        made = hooks[half](pieces) if half in hooks else ()
+        up, down = together((self.up(up[: rows // 2]), self.down(down[rows // 2 :])), made)
+        pieces += [(half, 0, up), (half, rows // 2, down)]
         return pieces
 
     def scatter(self, term, hooks=None):
@@ -123,18 +122,31 @@
     return value
 
 
-def dp_gather(chunk, n_dp):
-    rows, width = chunk.shape
-    me = lax.axis_index("dp")
-    held = [(0, chunk)]
-    for y in range(1, n_dp // CORES):
-        held.append((2 * y, lax.ppermute(chunk, "dp", [(i, i ^ (2 * y)) for i in range(n_dp)])))
-    swap = [(i, i ^ 1) for i in range(n_dp)]
-    held += [(rel ^ 1, lax.ppermute(part, "dp", swap)) for rel, part in held]
-    buffer = jnp.zeros((n_dp * rows, width), chunk.dtype)
-    for rel, part in held:
-        buffer = lax.dynamic_update_slice(buffer, part, ((me ^ rel) * rows, 0))
-    return buffer
+class DpGather:
+    def __init__(self, chunk, n_dp):
+        self.chunk, self.n_dp = chunk, n_dp
+
+    def over_y(self):
+        n_dp = self.n_dp
+        self.held = [(0, self.chunk)] + [
+            (2 * y, lax.ppermute(self.chunk, "dp", [(i, i ^ (2 * y)) for i in range(n_dp)]))
+            for y in range(1, n_dp // CORES)
+        ]
+        return tuple(part for _, part in self.held[1:])
+
+    def over_cores(self):
+        swap = [(i, i ^ 1) for i in range(self.n_dp)]
+        new = [(rel ^ 1, lax.ppermute(part, "dp", swap)) for rel, part in self.held]
+        self.held += new
+        return tuple(part for _, part in new)
+
+    def rows(self):
+        rows, width = self.chunk.shape
+        me = lax.axis_index("dp")
+        buffer = jnp.zeros((self.n_dp * rows, width), self.chunk.dtype)
+        for rel, part in self.held:
+            buffer = lax.dynamic_update_slice(buffer, part, ((me ^ rel) * rows, 0))
+        return buffer
 
 
 def dp_reduce(term, n_dp):
@@ -208,7 +220,7 @@
 
 
 def project_kernel(tokens_ref, gain_ref, w_ref, in_ref, qkv_ref, squares_ref):
-    own = w_ref.shape[1] // 3
+    own = qkv_ref.shape[1] // 3
     values = tokens_ref[...].astype(F32)
     normed = (values * norm_scale(values) * gain_ref[...]).astype(BF16)
     in_ref[...] = normed
@@ -220,9 +232,8 @@
     )
 
 
-def project(tokens, gain, w_qkv):
+def project(tokens, gain, w_qkv, columns):
     seq, width = tokens.shape
-    columns = w_qkv.shape[1]
     tile = min(256, seq)
     return pl.pallas_call(
         project_kernel,
@@ -768,38 +779,59 @@
         ],
         axis=2,
     )
-    got = lax.all_to_all(send, "expert", split_axis=0, concat_axis=0, tiled=True)
-    hits = got[:, :, 3 * own + extra_columns : 3 * own + extra_columns + hit_columns]
-    hits = hits.reshape(seq, local_experts).astype(F32)
-    projections = dp_gather(got.reshape(groups * weight_rows, -1), n_dp)
-    w_qkv = projections[:, : 3 * own]
-    small = projections[:, 3 * own : 3 * own + extra_columns]
-    gains_full = small[:, :4].T.astype(F32)
-    full_router = small[:, 4:]
     moves = [(e * n_dp + i, i * groups + e) for e in range(groups) for i in range(n_dp)]
-    own_out = dp_gather(lax.ppermute(w_out, both_axes, moves), n_dp)
-
-    resid_in = tokens.astype(F32)
-    attn_gain, ffn_gain = gains_full[0:1], gains_full[3:4]
-    tokens_all = place_blocks(ring, ring.gather(tokens), rows, width)
-    [cot_own] = together((cotangent,), (tokens_all,))
-    cot_all = lax.all_gather(cot_own, "expert", axis=0, tiled=True)
-    attn_in, qkv, squares = project(tokens_all, attn_gain, w_qkv)
-    own_out, squares = lax.optimization_barrier((own_out, squares))
-    squares = expert_sum(squares, groups)
-    gains_own = lax.dynamic_slice(gains_full, (1, me * own), (2, own))
     half = HEAD_DIM // 2
     frequency = ROPE_BASE ** (-(jnp.arange(half, dtype=F32) * 2.0) / HEAD_DIM)
     angles = positions.astype(F32)[:, None] * frequency[None, :]
     cosine, sine = jnp.cos(angles), jnp.sin(angles)
     cosine = jnp.concatenate([cosine, cosine], axis=1)
     sine = jnp.concatenate([-sine, sine], axis=1)
+    start = {}
+    far = groups // 2
+    arrival = [0] + [o for step in range(1, far) for o in (groups - step, step)] + [far]
+    per_call = 4
+    calls = groups // per_call
+    call_index = [
+        jnp.stack([ring.natural[o] for o in arrival[at : at + per_call]] + [me])
+        for at in range(0, groups, per_call)
+    ]
+
+    def make_got(pieces):
+        start["got"] = lax.all_to_all(send, "expert", split_axis=0, concat_axis=0, tiled=True)
+        start["in"] = DpGather(start["got"].reshape(groups * weight_rows, -1), n_dp)
+        return (start["got"], cosine, sine, *call_index)
+
+    def make_y(pieces):
+        start["out"] = DpGather(lax.ppermute(w_out, both_axes, moves), n_dp)
+        return (*start["in"].over_y(), start["out"].chunk)
+
+    hooks = {far - 1: make_got, far: make_y}
+    tokens_all = place_blocks(ring, ring.gather(tokens, hooks), rows, width)
+    start["in"].over_cores()
+    got, projections = start["got"], start["in"].rows()
+    hits = got[:, :, 3 * own + extra_columns : 3 * own + extra_columns + hit_columns]
+    hits = hits.reshape(seq, local_experts).astype(F32)
+    w_qkv = projections
+    small = projections[:, 3 * own : 3 * own + extra_columns]
+    gains_full = small[:, :4].T.astype(F32)
+    full_router = small[:, 4:]
+
+    resid_in = tokens.astype(F32)
+    attn_gain, ffn_gain = gains_full[0:1], gains_full[3:4]
+    [cot_own] = together((cotangent,), (tokens_all,))
+    cot_all = lax.all_gather(cot_own, "expert", axis=0, tiled=True)
+    attn_in, qkv, squares = project(tokens_all, attn_gain, w_qkv, 3 * own)
+    [start["out"].chunk] = together((start["out"].chunk,), (squares,))
+    out_over_y = start["out"].over_y()
+    [squares] = together((expert_sum(squares, groups),), out_over_y)
+    gains_own = lax.dynamic_slice(gains_full, (1, me * own), (2, own))
     q, k, v, attended = attend(seq_length, qkv, squares, gains_own, cosine, sine)
+    [attended] = together((attended,), start["out"].over_cores())
+    own_out = start["out"].rows()
 
     def block_of(value, o):
         return lax.dynamic_slice(value, (ring.natural[o] * rows, 0), (rows, value.shape[1]))
 
-    far = groups // 2
     out_far = matmul(block_of(attended, far), own_out).astype(BF16)
     out_part = matmul(attended, own_out).astype(BF16)
     backs = []
@@ -809,8 +841,12 @@
         return (backs[-1],)
 
     hooks = {
-        2: lambda: make_back(0),
-        3: lambda: [make_back(expert)[0] for expert in range(1, local_experts)],
+        far - 1: lambda: make_back(0),
+        far: lambda: (
+            *[make_back(expert)[0] for expert in range(1, local_experts)],
+            full_router,
+            hits,
+        ),
     }
     resid_mid = resid_in + ring.scatter(
         lambda o: out_far if o == far else block_of(out_part, o), hooks
@@ -824,15 +860,13 @@
     place_of = np.zeros((n_dp,), np.int32)
     place_of[np.array(distances)] = np.arange(n_dp)
     column_place = jnp.asarray(place_of)[jnp.arange(n_dp, dtype=jnp.int32) ^ dp]
-    per_call = 4
-    calls = groups // per_call
     held, drow_terms = [], {}
 
     def expert_pieces(pieces, at):
         given = pieces[at:] if at + per_call == groups else pieces[at : at + per_call]
         order = [o for o, _, _ in given[:per_call]]
         result, blocks = expert_call(
-            jnp.stack([ring.natural[o] for o in order] + [me]),
+            call_index[at // per_call],
             column_place,
             [piece for _, _, piece in given],
             hits,
@@ -975,12 +1009,9 @@
     hooks = {far - 2: middle, far: lambda: (rest,)}
     dattn = ring.scatter(lambda o: block_of(din_part, o), hooks)
     [rest] = together((rest,), (dattn,))
-    own_grads = []
-    for at in range(groups.bit_length() - 1):
-        rest = rest + lax.ppermute(rest, "expert", [(i, i ^ (1 << at)) for i in range(groups)])
-        if at < 3:
-            own_grads.append(make_own(at, (rest,)))
-            [rest] = together((rest,), ())
+    rest = expert_sum(rest, groups)
+    all_hops = rest
+    own_grads = [make_own(which, (rest,)) for which in range(3)]
     rest = dp_sum(rest, n_dp)
     grad_down, grad_gate_w, grad_up_w = own_grads
     in_scale = norm_scale(resid_in)
@@ -998,7 +1029,7 @@
         return matmul_tn(left, dqkv)
 
     reduced = dp_reduce(projection_term, n_dp).astype(BF16)
-    [reduced] = together((reduced,), (dattn,))
+    [reduced] = together((reduced,), (all_hops,))
     reduced = lax.all_to_all(
         reduced.reshape(groups, weight_rows, 3 * own),
         "expert",
@@ -1020,7 +1051,7 @@
         return lax.dynamic_slice(out_grads, ((dp ^ rel) * weight_rows, 0), (weight_rows, width))
 
     grad_out = dp_reduce(out_term, n_dp).astype(BF16)
-    [grad_out] = together((grad_out,), (dattn,))
+    [grad_out] = together((grad_out,), (all_hops,))
     grad_out = lax.ppermute(grad_out, both_axes, [(b, a) for a, b in moves]).astype(F32)
 
     mine = lax.dynamic_slice(

time: 659 us -> 652 us (0.989)
  starting transfers between devices: 126 us -> 107 us
  waiting for transfers between devices: 175 us -> 183 us
    ppermute x24, waiting for transfers between devices: 34.1 us -> 79.4 us  [down(): return lax.ppermute(value, 'expert', self.back)]
    ppermute x10 -> x7, waiting for transfers between devices: 36.7 us -> 2.32 us  [the longest x4 2.05 us: over_cores(): new = [(rel ^ 1, lax.ppermute(part, 'dp', swap)) for rel, part in self.held]]
    ppermute x10 -> x7, starting transfers between devices: 25.7 us -> 11.7 us  [the longest x2 7.55 us: over_y(): lax.ppermute(self.chunk, 'dp', [(i, i ^ 2 * y) for i in range(n_dp)])]
    ppermute x6 -> x9, waiting for transfers between devices: 15.7 us -> 28 us  [expert_sum(): lax.ppermute(value, 'expert', [(i, i ^ step) for i in range(groups)])]
    ppermute x24, starting transfers between devices: 31.1 us -> 20.6 us  [down(): return lax.ppermute(value, 'expert', self.back)]
    ppermute x24, waiting for transfers between devices: 76 us -> 68.3 us  [up(): return lax.ppermute(value, 'expert', self.ahead)]
    ppermute x2, waiting for transfers between devices: 12.2 us -> 5.05 us  [dp_reduce(): lax.ppermute(part, 'dp', [(i, i ^ 2 * y) for i in range(n_dp)]).astype(F32)]
    ppermute x6 -> x9, starting transfers between devices: 14.9 us -> 15.5 us  [expert_sum(): lax.ppermute(value, 'expert', [(i, i ^ step) for i in range(groups)])]
  transfers between devices with their start and end apart: 84 -> 84, of which waited for: 45 -> 41; matrix products, arithmetic and copies ran while one was open for 19% -> 20% of each run, Pallas kernels for 23% -> 23%
where the time goes in v4:
time: 652 us; the launch traced here: 644 us
  Pallas kernels  191 us (29%)
  waiting for transfers between devices  183 us (28%)
  starting transfers between devices  107 us (16%)
  local copies, waits for them, and re-layouts  54.9 us (8%)
  matrix products  42.8 us (7%)
  other arithmetic  40.8 us (6%)
  between operations  24.8 us (4%)
    ppermute x24, waiting for transfers between devices, down(): return lax.ppermute(value, 'expert', self.back)  79.4 us
    ppermute x24, waiting for transfers between devices, up(): return lax.ppermute(value, 'expert', self.ahead)  68.3 us
    pallas_call x9, Pallas kernels, weight_grad(): pl.pallas_call(lambda *refs: weight_grad_kernel(len(adds), *refs), out_sh...  67.8 us
    pallas_call x2, Pallas kernels, expert_call(): pl.pallas_call(lambda *refs: expert_kernel(len(pieces), rows, n_blocks, n...  63.3 us
    ppermute x24, starting transfers between devices, up(): return lax.ppermute(value, 'expert', self.ahead)  33.7 us
    ppermute x9, waiting for transfers between devices, expert_sum(): lax.ppermute(value, 'expert', [(i, i ^ step) for i in range(groups)])  28 us
    dot_general x5, matrix products, matmul(): return jnp.dot(left, right, preferred_element_type=F32)  21.4 us
    ppermute x24, starting transfers between devices, down(): return lax.ppermute(value, 'expert', self.back)  20.6 us
  transfers between devices with their start and end apart: 84, of which 41 were waited for; matrix products, arithmetic and copies ran while one was open for 20% of the time, Pallas kernels for 23%

profile of v4, /device:TPU:0, one launch (start us, length us, event | category | flops | bytes accessed | tf_op | source)
XLA Modules:
  0.0 643.9 jit_solution(14955210743045647469)
XLA Ops:
  7.2 3.1 collective-permute-start
  16.5 6.3 all-to-all-start
  22.8 3.6 collective-permute-start.9
  39.5 3.2 stack.27.refs_0_
  44.7 2.5 broadcast.211.clone
  48.9 3.1 collective-permute-done.2
  52.0 2.7 collective-permute-start.4
  54.7 4.3 collective-permute-done.3
  61.4 7.0 %collective-permute-start.8 = (bf16[512,896]{1,0:T(8,128)(2,1)S(1)}, bf16[512,896]{1,0:T(8,128)(2,1)S(1)}, u32[]{:S(2)}, u32[]{:S(2)}) collective-permute-start(bf16[512,896]{1,0:T(8,128)(2,1)S(1)} %bitcast.102), channel_id=1, source_target_pairs={{0,16},{8,24},{16,0},{24,8},{1,17},{9,25},{17,1},{25,9},{2,18},{10... | collective-permute-start | bytes 2752520 | tf_op jit(solution)/shard_map/ppermute | solution.py:132
  72.1 7.0 %collective-permute-done.5 = bf16[128,2048]{1,0:T(8,128)(2,1)S(1)} collective-permute-done((bf16[128,2048]{1,0:T(8,128)(2,1)}, bf16[128,2048]{1,0:T(8,128)(2,1)S(1)}, u32[]{:S(2)}, u32[]{:S(2)}) %collective-permute-start.5) | collective-permute-done | bytes 524320 | tf_op jit(solution)/shard_map/ppermute | solution.py:49
  83.2 2.9 collective-permute-done.6
  97.1 8.9 %shard_map.306 = (bf16[1024,2048]{1,0:T(8,128)(2,1)}, f32[1024,768]{1,0:T(8,128)}, f32[8,1024]{1,0:T(8,128)}) custom-call(bf16[1024,2048]{1,0:T(8,128)(2,1)} %constant_dynamic-update-slice_fusion.18.tokens_ref, f32[1,2048]{1,0:T(1,128)} %copy.86.gain_ref, bf16[2048,896]{1,0:T(8,128)(2,1)} %copy-done.5), custom_call_target="tpu_custom_call" | custom-call | flops 3221225472 | bytes 16777216 | tf_op jit(solution)/shard_map/pallas_call | solution.py:238
  105.9 3.6 collective-permute-start.12
  115.2 3.8 collective-permute-done.13
  120.8 3.0 collective-permute-done.14
  124.5 9.6 %shard_map.307 = (bf16[1024,256]{1,0:T(8,128)(2,1)}, bf16[1024,256]{1,0:T(8,128)(2,1)}, bf16[1024,256]{1,0:T(8,128)(2,1)}, bf16[1024,256]{1,0:T(8,128)(2,1)}) custom-call(s32[1]{0:T(128)} %dynamic_slice.85.length_ref, f32[1024,768]{1,0:T(8,128)} %get-tuple-element.91.qkv_ref, f32[8,1024]{1,0:T(8,128)} %add.353.squares_ref, f32[2,256]{1,0:T(2,128)} %copy.87.gain_ref, ...), custom_call_target="tpu_custom_call" | custom-call | flops 1073741824 | bytes 5242880 | tf_op jit(solution)/shard_map/pallas_call | solution.py:359
  138.8 17.1 %collective-permute-done.21 = bf16[64,2048]{1,0:T(8,128)(2,1)S(1)} collective-permute-done((bf16[64,2048]{1,0:T(8,128)(2,1)S(1)}, bf16[64,2048]{1,0:T(8,128)(2,1)S(1)}, u32[]{:S(2)}, u32[]{:S(2)}) %collective-permute-start.21) | collective-permute-done | bytes 262176 | tf_op jit(solution)/shard_map/ppermute | solution.py:49
  162.2 16.2 %collective-permute-done.22 = bf16[128,2048]{1,0:T(8,128)(2,1)} collective-permute-done((bf16[128,2048]{1,0:T(8,128)(2,1)S(1)}, bf16[128,2048]{1,0:T(8,128)(2,1)}, u32[]{:S(2)}, u32[]{:S(2)}) %collective-permute-start.22) | collective-permute-done | bytes 524320 | tf_op jit(solution)/shard_map/ppermute | solution.py:49
  181.0 2.5 collective-permute-start.20
  183.9 9.4 %fusion.6.refs_15_.refs_16_.refs_17_.refs_18_.refs_19_ = bf16[1024,1024]{1,0:T(8,128)(2,1)} fusion(bf16[1024,2048]{1,0:T(8,128)(2,1)} %all-gather.2.cloned.1.call-done.refs_0_, bf16[2,2048,1024]{2,1,0:T(8,128)(2,1)} %refs_3_.1), kind=kOutput, calls=%fused_computation.10 | convolution fusion | flops 4296015872 | bytes 10485760 | tf_op jit(solution)/shard_map/dot_general | solution.py:170
  194.5 2.7 collective-permute-done.23
  201.0 7.9 %fusion.9.refs_19_.refs_20_.refs_21_.refs_22_.refs_23_ = bf16[1024,1024]{1,0:T(8,128)(2,1)} fusion(bf16[1024,2048]{1,0:T(8,128)(2,1)S(1)} %copy-done.3, bf16[2,2048,1024]{2,1,0:T(8,128)(2,1)} %refs_3_.1), kind=kOutput, calls=%fused_computation.11 | convolution fusion | flops 4296015872 | bytes 10485760 | tf_op jit(solution)/shard_map/dot_general | solution.py:170
  215.0 9.9 %collective-permute-done.28.refs_3_ = bf16[128,2048]{1,0:T(8,128)(2,1)} collective-permute-done((bf16[128,2048]{1,0:T(8,128)(2,1)S(1)}, bf16[128,2048]{1,0:T(8,128)(2,1)}, u32[]{:S(2)}, u32[]{:S(2)}) %collective-permute-start.28) | collective-permute-done | bytes 524320 | tf_op jit(solution)/shard_map/ppermute | solution.py:46
  228.0 8.9 %collective-permute-done.29.refs_5_ = bf16[128,2048]{1,0:T(8,128)(2,1)} collective-permute-done((bf16[128,2048]{1,0:T(8,128)(2,1)}, bf16[128,2048]{1,0:T(8,128)(2,1)}, u32[]{:S(2)}, u32[]{:S(2)}) %collective-permute-start.29) | collective-permute-done | bytes 524320 | tf_op jit(solution)/shard_map/ppermute | solution.py:46
  239.0 31.6 %shard_map.308 = (bf16[1024,2048]{1,0:T(8,128)(2,1)}, f32[1024,128]{1,0:T(8,128)}, bf16[1024,2048]{1,0:T(8,128)(2,1)}, bf16[1024,2048]{1,0:T(8,128)(2,1)}, bf16[...) custom-call(s32[5]{0:T(128)} %stack.27.refs_0_, ...), custom_call_target="tpu_custom_call" | custom-call | flops 17179869184 | bytes 44040192 | tf_op jit(solution)/shard_map/pallas_call | solution.py:589
  273.0 4.1 collective-permute-done.32.refs_5_
  279.5 31.7 %shard_map.309 = (bf16[1024,2048]{1,0:T(8,128)(2,1)}, f32[1024,128]{1,0:T(8,128)}, bf16[1024,2048]{1,0:T(8,128)(2,1)}, bf16[1024,2048]{1,0:T(8,128)(2,1)}, bf16[...) custom-call(s32[5]{0:T(128)} %pad_add_fusion.refs_0_, ...), custom_call_target="tpu_custom_call", output_to_operand_aliasing={{0}: (24, {}), {1}: (25, {}), {2}: (26, {}), {3}: (27, {}),... | custom-call | flops 17179869184 | bytes 44040192 | tf_op jit(solution)/shard_map/pallas_call | solution.py:589
  311.3 8.6 %shard_map.311 = bf16[2048,1024]{1,0:T(8,128)(2,1)} custom-call(bf16[1024,2048]{1,0:T(8,128)(2,1)} %all-gather.2.cloned.1.call-done.refs_0_, bf16[1024,2048]{1,0:T(8,128)(2,1)} %get-tuple-element.109.refs_2_.refs_1_), custom_call_target="tpu_custom_call" | custom-call | flops 4294967296 | bytes 8388608 | tf_op jit(solution)/shard_map/pallas_call | solution.py:713
  322.0 8.5 %shard_map.312 = bf16[2048,1024]{1,0:T(8,128)(2,1)} custom-call(bf16[1024,2048]{1,0:T(8,128)(2,1)} %get-tuple-element.155.refs_0_, bf16[1024,2048]{1,0:T(8,128)(2,1)} %get-tuple-element.118.refs_1_), custom_call_target="tpu_custom_call" | custom-call | flops 4294967296 | bytes 8388608 | tf_op jit(solution)/shard_map/pallas_call | solution.py:713
  335.1 8.6 %shard_map.314 = bf16[2048,1024]{1,0:T(8,128)(2,1)} custom-call(bf16[1024,2048]{1,0:T(8,128)(2,1)} %get-tuple-element.155.refs_0_, bf16[1024,2048]{1,0:T(8,128)(2,1)} %get-tuple-element.124.refs_1_), custom_call_target="tpu_custom_call" | custom-call | flops 4294967296 | bytes 8388608 | tf_op jit(solution)/shard_map/pallas_call | solution.py:713
  343.7 2.4 collective-permute-done.35
  346.0 2.4 collective-permute-done.37
  358.0 3.3 all-to-all-start.1
  361.4 6.5 %shard_map.313 = bf16[2048,512]{1,0:T(8,128)(2,1)} custom-call(bf16[1024,2048]{1,0:T(8,128)(2,1)} %all-gather.2.cloned.1.call-done.refs_0_, bf16[1024,2048]{1,0:T(8,128)(2,1)} %get-tuple-element.109.refs_2_.refs_1_, bf16[2048,1024]{1,0:T(8,128)(2,1)} %collective-permute-done.40.refs_2_), custom_call_target="tpu_custom_call" | custom-call | flops 2147483648 | bytes 6291456 | tf_op jit(solution)/shard_map/pallas_call | solution.py:713
  374.0 6.5 %shard_map.315 = bf16[2048,512]{1,0:T(8,128)(2,1)} custom-call(bf16[1024,2048]{1,0:T(8,128)(2,1)} %get-tuple-element.155.refs_0_, bf16[1024,2048]{1,0:T(8,128)(2,1)} %get-tuple-element.118.refs_1_, bf16[2048,1024]{1,0:T(8,128)(2,1)} %collective-permute-done.43.refs_2_), custom_call_target="tpu_custom_call" | custom-call | flops 2147483648 | bytes 6291456 | tf_op jit(solution)/shard_map/pallas_call | solution.py:713
  380.5 2.4 collective-permute-done.41
  382.9 3.3 collective-permute-done.42
  386.2 2.9 multiply_reduce_fusion
  389.1 2.5 broadcast.211
  395.1 6.4 shard_map.316
  407.6 15.4 %shard_map.310 = bf16[1024,2048]{1,0:T(8,128)(2,1)} custom-call(s32[1]{0:T(128)} %constant.95.clone.1.refs_0_, s32[4]{0:T(128)} %gather_fusion.1, bf16[1024,2048]{1,0:T(8,128)(2,1)} %get-tuple-element.109.refs_2_.refs_1_, bf16[2,2048,1024]{2,1,0:T(8,128)(2,1)} %refs_3_.1), custom_call_target="tpu_custom_call" | custom-call | flops 8589934592 | bytes 8388608 | tf_op jit(solution)/shard_map/pallas_call | solution.py:664
  432.6 4.4 collective-permute-done.49
  446.2 4.3 convolution_convert_fusion.4.do_ref
  452.0 16.3 %shard_map.317 = (f32[1024,256]{1,0:T(8,128)}, f32[1024,256]{1,0:T(8,128)}, bf16[1024,256]{1,0:T(8,128)(2,1)}, f32[8,1024]{1,0:T(8,128)}, f32[2,256]{1,0:T(2,128)}) custom-call(s32[1]{0:T(128)} %dynamic_slice.85.length_ref, f32[1024,768]{1,0:T(8,128)} %get-tuple-element.91.qkv_ref, f32[8,1024]{1,0:T(8,128)} %add.353.squares_ref, f32[2,256]{1,0:T(2,128)} %copy.87.gain_ref, ...), custom_call_target="tpu_custom_call" | custom-call | flops 2684354560 | bytes 10485760 | tf_op jit(solution)/shard_map/pallas_call | solution.py:372
  469.1 3.5 fusion.51
  476.1 2.6 collective-permute-done.55
  480.0 5.6 collective-permute-done.56
  486.2 9.6 %shard_map.318 = (bf16[1024,768]{1,0:T(8,128)(2,1)}, bf16[1024,2048]{1,0:T(8,128)(2,1)}) custom-call(f32[1024,256]{1,0:T(8,128)} %get-tuple-element.139.dq_ref, f32[1024,256]{1,0:T(8,128)} %get-tuple-element.140.dk_ref, bf16[1024,256]{1,0:T(8,128)(2,1)} %get-tuple-element.141.dv_ref, f32[1024,768]{1,0:T(8,128)} %get-tuple-element.91.qkv_ref, ...), custom_call_target="tpu_custom_call" | custom-call | flops 3221225472 | bytes 8388608 | tf_op jit(solution)/shard_map/pallas_call | solution.py:411
  499.4 2.9 convolution_convert_fusion.2
  503.8 5.4 collective-permute-done.57
  513.6 8.7 %collective-permute-done.58 = bf16[128,2048]{1,0:T(8,128)(2,1)S(1)} collective-permute-done((bf16[128,2048]{1,0:T(8,128)(2,1)S(1)}, bf16[128,2048]{1,0:T(8,128)(2,1)S(1)}, u32[]{:S(2)}, u32[]{:S(2)}) %collective-permute-start.58) | collective-permute-done | bytes 524320 | tf_op jit(solution)/shard_map/ppermute | solution.py:46
  525.9 5.0 collective-permute-done.74
  535.8 19.0 %collective-permute-done.64 = bf16[128,2048]{1,0:T(8,128)(2,1)S(1)} collective-permute-done((bf16[128,2048]{1,0:T(8,128)(2,1)S(1)}, bf16[128,2048]{1,0:T(8,128)(2,1)S(1)}, u32[]{:S(2)}, u32[]{:S(2)}) %collective-permute-start.64) | collective-permute-done | bytes 524320 | tf_op jit(solution)/shard_map/ppermute | solution.py:49
  558.0 2.7 fusion.14
  562.1 7.6 %collective-permute-done.63 = bf16[128,2048]{1,0:T(8,128)(2,1)S(1)} collective-permute-done((bf16[128,2048]{1,0:T(8,128)(2,1)}, bf16[128,2048]{1,0:T(8,128)(2,1)S(1)}, u32[]{:S(2)}, u32[]{:S(2)}) %collective-permute-start.63) | collective-permute-done | bytes 524320 | tf_op jit(solution)/shard_map/ppermute | solution.py:46
  572.8 3.7 add_convert_fusion
  577.8 4.8 collective-permute-done.70
  582.7 3.8 collective-permute-start.71
  586.5 6.9 %collective-permute-done.71 = f32[20,2048]{1,0:T(8,128)S(1)} collective-permute-done((f32[20,2048]{1,0:T(8,128)S(1)}, f32[20,2048]{1,0:T(8,128)S(1)}, u32[]{:S(2)}, u32[]{:S(2)}) %collective-permute-start.71) | collective-permute-done | bytes 163872 | tf_op jit(solution)/shard_map/ppermute | solution.py:112
  594.1 5.0 all-to-all-start.2
  601.8 7.5 %shard_map.319 = f32[2,2048,256]{2,1,0:T(8,128)} custom-call(bf16[1024,2048]{1,0:T(8,128)(2,1)} %get-tuple-element.155.refs_0_, bf16[1024,2048]{1,0:T(8,128)(2,1)} %get-tuple-element.118.refs_1_, bf16[2048,1024]{1,0:T(8,128)(2,1)} %collective-permute-done.43.refs_2_, bf16[2048,512]{1,0:T(8,128)(2,1)} %copy-done.11), custom_call_target="tpu_custom_call" | custom-call | flops 2147483648 | bytes 6291456 | tf_op jit(solution)/shard_map/pallas_call | solution.py:713
  609.4 7.6 %shard_map.320 = f32[2,2048,256]{2,1,0:T(8,128)} custom-call(bf16[1024,2048]{1,0:T(8,128)(2,1)} %get-tuple-element.155.refs_0_, bf16[1024,2048]{1,0:T(8,128)(2,1)} %get-tuple-element.124.refs_1_, bf16[2048,1024]{1,0:T(8,128)(2,1)} %collective-permute-done.46.refs_2_, bf16[2048,512]{1,0:T(8,128)(2,1)} %collective-permute-done.78.refs_3_), custom_call_target="tpu_custom_call" | custom-call | flops 2147483648 | bytes 6291456 | tf_op jit(solution)/shard_map/pallas_call | solution.py:713
  617.0 3.9 collective-permute-start.77
  620.9 7.6 %shard_map.321 = f32[2,2048,256]{2,1,0:T(8,128)} custom-call(bf16[1024,2048]{1,0:T(8,128)(2,1)} %all-gather.2.cloned.1.call-done.refs_0_, bf16[1024,2048]{1,0:T(8,128)(2,1)} %get-tuple-element.109.refs_2_.refs_1_, bf16[2048,1024]{1,0:T(8,128)(2,1)} %collective-permute-done.40.refs_2_, bf16[2048,512]{1,0:T(8,128)(2,1)} %collective-permute-done.53.refs_3_), custom_call_target="tpu_custom_call" | custom-call | flops 2147483648 | bytes 6291456 | tf_op jit(solution)/shard_map/pallas_call | solution.py:713
  (372 shorter events, 174.5 us)
Async XLA Ops:
  7.2 25.0 %collective-permute-start = (bf16[128,2048]{1,0:T(8,128)(2,1)}, bf16[128,2048]{1,0:T(8,128)(2,1)S(1)}, u32[]{:S(2)}, u32[]{:S(2)}) collective-permute-start(bf16[128,2048]{1,0:T(8,128)(2,1)} %param.19), channel_id=1, source_target_pairs={{2,4},{4,6},{6,7},{7,5},{5,3},{3,1},{1,0},{0,2},{10,12},{12,14},{1... | collective-permute-start | bytes 1572872 | tf_op jit(solution)/shard_map/ppermute | solution.py:46
  10.3 23.3 %collective-permute-start.1 = (bf16[128,2048]{1,0:T(8,128)(2,1)}, bf16[128,2048]{1,0:T(8,128)(2,1)S(1)}, u32[]{:S(2)}, u32[]{:S(2)}) collective-permute-start(bf16[128,2048]{1,0:T(8,128)(2,1)} %param.19), channel_id=1, source_target_pairs={{4,2},{6,4},{7,6},{5,7},{3,5},{1,3},{0,1},{2,0},{12,10},{14,12},{1... | collective-permute-start | bytes 1572872 | tf_op jit(solution)/shard_map/ppermute | solution.py:49
  16.5 44.9 %all-to-all-start = ((bf16[8,64,896]{2,1,0:T(8,128)(2,1)}), bf16[8,64,896]{2,1,0:T(8,128)(2,1)S(1)}, u32[]{:S(2)}, u32[]{:S(2)}) async-start(bf16[8,64,896]{2,1,0:T(8,128)(2,1)} %concatenate.34), calls=%async_computation | async-start | bytes 1835008 | tf_op jit(solution)/shard_map/all_to_all | solution.py:800
  22.7 161.2 %all-gather.2.cloned.1.call-start = ((), (), s32[]{:S(2)}) async-start(), calls=%async_computation.4 | async-start | bytes 4718592 | tf_op jit(solution)/shard_map/all_gather | solution.py:822
  22.8 60.4 %collective-permute-start.9 = (bf16[64,2048]{1,0:T(8,128)(2,1)}, bf16[64,2048]{1,0:T(8,128)(2,1)}, u32[]{:S(2)}, u32[]{:S(2)}) collective-permute-start(bf16[64,2048]{1,0:T(8,128)(2,1)} %param.25), channel_id=1, source_target_pairs={{0,0},{1,8},{2,16},{3,24},{4,1},{5,9},{6,17},{7,25},{8,2},{9,10},{... | collective-permute-start | bytes 786440 | tf_op jit(solution)/shard_map/ppermute | solution.py:805
  32.2 19.8 %collective-permute-start.2 = (bf16[128,2048]{1,0:T(8,128)(2,1)S(1)}, bf16[128,2048]{1,0:T(8,128)(2,1)}, u32[]{:S(2)}, u32[]{:S(2)}) collective-permute-start(bf16[128,2048]{1,0:T(8,128)(2,1)S(1)} %collective-permute-done), channel_id=1, source_target_pairs={{2,4},{4,6},{6,7},{7,5},{5,3},{3,1},{1,0},{0,2},{10,12},{12,14},{1... | collective-permute-start | bytes 1572872 | tf_op jit(solution)/shard_map/ppermute | solution.py:46
  33.6 25.5 %collective-permute-start.3 = (bf16[128,2048]{1,0:T(8,128)(2,1)S(1)}, bf16[128,2048]{1,0:T(8,128)(2,1)}, u32[]{:S(2)}, u32[]{:S(2)}) collective-permute-start(bf16[128,2048]{1,0:T(8,128)(2,1)S(1)} %collective-permute-done.1), channel_id=1, source_target_pairs={{4,2},{6,4},{7,6},{5,7},{3,5},{1,3},{0,1},{2,0},{12,10},{14,12},{1... | collective-permute-start | bytes 1572872 | tf_op jit(solution)/shard_map/ppermute | solution.py:49
  52.0 20.1 %collective-permute-start.4 = (bf16[128,2048]{1,0:T(8,128)(2,1)}, bf16[128,2048]{1,0:T(8,128)(2,1)S(1)}, u32[]{:S(2)}, u32[]{:S(2)}) collective-permute-start(bf16[128,2048]{1,0:T(8,128)(2,1)} %collective-permute-done.2), channel_id=1, source_target_pairs={{2,4},{4,6},{6,7},{7,5},{5,3},{3,1},{1,0},{0,2},{10,12},{12,14},{1... | collective-permute-start | bytes 1572872 | tf_op jit(solution)/shard_map/ppermute | solution.py:46
  59.1 20.1 %collective-permute-start.5 = (bf16[128,2048]{1,0:T(8,128)(2,1)}, bf16[128,2048]{1,0:T(8,128)(2,1)S(1)}, u32[]{:S(2)}, u32[]{:S(2)}) collective-permute-start(bf16[128,2048]{1,0:T(8,128)(2,1)} %collective-permute-done.3), channel_id=1, source_target_pairs={{4,2},{6,4},{7,6},{5,7},{3,5},{1,3},{0,1},{2,0},{12,10},{14,12},{1... | collective-permute-start | bytes 1572872 | tf_op jit(solution)/shard_map/ppermute | solution.py:49
  61.4 26.5 %collective-permute-start.8 = (bf16[512,896]{1,0:T(8,128)(2,1)S(1)}, bf16[512,896]{1,0:T(8,128)(2,1)S(1)}, u32[]{:S(2)}, u32[]{:S(2)}) collective-permute-start(bf16[512,896]{1,0:T(8,128)(2,1)S(1)} %bitcast.102), channel_id=1, source_target_pairs={{0,16},{8,24},{16,0},{24,8},{1,17},{9,25},{17,1},{25,9},{2,18},{10... | collective-permute-start | bytes 2752520 | tf_op jit(solution)/shard_map/ppermute | solution.py:132
  110.1 14.3 %collective-permute-start.15 = (bf16[64,2048]{1,0:T(8,128)(2,1)}, bf16[64,2048]{1,0:T(8,128)(2,1)S(1)}, u32[]{:S(2)}, u32[]{:S(2)}) collective-permute-start(bf16[64,2048]{1,0:T(8,128)(2,1)} %collective-permute-done.9), channel_id=1, source_target_pairs={{0,16},{8,24},{16,0},{24,8},{1,17},{9,25},{17,1},{25,9},{2,18},{10... | collective-permute-start | bytes 786440 | tf_op jit(solution)/shard_map/ppermute | solution.py:132
  110.7 23.4 %collective-permute-start.16 = (bf16[64,2048]{1,0:T(8,128)(2,1)}, bf16[64,2048]{1,0:T(8,128)(2,1)S(1)}, u32[]{:S(2)}, u32[]{:S(2)}) collective-permute-start(bf16[64,2048]{1,0:T(8,128)(2,1)} %collective-permute-done.9), channel_id=1, source_target_pairs={{0,8},{8,0},{16,24},{24,16},{1,9},{9,1},{17,25},{25,17},{2,10},{10... | collective-permute-start | bytes 786440 | tf_op jit(solution)/shard_map/ppermute | solution.py:139
  135.4 20.5 %collective-permute-start.21 = (bf16[64,2048]{1,0:T(8,128)(2,1)S(1)}, bf16[64,2048]{1,0:T(8,128)(2,1)S(1)}, u32[]{:S(2)}, u32[]{:S(2)}) collective-permute-start(bf16[64,2048]{1,0:T(8,128)(2,1)S(1)} %get-tuple-element.201), channel_id=1, source_target_pairs={{4,2},{6,4},{7,6},{5,7},{3,5},{1,3},{0,1},{2,0},{12,10},{14,12},{1... | collective-permute-start | bytes 786440 | tf_op jit(solution)/shard_map/ppermute | solution.py:49
  137.1 18.8 %collective-permute-start.18 = (bf16[64,2048]{1,0:T(8,128)(2,1)S(1)}, bf16[64,2048]{1,0:T(8,128)(2,1)S(1)}, u32[]{:S(2)}, u32[]{:S(2)}) collective-permute-start(bf16[64,2048]{1,0:T(8,128)(2,1)S(1)} %get-tuple-element.202), channel_id=1, source_target_pairs={{2,4},{4,6},{6,7},{7,5},{5,3},{3,1},{1,0},{0,2},{10,12},{12,14},{1... | collective-permute-start | bytes 786440 | tf_op jit(solution)/shard_map/ppermute | solution.py:46
  156.1 22.3 %collective-permute-start.22 = (bf16[128,2048]{1,0:T(8,128)(2,1)S(1)}, bf16[128,2048]{1,0:T(8,128)(2,1)}, u32[]{:S(2)}, u32[]{:S(2)}) collective-permute-start(bf16[128,2048]{1,0:T(8,128)(2,1)S(1)} %pad_maximum_fusion.3), channel_id=1, source_target_pairs={{4,2},{6,4},{7,6},{5,7},{3,5},{1,3},{0,1},{2,0},{12,10},{14,12},{1... | collective-permute-start | bytes 1572872 | tf_op jit(solution)/shard_map/ppermute | solution.py:49
  158.6 20.5 %collective-permute-start.19 = (bf16[128,2048]{1,0:T(8,128)(2,1)}, bf16[128,2048]{1,0:T(8,128)(2,1)}, u32[]{:S(2)}, u32[]{:S(2)}) collective-permute-start(bf16[128,2048]{1,0:T(8,128)(2,1)} %pad_maximum_fusion.2), channel_id=1, source_target_pairs={{2,4},{4,6},{6,7},{7,5},{5,3},{3,1},{1,0},{0,2},{10,12},{12,14},{1... | collective-permute-start | bytes 1572872 | tf_op jit(solution)/shard_map/ppermute | solution.py:46
  181.0 13.5 %collective-permute-start.20 = (bf16[128,2048]{1,0:T(8,128)(2,1)S(1)}, bf16[128,2048]{1,0:T(8,128)(2,1)S(1)}, u32[]{:S(2)}, u32[]{:S(2)}) collective-permute-start(bf16[128,2048]{1,0:T(8,128)(2,1)S(1)} %get-tuple-element.184), channel_id=1, source_target_pairs={{2,4},{4,6},{6,7},{7,5},{5,3},{3,1},{1,0},{0,2},{10,12},{12,14},{1... | collective-permute-start | bytes 1572872 | tf_op jit(solution)/shard_map/ppermute | solution.py:46
  183.5 13.7 %collective-permute-start.23 = (bf16[128,2048]{1,0:T(8,128)(2,1)S(1)}, bf16[128,2048]{1,0:T(8,128)(2,1)}, u32[]{:S(2)}, u32[]{:S(2)}) collective-permute-start(bf16[128,2048]{1,0:T(8,128)(2,1)S(1)} %get-tuple-element.183), channel_id=1, source_target_pairs={{4,2},{6,4},{7,6},{5,7},{3,5},{1,3},{0,1},{2,0},{12,10},{14,12},{1... | collective-permute-start | bytes 1572872 | tf_op jit(solution)/shard_map/ppermute | solution.py:49
  198.9 12.3 %collective-permute-start.24 = (bf16[128,2048]{1,0:T(8,128)(2,1)S(1)}, bf16[128,2048]{1,0:T(8,128)(2,1)S(1)}, u32[]{:S(2)}, u32[]{:S(2)}) collective-permute-start(bf16[128,2048]{1,0:T(8,128)(2,1)S(1)} %get-tuple-element.182), channel_id=1, source_target_pairs={{2,4},{4,6},{6,7},{7,5},{5,3},{3,1},{1,0},{0,2},{10,12},{12,14},{1... | collective-permute-start | bytes 1572872 | tf_op jit(solution)/shard_map/ppermute | solution.py:46
  199.3 12.0 %collective-permute-start.25 = (bf16[128,2048]{1,0:T(8,128)(2,1)S(1)}, bf16[128,2048]{1,0:T(8,128)(2,1)S(1)}, u32[]{:S(2)}, u32[]{:S(2)}) collective-permute-start(bf16[128,2048]{1,0:T(8,128)(2,1)S(1)} %get-tuple-element.181), channel_id=1, source_target_pairs={{4,2},{6,4},{7,6},{5,7},{3,5},{1,3},{0,1},{2,0},{12,10},{14,12},{1... | collective-permute-start | bytes 1572872 | tf_op jit(solution)/shard_map/ppermute | solution.py:49
  212.9 11.9 %collective-permute-start.28 = (bf16[128,2048]{1,0:T(8,128)(2,1)S(1)}, bf16[128,2048]{1,0:T(8,128)(2,1)}, u32[]{:S(2)}, u32[]{:S(2)}) collective-permute-start(bf16[128,2048]{1,0:T(8,128)(2,1)S(1)} %multiply_convert_fusion.refs_2_), channel_id=1, source_target_pairs={{2,4},{4,6},{6,7},{7,5},{5,3},{3,1},{1,0},{0,2},{10,12},{12,14},{1... | collective-permute-start | bytes 1572872 | tf_op jit(solution)/shard_map/ppermute | solution.py:46
  214.4 11.9 %collective-permute-start.26 = (bf16[128,2048]{1,0:T(8,128)(2,1)S(1)}, bf16[128,2048]{1,0:T(8,128)(2,1)}, u32[]{:S(2)}, u32[]{:S(2)}) collective-permute-start(bf16[128,2048]{1,0:T(8,128)(2,1)S(1)} %multiply_convert_fusion.refs_2_), channel_id=1, source_target_pairs={{4,2},{6,4},{7,6},{5,7},{3,5},{1,3},{0,1},{2,0},{12,10},{14,12},{1... | collective-permute-start | bytes 1572872 | tf_op jit(solution)/shard_map/ppermute | solution.py:49
  224.8 12.1 %collective-permute-start.29 = (bf16[128,2048]{1,0:T(8,128)(2,1)}, bf16[128,2048]{1,0:T(8,128)(2,1)}, u32[]{:S(2)}, u32[]{:S(2)}) collective-permute-start(bf16[128,2048]{1,0:T(8,128)(2,1)} %collective-permute-done.28.refs_3_), channel_id=1, source_target_pairs={{2,4},{4,6},{6,7},{7,5},{5,3},{3,1},{1,0},{0,2},{10,12},{12,14},{1... | collective-permute-start | bytes 1572872 | tf_op jit(solution)/shard_map/ppermute | solution.py:46
  226.3 12.1 %collective-permute-start.27 = (bf16[128,2048]{1,0:T(8,128)(2,1)}, bf16[128,2048]{1,0:T(8,128)(2,1)}, u32[]{:S(2)}, u32[]{:S(2)}) collective-permute-start(bf16[128,2048]{1,0:T(8,128)(2,1)} %collective-permute-done.26.refs_4_), channel_id=1, source_target_pairs={{4,2},{6,4},{7,6},{5,7},{3,5},{1,3},{0,1},{2,0},{12,10},{14,12},{1... | collective-permute-start | bytes 1572872 | tf_op jit(solution)/shard_map/ppermute | solution.py:49
  236.9 33.7 %collective-permute-start.30 = (bf16[128,2048]{1,0:T(8,128)(2,1)}, bf16[128,2048]{1,0:T(8,128)(2,1)S(1)}, u32[]{:S(2)}, u32[]{:S(2)}) collective-permute-start(bf16[128,2048]{1,0:T(8,128)(2,1)} %collective-permute-done.29.refs_5_), channel_id=1, source_target_pairs={{2,4},{4,6},{6,7},{7,5},{5,3},{3,1},{1,0},{0,2},{10,12},{12,14},{1... | collective-permute-start | bytes 1572872 | tf_op jit(solution)/shard_map/ppermute | solution.py:46
  238.4 32.2 %collective-permute-start.31 = (bf16[128,2048]{1,0:T(8,128)(2,1)}, bf16[128,2048]{1,0:T(8,128)(2,1)S(1)}, u32[]{:S(2)}, u32[]{:S(2)}) collective-permute-start(bf16[128,2048]{1,0:T(8,128)(2,1)} %collective-permute-done.27.refs_2_), channel_id=1, source_target_pairs={{4,2},{6,4},{7,6},{5,7},{3,5},{1,3},{0,1},{2,0},{12,10},{14,12},{1... | collective-permute-start | bytes 1572872 | tf_op jit(solution)/shard_map/ppermute | solution.py:49
  319.8 41.5 %collective-permute-start.40 = (bf16[2048,1024]{1,0:T(8,128)(2,1)}, bf16[2048,1024]{1,0:T(8,128)(2,1)}, u32[]{:S(2)}, u32[]{:S(2)}) collective-permute-start(bf16[2048,1024]{1,0:T(8,128)(2,1)} %shard_map.311), channel_id=1, source_target_pairs={{0,8},{8,0},{16,24},{24,16},{1,9},{9,1},{17,25},{25,17},{2,10},{10... | collective-permute-start | bytes 12582920 | tf_op jit(solution)/shard_map/ppermute | solution.py:905
  319.9 10.6 %collective-permute-start.34 = (bf16[64,2048]{1,0:T(8,128)(2,1)S(1)}, bf16[64,2048]{1,0:T(8,128)(2,1)S(1)}, u32[]{:S(2)}, u32[]{:S(2)}) collective-permute-start(bf16[64,2048]{1,0:T(8,128)(2,1)S(1)} %get-tuple-element.200), channel_id=1, source_target_pairs={{2,4},{4,6},{6,7},{7,5},{5,3},{3,1},{1,0},{0,2},{10,12},{12,14},{1... | collective-permute-start | bytes 786440 | tf_op jit(solution)/shard_map/ppermute | solution.py:46
  321.7 11.4 %collective-permute-start.36 = (bf16[64,2048]{1,0:T(8,128)(2,1)S(1)}, bf16[64,2048]{1,0:T(8,128)(2,1)S(1)}, u32[]{:S(2)}, u32[]{:S(2)}) collective-permute-start(bf16[64,2048]{1,0:T(8,128)(2,1)S(1)} %get-tuple-element.199), channel_id=1, source_target_pairs={{4,2},{6,4},{7,6},{5,7},{3,5},{1,3},{0,1},{2,0},{12,10},{14,12},{1... | collective-permute-start | bytes 786440 | tf_op jit(solution)/shard_map/ppermute | solution.py:49
  330.5 43.5 %collective-permute-start.43 = (bf16[2048,1024]{1,0:T(8,128)(2,1)}, bf16[2048,1024]{1,0:T(8,128)(2,1)}, u32[]{:S(2)}, u32[]{:S(2)}) collective-permute-start(bf16[2048,1024]{1,0:T(8,128)(2,1)} %shard_map.312), channel_id=1, source_target_pairs={{0,8},{8,0},{16,24},{24,16},{1,9},{9,1},{17,25},{25,17},{2,10},{10... | collective-permute-start | bytes 12582920 | tf_op jit(solution)/shard_map/ppermute | solution.py:905
  331.4 14.6 %collective-permute-start.35 = (bf16[128,2048]{1,0:T(8,128)(2,1)}, bf16[128,2048]{1,0:T(8,128)(2,1)}, u32[]{:S(2)}, u32[]{:S(2)}) collective-permute-start(bf16[128,2048]{1,0:T(8,128)(2,1)} %pad_maximum_fusion.4), channel_id=1, source_target_pairs={{2,4},{4,6},{6,7},{7,5},{5,3},{3,1},{1,0},{0,2},{10,12},{12,14},{1... | collective-permute-start | bytes 1572872 | tf_op jit(solution)/shard_map/ppermute | solution.py:46
  334.1 14.4 %collective-permute-start.37 = (bf16[128,2048]{1,0:T(8,128)(2,1)}, bf16[128,2048]{1,0:T(8,128)(2,1)}, u32[]{:S(2)}, u32[]{:S(2)}) collective-permute-start(bf16[128,2048]{1,0:T(8,128)(2,1)} %pad_maximum_fusion.5), channel_id=1, source_target_pairs={{4,2},{6,4},{7,6},{5,7},{3,5},{1,3},{0,1},{2,0},{12,10},{14,12},{1... | collective-permute-start | bytes 1572872 | tf_op jit(solution)/shard_map/ppermute | solution.py:49
  343.7 51.4 %collective-permute-start.46 = (bf16[2048,1024]{1,0:T(8,128)(2,1)}, bf16[2048,1024]{1,0:T(8,128)(2,1)}, u32[]{:S(2)}, u32[]{:S(2)}) collective-permute-start(bf16[2048,1024]{1,0:T(8,128)(2,1)} %shard_map.314), channel_id=1, source_target_pairs={{0,8},{8,0},{16,24},{24,16},{1,9},{9,1},{17,25},{25,17},{2,10},{10... | collective-permute-start | bytes 12582920 | tf_op jit(solution)/shard_map/ppermute | solution.py:905
  350.4 17.5 %collective-permute-start.38 = (bf16[128,2048]{1,0:T(8,128)(2,1)}, bf16[128,2048]{1,0:T(8,128)(2,1)}, u32[]{:S(2)}, u32[]{:S(2)}) collective-permute-start(bf16[128,2048]{1,0:T(8,128)(2,1)} %add_convert_fusion.9), channel_id=1, source_target_pairs={{2,4},{4,6},{6,7},{7,5},{5,3},{3,1},{1,0},{0,2},{10,12},{12,14},{1... | collective-permute-start | bytes 1572872 | tf_op jit(solution)/shard_map/ppermute | solution.py:46
  353.8 14.1 %collective-permute-start.39 = (bf16[128,2048]{1,0:T(8,128)(2,1)}, bf16[128,2048]{1,0:T(8,128)(2,1)}, u32[]{:S(2)}, u32[]{:S(2)}) collective-permute-start(bf16[128,2048]{1,0:T(8,128)(2,1)} %add_convert_fusion.8), channel_id=1, source_target_pairs={{4,2},{6,4},{7,6},{5,7},{3,5},{1,3},{0,1},{2,0},{12,10},{14,12},{1... | collective-permute-start | bytes 1572872 | tf_op jit(solution)/shard_map/ppermute | solution.py:49
  358.0 16.0 %all-to-all-start.1 = ((f32[8,2,128]{2,1,0:T(2,128)}), f32[8,2,128]{2,1,0:T(2,128)S(1)}, u32[]{:S(2)}, u32[]{:S(2)}) async-start(f32[8,2,128]{2,1,0:T(2,128)} %bitcast.28), calls=%async_computation.1 | async-start | bytes 16384 | tf_op jit(solution)/shard_map/all_to_all | solution.py:895
  361.3 196.7 %reduce-scatter.2.cloned.1.call-start = ((), (), s32[]{:S(2)}) async-start(), calls=%async_computation.5 | async-start | bytes 4718592 | tf_op jit(solution)/shard_map/reduce_scatter | solution.py:975
  369.9 13.0 %collective-permute-start.41 = (bf16[128,2048]{1,0:T(8,128)(2,1)}, bf16[128,2048]{1,0:T(8,128)(2,1)}, u32[]{:S(2)}, u32[]{:S(2)}) collective-permute-start(bf16[128,2048]{1,0:T(8,128)(2,1)} %add_convert_fusion.7), channel_id=1, source_target_pairs={{2,4},{4,6},{6,7},{7,5},{5,3},{3,1},{1,0},{0,2},{10,12},{12,14},{1... | collective-permute-start | bytes 1572872 | tf_op jit(solution)/shard_map/ppermute | solution.py:46
  373.8 12.4 %collective-permute-start.42 = (bf16[128,2048]{1,0:T(8,128)(2,1)}, bf16[128,2048]{1,0:T(8,128)(2,1)}, u32[]{:S(2)}, u32[]{:S(2)}) collective-permute-start(bf16[128,2048]{1,0:T(8,128)(2,1)} %add_convert_fusion.6), channel_id=1, source_target_pairs={{4,2},{6,4},{7,6},{5,7},{3,5},{1,3},{0,1},{2,0},{12,10},{14,12},{1... | collective-permute-start | bytes 1572872 | tf_op jit(solution)/shard_map/ppermute | solution.py:49
  393.1 11.3 %collective-permute-start.44 = (bf16[128,2048]{1,0:T(8,128)(2,1)S(1)}, bf16[128,2048]{1,0:T(8,128)(2,1)}, u32[]{:S(2)}, u32[]{:S(2)}) collective-permute-start(bf16[128,2048]{1,0:T(8,128)(2,1)S(1)} %get-tuple-element.167), channel_id=1, source_target_pairs={{2,4},{4,6},{6,7},{7,5},{5,3},{3,1},{1,0},{0,2},{10,12},{12,14},{1... | collective-permute-start | bytes 1572872 | tf_op jit(solution)/shard_map/ppermute | solution.py:46
  394.5 11.0 %collective-permute-start.45 = (bf16[128,2048]{1,0:T(8,128)(2,1)S(1)}, bf16[128,2048]{1,0:T(8,128)(2,1)}, u32[]{:S(2)}, u32[]{:S(2)}) collective-permute-start(bf16[128,2048]{1,0:T(8,128)(2,1)S(1)} %get-tuple-element.167), channel_id=1, source_target_pairs={{4,2},{6,4},{7,6},{5,7},{3,5},{1,3},{0,1},{2,0},{12,10},{14,12},{1... | collective-permute-start | bytes 1572872 | tf_op jit(solution)/shard_map/ppermute | solution.py:49
  401.5 44.7 %collective-permute-start.53 = (bf16[2048,512]{1,0:T(8,128)(2,1)}, bf16[2048,512]{1,0:T(8,128)(2,1)}, u32[]{:S(2)}, u32[]{:S(2)}) collective-permute-start(bf16[2048,512]{1,0:T(8,128)(2,1)} %shard_map.313), channel_id=1, source_target_pairs={{0,16},{8,24},{16,0},{24,8},{1,17},{9,25},{17,1},{25,9},{2,18},{10... | collective-permute-start | bytes 6291464 | tf_op jit(solution)/shard_map/ppermute | solution.py:926
  405.6 19.3 %collective-permute-start.47 = (bf16[128,2048]{1,0:T(8,128)(2,1)}, bf16[128,2048]{1,0:T(8,128)(2,1)}, u32[]{:S(2)}, u32[]{:S(2)}) collective-permute-start(bf16[128,2048]{1,0:T(8,128)(2,1)} %collective-permute-done.44), channel_id=1, source_target_pairs={{2,4},{4,6},{6,7},{7,5},{5,3},{3,1},{1,0},{0,2},{10,12},{12,14},{1... | collective-permute-start | bytes 1572872 | tf_op jit(solution)/shard_map/ppermute | solution.py:46
  407.1 17.7 %collective-permute-start.48 = (bf16[128,2048]{1,0:T(8,128)(2,1)}, bf16[128,2048]{1,0:T(8,128)(2,1)}, u32[]{:S(2)}, u32[]{:S(2)}) collective-permute-start(bf16[128,2048]{1,0:T(8,128)(2,1)} %collective-permute-done.45), channel_id=1, source_target_pairs={{4,2},{6,4},{7,6},{5,7},{3,5},{1,3},{0,1},{2,0},{12,10},{14,12},{1... | collective-permute-start | bytes 1572872 | tf_op jit(solution)/shard_map/ppermute | solution.py:49
  424.8 12.1 %collective-permute-start.49 = (bf16[128,2048]{1,0:T(8,128)(2,1)}, bf16[128,2048]{1,0:T(8,128)(2,1)S(1)}, u32[]{:S(2)}, u32[]{:S(2)}) collective-permute-start(bf16[128,2048]{1,0:T(8,128)(2,1)} %collective-permute-done.47), channel_id=1, source_target_pairs={{2,4},{4,6},{6,7},{7,5},{5,3},{3,1},{1,0},{0,2},{10,12},{12,14},{1... | collective-permute-start | bytes 1572872 | tf_op jit(solution)/shard_map/ppermute | solution.py:46
  426.4 12.2 %collective-permute-start.50 = (bf16[128,2048]{1,0:T(8,128)(2,1)}, bf16[128,2048]{1,0:T(8,128)(2,1)S(1)}, u32[]{:S(2)}, u32[]{:S(2)}) collective-permute-start(bf16[128,2048]{1,0:T(8,128)(2,1)} %collective-permute-done.48), channel_id=1, source_target_pairs={{4,2},{6,4},{7,6},{5,7},{3,5},{1,3},{0,1},{2,0},{12,10},{14,12},{1... | collective-permute-start | bytes 1572872 | tf_op jit(solution)/shard_map/ppermute | solution.py:49
  472.6 50.8 %collective-permute-start.61 = (bf16[2048,512]{1,0:T(8,128)(2,1)S(1)}, bf16[2048,512]{1,0:T(8,128)(2,1)S(1)}, u32[]{:S(2)}, u32[]{:S(2)}) collective-permute-start(bf16[2048,512]{1,0:T(8,128)(2,1)S(1)} %copy-done.10), channel_id=1, source_target_pairs={{0,16},{8,24},{16,0},{24,8},{1,17},{9,25},{17,1},{25,9},{2,18},{10... | collective-permute-start | bytes 6291464 | tf_op jit(solution)/shard_map/ppermute | solution.py:926
  475.5 38.0 %collective-permute-start.73 = (bf16[64,2048]{1,0:T(8,128)(2,1)S(1)}, bf16[64,2048]{1,0:T(8,128)(2,1)S(1)}, u32[]{:S(2)}, u32[]{:S(2)}) collective-permute-start(bf16[64,2048]{1,0:T(8,128)(2,1)S(1)} %get-tuple-element.192), channel_id=1, source_target_pairs={{0,8},{8,0},{16,24},{24,16},{1,9},{9,1},{17,25},{25,17},{2,10},{10... | collective-permute-start | bytes 786440 | tf_op jit(solution)/shard_map/ppermute | solution.py:155
  475.5 48.7 %collective-permute-start.72 = (bf16[64,2048]{1,0:T(8,128)(2,1)}, bf16[64,2048]{1,0:T(8,128)(2,1)S(1)}, u32[]{:S(2)}, u32[]{:S(2)}) collective-permute-start(bf16[64,2048]{1,0:T(8,128)(2,1)} %get-tuple-element.191), channel_id=1, source_target_pairs={{0,8},{8,0},{16,24},{24,16},{1,9},{9,1},{17,25},{25,17},{2,10},{10... | collective-permute-start | bytes 786440 | tf_op jit(solution)/shard_map/ppermute | solution.py:155
  509.4 12.9 %collective-permute-start.58 = (bf16[128,2048]{1,0:T(8,128)(2,1)S(1)}, bf16[128,2048]{1,0:T(8,128)(2,1)S(1)}, u32[]{:S(2)}, u32[]{:S(2)}) collective-permute-start(bf16[128,2048]{1,0:T(8,128)(2,1)S(1)} %pad_maximum_fusion.6), channel_id=1, source_target_pairs={{2,4},{4,6},{6,7},{7,5},{5,3},{3,1},{1,0},{0,2},{10,12},{12,14},{1... | collective-permute-start | bytes 1572872 | tf_op jit(solution)/shard_map/ppermute | solution.py:46
  509.5 12.8 %collective-permute-start.60 = (bf16[128,2048]{1,0:T(8,128)(2,1)S(1)}, bf16[128,2048]{1,0:T(8,128)(2,1)S(1)}, u32[]{:S(2)}, u32[]{:S(2)}) collective-permute-start(bf16[128,2048]{1,0:T(8,128)(2,1)S(1)} %pad_maximum_fusion.7), channel_id=1, source_target_pairs={{4,2},{6,4},{7,6},{5,7},{3,5},{1,3},{0,1},{2,0},{12,10},{14,12},{1... | collective-permute-start | bytes 1572872 | tf_op jit(solution)/shard_map/ppermute | solution.py:49
  513.5 18.3 %collective-permute-start.67 = (bf16[512,768]{1,0:T(8,128)(2,1)S(1)}, bf16[512,768]{1,0:T(8,128)(2,1)S(1)}, u32[]{:S(2)}, u32[]{:S(2)}) collective-permute-start(bf16[512,768]{1,0:T(8,128)(2,1)S(1)} %convolution_convert_fusion.2), channel_id=1, source_target_pairs={{0,8},{8,0},{16,24},{24,16},{1,9},{9,1},{17,25},{25,17},{2,10},{10... | collective-permute-start | bytes 2359304 | tf_op jit(solution)/shard_map/ppermute | solution.py:155
  522.3 50.5 %collective-permute-start.66 = (bf16[512,768]{1,0:T(8,128)(2,1)}, bf16[512,768]{1,0:T(8,128)(2,1)}, u32[]{:S(2)}, u32[]{:S(2)}) collective-permute-start(bf16[512,768]{1,0:T(8,128)(2,1)} %convolution_convert_fusion.3), channel_id=1, source_target_pairs={{0,8},{8,0},{16,24},{24,16},{1,9},{9,1},{17,25},{25,17},{2,10},{10... | collective-permute-start | bytes 2359304 | tf_op jit(solution)/shard_map/ppermute | solution.py:155
  523.9 31.0 %collective-permute-start.64 = (bf16[128,2048]{1,0:T(8,128)(2,1)S(1)}, bf16[128,2048]{1,0:T(8,128)(2,1)S(1)}, u32[]{:S(2)}, u32[]{:S(2)}) collective-permute-start(bf16[128,2048]{1,0:T(8,128)(2,1)S(1)} %get-tuple-element.173), channel_id=1, source_target_pairs={{4,2},{6,4},{7,6},{5,7},{3,5},{1,3},{0,1},{2,0},{12,10},{14,12},{1... | collective-permute-start | bytes 1572872 | tf_op jit(solution)/shard_map/ppermute | solution.py:49
  524.3 30.6 %collective-permute-start.62 = (bf16[128,2048]{1,0:T(8,128)(2,1)S(1)}, bf16[128,2048]{1,0:T(8,128)(2,1)S(1)}, u32[]{:S(2)}, u32[]{:S(2)}) collective-permute-start(bf16[128,2048]{1,0:T(8,128)(2,1)S(1)} %get-tuple-element.174), channel_id=1, source_target_pairs={{2,4},{4,6},{6,7},{7,5},{5,3},{3,1},{1,0},{0,2},{10,12},{12,14},{1... | collective-permute-start | bytes 1572872 | tf_op jit(solution)/shard_map/ppermute | solution.py:46
  533.7 39.0 %collective-permute-start.68 = (bf16[512,768]{1,0:T(8,128)(2,1)}, bf16[512,768]{1,0:T(8,128)(2,1)}, u32[]{:S(2)}, u32[]{:S(2)}) collective-permute-start(bf16[512,768]{1,0:T(8,128)(2,1)} %add_convert_fusion.1), channel_id=1, source_target_pairs={{0,16},{8,24},{16,0},{24,8},{1,17},{9,25},{17,1},{25,9},{2,18},{10... | collective-permute-start | bytes 2359304 | tf_op jit(solution)/shard_map/ppermute | solution.py:159
  534.9 74.4 %collective-permute-start.78 = (bf16[2048,512]{1,0:T(8,128)(2,1)}, bf16[2048,512]{1,0:T(8,128)(2,1)}, u32[]{:S(2)}, u32[]{:S(2)}) collective-permute-start(bf16[2048,512]{1,0:T(8,128)(2,1)} %shard_map.316), channel_id=1, source_target_pairs={{0,16},{8,24},{16,0},{24,8},{1,17},{9,25},{17,1},{25,9},{2,18},{10... | collective-permute-start | bytes 6291464 | tf_op jit(solution)/shard_map/ppermute | solution.py:926
  556.0 13.7 %collective-permute-start.63 = (bf16[128,2048]{1,0:T(8,128)(2,1)}, bf16[128,2048]{1,0:T(8,128)(2,1)S(1)}, u32[]{:S(2)}, u32[]{:S(2)}) collective-permute-start(bf16[128,2048]{1,0:T(8,128)(2,1)} %get-tuple-element.172), channel_id=1, source_target_pairs={{2,4},{4,6},{6,7},{7,5},{5,3},{3,1},{1,0},{0,2},{10,12},{12,14},{1... | collective-permute-start | bytes 1572872 | tf_op jit(solution)/shard_map/ppermute | solution.py:46
  556.0 13.7 %collective-permute-start.65 = (bf16[128,2048]{1,0:T(8,128)(2,1)S(1)}, bf16[128,2048]{1,0:T(8,128)(2,1)S(1)}, u32[]{:S(2)}, u32[]{:S(2)}) collective-permute-start(bf16[128,2048]{1,0:T(8,128)(2,1)S(1)} %get-tuple-element.171), channel_id=1, source_target_pairs={{4,2},{6,4},{7,6},{5,7},{3,5},{1,3},{0,1},{2,0},{12,10},{14,12},{1... | collective-permute-start | bytes 1572872 | tf_op jit(solution)/shard_map/ppermute | solution.py:49
  582.7 10.7 %collective-permute-start.71 = (f32[20,2048]{1,0:T(8,128)S(1)}, f32[20,2048]{1,0:T(8,128)S(1)}, u32[]{:S(2)}, u32[]{:S(2)}) collective-permute-start(f32[20,2048]{1,0:T(8,128)S(1)} %add.400), channel_id=1, source_target_pairs={{0,4},{1,5},{2,6},{3,7},{4,0},{5,1},{6,2},{7,3},{8,12},{9,13},{10,... | collective-permute-start | bytes 491528 | tf_op jit(solution)/shard_map/ppermute | solution.py:112
  594.1 38.6 %all-to-all-start.2 = ((bf16[8,64,768]{2,1,0:T(8,128)(2,1)}), bf16[8,64,768]{2,1,0:T(8,128)(2,1)S(1)}, u32[]{:S(2)}, u32[]{:S(2)}) async-start(bf16[8,64,768]{2,1,0:T(8,128)(2,1)} %bitcast.116), calls=%async_computation.3 | async-start | bytes 1572864 | tf_op jit(solution)/shard_map/all_to_all | solution.py:1033
  600.2 16.7 %collective-permute-start.76 = (f32[20,2048]{1,0:T(8,128)}, f32[20,2048]{1,0:T(8,128)S(1)}, u32[]{:S(2)}, u32[]{:S(2)}) collective-permute-start(f32[20,2048]{1,0:T(8,128)} %add.401), channel_id=1, source_target_pairs={{0,8},{8,0},{16,24},{24,16},{1,9},{9,1},{17,25},{25,17},{2,10},{10... | collective-permute-start | bytes 491528 | tf_op jit(solution)/shard_map/ppermute | solution.py:120
  600.2 28.3 %collective-permute-start.75 = (bf16[64,2048]{1,0:T(8,128)(2,1)}, bf16[64,2048]{1,0:T(8,128)(2,1)S(1)}, u32[]{:S(2)}, u32[]{:S(2)}) collective-permute-start(bf16[64,2048]{1,0:T(8,128)(2,1)} %add_convert_fusion.14), channel_id=1, source_target_pairs={{0,0},{8,1},{16,2},{24,3},{1,4},{9,5},{17,6},{25,7},{2,8},{10,9},{... | collective-permute-start | bytes 786440 | tf_op jit(solution)/shard_map/ppermute | solution.py:1055
  617.0 12.3 %collective-permute-start.77 = (f32[20,2048]{1,0:T(8,128)S(1)}, f32[20,2048]{1,0:T(8,128)S(1)}, u32[]{:S(2)}, u32[]{:S(2)}) collective-permute-start(f32[20,2048]{1,0:T(8,128)S(1)} %add.407), channel_id=1, source_target_pairs={{0,16},{8,24},{16,0},{24,8},{1,17},{9,25},{17,1},{25,9},{2,18},{10... | collective-permute-start | bytes 491528 | tf_op jit(solution)/shard_map/ppermute | solution.py:120
  (68 other events, 695.4 us)
Sparse Core Ops, SparseCore 0:
  89.4 87.3 all-gather.1
  450.6 103.9 reduce-scatter.1

commit v5 on v4

--- a/solution.py
+++ b/solution.py
@@ -1006,12 +1006,18 @@
         jnp.where(lane == 1, jnp.sum(used * moe_rows * moe_rows), 0.0),
     )
     rest = jnp.concatenate([spread_gains, grad_gain_ffn, sums, grad_router.T], axis=0)
-    hooks = {far - 2: middle, far: lambda: (rest,)}
+    own_grads = []
+
+    def first_own():
+        own_grads.append(make_own(0, second))
+        return tuple(own_grads)
+
+    hooks = {far - 3: middle, far - 1: first_own, far: lambda: (rest,)}
     dattn = ring.scatter(lambda o: block_of(din_part, o), hooks)
     [rest] = together((rest,), (dattn,))
     rest = expert_sum(rest, groups)
     all_hops = rest
-    own_grads = [make_own(which, (rest,)) for which in range(3)]
+    own_grads += [make_own(which, (rest,)) for which in (1, 2)]
     rest = dp_sum(rest, n_dp)
     grad_down, grad_gate_w, grad_up_w = own_grads
     in_scale = norm_scale(resid_in)

time: 652 us -> 651 us (level)
  waiting for transfers between devices: 183 us -> 173 us
  transfers between devices with their start and end apart: 84 -> 84, of which waited for: 41 -> 41; matrix products, arithmetic and copies ran while one was open for 20% -> 20% of each run, Pallas kernels for 23% -> 24%
where the time goes in v5:
time: 651 us; the launch traced here: 640 us
  Pallas kernels  191 us (29%)
  waiting for transfers between devices  173 us (27%)
  starting transfers between devices  109 us (17%)
  local copies, waits for them, and re-layouts  54.8 us (8%)
  other arithmetic  45.1 us (7%)
  matrix products  42.9 us (7%)
  between operations  24.8 us (4%)
    ppermute x24, waiting for transfers between devices, down(): return lax.ppermute(value, 'expert', self.back)  75 us
    pallas_call x9, Pallas kernels, weight_grad(): pl.pallas_call(lambda *refs: weight_grad_kernel(len(adds), *refs), out_sh...  67.6 us
    pallas_call x2, Pallas kernels, expert_call(): pl.pallas_call(lambda *refs: expert_kernel(len(pieces), rows, n_blocks, n...  63.3 us
    ppermute x24, waiting for transfers between devices, up(): return lax.ppermute(value, 'expert', self.ahead)  63.1 us
    ppermute x24, starting transfers between devices, up(): return lax.ppermute(value, 'expert', self.ahead)  34.6 us
    ppermute x9, waiting for transfers between devices, expert_sum(): lax.ppermute(value, 'expert', [(i, i ^ step) for i in range(groups)])  27.3 us
    dot_general x5, matrix products, matmul(): return jnp.dot(left, right, preferred_element_type=F32)  21.5 us
    ppermute x24, starting transfers between devices, down(): return lax.ppermute(value, 'expert', self.back)  20.3 us
  transfers between devices with their start and end apart: 84, of which 41 were waited for; matrix products, arithmetic and copies ran while one was open for 20% of the time, Pallas kernels for 24%

profile of v5, /device:TPU:0, one launch (start us, length us, event | category | flops | bytes accessed | tf_op | source)
XLA Modules:
  0.0 639.7 jit_solution(10108888877131730983)
XLA Ops:
  7.2 3.1 collective-permute-start
  16.5 6.3 all-to-all-start
  22.8 3.6 collective-permute-start.9
  39.5 3.2 stack.27.refs_0_
  44.7 2.5 broadcast.211.clone
  48.9 3.1 collective-permute-done.2
  52.0 2.7 collective-permute-start.4
  54.7 4.3 collective-permute-done.3
  61.4 7.0 %collective-permute-start.8 = (bf16[512,896]{1,0:T(8,128)(2,1)S(1)}, bf16[512,896]{1,0:T(8,128)(2,1)S(1)}, u32[]{:S(2)}, u32[]{:S(2)}) collective-permute-start(bf16[512,896]{1,0:T(8,128)(2,1)S(1)} %bitcast.102), channel_id=1, source_target_pairs={{0,16},{8,24},{16,0},{24,8},{1,17},{9,25},{17,1},{25,9},{2,18},{10... | collective-permute-start | bytes 2752520 | tf_op jit(solution)/shard_map/ppermute | solution.py:132
  72.1 7.0 %collective-permute-done.5 = bf16[128,2048]{1,0:T(8,128)(2,1)S(1)} collective-permute-done((bf16[128,2048]{1,0:T(8,128)(2,1)}, bf16[128,2048]{1,0:T(8,128)(2,1)S(1)}, u32[]{:S(2)}, u32[]{:S(2)}) %collective-permute-start.5) | collective-permute-done | bytes 524320 | tf_op jit(solution)/shard_map/ppermute | solution.py:49
  83.2 2.9 collective-permute-done.6
  97.1 8.8 %shard_map.306 = (bf16[1024,2048]{1,0:T(8,128)(2,1)}, f32[1024,768]{1,0:T(8,128)}, f32[8,1024]{1,0:T(8,128)}) custom-call(bf16[1024,2048]{1,0:T(8,128)(2,1)} %constant_dynamic-update-slice_fusion.18.tokens_ref, f32[1,2048]{1,0:T(1,128)} %copy.86.gain_ref, bf16[2048,896]{1,0:T(8,128)(2,1)} %copy-done.5), custom_call_target="tpu_custom_call" | custom-call | flops 3221225472 | bytes 16777216 | tf_op jit(solution)/shard_map/pallas_call | solution.py:238
  105.9 3.6 collective-permute-start.12
  115.1 3.8 collective-permute-done.13
  120.7 3.1 collective-permute-done.14
  124.4 9.6 %shard_map.307 = (bf16[1024,256]{1,0:T(8,128)(2,1)}, bf16[1024,256]{1,0:T(8,128)(2,1)}, bf16[1024,256]{1,0:T(8,128)(2,1)}, bf16[1024,256]{1,0:T(8,128)(2,1)}) custom-call(s32[1]{0:T(128)} %dynamic_slice.85.length_ref, f32[1024,768]{1,0:T(8,128)} %get-tuple-element.93.qkv_ref, f32[8,1024]{1,0:T(8,128)} %add.353.squares_ref, f32[2,256]{1,0:T(2,128)} %copy.87.gain_ref, ...), custom_call_target="tpu_custom_call" | custom-call | flops 1073741824 | bytes 5242880 | tf_op jit(solution)/shard_map/pallas_call | solution.py:359
  138.8 17.1 %collective-permute-done.21 = bf16[64,2048]{1,0:T(8,128)(2,1)S(1)} collective-permute-done((bf16[64,2048]{1,0:T(8,128)(2,1)S(1)}, bf16[64,2048]{1,0:T(8,128)(2,1)S(1)}, u32[]{:S(2)}, u32[]{:S(2)}) %collective-permute-start.21) | collective-permute-done | bytes 262176 | tf_op jit(solution)/shard_map/ppermute | solution.py:49
  162.2 16.2 %collective-permute-done.22 = bf16[128,2048]{1,0:T(8,128)(2,1)} collective-permute-done((bf16[128,2048]{1,0:T(8,128)(2,1)S(1)}, bf16[128,2048]{1,0:T(8,128)(2,1)}, u32[]{:S(2)}, u32[]{:S(2)}) %collective-permute-start.22) | collective-permute-done | bytes 524320 | tf_op jit(solution)/shard_map/ppermute | solution.py:49
  181.0 2.5 collective-permute-start.20
  184.0 9.4 %fusion.6.refs_15_.refs_16_.refs_17_.refs_18_.refs_19_ = bf16[1024,1024]{1,0:T(8,128)(2,1)} fusion(bf16[1024,2048]{1,0:T(8,128)(2,1)} %all-gather.2.cloned.1.call-done.refs_0_, bf16[2,2048,1024]{2,1,0:T(8,128)(2,1)} %refs_3_.1), kind=kOutput, calls=%fused_computation.10 | convolution fusion | flops 4296015872 | bytes 10485760 | tf_op jit(solution)/shard_map/dot_general | solution.py:170
  194.5 2.7 collective-permute-done.23
  201.0 7.9 %fusion.9.refs_19_.refs_20_.refs_21_.refs_22_.refs_23_ = bf16[1024,1024]{1,0:T(8,128)(2,1)} fusion(bf16[1024,2048]{1,0:T(8,128)(2,1)S(1)} %copy-done.3, bf16[2,2048,1024]{2,1,0:T(8,128)(2,1)} %refs_3_.1), kind=kOutput, calls=%fused_computation.11 | convolution fusion | flops 4296015872 | bytes 10485760 | tf_op jit(solution)/shard_map/dot_general | solution.py:170
  215.0 9.9 %collective-permute-done.28.refs_3_ = bf16[128,2048]{1,0:T(8,128)(2,1)} collective-permute-done((bf16[128,2048]{1,0:T(8,128)(2,1)S(1)}, bf16[128,2048]{1,0:T(8,128)(2,1)}, u32[]{:S(2)}, u32[]{:S(2)}) %collective-permute-start.28) | collective-permute-done | bytes 524320 | tf_op jit(solution)/shard_map/ppermute | solution.py:46
  228.1 8.9 %collective-permute-done.29.refs_5_ = bf16[128,2048]{1,0:T(8,128)(2,1)} collective-permute-done((bf16[128,2048]{1,0:T(8,128)(2,1)}, bf16[128,2048]{1,0:T(8,128)(2,1)}, u32[]{:S(2)}, u32[]{:S(2)}) %collective-permute-start.29) | collective-permute-done | bytes 524320 | tf_op jit(solution)/shard_map/ppermute | solution.py:46
  239.0 31.6 %shard_map.308 = (bf16[1024,2048]{1,0:T(8,128)(2,1)}, f32[1024,128]{1,0:T(8,128)}, bf16[1024,2048]{1,0:T(8,128)(2,1)}, bf16[1024,2048]{1,0:T(8,128)(2,1)}, bf16[...) custom-call(s32[5]{0:T(128)} %stack.27.refs_0_, ...), custom_call_target="tpu_custom_call" | custom-call | flops 17179869184 | bytes 44040192 | tf_op jit(solution)/shard_map/pallas_call | solution.py:589
  273.0 4.1 collective-permute-done.32.refs_5_
  279.5 31.7 %shard_map.309 = (bf16[1024,2048]{1,0:T(8,128)(2,1)}, f32[1024,128]{1,0:T(8,128)}, bf16[1024,2048]{1,0:T(8,128)(2,1)}, bf16[1024,2048]{1,0:T(8,128)(2,1)}, bf16[...) custom-call(s32[5]{0:T(128)} %pad_add_fusion.refs_0_, ...), custom_call_target="tpu_custom_call", output_to_operand_aliasing={{0}: (24, {}), {1}: (25, {}), {2}: (26, {}), {3}: (27, {}),... | custom-call | flops 17179869184 | bytes 44040192 | tf_op jit(solution)/shard_map/pallas_call | solution.py:589
  311.3 8.6 %shard_map.311 = bf16[2048,1024]{1,0:T(8,128)(2,1)} custom-call(bf16[1024,2048]{1,0:T(8,128)(2,1)} %all-gather.2.cloned.1.call-done.refs_0_, bf16[1024,2048]{1,0:T(8,128)(2,1)} %get-tuple-element.111.refs_2_.refs_1_), custom_call_target="tpu_custom_call" | custom-call | flops 4294967296 | bytes 8388608 | tf_op jit(solution)/shard_map/pallas_call | solution.py:713
  322.0 8.5 %shard_map.312 = bf16[2048,1024]{1,0:T(8,128)(2,1)} custom-call(bf16[1024,2048]{1,0:T(8,128)(2,1)} %get-tuple-element.160.refs_0_, bf16[1024,2048]{1,0:T(8,128)(2,1)} %get-tuple-element.120.refs_1_), custom_call_target="tpu_custom_call" | custom-call | flops 4294967296 | bytes 8388608 | tf_op jit(solution)/shard_map/pallas_call | solution.py:713
  335.1 8.6 %shard_map.314 = bf16[2048,1024]{1,0:T(8,128)(2,1)} custom-call(bf16[1024,2048]{1,0:T(8,128)(2,1)} %get-tuple-element.160.refs_0_, bf16[1024,2048]{1,0:T(8,128)(2,1)} %get-tuple-element.126.refs_1_), custom_call_target="tpu_custom_call" | custom-call | flops 4294967296 | bytes 8388608 | tf_op jit(solution)/shard_map/pallas_call | solution.py:713
  343.7 2.4 collective-permute-done.35
  346.1 2.4 collective-permute-done.37
  358.0 3.3 all-to-all-start.1
  361.4 6.5 %shard_map.313 = bf16[2048,512]{1,0:T(8,128)(2,1)} custom-call(bf16[1024,2048]{1,0:T(8,128)(2,1)} %all-gather.2.cloned.1.call-done.refs_0_, bf16[1024,2048]{1,0:T(8,128)(2,1)} %get-tuple-element.111.refs_2_.refs_1_, bf16[2048,1024]{1,0:T(8,128)(2,1)} %collective-permute-done.40.refs_2_), custom_call_target="tpu_custom_call" | custom-call | flops 2147483648 | bytes 6291456 | tf_op jit(solution)/shard_map/pallas_call | solution.py:713
  374.0 6.5 %shard_map.315 = bf16[2048,512]{1,0:T(8,128)(2,1)} custom-call(bf16[1024,2048]{1,0:T(8,128)(2,1)} %get-tuple-element.160.refs_0_, bf16[1024,2048]{1,0:T(8,128)(2,1)} %get-tuple-element.120.refs_1_, bf16[2048,1024]{1,0:T(8,128)(2,1)} %collective-permute-done.43.refs_2_), custom_call_target="tpu_custom_call" | custom-call | flops 2147483648 | bytes 6291456 | tf_op jit(solution)/shard_map/pallas_call | solution.py:713
  380.5 2.4 collective-permute-done.41
  382.9 3.3 collective-permute-done.42
  386.2 2.9 multiply_reduce_fusion
  389.0 2.5 broadcast.211
  395.1 6.4 %shard_map.316 = bf16[2048,512]{1,0:T(8,128)(2,1)} custom-call(bf16[1024,2048]{1,0:T(8,128)(2,1)} %get-tuple-element.160.refs_0_, bf16[1024,2048]{1,0:T(8,128)(2,1)} %get-tuple-element.126.refs_1_, bf16[2048,1024]{1,0:T(8,128)(2,1)} %collective-permute-done.46.refs_2_), custom_call_target="tpu_custom_call" | custom-call | flops 2147483648 | bytes 6291456 | tf_op jit(solution)/shard_map/pallas_call | solution.py:713
  407.6 15.4 %shard_map.310 = bf16[1024,2048]{1,0:T(8,128)(2,1)} custom-call(s32[1]{0:T(128)} %constant.95.clone.1.refs_0_, s32[4]{0:T(128)} %gather_fusion.1, bf16[1024,2048]{1,0:T(8,128)(2,1)} %get-tuple-element.111.refs_2_.refs_1_, bf16[2,2048,1024]{2,1,0:T(8,128)(2,1)} %refs_3_.1), custom_call_target="tpu_custom_call" | custom-call | flops 8589934592 | bytes 8388608 | tf_op jit(solution)/shard_map/pallas_call | solution.py:664
  432.6 4.5 collective-permute-done.49
  446.3 4.3 convolution_convert_fusion.4.do_ref
  453.3 16.3 %shard_map.317 = (f32[1024,256]{1,0:T(8,128)}, f32[1024,256]{1,0:T(8,128)}, bf16[1024,256]{1,0:T(8,128)(2,1)}, f32[8,1024]{1,0:T(8,128)}, f32[2,256]{1,0:T(2,128)}) custom-call(s32[1]{0:T(128)} %dynamic_slice.85.length_ref, f32[1024,768]{1,0:T(8,128)} %get-tuple-element.93.qkv_ref, f32[8,1024]{1,0:T(8,128)} %add.353.squares_ref, f32[2,256]{1,0:T(2,128)} %copy.87.gain_ref, ...), custom_call_target="tpu_custom_call" | custom-call | flops 2684354560 | bytes 10485760 | tf_op jit(solution)/shard_map/pallas_call | solution.py:372
  470.3 3.5 fusion.51
  480.8 5.5 collective-permute-done.56
  486.9 9.7 %shard_map.318 = (bf16[1024,768]{1,0:T(8,128)(2,1)}, bf16[1024,2048]{1,0:T(8,128)(2,1)}) custom-call(f32[1024,256]{1,0:T(8,128)} %get-tuple-element.141.dq_ref, f32[1024,256]{1,0:T(8,128)} %get-tuple-element.142.dk_ref, bf16[1024,256]{1,0:T(8,128)(2,1)} %get-tuple-element.143.dv_ref, f32[1024,768]{1,0:T(8,128)} %get-tuple-element.93.qkv_ref, ...), custom_call_target="tpu_custom_call" | custom-call | flops 3221225472 | bytes 8388608 | tf_op jit(solution)/shard_map/pallas_call | solution.py:411
  500.1 2.9 convolution_convert_fusion.2
  503.0 4.5 collective-permute-done.57
  507.9 2.7 collective-permute-start.60
  514.9 6.0 collective-permute-done.62
  529.0 7.5 %shard_map.319 = f32[2,2048,256]{2,1,0:T(8,128)} custom-call(bf16[1024,2048]{1,0:T(8,128)(2,1)} %all-gather.2.cloned.1.call-done.refs_0_, bf16[1024,2048]{1,0:T(8,128)(2,1)} %get-tuple-element.111.refs_2_.refs_1_, bf16[2048,1024]{1,0:T(8,128)(2,1)} %collective-permute-done.40.refs_2_, bf16[2048,512]{1,0:T(8,128)(2,1)} %collective-permute-done.53.refs_3_), custom_call_target="tpu_custom_call" | custom-call | flops 2147483648 | bytes 6291456 | tf_op jit(solution)/shard_map/pallas_call | solution.py:713
  536.6 8.3 %collective-permute-done.61 = bf16[128,2048]{1,0:T(8,128)(2,1)S(1)} collective-permute-done((bf16[128,2048]{1,0:T(8,128)(2,1)}, bf16[128,2048]{1,0:T(8,128)(2,1)S(1)}, u32[]{:S(2)}, u32[]{:S(2)}) %collective-permute-start.61) | collective-permute-done | bytes 524320 | tf_op jit(solution)/shard_map/ppermute | solution.py:46
  544.9 10.0 %collective-permute-done.63 = bf16[128,2048]{1,0:T(8,128)(2,1)S(1)} collective-permute-done((bf16[128,2048]{1,0:T(8,128)(2,1)S(1)}, bf16[128,2048]{1,0:T(8,128)(2,1)S(1)}, u32[]{:S(2)}, u32[]{:S(2)}) %collective-permute-start.63) | collective-permute-done | bytes 524320 | tf_op jit(solution)/shard_map/ppermute | solution.py:49
  558.1 2.7 fusion.14
  562.9 2.6 collective-permute-done.64
  570.1 4.8 collective-permute-done.74
  576.9 3.7 add_convert_fusion
  580.6 2.9 collective-permute-done.70
  584.1 8.9 %collective-permute-done.71 = f32[20,2048]{1,0:T(8,128)S(1)} collective-permute-done((f32[20,2048]{1,0:T(8,128)S(1)}, f32[20,2048]{1,0:T(8,128)S(1)}, u32[]{:S(2)}, u32[]{:S(2)}) %collective-permute-start.71) | collective-permute-done | bytes 163872 | tf_op jit(solution)/shard_map/ppermute | solution.py:112
  593.7 8.6 %all-to-all-start.2 = ((bf16[8,64,768]{2,1,0:T(8,128)(2,1)}), bf16[8,64,768]{2,1,0:T(8,128)(2,1)S(1)}, u32[]{:S(2)}, u32[]{:S(2)}) async-start(bf16[8,64,768]{2,1,0:T(8,128)(2,1)} %bitcast.116), calls=%async_computation.3 | async-start | bytes 1572864 | tf_op jit(solution)/shard_map/all_to_all | solution.py:1039
  605.3 7.5 %shard_map.320 = f32[2,2048,256]{2,1,0:T(8,128)} custom-call(bf16[1024,2048]{1,0:T(8,128)(2,1)} %get-tuple-element.160.refs_0_, bf16[1024,2048]{1,0:T(8,128)(2,1)} %get-tuple-element.120.refs_1_, bf16[2048,1024]{1,0:T(8,128)(2,1)} %collective-permute-done.43.refs_2_, bf16[2048,512]{1,0:T(8,128)(2,1)} %collective-permute-done.59.refs_3_), custom_call_target="tpu_custom_call" | custom-call | flops 2147483648 | bytes 6291456 | tf_op jit(solution)/shard_map/pallas_call | solution.py:713
  612.9 3.9 collective-permute-start.77
  616.7 7.5 %shard_map.321 = f32[2,2048,256]{2,1,0:T(8,128)} custom-call(bf16[1024,2048]{1,0:T(8,128)(2,1)} %get-tuple-element.160.refs_0_, bf16[1024,2048]{1,0:T(8,128)(2,1)} %get-tuple-element.126.refs_1_, bf16[2048,1024]{1,0:T(8,128)(2,1)} %collective-permute-done.46.refs_2_, bf16[2048,512]{1,0:T(8,128)(2,1)} %collective-permute-done.78.refs_3_), custom_call_target="tpu_custom_call" | custom-call | flops 2147483648 | bytes 6291456 | tf_op jit(solution)/shard_map/pallas_call | solution.py:713
  (362 shorter events, 179.5 us)
Async XLA Ops:
  7.2 25.0 %collective-permute-start = (bf16[128,2048]{1,0:T(8,128)(2,1)}, bf16[128,2048]{1,0:T(8,128)(2,1)S(1)}, u32[]{:S(2)}, u32[]{:S(2)}) collective-permute-start(bf16[128,2048]{1,0:T(8,128)(2,1)} %param.19), channel_id=1, source_target_pairs={{2,4},{4,6},{6,7},{7,5},{5,3},{3,1},{1,0},{0,2},{10,12},{12,14},{1... | collective-permute-start | bytes 1572872 | tf_op jit(solution)/shard_map/ppermute | solution.py:46
  10.3 23.3 %collective-permute-start.1 = (bf16[128,2048]{1,0:T(8,128)(2,1)}, bf16[128,2048]{1,0:T(8,128)(2,1)S(1)}, u32[]{:S(2)}, u32[]{:S(2)}) collective-permute-start(bf16[128,2048]{1,0:T(8,128)(2,1)} %param.19), channel_id=1, source_target_pairs={{4,2},{6,4},{7,6},{5,7},{3,5},{1,3},{0,1},{2,0},{12,10},{14,12},{1... | collective-permute-start | bytes 1572872 | tf_op jit(solution)/shard_map/ppermute | solution.py:49
  16.5 44.9 %all-to-all-start = ((bf16[8,64,896]{2,1,0:T(8,128)(2,1)}), bf16[8,64,896]{2,1,0:T(8,128)(2,1)S(1)}, u32[]{:S(2)}, u32[]{:S(2)}) async-start(bf16[8,64,896]{2,1,0:T(8,128)(2,1)} %concatenate.34), calls=%async_computation | async-start | bytes 1835008 | tf_op jit(solution)/shard_map/all_to_all | solution.py:800
  22.7 161.2 %all-gather.2.cloned.1.call-start = ((), (), s32[]{:S(2)}) async-start(), calls=%async_computation.4 | async-start | bytes 4718592 | tf_op jit(solution)/shard_map/all_gather | solution.py:822
  22.8 60.4 %collective-permute-start.9 = (bf16[64,2048]{1,0:T(8,128)(2,1)}, bf16[64,2048]{1,0:T(8,128)(2,1)}, u32[]{:S(2)}, u32[]{:S(2)}) collective-permute-start(bf16[64,2048]{1,0:T(8,128)(2,1)} %param.25), channel_id=1, source_target_pairs={{0,0},{1,8},{2,16},{3,24},{4,1},{5,9},{6,17},{7,25},{8,2},{9,10},{... | collective-permute-start | bytes 786440 | tf_op jit(solution)/shard_map/ppermute | solution.py:805
  32.2 19.8 %collective-permute-start.2 = (bf16[128,2048]{1,0:T(8,128)(2,1)S(1)}, bf16[128,2048]{1,0:T(8,128)(2,1)}, u32[]{:S(2)}, u32[]{:S(2)}) collective-permute-start(bf16[128,2048]{1,0:T(8,128)(2,1)S(1)} %collective-permute-done), channel_id=1, source_target_pairs={{2,4},{4,6},{6,7},{7,5},{5,3},{3,1},{1,0},{0,2},{10,12},{12,14},{1... | collective-permute-start | bytes 1572872 | tf_op jit(solution)/shard_map/ppermute | solution.py:46
  33.6 25.5 %collective-permute-start.3 = (bf16[128,2048]{1,0:T(8,128)(2,1)S(1)}, bf16[128,2048]{1,0:T(8,128)(2,1)}, u32[]{:S(2)}, u32[]{:S(2)}) collective-permute-start(bf16[128,2048]{1,0:T(8,128)(2,1)S(1)} %collective-permute-done.1), channel_id=1, source_target_pairs={{4,2},{6,4},{7,6},{5,7},{3,5},{1,3},{0,1},{2,0},{12,10},{14,12},{1... | collective-permute-start | bytes 1572872 | tf_op jit(solution)/shard_map/ppermute | solution.py:49
  52.0 20.1 %collective-permute-start.4 = (bf16[128,2048]{1,0:T(8,128)(2,1)}, bf16[128,2048]{1,0:T(8,128)(2,1)S(1)}, u32[]{:S(2)}, u32[]{:S(2)}) collective-permute-start(bf16[128,2048]{1,0:T(8,128)(2,1)} %collective-permute-done.2), channel_id=1, source_target_pairs={{2,4},{4,6},{6,7},{7,5},{5,3},{3,1},{1,0},{0,2},{10,12},{12,14},{1... | collective-permute-start | bytes 1572872 | tf_op jit(solution)/shard_map/ppermute | solution.py:46
  59.1 20.1 %collective-permute-start.5 = (bf16[128,2048]{1,0:T(8,128)(2,1)}, bf16[128,2048]{1,0:T(8,128)(2,1)S(1)}, u32[]{:S(2)}, u32[]{:S(2)}) collective-permute-start(bf16[128,2048]{1,0:T(8,128)(2,1)} %collective-permute-done.3), channel_id=1, source_target_pairs={{4,2},{6,4},{7,6},{5,7},{3,5},{1,3},{0,1},{2,0},{12,10},{14,12},{1... | collective-permute-start | bytes 1572872 | tf_op jit(solution)/shard_map/ppermute | solution.py:49
  61.4 26.5 %collective-permute-start.8 = (bf16[512,896]{1,0:T(8,128)(2,1)S(1)}, bf16[512,896]{1,0:T(8,128)(2,1)S(1)}, u32[]{:S(2)}, u32[]{:S(2)}) collective-permute-start(bf16[512,896]{1,0:T(8,128)(2,1)S(1)} %bitcast.102), channel_id=1, source_target_pairs={{0,16},{8,24},{16,0},{24,8},{1,17},{9,25},{17,1},{25,9},{2,18},{10... | collective-permute-start | bytes 2752520 | tf_op jit(solution)/shard_map/ppermute | solution.py:132
  110.0 14.4 %collective-permute-start.15 = (bf16[64,2048]{1,0:T(8,128)(2,1)}, bf16[64,2048]{1,0:T(8,128)(2,1)S(1)}, u32[]{:S(2)}, u32[]{:S(2)}) collective-permute-start(bf16[64,2048]{1,0:T(8,128)(2,1)} %collective-permute-done.9), channel_id=1, source_target_pairs={{0,16},{8,24},{16,0},{24,8},{1,17},{9,25},{17,1},{25,9},{2,18},{10... | collective-permute-start | bytes 786440 | tf_op jit(solution)/shard_map/ppermute | solution.py:132
  110.6 23.4 %collective-permute-start.16 = (bf16[64,2048]{1,0:T(8,128)(2,1)}, bf16[64,2048]{1,0:T(8,128)(2,1)S(1)}, u32[]{:S(2)}, u32[]{:S(2)}) collective-permute-start(bf16[64,2048]{1,0:T(8,128)(2,1)} %collective-permute-done.9), channel_id=1, source_target_pairs={{0,8},{8,0},{16,24},{24,16},{1,9},{9,1},{17,25},{25,17},{2,10},{10... | collective-permute-start | bytes 786440 | tf_op jit(solution)/shard_map/ppermute | solution.py:139
  124.4 9.7 %collective-permute-start.17 = (bf16[64,2048]{1,0:T(8,128)(2,1)S(1)}, bf16[64,2048]{1,0:T(8,128)(2,1)S(1)}, u32[]{:S(2)}, u32[]{:S(2)}) collective-permute-start(bf16[64,2048]{1,0:T(8,128)(2,1)S(1)} %collective-permute-done.15), channel_id=1, source_target_pairs={{0,8},{8,0},{16,24},{24,16},{1,9},{9,1},{17,25},{25,17},{2,10},{10... | collective-permute-start | bytes 786440 | tf_op jit(solution)/shard_map/ppermute | solution.py:139
  135.4 20.6 %collective-permute-start.21 = (bf16[64,2048]{1,0:T(8,128)(2,1)S(1)}, bf16[64,2048]{1,0:T(8,128)(2,1)S(1)}, u32[]{:S(2)}, u32[]{:S(2)}) collective-permute-start(bf16[64,2048]{1,0:T(8,128)(2,1)S(1)} %get-tuple-element.205), channel_id=1, source_target_pairs={{4,2},{6,4},{7,6},{5,7},{3,5},{1,3},{0,1},{2,0},{12,10},{14,12},{1... | collective-permute-start | bytes 786440 | tf_op jit(solution)/shard_map/ppermute | solution.py:49
  137.0 19.0 %collective-permute-start.18 = (bf16[64,2048]{1,0:T(8,128)(2,1)S(1)}, bf16[64,2048]{1,0:T(8,128)(2,1)S(1)}, u32[]{:S(2)}, u32[]{:S(2)}) collective-permute-start(bf16[64,2048]{1,0:T(8,128)(2,1)S(1)} %get-tuple-element.206), channel_id=1, source_target_pairs={{2,4},{4,6},{6,7},{7,5},{5,3},{3,1},{1,0},{0,2},{10,12},{12,14},{1... | collective-permute-start | bytes 786440 | tf_op jit(solution)/shard_map/ppermute | solution.py:46
  156.1 22.3 %collective-permute-start.22 = (bf16[128,2048]{1,0:T(8,128)(2,1)S(1)}, bf16[128,2048]{1,0:T(8,128)(2,1)}, u32[]{:S(2)}, u32[]{:S(2)}) collective-permute-start(bf16[128,2048]{1,0:T(8,128)(2,1)S(1)} %pad_maximum_fusion.3), channel_id=1, source_target_pairs={{4,2},{6,4},{7,6},{5,7},{3,5},{1,3},{0,1},{2,0},{12,10},{14,12},{1... | collective-permute-start | bytes 1572872 | tf_op jit(solution)/shard_map/ppermute | solution.py:49
  158.5 20.6 %collective-permute-start.19 = (bf16[128,2048]{1,0:T(8,128)(2,1)}, bf16[128,2048]{1,0:T(8,128)(2,1)}, u32[]{:S(2)}, u32[]{:S(2)}) collective-permute-start(bf16[128,2048]{1,0:T(8,128)(2,1)} %pad_maximum_fusion.2), channel_id=1, source_target_pairs={{2,4},{4,6},{6,7},{7,5},{5,3},{3,1},{1,0},{0,2},{10,12},{12,14},{1... | collective-permute-start | bytes 1572872 | tf_op jit(solution)/shard_map/ppermute | solution.py:46
  181.0 13.5 %collective-permute-start.20 = (bf16[128,2048]{1,0:T(8,128)(2,1)S(1)}, bf16[128,2048]{1,0:T(8,128)(2,1)S(1)}, u32[]{:S(2)}, u32[]{:S(2)}) collective-permute-start(bf16[128,2048]{1,0:T(8,128)(2,1)S(1)} %get-tuple-element.188), channel_id=1, source_target_pairs={{2,4},{4,6},{6,7},{7,5},{5,3},{3,1},{1,0},{0,2},{10,12},{12,14},{1... | collective-permute-start | bytes 1572872 | tf_op jit(solution)/shard_map/ppermute | solution.py:46
  183.5 13.7 %collective-permute-start.23 = (bf16[128,2048]{1,0:T(8,128)(2,1)S(1)}, bf16[128,2048]{1,0:T(8,128)(2,1)}, u32[]{:S(2)}, u32[]{:S(2)}) collective-permute-start(bf16[128,2048]{1,0:T(8,128)(2,1)S(1)} %get-tuple-element.187), channel_id=1, source_target_pairs={{4,2},{6,4},{7,6},{5,7},{3,5},{1,3},{0,1},{2,0},{12,10},{14,12},{1... | collective-permute-start | bytes 1572872 | tf_op jit(solution)/shard_map/ppermute | solution.py:49
  198.9 12.3 %collective-permute-start.24 = (bf16[128,2048]{1,0:T(8,128)(2,1)S(1)}, bf16[128,2048]{1,0:T(8,128)(2,1)S(1)}, u32[]{:S(2)}, u32[]{:S(2)}) collective-permute-start(bf16[128,2048]{1,0:T(8,128)(2,1)S(1)} %get-tuple-element.186), channel_id=1, source_target_pairs={{2,4},{4,6},{6,7},{7,5},{5,3},{3,1},{1,0},{0,2},{10,12},{12,14},{1... | collective-permute-start | bytes 1572872 | tf_op jit(solution)/shard_map/ppermute | solution.py:46
  199.3 12.0 %collective-permute-start.25 = (bf16[128,2048]{1,0:T(8,128)(2,1)S(1)}, bf16[128,2048]{1,0:T(8,128)(2,1)S(1)}, u32[]{:S(2)}, u32[]{:S(2)}) collective-permute-start(bf16[128,2048]{1,0:T(8,128)(2,1)S(1)} %get-tuple-element.185), channel_id=1, source_target_pairs={{4,2},{6,4},{7,6},{5,7},{3,5},{1,3},{0,1},{2,0},{12,10},{14,12},{1... | collective-permute-start | bytes 1572872 | tf_op jit(solution)/shard_map/ppermute | solution.py:49
  212.9 11.9 %collective-permute-start.28 = (bf16[128,2048]{1,0:T(8,128)(2,1)S(1)}, bf16[128,2048]{1,0:T(8,128)(2,1)}, u32[]{:S(2)}, u32[]{:S(2)}) collective-permute-start(bf16[128,2048]{1,0:T(8,128)(2,1)S(1)} %multiply_convert_fusion.refs_2_), channel_id=1, source_target_pairs={{2,4},{4,6},{6,7},{7,5},{5,3},{3,1},{1,0},{0,2},{10,12},{12,14},{1... | collective-permute-start | bytes 1572872 | tf_op jit(solution)/shard_map/ppermute | solution.py:46
  214.4 11.9 %collective-permute-start.26 = (bf16[128,2048]{1,0:T(8,128)(2,1)S(1)}, bf16[128,2048]{1,0:T(8,128)(2,1)}, u32[]{:S(2)}, u32[]{:S(2)}) collective-permute-start(bf16[128,2048]{1,0:T(8,128)(2,1)S(1)} %multiply_convert_fusion.refs_2_), channel_id=1, source_target_pairs={{4,2},{6,4},{7,6},{5,7},{3,5},{1,3},{0,1},{2,0},{12,10},{14,12},{1... | collective-permute-start | bytes 1572872 | tf_op jit(solution)/shard_map/ppermute | solution.py:49
  224.9 12.1 %collective-permute-start.29 = (bf16[128,2048]{1,0:T(8,128)(2,1)}, bf16[128,2048]{1,0:T(8,128)(2,1)}, u32[]{:S(2)}, u32[]{:S(2)}) collective-permute-start(bf16[128,2048]{1,0:T(8,128)(2,1)} %collective-permute-done.28.refs_3_), channel_id=1, source_target_pairs={{2,4},{4,6},{6,7},{7,5},{5,3},{3,1},{1,0},{0,2},{10,12},{12,14},{1... | collective-permute-start | bytes 1572872 | tf_op jit(solution)/shard_map/ppermute | solution.py:46
  226.3 12.1 %collective-permute-start.27 = (bf16[128,2048]{1,0:T(8,128)(2,1)}, bf16[128,2048]{1,0:T(8,128)(2,1)}, u32[]{:S(2)}, u32[]{:S(2)}) collective-permute-start(bf16[128,2048]{1,0:T(8,128)(2,1)} %collective-permute-done.26.refs_4_), channel_id=1, source_target_pairs={{4,2},{6,4},{7,6},{5,7},{3,5},{1,3},{0,1},{2,0},{12,10},{14,12},{1... | collective-permute-start | bytes 1572872 | tf_op jit(solution)/shard_map/ppermute | solution.py:49
  237.0 33.7 %collective-permute-start.30 = (bf16[128,2048]{1,0:T(8,128)(2,1)}, bf16[128,2048]{1,0:T(8,128)(2,1)S(1)}, u32[]{:S(2)}, u32[]{:S(2)}) collective-permute-start(bf16[128,2048]{1,0:T(8,128)(2,1)} %collective-permute-done.29.refs_5_), channel_id=1, source_target_pairs={{2,4},{4,6},{6,7},{7,5},{5,3},{3,1},{1,0},{0,2},{10,12},{12,14},{1... | collective-permute-start | bytes 1572872 | tf_op jit(solution)/shard_map/ppermute | solution.py:46
  238.4 32.2 %collective-permute-start.31 = (bf16[128,2048]{1,0:T(8,128)(2,1)}, bf16[128,2048]{1,0:T(8,128)(2,1)S(1)}, u32[]{:S(2)}, u32[]{:S(2)}) collective-permute-start(bf16[128,2048]{1,0:T(8,128)(2,1)} %collective-permute-done.27.refs_2_), channel_id=1, source_target_pairs={{4,2},{6,4},{7,6},{5,7},{3,5},{1,3},{0,1},{2,0},{12,10},{14,12},{1... | collective-permute-start | bytes 1572872 | tf_op jit(solution)/shard_map/ppermute | solution.py:49
  319.8 41.6 %collective-permute-start.40 = (bf16[2048,1024]{1,0:T(8,128)(2,1)}, bf16[2048,1024]{1,0:T(8,128)(2,1)}, u32[]{:S(2)}, u32[]{:S(2)}) collective-permute-start(bf16[2048,1024]{1,0:T(8,128)(2,1)} %shard_map.311), channel_id=1, source_target_pairs={{0,8},{8,0},{16,24},{24,16},{1,9},{9,1},{17,25},{25,17},{2,10},{10... | collective-permute-start | bytes 12582920 | tf_op jit(solution)/shard_map/ppermute | solution.py:905
  319.9 10.6 %collective-permute-start.34 = (bf16[64,2048]{1,0:T(8,128)(2,1)S(1)}, bf16[64,2048]{1,0:T(8,128)(2,1)S(1)}, u32[]{:S(2)}, u32[]{:S(2)}) collective-permute-start(bf16[64,2048]{1,0:T(8,128)(2,1)S(1)} %get-tuple-element.204), channel_id=1, source_target_pairs={{2,4},{4,6},{6,7},{7,5},{5,3},{3,1},{1,0},{0,2},{10,12},{12,14},{1... | collective-permute-start | bytes 786440 | tf_op jit(solution)/shard_map/ppermute | solution.py:46
  321.7 11.5 %collective-permute-start.36 = (bf16[64,2048]{1,0:T(8,128)(2,1)S(1)}, bf16[64,2048]{1,0:T(8,128)(2,1)S(1)}, u32[]{:S(2)}, u32[]{:S(2)}) collective-permute-start(bf16[64,2048]{1,0:T(8,128)(2,1)S(1)} %get-tuple-element.203), channel_id=1, source_target_pairs={{4,2},{6,4},{7,6},{5,7},{3,5},{1,3},{0,1},{2,0},{12,10},{14,12},{1... | collective-permute-start | bytes 786440 | tf_op jit(solution)/shard_map/ppermute | solution.py:49
  330.5 43.5 %collective-permute-start.43 = (bf16[2048,1024]{1,0:T(8,128)(2,1)}, bf16[2048,1024]{1,0:T(8,128)(2,1)}, u32[]{:S(2)}, u32[]{:S(2)}) collective-permute-start(bf16[2048,1024]{1,0:T(8,128)(2,1)} %shard_map.312), channel_id=1, source_target_pairs={{0,8},{8,0},{16,24},{24,16},{1,9},{9,1},{17,25},{25,17},{2,10},{10... | collective-permute-start | bytes 12582920 | tf_op jit(solution)/shard_map/ppermute | solution.py:905
  331.4 14.6 %collective-permute-start.35 = (bf16[128,2048]{1,0:T(8,128)(2,1)}, bf16[128,2048]{1,0:T(8,128)(2,1)}, u32[]{:S(2)}, u32[]{:S(2)}) collective-permute-start(bf16[128,2048]{1,0:T(8,128)(2,1)} %pad_maximum_fusion.4), channel_id=1, source_target_pairs={{2,4},{4,6},{6,7},{7,5},{5,3},{3,1},{1,0},{0,2},{10,12},{12,14},{1... | collective-permute-start | bytes 1572872 | tf_op jit(solution)/shard_map/ppermute | solution.py:46
  334.1 14.4 %collective-permute-start.37 = (bf16[128,2048]{1,0:T(8,128)(2,1)}, bf16[128,2048]{1,0:T(8,128)(2,1)}, u32[]{:S(2)}, u32[]{:S(2)}) collective-permute-start(bf16[128,2048]{1,0:T(8,128)(2,1)} %pad_maximum_fusion.5), channel_id=1, source_target_pairs={{4,2},{6,4},{7,6},{5,7},{3,5},{1,3},{0,1},{2,0},{12,10},{14,12},{1... | collective-permute-start | bytes 1572872 | tf_op jit(solution)/shard_map/ppermute | solution.py:49
  343.7 51.5 %collective-permute-start.46 = (bf16[2048,1024]{1,0:T(8,128)(2,1)}, bf16[2048,1024]{1,0:T(8,128)(2,1)}, u32[]{:S(2)}, u32[]{:S(2)}) collective-permute-start(bf16[2048,1024]{1,0:T(8,128)(2,1)} %shard_map.314), channel_id=1, source_target_pairs={{0,8},{8,0},{16,24},{24,16},{1,9},{9,1},{17,25},{25,17},{2,10},{10... | collective-permute-start | bytes 12582920 | tf_op jit(solution)/shard_map/ppermute | solution.py:905
  350.5 17.5 %collective-permute-start.38 = (bf16[128,2048]{1,0:T(8,128)(2,1)}, bf16[128,2048]{1,0:T(8,128)(2,1)}, u32[]{:S(2)}, u32[]{:S(2)}) collective-permute-start(bf16[128,2048]{1,0:T(8,128)(2,1)} %add_convert_fusion.9), channel_id=1, source_target_pairs={{2,4},{4,6},{6,7},{7,5},{5,3},{3,1},{1,0},{0,2},{10,12},{12,14},{1... | collective-permute-start | bytes 1572872 | tf_op jit(solution)/shard_map/ppermute | solution.py:46
  353.9 14.1 %collective-permute-start.39 = (bf16[128,2048]{1,0:T(8,128)(2,1)}, bf16[128,2048]{1,0:T(8,128)(2,1)}, u32[]{:S(2)}, u32[]{:S(2)}) collective-permute-start(bf16[128,2048]{1,0:T(8,128)(2,1)} %add_convert_fusion.8), channel_id=1, source_target_pairs={{4,2},{6,4},{7,6},{5,7},{3,5},{1,3},{0,1},{2,0},{12,10},{14,12},{1... | collective-permute-start | bytes 1572872 | tf_op jit(solution)/shard_map/ppermute | solution.py:49
  358.0 15.9 %all-to-all-start.1 = ((f32[8,2,128]{2,1,0:T(2,128)}), f32[8,2,128]{2,1,0:T(2,128)S(1)}, u32[]{:S(2)}, u32[]{:S(2)}) async-start(f32[8,2,128]{2,1,0:T(2,128)} %bitcast.28), calls=%async_computation.1 | async-start | bytes 16384 | tf_op jit(solution)/shard_map/all_to_all | solution.py:895
  361.3 196.7 %reduce-scatter.2.cloned.1.call-start = ((), (), s32[]{:S(2)}) async-start(), calls=%async_computation.5 | async-start | bytes 4718592 | tf_op jit(solution)/shard_map/reduce_scatter | solution.py:975
  369.9 13.0 %collective-permute-start.41 = (bf16[128,2048]{1,0:T(8,128)(2,1)}, bf16[128,2048]{1,0:T(8,128)(2,1)}, u32[]{:S(2)}, u32[]{:S(2)}) collective-permute-start(bf16[128,2048]{1,0:T(8,128)(2,1)} %add_convert_fusion.7), channel_id=1, source_target_pairs={{2,4},{4,6},{6,7},{7,5},{5,3},{3,1},{1,0},{0,2},{10,12},{12,14},{1... | collective-permute-start | bytes 1572872 | tf_op jit(solution)/shard_map/ppermute | solution.py:46
  373.7 12.4 %collective-permute-start.42 = (bf16[128,2048]{1,0:T(8,128)(2,1)}, bf16[128,2048]{1,0:T(8,128)(2,1)}, u32[]{:S(2)}, u32[]{:S(2)}) collective-permute-start(bf16[128,2048]{1,0:T(8,128)(2,1)} %add_convert_fusion.6), channel_id=1, source_target_pairs={{4,2},{6,4},{7,6},{5,7},{3,5},{1,3},{0,1},{2,0},{12,10},{14,12},{1... | collective-permute-start | bytes 1572872 | tf_op jit(solution)/shard_map/ppermute | solution.py:49
  393.1 11.3 %collective-permute-start.44 = (bf16[128,2048]{1,0:T(8,128)(2,1)S(1)}, bf16[128,2048]{1,0:T(8,128)(2,1)}, u32[]{:S(2)}, u32[]{:S(2)}) collective-permute-start(bf16[128,2048]{1,0:T(8,128)(2,1)S(1)} %get-tuple-element.171), channel_id=1, source_target_pairs={{2,4},{4,6},{6,7},{7,5},{5,3},{3,1},{1,0},{0,2},{10,12},{12,14},{1... | collective-permute-start | bytes 1572872 | tf_op jit(solution)/shard_map/ppermute | solution.py:46
  394.6 11.0 %collective-permute-start.45 = (bf16[128,2048]{1,0:T(8,128)(2,1)S(1)}, bf16[128,2048]{1,0:T(8,128)(2,1)}, u32[]{:S(2)}, u32[]{:S(2)}) collective-permute-start(bf16[128,2048]{1,0:T(8,128)(2,1)S(1)} %get-tuple-element.171), channel_id=1, source_target_pairs={{4,2},{6,4},{7,6},{5,7},{3,5},{1,3},{0,1},{2,0},{12,10},{14,12},{1... | collective-permute-start | bytes 1572872 | tf_op jit(solution)/shard_map/ppermute | solution.py:49
  401.6 44.7 %collective-permute-start.53 = (bf16[2048,512]{1,0:T(8,128)(2,1)}, bf16[2048,512]{1,0:T(8,128)(2,1)}, u32[]{:S(2)}, u32[]{:S(2)}) collective-permute-start(bf16[2048,512]{1,0:T(8,128)(2,1)} %shard_map.313), channel_id=1, source_target_pairs={{0,16},{8,24},{16,0},{24,8},{1,17},{9,25},{17,1},{25,9},{2,18},{10... | collective-permute-start | bytes 6291464 | tf_op jit(solution)/shard_map/ppermute | solution.py:926
  405.6 19.3 %collective-permute-start.47 = (bf16[128,2048]{1,0:T(8,128)(2,1)}, bf16[128,2048]{1,0:T(8,128)(2,1)}, u32[]{:S(2)}, u32[]{:S(2)}) collective-permute-start(bf16[128,2048]{1,0:T(8,128)(2,1)} %collective-permute-done.44), channel_id=1, source_target_pairs={{2,4},{4,6},{6,7},{7,5},{5,3},{3,1},{1,0},{0,2},{10,12},{12,14},{1... | collective-permute-start | bytes 1572872 | tf_op jit(solution)/shard_map/ppermute | solution.py:46
  407.1 17.8 %collective-permute-start.48 = (bf16[128,2048]{1,0:T(8,128)(2,1)}, bf16[128,2048]{1,0:T(8,128)(2,1)}, u32[]{:S(2)}, u32[]{:S(2)}) collective-permute-start(bf16[128,2048]{1,0:T(8,128)(2,1)} %collective-permute-done.45), channel_id=1, source_target_pairs={{4,2},{6,4},{7,6},{5,7},{3,5},{1,3},{0,1},{2,0},{12,10},{14,12},{1... | collective-permute-start | bytes 1572872 | tf_op jit(solution)/shard_map/ppermute | solution.py:49
  424.9 12.1 %collective-permute-start.49 = (bf16[128,2048]{1,0:T(8,128)(2,1)}, bf16[128,2048]{1,0:T(8,128)(2,1)S(1)}, u32[]{:S(2)}, u32[]{:S(2)}) collective-permute-start(bf16[128,2048]{1,0:T(8,128)(2,1)} %collective-permute-done.47), channel_id=1, source_target_pairs={{2,4},{4,6},{6,7},{7,5},{5,3},{3,1},{1,0},{0,2},{10,12},{12,14},{1... | collective-permute-start | bytes 1572872 | tf_op jit(solution)/shard_map/ppermute | solution.py:46
  426.4 12.2 %collective-permute-start.50 = (bf16[128,2048]{1,0:T(8,128)(2,1)}, bf16[128,2048]{1,0:T(8,128)(2,1)S(1)}, u32[]{:S(2)}, u32[]{:S(2)}) collective-permute-start(bf16[128,2048]{1,0:T(8,128)(2,1)} %collective-permute-done.48), channel_id=1, source_target_pairs={{4,2},{6,4},{7,6},{5,7},{3,5},{1,3},{0,1},{2,0},{12,10},{14,12},{1... | collective-permute-start | bytes 1572872 | tf_op jit(solution)/shard_map/ppermute | solution.py:49
  450.6 57.0 %collective-permute-start.59 = (bf16[2048,512]{1,0:T(8,128)(2,1)}, bf16[2048,512]{1,0:T(8,128)(2,1)}, u32[]{:S(2)}, u32[]{:S(2)}) collective-permute-start(bf16[2048,512]{1,0:T(8,128)(2,1)} %shard_map.315), channel_id=1, source_target_pairs={{0,16},{8,24},{16,0},{24,8},{1,17},{9,25},{17,1},{25,9},{2,18},{10... | collective-permute-start | bytes 6291464 | tf_op jit(solution)/shard_map/ppermute | solution.py:926
  476.7 35.9 %collective-permute-start.73 = (bf16[64,2048]{1,0:T(8,128)(2,1)S(1)}, bf16[64,2048]{1,0:T(8,128)(2,1)S(1)}, u32[]{:S(2)}, u32[]{:S(2)}) collective-permute-start(bf16[64,2048]{1,0:T(8,128)(2,1)S(1)} %get-tuple-element.196), channel_id=1, source_target_pairs={{0,8},{8,0},{16,24},{24,16},{1,9},{9,1},{17,25},{25,17},{2,10},{10... | collective-permute-start | bytes 786440 | tf_op jit(solution)/shard_map/ppermute | solution.py:155
  476.7 92.3 %collective-permute-start.72 = (bf16[64,2048]{1,0:T(8,128)(2,1)}, bf16[64,2048]{1,0:T(8,128)(2,1)S(1)}, u32[]{:S(2)}, u32[]{:S(2)}) collective-permute-start(bf16[64,2048]{1,0:T(8,128)(2,1)} %get-tuple-element.195), channel_id=1, source_target_pairs={{0,8},{8,0},{16,24},{24,16},{1,9},{9,1},{17,25},{25,17},{2,10},{10... | collective-permute-start | bytes 786440 | tf_op jit(solution)/shard_map/ppermute | solution.py:155
  498.0 9.5 %collective-permute-start.57 = (bf16[64,2048]{1,0:T(8,128)(2,1)S(1)}, bf16[64,2048]{1,0:T(8,128)(2,1)S(1)}, u32[]{:S(2)}, u32[]{:S(2)}) collective-permute-start(bf16[64,2048]{1,0:T(8,128)(2,1)S(1)} %get-tuple-element.180), channel_id=1, source_target_pairs={{2,4},{4,6},{6,7},{7,5},{5,3},{3,1},{1,0},{0,2},{10,12},{12,14},{1... | collective-permute-start | bytes 786440 | tf_op jit(solution)/shard_map/ppermute | solution.py:46
  507.8 13.1 %collective-permute-start.62 = (bf16[128,2048]{1,0:T(8,128)(2,1)S(1)}, bf16[128,2048]{1,0:T(8,128)(2,1)S(1)}, u32[]{:S(2)}, u32[]{:S(2)}) collective-permute-start(bf16[128,2048]{1,0:T(8,128)(2,1)S(1)} %pad_maximum_fusion.7), channel_id=1, source_target_pairs={{4,2},{6,4},{7,6},{5,7},{3,5},{1,3},{0,1},{2,0},{12,10},{14,12},{1... | collective-permute-start | bytes 1572872 | tf_op jit(solution)/shard_map/ppermute | solution.py:49
  507.9 14.7 %collective-permute-start.60 = (bf16[128,2048]{1,0:T(8,128)(2,1)S(1)}, bf16[128,2048]{1,0:T(8,128)(2,1)S(1)}, u32[]{:S(2)}, u32[]{:S(2)}) collective-permute-start(bf16[128,2048]{1,0:T(8,128)(2,1)S(1)} %pad_maximum_fusion.6), channel_id=1, source_target_pairs={{2,4},{4,6},{6,7},{7,5},{5,3},{3,1},{1,0},{0,2},{10,12},{12,14},{1... | collective-permute-start | bytes 1572872 | tf_op jit(solution)/shard_map/ppermute | solution.py:46
  512.6 13.2 %collective-permute-start.67 = (bf16[512,768]{1,0:T(8,128)(2,1)S(1)}, bf16[512,768]{1,0:T(8,128)(2,1)S(1)}, u32[]{:S(2)}, u32[]{:S(2)}) collective-permute-start(bf16[512,768]{1,0:T(8,128)(2,1)S(1)} %convolution_convert_fusion.2), channel_id=1, source_target_pairs={{0,8},{8,0},{16,24},{24,16},{1,9},{9,1},{17,25},{25,17},{2,10},{10... | collective-permute-start | bytes 2359304 | tf_op jit(solution)/shard_map/ppermute | solution.py:155
  512.6 64.3 %collective-permute-start.66 = (bf16[512,768]{1,0:T(8,128)(2,1)}, bf16[512,768]{1,0:T(8,128)(2,1)}, u32[]{:S(2)}, u32[]{:S(2)}) collective-permute-start(bf16[512,768]{1,0:T(8,128)(2,1)} %convolution_convert_fusion.3), channel_id=1, source_target_pairs={{0,8},{8,0},{16,24},{24,16},{1,9},{9,1},{17,25},{25,17},{2,10},{10... | collective-permute-start | bytes 2359304 | tf_op jit(solution)/shard_map/ppermute | solution.py:155
  523.7 21.1 %collective-permute-start.61 = (bf16[128,2048]{1,0:T(8,128)(2,1)}, bf16[128,2048]{1,0:T(8,128)(2,1)S(1)}, u32[]{:S(2)}, u32[]{:S(2)}) collective-permute-start(bf16[128,2048]{1,0:T(8,128)(2,1)} %get-tuple-element.178), channel_id=1, source_target_pairs={{2,4},{4,6},{6,7},{7,5},{5,3},{3,1},{1,0},{0,2},{10,12},{12,14},{1... | collective-permute-start | bytes 1572872 | tf_op jit(solution)/shard_map/ppermute | solution.py:46
  523.7 31.1 %collective-permute-start.63 = (bf16[128,2048]{1,0:T(8,128)(2,1)S(1)}, bf16[128,2048]{1,0:T(8,128)(2,1)S(1)}, u32[]{:S(2)}, u32[]{:S(2)}) collective-permute-start(bf16[128,2048]{1,0:T(8,128)(2,1)S(1)} %get-tuple-element.177), channel_id=1, source_target_pairs={{4,2},{6,4},{7,6},{5,7},{3,5},{1,3},{0,1},{2,0},{12,10},{14,12},{1... | collective-permute-start | bytes 1572872 | tf_op jit(solution)/shard_map/ppermute | solution.py:49
  527.7 49.2 %collective-permute-start.68 = (bf16[512,768]{1,0:T(8,128)(2,1)}, bf16[512,768]{1,0:T(8,128)(2,1)}, u32[]{:S(2)}, u32[]{:S(2)}) collective-permute-start(bf16[512,768]{1,0:T(8,128)(2,1)} %add_convert_fusion.1), channel_id=1, source_target_pairs={{0,16},{8,24},{16,0},{24,8},{1,17},{9,25},{17,1},{25,9},{2,18},{10... | collective-permute-start | bytes 2359304 | tf_op jit(solution)/shard_map/ppermute | solution.py:159
  556.1 10.2 %collective-permute-start.65 = (bf16[128,2048]{1,0:T(8,128)(2,1)S(1)}, bf16[128,2048]{1,0:T(8,128)(2,1)S(1)}, u32[]{:S(2)}, u32[]{:S(2)}) collective-permute-start(bf16[128,2048]{1,0:T(8,128)(2,1)S(1)} %get-tuple-element.175), channel_id=1, source_target_pairs={{4,2},{6,4},{7,6},{5,7},{3,5},{1,3},{0,1},{2,0},{12,10},{14,12},{1... | collective-permute-start | bytes 1572872 | tf_op jit(solution)/shard_map/ppermute | solution.py:49
  565.5 9.5 %collective-permute-start.74 = (bf16[64,2048]{1,0:T(8,128)(2,1)}, bf16[64,2048]{1,0:T(8,128)(2,1)S(1)}, u32[]{:S(2)}, u32[]{:S(2)}) collective-permute-start(bf16[64,2048]{1,0:T(8,128)(2,1)} %add_convert_fusion.15), channel_id=1, source_target_pairs={{0,16},{8,24},{16,0},{24,8},{1,17},{9,25},{17,1},{25,9},{2,18},{10... | collective-permute-start | bytes 786440 | tf_op jit(solution)/shard_map/ppermute | solution.py:159
  566.3 50.4 %collective-permute-start.78 = (bf16[2048,512]{1,0:T(8,128)(2,1)}, bf16[2048,512]{1,0:T(8,128)(2,1)}, u32[]{:S(2)}, u32[]{:S(2)}) collective-permute-start(bf16[2048,512]{1,0:T(8,128)(2,1)} %shard_map.316), channel_id=1, source_target_pairs={{0,16},{8,24},{16,0},{24,8},{1,17},{9,25},{17,1},{25,9},{2,18},{10... | collective-permute-start | bytes 6291464 | tf_op jit(solution)/shard_map/ppermute | solution.py:926
  593.7 34.7 %all-to-all-start.2 = ((bf16[8,64,768]{2,1,0:T(8,128)(2,1)}), bf16[8,64,768]{2,1,0:T(8,128)(2,1)S(1)}, u32[]{:S(2)}, u32[]{:S(2)}) async-start(bf16[8,64,768]{2,1,0:T(8,128)(2,1)} %bitcast.116), calls=%async_computation.3 | async-start | bytes 1572864 | tf_op jit(solution)/shard_map/all_to_all | solution.py:1039
  603.5 20.7 %collective-permute-start.75 = (bf16[64,2048]{1,0:T(8,128)(2,1)}, bf16[64,2048]{1,0:T(8,128)(2,1)S(1)}, u32[]{:S(2)}, u32[]{:S(2)}) collective-permute-start(bf16[64,2048]{1,0:T(8,128)(2,1)} %add_convert_fusion.14), channel_id=1, source_target_pairs={{0,0},{8,1},{16,2},{24,3},{1,4},{9,5},{17,6},{25,7},{2,8},{10,9},{... | collective-permute-start | bytes 786440 | tf_op jit(solution)/shard_map/ppermute | solution.py:1061
  612.9 12.2 %collective-permute-start.77 = (f32[20,2048]{1,0:T(8,128)S(1)}, f32[20,2048]{1,0:T(8,128)S(1)}, u32[]{:S(2)}, u32[]{:S(2)}) collective-permute-start(f32[20,2048]{1,0:T(8,128)S(1)} %add.407), channel_id=1, source_target_pairs={{0,16},{8,24},{16,0},{24,8},{1,17},{9,25},{17,1},{25,9},{2,18},{10... | collective-permute-start | bytes 491528 | tf_op jit(solution)/shard_map/ppermute | solution.py:120
  (63 other events, 625.3 us)
Sparse Core Ops, SparseCore 0:
  89.4 87.4 all-gather.1
  450.7 104.1 reduce-scatter.1
